TPU v7x, 32 devices: a whole 2x2x4 slice. The times are simulated.
32 devices in a mesh: tract: 2 (over x), sky: 8 (over z, y), visit: 2 (over core).
Axes of the slice: x: 2, y: 2, z: 4, core: 2. Of those that a mesh axis runs over, the one named last changes fastest.
Arguments:
- warps: bfloat16 [16, 256, 4096], P(('tract', 'visit'), 'sky'), parts along dimension 0, may hold values from -6 to 6
- badbits: int32 [16, 256, 4096], P(('tract', 'visit'), 'sky'), parts along dimension 0, may hold values from 0 to 15
- coverage: int32 [16, 8], P(('tract', 'visit'), 'sky'), parts along dimension 0, may hold values from 0 to 1, as said below
- variance: float32 [16, 8], P(('tract', 'visit'), 'sky'), parts along dimension 0, may hold values from 0.05 to 5
- psf_index: int32 [16], P(('tract', 'visit')), parts along dimension 0, may hold values from 0 to 15
- psf_table: float32 [16, 8], replicated, may hold values from -2 to 2
- row_basis: bfloat16 [8, 21], replicated, may hold values from -1.25 to 1.25
- col_basis: bfloat16 [8, 21], replicated, may hold values from -1.25 to 1.25
Outputs:
- coadd: float32 [512, 4096], P(('tract', 'sky'), 'visit'), parts along dimension 0
- visit_chi: float32 [16], P(('tract', 'visit')), parts along dimension 0
There are 2 independent parts, one for each index of `tract`. A program takes and returns all parts, laid end to end along the dimension named above; an argument that names none is the same for every part. Nothing has to cross between parts.
Inputs may be any that keep to these rules, and one draw needn't show every extreme that they name: `coverage`: each visit covers one run of 2 or more consecutive bands and no other; every band is covered by some visit.
All inputs are finite; a program needn't handle non-finite values.
Results may differ from a plain program's by a relative error of at most 0.0038.
Values may be sent and summed in bfloat16 or wider, within the bound.
No kernel may reach another device: no remote copies, remote signals or barrier semaphores. Data moves between devices by JAX's collectives and lax.ppermute only.
A program may use at most 64 MiB of HBM per device.

v0:
```python
import jax
import jax.numpy as jnp
from jax import lax
from jax.sharding import PartitionSpec as P

PRIOR_WEIGHT = 1.0
CLIP_LEVEL = 9.0
CHI_OFFSET = 0.5


def padded_2(array, sides, width):
    for axis, dim in sides:
        count, length = (lax.axis_size(axis), array.shape[dim])
        up = [(i, (i + 1) % count) for i in range(count - 1)]
        down = [(j, i) for i, j in up]
        last = lax.slice_in_dim(array, length - width, length, axis=dim)
        leading = lax.slice_in_dim(array, 0, width, axis=dim)
        before = lax.ppermute(last, axis, up)
        after = lax.ppermute(leading, axis, down)
        array = jnp.concatenate([before, array, after], axis=dim)
    return array


def banded(profile, offset):
    taps = profile.shape[1]
    onehot = (offset[None] == jnp.arange(taps)[:, None, None]).astype(jnp.float32)
    return jnp.einsum("bk,kac->bac", profile.astype(jnp.float32), onehot).astype(jnp.bfloat16)


def per_device(warps, badbits, coverage, variance, psf_index, psf_table, row_basis, col_basis):
    visits_here, rows_here, columns = warps.shape
    bases, taps = col_basis.shape
    half_width = taps // 2
    band_count = coverage.shape[1]
    band_height = rows_here // band_count
    extended = rows_here + 2 * half_width
    block_width = min(128, columns)
    block_count = columns // block_width
    side_width = block_width // 2
    window_index = jnp.arange(2 * block_width) - side_width
    output_index = jnp.arange(block_width)
    column_table = banded(col_basis, window_index[:, None] - output_index[None, :] + half_width)
    column_matrix = jnp.transpose(column_table, (1, 0, 2)).reshape(
        2 * block_width, bases * block_width
    )
    row_table = banded(row_basis, jnp.arange(extended)[None, :] - jnp.arange(rows_here)[:, None])
    selector = (psf_index[:, None] == jnp.arange(psf_table.shape[0])[None, :]).astype(jnp.float32)
    coefficients = jnp.dot(selector, psf_table, precision=lax.Precision.HIGHEST)
    covered = (
        jnp.broadcast_to(coverage[:, :, None], (visits_here, band_count, band_height))
        .reshape(visits_here, rows_here)
        .astype(jnp.float32)
    )
    spread_variance = jnp.broadcast_to(
        variance[:, :, None], (visits_here, band_count, band_height)
    ).reshape(visits_here, rows_here)
    usable = covered[:, :, None] * (jnp.bitwise_and(badbits, 7) != 7).astype(jnp.float32)
    weight = usable / spread_variance[:, :, None]
    active = jnp.sum(coverage, axis=1) > 0

    def row_pass(layers, coefficient):
        stacked = layers.reshape(extended, block_count, bases, block_width)
        rows_sum = jnp.einsum(
            "bre,enbc->brnc", row_table, stacked, preferred_element_type=jnp.float32
        )
        combined = jnp.sum(coefficient[:, None, None, None] * rows_sum, axis=0)
        return combined.reshape(rows_here, columns).astype(jnp.bfloat16)

    def convolve(member):
        layers, coefficient, covers = member
        return row_pass(layers, coefficient)

    padded = padded_2(warps, (("sky", 1),), half_width)
    count = padded.shape[0]
    height = padded.shape[1]
    blocks = padded.reshape(count, height, block_count, block_width)
    zeros_side = jnp.zeros((count, height, 1, side_width), padded.dtype)
    left_side = jnp.concatenate([zeros_side, blocks[:, :, :-1, block_width - side_width :]], axis=2)
    right_side = jnp.concatenate([blocks[:, :, 1:, :side_width], zeros_side], axis=2)
    window = jnp.concatenate([left_side, blocks, right_side], axis=3)
    layers_all = jnp.einsum(
        "vrnk,kq->vrnq", window, column_matrix, preferred_element_type=jnp.float32
    ).astype(jnp.bfloat16)
    matched = lax.map(convolve, (layers_all, coefficients, active))
    values = matched.astype(jnp.float32)
    numer = jnp.sum(weight * values, axis=0)
    denom = jnp.sum(weight, axis=0)
    numer, denom = lax.psum((numer, denom), "visit")
    first = numer / (denom + PRIOR_WEIGHT)
    residual = values - first[None]
    squared = residual * residual
    chi_terms = jnp.sum(weight * squared, axis=(1, 2))
    counts = jnp.sum(usable, axis=(1, 2))
    chi_terms, counts = lax.psum((chi_terms, counts), "sky")
    visit_chi = chi_terms / counts
    revised = weight / (
        (CHI_OFFSET + visit_chi)[:, None, None] * (1.0 + weight * squared / CLIP_LEVEL)
    )
    numer, denom = (
        lax.psum_scatter(
            jnp.sum(revised * values, axis=0), "visit", scatter_dimension=1, tiled=True
        ),
        lax.psum_scatter(jnp.sum(revised, axis=0), "visit", scatter_dimension=1, tiled=True),
    )
    return (numer / (denom + PRIOR_WEIGHT), visit_chi)


def solution(mesh):
    placed = (
        P(("tract", "visit"), "sky", None),
        P(("tract", "visit"), "sky", None),
        P(("tract", "visit"), "sky"),
        P(("tract", "visit"), "sky"),
        P(("tract", "visit")),
        P(),
        P(),
        P(),
    )
    return jax.shard_map(
        per_device,
        mesh=mesh,
        in_specs=placed,
        out_specs=(P(("tract", "sky"), "visit"), P(("tract", "visit"))),
        check_vma=False,
    )
```

profile of v0, /device:TPU:0, one launch (start us, length us, event | category | flops | bytes accessed | tf_op | source)
XLA Modules:
  0.0 159.4 jit_solution(8322114165916315864)
XLA Ops:
  7.2 0.0 copy-start
  7.2 0.0 copy-start.1
  7.2 0.0 copy-start.4
  7.2 0.0 copy-start.5
  7.2 0.0 copy-start.6
  7.2 0.0 copy-start.7
  7.2 0.0 all-reduce.6.cloned.1.call-start
  7.3 2.4 %fusion.41 = (bf16[4,10,4096]{2,1,0:T(8,128)(2,1)}, bf16[4,10,4096]{2,1,0:T(8,128)(2,1)}) fusion(bf16[4,32,4096]{2,1,0:T(8,128)(2,1)} %param.10), kind=kLoop, calls=%fused_computation.64 | loop fusion | bytes 1310720 | tf_op jit(solution)/shard_map/slice | solution.py:16
  9.7 4.9 %collective-permute-start = (bf16[4,10,4096]{2,1,0:T(8,128)(2,1)}, bf16[4,10,4096]{2,1,0:T(8,128)(2,1)S(1)}, u32[]{:S(2)}, u32[]{:S(2)}) collective-permute-start(bf16[4,10,4096]{2,1,0:T(8,128)(2,1)} %get-tuple-element.74), channel_id=1, source_target_pairs={{0,2},{2,4},{4,6},{6,8},{8,10},{10,12},{12,14},{1,3},{3,5},{5,7},{... | collective-permute-start | bytes 983048 | tf_op jit(solution)/shard_map/ppermute | solution.py:18
  14.6 1.3 collective-permute-start.1
  15.9 0.1 subtract_add_fusion
  16.0 0.0 copy-done.4
  16.0 1.5 fusion.25
  17.5 0.0 copy-done.5
  17.6 0.2 fusion.27
  17.7 0.0 copy-done.6
  17.8 2.1 %reshape.85 = bf16[256,1024,1,1]{1,0,2,3:T(8,128)(2,1)} reshape(bf16[256,8,128]{2,1,0:T(8,128)(2,1)} %fusion.25) | data formatting | bytes 1048576 | tf_op jit(solution)/shard_map/reshape | solution.py:43
  19.9 0.0 copy-done
  19.9 0.0 copy-done.7
  19.9 0.2 fusion.32
  20.1 17.2 %collective-permute-done = bf16[4,10,4096]{2,1,0:T(8,128)(2,1)S(1)} collective-permute-done((bf16[4,10,4096]{2,1,0:T(8,128)(2,1)}, bf16[4,10,4096]{2,1,0:T(8,128)(2,1)S(1)}, u32[]{:S(2)}, u32[]{:S(2)}) %collective-permute-start) | collective-permute-done | bytes 327712 | tf_op jit(solution)/shard_map/ppermute | solution.py:18
  37.3 0.0 collective-permute-done.1
  37.3 1.7 %pad_maximum_fusion = bf16[4,52,4096]{2,1,0:T(8,128)(2,1)} fusion(bf16[4,10,4096]{2,1,0:T(8,128)(2,1)S(1)} %collective-permute-done.1, bf16[4,32,4096]{2,1,0:T(8,128)(2,1)S(1)} %copy-done.1, bf16[4,10,4096]{2,1,0:T(8,128)(2,1)S(1)} %collective-permute-done), kind=kLoop, calls=%fused_computation.34 | loop fusion | flops 5111808 | bytes 3407872 | tf_op jit(solution)/shard_map/concatenate | solution.py:20
  39.0 2.1 %reshape.81 = bf16[4,52,32,128]{3,2,1,0:T(8,128)(2,1)S(1)} reshape(bf16[4,52,4096]{2,1,0:T(8,128)(2,1)} %pad_maximum_fusion) | data formatting | bytes 3407872 | tf_op jit(solution)/shard_map/reshape | solution.py:76
  41.1 1.4 fusion.40
  42.6 0.0 copy-done.2
  42.6 7.5 %convolution_convert_fusion = bf16[4,52,32,1024]{3,2,1,0:T(8,128)(2,1)} fusion(bf16[4,52,31,64]{3,2,1,0:T(8,128)(2,1)S(1)} %get-tuple-element.73, bf16[4,52,31,64]{3,2,1,0:T(8,128)(2,1)S(1)} %get-tuple-element.72, bf16[4,52,32,128]{3,2,1,0:T(8,128)(2,1)S(1)} %reshape.81, bf16[256,1024,1,1]{1,0,2,3:T(8,128)(2,1)S(1)} %copy-done.2), kind=kOutput, calls=%fused_computation.9 | convolution fusion | flops 3513516032 | bytes 17510400 | tf_op jit(solution)/shard_map/vrnk,kq->vrnq/dot_general | solution.py:81
  50.1 32.2 %while.10 = (s32[]{:T(128)}, bf16[4,32,4096]{2,1,0:T(8,128)(2,1)S(1)}, f32[4,8]{1,0:T(4,128)S(1)}, bf16[4,52,32,1024]{3,2,1,0:T(8,128)(2,1)}, bf16[8,32,52]{2,1,0:T(8,128)(2,1)S(1)}, /*index=5*/s32[]{:T(128)}) while((s32[]{:T(128)}, bf16[4,32,4096]{2,1,0:T(8,128)(2,1)S(1)}, f32[4,8]{1,0:T(4,128)S(1)}, bf16[4,52,32,1024]{3,2,1,0:T(8,128)(2,1)}, ...), condition=%wide.region_2.3_spmd, body=%wide.region_0.2_spmd.sunk | while | flops 111017984 | bytes 18901168 | solution.py:84
  50.1 2.4 %constant_dynamic-slice_fusion.3 = bf16[1,52,32,1024]{3,2,1,0:T(8,128)(2,1)S(1)} fusion(bf16[4,52,32,1024]{3,2,1,0:T(8,128)(2,1)} %get-tuple-element.122, s32[]{:T(128)} %get-tuple-element.113), kind=kLoop, calls=%fused_computation.6.clone.1 | loop fusion | bytes 6815748 | tf_op jit(solution)/shard_map/while/body/jit(dynamic_index_in_dim)/dynamic_slice | solution.py:84
  52.5 0.9 copy.29
  53.4 4.5 %multiply_reduce_fusion.2 = bf16[32,128,32]{1,2,0:T(8,128)(2,1)S(1)} fusion(f32[8]{0:T(128)S(1)} %fusion.48, bf16[52,32,8,128]{3,2,1,0:T(8,128)(2,1)S(1)} %bitcast.43, bf16[8,32,52]{2,1,0:T(8,128)(2,1)S(1)} %get-tuple-element.123), kind=kOutput, calls=%fused_computation.clone.1 | convolution fusion | flops 111017984 | bytes 3696672 | tf_op jit(solution)/shard_map/while/body/eval_jaxpr/bre,enbc->brnc/dot_general | solution.py:63
  57.8 0.1 copy.30
  57.9 0.1 convert_element_type.82
  58.1 2.4 %constant_dynamic-slice_fusion.3 = bf16[1,52,32,1024]{3,2,1,0:T(8,128)(2,1)S(1)} fusion(bf16[4,52,32,1024]{3,2,1,0:T(8,128)(2,1)} %get-tuple-element.122, s32[]{:T(128)} %get-tuple-element.113), kind=kLoop, calls=%fused_computation.6.clone.1 | loop fusion | bytes 6815748 | tf_op jit(solution)/shard_map/while/body/jit(dynamic_index_in_dim)/dynamic_slice | solution.py:84
  60.5 0.9 copy.29
  61.4 4.5 %multiply_reduce_fusion.2 = bf16[32,128,32]{1,2,0:T(8,128)(2,1)S(1)} fusion(f32[8]{0:T(128)S(1)} %fusion.48, bf16[52,32,8,128]{3,2,1,0:T(8,128)(2,1)S(1)} %bitcast.43, bf16[8,32,52]{2,1,0:T(8,128)(2,1)S(1)} %get-tuple-element.123), kind=kOutput, calls=%fused_computation.clone.1 | convolution fusion | flops 111017984 | bytes 3696672 | tf_op jit(solution)/shard_map/while/body/eval_jaxpr/bre,enbc->brnc/dot_general | solution.py:63
  65.9 0.1 copy.30
  66.0 0.1 convert_element_type.82
  66.1 2.4 %constant_dynamic-slice_fusion.3 = bf16[1,52,32,1024]{3,2,1,0:T(8,128)(2,1)S(1)} fusion(bf16[4,52,32,1024]{3,2,1,0:T(8,128)(2,1)} %get-tuple-element.122, s32[]{:T(128)} %get-tuple-element.113), kind=kLoop, calls=%fused_computation.6.clone.1 | loop fusion | bytes 6815748 | tf_op jit(solution)/shard_map/while/body/jit(dynamic_index_in_dim)/dynamic_slice | solution.py:84
  68.5 0.9 copy.29
  69.4 4.5 %multiply_reduce_fusion.2 = bf16[32,128,32]{1,2,0:T(8,128)(2,1)S(1)} fusion(f32[8]{0:T(128)S(1)} %fusion.48, bf16[52,32,8,128]{3,2,1,0:T(8,128)(2,1)S(1)} %bitcast.43, bf16[8,32,52]{2,1,0:T(8,128)(2,1)S(1)} %get-tuple-element.123), kind=kOutput, calls=%fused_computation.clone.1 | convolution fusion | flops 111017984 | bytes 3696672 | tf_op jit(solution)/shard_map/while/body/eval_jaxpr/bre,enbc->brnc/dot_general | solution.py:63
  73.9 0.1 copy.30
  74.0 0.1 convert_element_type.82
  74.2 2.4 %constant_dynamic-slice_fusion.3 = bf16[1,52,32,1024]{3,2,1,0:T(8,128)(2,1)S(1)} fusion(bf16[4,52,32,1024]{3,2,1,0:T(8,128)(2,1)} %get-tuple-element.122, s32[]{:T(128)} %get-tuple-element.113), kind=kLoop, calls=%fused_computation.6.clone.1 | loop fusion | bytes 6815748 | tf_op jit(solution)/shard_map/while/body/jit(dynamic_index_in_dim)/dynamic_slice | solution.py:84
  76.6 0.9 copy.29
  77.5 4.5 %multiply_reduce_fusion.2 = bf16[32,128,32]{1,2,0:T(8,128)(2,1)S(1)} fusion(f32[8]{0:T(128)S(1)} %fusion.48, bf16[52,32,8,128]{3,2,1,0:T(8,128)(2,1)S(1)} %bitcast.43, bf16[8,32,52]{2,1,0:T(8,128)(2,1)S(1)} %get-tuple-element.123), kind=kOutput, calls=%fused_computation.clone.1 | convolution fusion | flops 111017984 | bytes 3696672 | tf_op jit(solution)/shard_map/while/body/eval_jaxpr/bre,enbc->brnc/dot_general | solution.py:63
  81.9 0.1 copy.30
  82.1 0.1 convert_element_type.82
  82.2 0.0 copy-done.3
  82.2 4.0 %fusion.38 = (f32[32,4096]{1,0:T(8,128)}, f32[32,4096]{1,0:T(8,128)}, f32[4]{0:T(128)S(1)}, pred[4,32,4096]{2,1,0:T(8,128)(4,1)S(1)}) fusion(f32[4]{0:T(128)S(1)} %bitcast.45, f32[4]{0:T(128)S(1)} %convert_bitcast_fusion.1, bf16[4,32,4096]{2,1,0:T(8,128)(2,1)S(1)} %get-tuple-element.29, s32[4,32,4096]{2,1,0:T(8,128)} %param.11), kind=kLoop, calls=%fused_computation.61 | loop fusion | flops 4456444 | bytes 4718640 | tf_op jit(solution)/shard_map/reduce_sum | solution.py:87
  86.2 0.0 all-reduce.6.cloned.1.call-update
  86.2 0.0 reduce-scatter.3.cloned.1.call-start
  86.3 21.7 %all-reduce.6.cloned.1.call-done = (f32[32,4096]{1,0:T(8,128)}, f32[32,4096]{1,0:T(8,128)}) async-done(((f32[32,4096]{1,0:T(8,128)}, f32[32,4096]{1,0:T(8,128)}), (f32[32,4096]{1,0:T(8,128)}, f32[32,4096]{1,0:T(8,128)})) %all-reduce.6.cloned.1.call-update) | async-done | bytes 1048592 | tf_op jit(solution)/shard_map/psum | solution.py:88
  107.9 1.3 add_divide_fusion
  109.2 0.7 fusion.26
  110.0 21.6 %all-reduce.2 = (f32[4]{0:T(128)S(1)}, f32[4]{0:T(128)S(1)}) all-reduce(f32[4]{0:T(128)S(1)} %fusion.26, f32[4]{0:T(128)S(1)} %get-tuple-element.54), channel_id=1, replica_groups=mesh['tract'=2,'sky'=8,'visit'=2] {'sky'}, use_global_device_ids=true, to_apply=%region_8.9 | all-reduce | flops 8 | bytes 64 | tf_op jit(solution)/shard_map/psum | solution.py:94
  131.6 0.5 broadcast_add_fusion
  132.1 2.3 %fusion.39 = (f32[32,4096]{1,0:T(8,128)}, f32[32,4096]{1,0:T(8,128)}) fusion(bf16[4,32,4096]{2,1,0:T(8,128)(2,1)S(1)} %get-tuple-element.29, f32[32,4096]{1,0:T(8,128)S(1)} %add_divide_fusion, f32[4]{0:T(128)S(1)} %get-tuple-element.69, f32[4]{0:T(128)S(1)} %bitcast.47, pred[4,32,4096]{2,1,0:T(8,128)(4,1)S(1)} %get-tuple-element.71, ...), kind=kLoop, calls=%fused_computation.62 | loop fusion | flops 7077888 | bytes 3145776 | tf_op jit(solution)/shard_map/reduce_sum | solution.py:103
  134.4 0.0 reduce-scatter.3.cloned.1.call-update
  134.5 0.0 reduce-scatter.5.cloned.1.call-start
  134.5 0.7 reduce-scatter.5.cloned.1.call-update
  135.2 4.6 %reduce-scatter.3.cloned.1.call-done = f32[32,2048]{1,0:T(8,128)} async-done(((f32[32,4096]{1,0:T(8,128)}), f32[32,2048]{1,0:T(8,128)}) %reduce-scatter.3.cloned.1.call-update) | async-done | bytes 262160 | tf_op jit(solution)/shard_map/reduce_scatter | solution.py:100
  139.8 11.4 %reduce-scatter.5.cloned.1.call-done = f32[32,2048]{1,0:T(8,128)} async-done(((f32[32,4096]{1,0:T(8,128)}), f32[32,2048]{1,0:T(8,128)}) %reduce-scatter.5.cloned.1.call-update) | async-done | bytes 262160 | tf_op jit(solution)/shard_map/reduce_scatter | solution.py:103
  151.1 1.8 %add_divide_fusion.1 = f32[32,2048]{1,0:T(8,128)} fusion(f32[32,2048]{1,0:T(8,128)} %reduce-scatter.3.cloned.1.call-done, f32[32,2048]{1,0:T(8,128)} %reduce-scatter.5.cloned.1.call-done), kind=kLoop, calls=%fused_computation.45 | loop fusion | flops 131072 | bytes 786432 | tf_op jit(solution)/shard_map/div | solution.py:105
  (16 shorter events, 0.2 us)
Async XLA Ops:
  7.2 12.7 %copy-start = (f32[16,8]{0,1:T(8,128)S(1)}, f32[16,8]{0,1:T(8,128)}, u32[]{:S(2)}) copy-start(f32[16,8]{0,1:T(8,128)} %param.15) | copy-start | bytes 1540
  7.2 30.1 %copy-start.1 = (bf16[4,32,4096]{2,1,0:T(8,128)(2,1)S(1)}, bf16[4,32,4096]{2,1,0:T(8,128)(2,1)}, u32[]{:S(2)}) copy-start(bf16[4,32,4096]{2,1,0:T(8,128)(2,1)} %param.10) | copy-start | bytes 3145732
  7.2 8.8 %copy-start.4 = (bf16[8,21]{1,0:T(8,128)(2,1)S(1)}, bf16[8,21]{1,0:T(8,128)(2,1)}, u32[]{:S(2)}) copy-start(bf16[8,21]{1,0:T(8,128)(2,1)} %param.17) | copy-start | bytes 1012
  7.2 10.4 %copy-start.5 = (bf16[8,21]{1,0:T(8,128)(2,1)S(1)}, bf16[8,21]{1,0:T(8,128)(2,1)}, u32[]{:S(2)}) copy-start(bf16[8,21]{1,0:T(8,128)(2,1)} %param.16) | copy-start | bytes 1012
  7.2 10.5 %copy-start.6 = (s32[4,1]{0,1:T(1,128)S(1)}, s32[4,1]{0,1:T(1,128)}, u32[]{:S(2)}) copy-start(s32[4,1]{0,1:T(1,128)} %param.12) | copy-start | bytes 52
  7.2 12.6 %copy-start.7 = (s32[4]{0:T(128)S(1)}, s32[4]{0:T(128)}, u32[]{:S(2)}) copy-start(s32[4]{0:T(128)} %param.14) | copy-start | bytes 52
  7.2 100.7 %all-reduce.6.cloned.1.call-start = ((), (), s32[]{:S(2)}) async-start(), calls=%async_computation.4 | async-start | bytes 2097152 | tf_op jit(solution)/shard_map/psum | solution.py:88
  9.7 27.6 %collective-permute-start = (bf16[4,10,4096]{2,1,0:T(8,128)(2,1)}, bf16[4,10,4096]{2,1,0:T(8,128)(2,1)S(1)}, u32[]{:S(2)}, u32[]{:S(2)}) collective-permute-start(bf16[4,10,4096]{2,1,0:T(8,128)(2,1)} %get-tuple-element.74), channel_id=1, source_target_pairs={{0,2},{2,4},{4,6},{6,8},{8,10},{10,12},{12,14},{1,3},{3,5},{5,7},{... | collective-permute-start | bytes 983048 | tf_op jit(solution)/shard_map/ppermute | solution.py:18
  14.6 22.7 %collective-permute-start.1 = (bf16[4,10,4096]{2,1,0:T(8,128)(2,1)}, bf16[4,10,4096]{2,1,0:T(8,128)(2,1)S(1)}, u32[]{:S(2)}, u32[]{:S(2)}) collective-permute-start(bf16[4,10,4096]{2,1,0:T(8,128)(2,1)} %get-tuple-element.75), channel_id=1, source_target_pairs={{2,0},{4,2},{6,4},{8,6},{10,8},{12,10},{14,12},{3,1},{5,3},{7,5},{... | collective-permute-start | bytes 983048 | tf_op jit(solution)/shard_map/ppermute | solution.py:19
  41.1 1.4 copy-start.2
  50.1 32.2 %copy-start.3 = (f32[4,1]{0,1:T(1,128)S(1)}, f32[4,1]{0,1:T(1,128)}, u32[]{:S(2)}) copy-start(f32[4,1]{0,1:T(1,128)} %param.13) | copy-start | bytes 52
  86.2 53.5 %reduce-scatter.3.cloned.1.call-start = ((), (), s32[]{:S(2)}) async-start(), calls=%async_computation.2 | async-start | bytes 786432 | tf_op jit(solution)/shard_map/reduce_scatter | solution.py:100
  134.5 16.7 %reduce-scatter.5.cloned.1.call-start = ((), (), s32[]{:S(2)}) async-start(), calls=%async_computation.3 | async-start | bytes 786432 | tf_op jit(solution)/shard_map/reduce_scatter | solution.py:103
Sparse Core Ops, SparseCore 0:
  86.4 21.5 all-reduce.5
  134.6 5.1 reduce-scatter.2
  142.0 9.0 reduce-scatter.4
where the time goes:
time: 160 us; the launch traced here: 159 us
  waiting for transfers between devices  55.5 us (35%)
  matrix products  27.2 us (17%)
  local copies, waits for them, and re-layouts  22.1 us (14%)
  blocking collectives  21.6 us (14%)
  between operations  13.9 us (9%)
  other arithmetic  12.5 us (8%)
  starting transfers between devices  6.33 us (4%)
    psum x1, waiting for transfers between devices, per_device(): numer, denom = lax.psum((numer, denom), 'visit')  21.7 us
    psum x1, blocking collectives, per_device(): chi_terms, counts = lax.psum((chi_terms, counts), 'sky')  21.6 us
    dot_general x4, matrix products, row_pass(): jnp.einsum('bre,enbc->brnc', row_table, stacked, preferred_element_type=j...  17.8 us
    ppermute x1, waiting for transfers between devices, padded_2(): before = lax.ppermute(last, axis, up)  17.2 us
    reduce_scatter x1, waiting for transfers between devices, per_device(): lax.psum_scatter(jnp.sum(revised, axis=0), 'visit', scatter_dimension=1,...  11.4 us
    dynamic_slice x4, local copies, waits for them, and re-layouts, per_device(): matched = lax.map(convolve, (layers_all, coefficients, active))  9.52 us
    dot_general x1, matrix products, per_device(): jnp.einsum('vrnk,kq->vrnq', window, column_matrix, preferred_element_type...  7.48 us
    ppermute x1, starting transfers between devices, padded_2(): before = lax.ppermute(last, axis, up)  4.92 us
  transfers between devices with their start and end apart: 5, of which 4 were waited for; matrix products, arithmetic and copies ran while one was open for 3% of the time, Pallas kernels for 0%

commit v1 on v0

v1 whole, which is shorter than its diff:
```python
import functools

import jax
import jax.numpy as jnp
import numpy as np
from jax import lax
from jax.experimental import pallas as pl
from jax.experimental.pallas import tpu as pltpu
from jax.sharding import PartitionSpec as P

PRIOR_WEIGHT = 1.0
CLIP_LEVEL = 9.0
CHI_OFFSET = 0.5
LANES = 128
SHIFT = LANES // 2
F32 = jnp.float32
BF16 = jnp.bfloat16


def whole(space=pltpu.VMEM):
    return pl.BlockSpec(memory_space=space)


def lane_index(shape):
    return lax.broadcasted_iota(jnp.int32, shape, len(shape) - 1)


def rotated(groups):
    turned = [pltpu.roll(group, SHIFT, 1) for group in groups]
    low = lane_index(groups[0].shape) < SHIFT
    return [jnp.where(low, turned[g - 1], turned[g]) for g in range(len(groups))]


def pack_kernel(half, select_ref, x_ref, up_ref, down_ref):
    columns = x_ref.shape[1]
    edge = up_ref.shape[0]
    step = 2 * LANES
    groups = []
    for start in range(0, columns, step):
        rows = jnp.dot(
            select_ref[...], x_ref[:, start : start + step], preferred_element_type=F32
        )
        groups += [rows[:, :LANES], rows[:, LANES:]]
    for g, group in enumerate(rotated(groups)):
        lanes = slice(g * LANES, (g + 1) * LANES)
        up_ref[:, lanes] = group[:edge].astype(BF16)
        down_ref[:, lanes] = group[edge:].astype(BF16)


def pack_rows(warps, half):
    visits, rows, columns = warps.shape
    edge = visits * half
    select = np.zeros((2 * edge, visits * rows), np.float32)
    for v in range(visits):
        for i in range(half):
            select[v * half + i, v * rows + rows - half + i] = 1
            select[edge + v * half + i, v * rows + i] = 1
    shape = jax.ShapeDtypeStruct((edge, columns), BF16)
    return pl.pallas_call(
        functools.partial(pack_kernel, half),
        out_shape=(shape, shape),
        in_specs=[whole(), whole()],
        out_specs=(whole(), whole()),
        name="pack",
    )(jnp.asarray(select, BF16), warps.reshape(visits * rows, columns))


def weight_kernel(visits, bands, side_ref, cover_ref, var_ref, send_bits, keep_bits, send_ref, keep_ref):
    rows = send_bits.shape[0] // visits
    high = rows // bands
    tile = (high, send_bits.shape[1])
    for v in range(visits):
        for b in range(bands):
            at = slice(v * rows + b * high, v * rows + (b + 1) * high)
            cover = jnp.full((8, LANES), cover_ref[v, b].astype(F32), F32)
            level = (cover / jnp.full((8, LANES), var_ref[v, b], F32))[:1, :1]
            level = jnp.broadcast_to(level, tile)
            for bits_ref, out_ref in ((send_bits, send_ref), (keep_bits, keep_ref)):
                usable = jnp.bitwise_and(bits_ref[at, :], 7) != 7
                out_ref[at, :] = jnp.where(usable, level, 0.0)


def pixel_weights(badbits, coverage, variance, side):
    visits, rows, columns = badbits.shape
    bits = badbits.reshape(visits * rows, columns)
    width = columns // 2
    tile = min(512, width)
    count = width // tile
    block = (visits * rows, tile)
    shape = jax.ShapeDtypeStruct((visits * rows, width), F32)
    spec = pl.BlockSpec(block, lambda i, s: (0, i))
    return pl.pallas_call(
        functools.partial(weight_kernel, visits, coverage.shape[1]),
        out_shape=(shape, shape),
        grid_spec=pltpu.PrefetchScalarGridSpec(
            num_scalar_prefetch=1,
            grid=(count,),
            in_specs=[
                whole(pltpu.SMEM),
                whole(pltpu.SMEM),
                pl.BlockSpec(block, lambda i, s: (0, (1 - s[0]) * count + i)),
                pl.BlockSpec(block, lambda i, s: (0, s[0] * count + i)),
            ],
            out_specs=(spec, spec),
        ),
        name="weights",
    )(side, coverage, variance, bits, bits)


def split(value):
    high = value.astype(BF16)
    return high, (value - high.astype(F32)).astype(BF16)


def table_kernel(visits, rows, half, index_ref, table_ref, row_ref, col_ref, column_out, own_out, edge_out):
    bases, taps = row_ref.shape
    outputs = visits * rows
    window = 2 * LANES
    k = lax.broadcasted_iota(jnp.int32, (window, LANES), 0)
    gap = k - lane_index((window, LANES)) - (SHIFT - half)
    for b in range(bases):
        band = jnp.zeros((window, LANES), F32)
        for t in range(taps):
            band = jnp.where(gap == t, col_ref[b, t], band)
        column_out[:, b * LANES : (b + 1) * LANES] = band.astype(BF16)
    out_row = lax.broadcasted_iota(jnp.int32, (rows, outputs), 0)
    lane = lane_index((rows, outputs))
    own_gap = lax.rem(lane, rows) - out_row + half
    member = lax.div(lane, rows)
    edge = visits * half
    source = lax.broadcasted_iota(jnp.int32, (2 * edge, outputs), 0)
    target = lane_index((2 * edge, outputs))
    i = lax.rem(source, half)
    line = lax.rem(target, rows)
    above = source < edge
    edge_gap = jnp.where(above, i - line, i + rows + half - line)
    same = lax.div(lax.rem(source, edge), half) == lax.div(target, rows)
    edge_gap = jnp.where(same, edge_gap, -1)
    owner = lax.div(target, rows)
    for b in range(bases):
        band = jnp.zeros((rows, outputs), F32)
        rim = jnp.zeros((2 * edge, outputs), F32)
        for t in range(taps):
            band = jnp.where(own_gap == t, row_ref[b, t], band)
            rim = jnp.where(edge_gap == t, row_ref[b, t], rim)
        scale = jnp.zeros((2 * edge, outputs), F32)
        for v in range(visits):
            factor = table_ref[index_ref[v], b]
            high, low = split(jnp.where(member == v, band * factor, 0.0))
            lanes = slice(b * outputs, (b + 1) * outputs)
            own_out[v * rows : (v + 1) * rows, lanes] = high
            own_out[outputs + v * rows : outputs + (v + 1) * rows, lanes] = low
            scale = jnp.where(owner == v, factor, scale)
        rim = rim * scale
        edge_out[b * 2 * edge : (b + 1) * 2 * edge, :] = rim


def turn_kernel(rim_ref, out_ref):
    count = rim_ref.shape[1]
    for start in range(0, rim_ref.shape[0], LANES):
        high, low = split(rim_ref[start : start + LANES, :].T)
        out_ref[:count, start : start + LANES] = high
        out_ref[count:, start : start + LANES] = low


def tables(psf_index, psf_table, row_basis, col_basis, visits, rows):
    bases, taps = row_basis.shape
    half = taps // 2
    outputs = visits * rows
    column, own, rim = pl.pallas_call(
        functools.partial(table_kernel, visits, rows, half),
        out_shape=(
            jax.ShapeDtypeStruct((2 * LANES, bases * LANES), BF16),
            jax.ShapeDtypeStruct((2 * outputs, bases * outputs), BF16),
            jax.ShapeDtypeStruct((bases * 2 * visits * half, outputs), F32),
        ),
        in_specs=[whole(pltpu.SMEM)] * 4,
        out_specs=(whole(),) * 3,
        name="tables",
    )(psf_index, psf_table, row_basis.astype(F32), col_basis.astype(F32))
    edge = pl.pallas_call(
        turn_kernel,
        out_shape=jax.ShapeDtypeStruct((2 * outputs, rim.shape[0]), BF16),
        in_specs=[whole()],
        out_specs=whole(),
        name="turn",
    )(rim)
    return column, own, edge


def convolve(window, column_ref, row_ref, step):
    bases = column_ref.shape[1] // LANES
    sides = []
    for n in range(2):
        layers = jnp.dot(window(2 * step + n), column_ref[...], preferred_element_type=F32)
        layers = layers.astype(BF16)
        sides.append(
            jnp.concatenate([layers[:, b * LANES : (b + 1) * LANES] for b in range(bases)], axis=0)
        )
    total = jnp.dot(row_ref[...], jnp.concatenate(sides, axis=1), preferred_element_type=F32)
    count = total.shape[0] // 2
    return total[:count] + total[count:]


def own_kernel(x_ref, column_ref, row_ref, out_ref, shifted):
    rows, columns = x_ref.shape
    groups = columns // LANES
    low = lane_index((rows, LANES)) < SHIFT

    def turn(g):
        return pltpu.roll(x_ref[:, g * LANES : (g + 1) * LANES].astype(F32), SHIFT, 1)

    before = jnp.zeros((rows, LANES), F32)
    for g in range(groups + 1):
        here = turn(g) if g < groups else jnp.zeros((rows, LANES), F32)
        shifted[:, g * LANES : (g + 1) * LANES] = jnp.where(low, before, here).astype(BF16)
        before = here

    def window(n):
        return shifted[:, pl.ds(pl.multiple_of(n * LANES, LANES), 2 * LANES)]

    def body(step, carry):
        at = pl.ds(pl.multiple_of(step * 2 * LANES, 2 * LANES), 2 * LANES)
        out_ref[:, at] = convolve(window, column_ref, row_ref, step)
        return carry

    lax.fori_loop(0, columns // (2 * LANES), body, 0)


def own_part(warps, column, own):
    visits, rows, columns = warps.shape
    count = visits * rows
    return pl.pallas_call(
        own_kernel,
        out_shape=jax.ShapeDtypeStruct((count, columns), F32),
        in_specs=[whole()] * 3,
        out_specs=whole(),
        scratch_shapes=[pltpu.VMEM((count, columns + LANES), BF16)],
        name="own_rows",
    )(warps.reshape(count, columns), column, own)


def edge_kernel(side_ref, up_ref, down_ref, column_ref, row_ref, part_ref, out_ref, shifted):
    edge, columns = up_ref.shape
    width = shifted.shape[1] - LANES
    groups = columns // LANES

    @pl.when(pl.program_id(0) == 0)
    def _():
        first = side_ref[0] * (width // LANES)
        lane = lane_index((2 * edge, LANES))
        for g in range(width // LANES + 1):
            at = first + g
            lanes = pl.ds(pl.multiple_of(lax.rem(at, groups) * LANES, LANES), LANES)
            value = jnp.concatenate(
                [up_ref[:, lanes].astype(F32), down_ref[:, lanes].astype(F32)], axis=0
            )
            bottom = jnp.where(at == 0, SHIFT, 0)
            top = jnp.where(at == groups, SHIFT, LANES)
            value = jnp.where((lane >= bottom) & (lane < top), value, 0.0)
            shifted[:, g * LANES : (g + 1) * LANES] = value.astype(BF16)

    start = pl.program_id(0) * (out_ref.shape[1] // LANES)

    def window(n):
        return shifted[:, pl.ds(pl.multiple_of((start + n) * LANES, LANES), 2 * LANES)]

    for step in range(out_ref.shape[1] // (2 * LANES)):
        at = slice(step * 2 * LANES, (step + 1) * 2 * LANES)
        total = convolve(window, column_ref, row_ref, step) + part_ref[:, at]
        out_ref[:, at] = total.astype(BF16)


def edge_part(side, up, down, column, edge, part):
    count, columns = part.shape
    width = columns // 2
    tile = min(512, width)
    steps = width // tile
    return pl.pallas_call(
        edge_kernel,
        out_shape=jax.ShapeDtypeStruct((count, width), BF16),
        grid_spec=pltpu.PrefetchScalarGridSpec(
            num_scalar_prefetch=1,
            grid=(steps,),
            in_specs=[whole()] * 4
            + [pl.BlockSpec((count, tile), lambda i, s: (0, s[0] * steps + i))],
            out_specs=pl.BlockSpec((count, tile), lambda i, s: (0, i)),
            scratch_shapes=[pltpu.VMEM((2 * up.shape[0], width + LANES), BF16)],
        ),
        name="edge_rows",
    )(side, up, down, column, edge, part)


def residual_kernel(visits, *refs):
    value_refs, weight_refs = refs[0:2], refs[2:4]
    factor_ref, sums_ref, chi_ref, count_ref = refs[4:]
    rows = value_refs[0].shape[0] // visits
    width = value_refs[0].shape[1]
    high = min(16, rows)

    @pl.when(pl.program_id(0) == 0)
    def _():
        chi_ref[...] = jnp.zeros_like(chi_ref)
        count_ref[...] = jnp.zeros_like(count_ref)

    def folded(value):
        total = value[:8]
        for start in range(8, high, 8):
            total = total + value[start : start + 8]
        return total

    members = [(side, v) for side in range(2) for v in range(visits)]
    for lane in range(0, width, LANES):
        for row in range(0, rows, high):
            lanes = slice(lane, lane + LANES)
            values, weights = [], []
            numer = denom = None
            for side, v in members:
                at = slice(v * rows + row, v * rows + row + high)
                value = value_refs[side][at, lanes].astype(F32)
                weight = weight_refs[side][at, lanes]
                values.append(value)
                weights.append(weight)
                numer = weight * value if numer is None else numer + weight * value
                denom = weight if denom is None else denom + weight
            first = numer / (denom + PRIOR_WEIGHT)
            for m, (side, v) in enumerate(members):
                residual = values[m] - first
                term = weights[m] * (residual * residual)
                at = slice(m * 8, (m + 1) * 8)
                chi_ref[at, :] += folded(term)
                count_ref[at, :] += folded(jnp.where(weights[m] > 0.0, 1.0, 0.0))
                target = slice(m * rows + row, m * rows + row + high)
                factor_ref[target, lanes] = weights[m] / (1.0 + term / CLIP_LEVEL)

    @pl.when(pl.program_id(0) == pl.num_programs(0) - 1)
    def _():
        count = len(members)
        for m in range(count):
            at = slice(m * 8, (m + 1) * 8)
            sums_ref[0, m : m + 1, :] = jnp.sum(chi_ref[at, :], axis=0, keepdims=True)
            sums_ref[1, m : m + 1, :] = jnp.sum(count_ref[at, :], axis=0, keepdims=True)


def residual_pass(values, weights, visits):
    count, width = values[0].shape
    tile = min(512, width)
    spec = pl.BlockSpec((count, tile), lambda i: (0, i))
    members = 2 * visits
    return pl.pallas_call(
        functools.partial(residual_kernel, visits),
        out_shape=(
            jax.ShapeDtypeStruct((2 * count, width), F32),
            jax.ShapeDtypeStruct((2, members, LANES), F32),
        ),
        grid=(width // tile,),
        in_specs=[spec] * 4,
        out_specs=(
            pl.BlockSpec((2 * count, tile), lambda i: (0, i)),
            pl.BlockSpec((2, members, LANES), lambda i: (0, 0, 0)),
        ),
        scratch_shapes=[pltpu.VMEM((members * 8, LANES), F32)] * 2,
        name="residual",
    )(*values, *weights)


def final_kernel(visits, sums_ref, own_ref, other_ref, factor_ref, out_ref, chi_ref):
    rows = own_ref.shape[0] // visits
    width = own_ref.shape[1]
    high = min(16, rows)
    chi = jnp.sum(sums_ref[0], axis=1, keepdims=True) / jnp.sum(
        sums_ref[1], axis=1, keepdims=True
    )
    scale = 1.0 / (CHI_OFFSET + chi)

    @pl.when(pl.program_id(0) == 0)
    def _():
        chi_ref[...] = jnp.broadcast_to(chi, chi_ref.shape)

    scales = [jnp.broadcast_to(scale[m : m + 1], (high, LANES)) for m in range(2 * visits)]
    for lane in range(0, width, LANES):
        for row in range(0, rows, high):
            lanes = slice(lane, lane + LANES)
            numer = denom = None
            for m in range(2 * visits):
                source = own_ref if m < visits else other_ref
                v = m % visits
                value = source[v * rows + row : v * rows + row + high, lanes].astype(F32)
                revised = factor_ref[m * rows + row : m * rows + row + high, lanes] * scales[m]
                numer = revised * value if numer is None else numer + revised * value
                denom = revised if denom is None else denom + revised
            out_ref[row : row + high, lanes] = numer / (denom + PRIOR_WEIGHT)


def final_pass(sums, values, factors, visits):
    count, width = values[0].shape
    rows = count // visits
    tile = min(512, width)
    spec = pl.BlockSpec((count, tile), lambda i: (0, i))
    members = 2 * visits
    return pl.pallas_call(
        functools.partial(final_kernel, visits),
        out_shape=(
            jax.ShapeDtypeStruct((rows, width), F32),
            jax.ShapeDtypeStruct((members, LANES), F32),
        ),
        grid=(width // tile,),
        in_specs=[
            pl.BlockSpec((2, members, LANES), lambda i: (0, 0, 0)),
            spec,
            spec,
            pl.BlockSpec((2 * count, tile), lambda i: (0, i)),
        ],
        out_specs=(
            pl.BlockSpec((rows, tile), lambda i: (0, i)),
            pl.BlockSpec((members, LANES), lambda i: (0, 0)),
        ),
        name="final",
    )(sums, *values, factors)


def per_device(warps, badbits, coverage, variance, psf_index, psf_table, row_basis, col_basis):
    visits, rows, columns = warps.shape
    half = row_basis.shape[1] // 2
    strips = lax.axis_size("sky")
    up = [(i, i + 1) for i in range(strips - 1)]
    down = [(j, i) for i, j in up]
    swap = [(0, 1), (1, 0)]
    side = lax.axis_index("visit").astype(jnp.int32).reshape(1)

    last, leading = pack_rows(warps, half)
    before = lax.ppermute(last, "sky", up)
    after = lax.ppermute(leading, "sky", down)
    send_weight, own_weight = pixel_weights(badbits, coverage, variance, side)
    other_weight = lax.ppermute(send_weight, "visit", swap)
    column, own, edge = tables(psf_index, psf_table, row_basis, col_basis, visits, rows)
    part = own_part(warps, column, own)
    send_value = edge_part(1 - side, before, after, column, edge, part)
    other_value = lax.ppermute(send_value, "visit", swap)
    own_value = edge_part(side, before, after, column, edge, part)
    values = (own_value, other_value)
    factors, sums = residual_pass(values, (own_weight, other_weight), visits)
    theirs = lax.ppermute(sums, "visit", swap)
    sums = sums + jnp.concatenate([theirs[:, visits:], theirs[:, :visits]], axis=1)
    step = 1
    while step < strips:
        sums = sums + lax.ppermute(sums, "sky", [(i, i ^ step) for i in range(strips)])
        step *= 2
    coadd, chi = final_pass(sums, values, factors, visits)
    return coadd, chi[:visits, 0]


def solution(mesh):
    placed = (
        P(("tract", "visit"), "sky", None),
        P(("tract", "visit"), "sky", None),
        P(("tract", "visit"), "sky"),
        P(("tract", "visit"), "sky"),
        P(("tract", "visit")),
        P(),
        P(),
        P(),
    )
    return jax.shard_map(
        per_device,
        mesh=mesh,
        in_specs=placed,
        out_specs=(P(("tract", "sky"), "visit"), P(("tract", "visit"))),
        check_vma=False,
    )
```

time: 160 us -> 78.4 us (0.49)
  waiting for transfers between devices: 55.5 us -> 6.01 us
  Pallas kernels: 0 us -> 46 us
  matrix products: 27.2 us -> 0 us
  blocking collectives: 21.6 us -> 0 us
  local copies, waits for them, and re-layouts: 22.1 us -> 7.21 us
  between operations: 13.9 us -> 0.7 us
  other arithmetic: 12.5 us -> 2.48 us
  starting transfers between devices: 6.33 us -> 15.3 us
    pallas_call x0 -> x9, Pallas kernels: none -> 46 us  [the longest x2 13.1 us: edge_part(): pl.pallas_call(edge_kernel, out_shape=jax.ShapeDtypeStruct((count, width)...]
    dot_general x8 -> x0, matrix products: 27.2 us -> none  [the longest x4 17.8 us: row_pass(): jnp.einsum('bre,enbc->brnc', row_table, stacked, preferred_element_type=j...]
    psum x1 -> x0, waiting for transfers between devices: 21.7 us -> none  [per_device(): numer, denom = lax.psum((numer, denom), 'visit')]
    psum x1 -> x0, blocking collectives: 21.6 us -> none  [per_device(): chi_terms, counts = lax.psum((chi_terms, counts), 'sky')]
    reduce_scatter x2 -> x0, waiting for transfers between devices: 15.9 us -> none  [the longest x1 11.4 us: per_device(): lax.psum_scatter(jnp.sum(revised, axis=0), 'visit', scatter_dimension=1,...]
    ppermute x2 -> x8, waiting for transfers between devices: 17.2 us -> 6.01 us  [the longest x3 4.88 us: per_device(): lax.ppermute(sums, 'sky', [(i, i ^ step) for i in range(strips)])]
    dynamic_slice x4 -> x0, local copies, waits for them, and re-layouts: 9.52 us -> none  [per_device(): matched = lax.map(convolve, (layers_all, coefficients, active))]
    ppermute x2 -> x8, starting transfers between devices: 6.21 us -> 15.3 us  [the longest x3 8.56 us: per_device(): lax.ppermute(sums, 'sky', [(i, i ^ step) for i in range(strips)])]
  transfers between devices with their start and end apart: 5 -> 8, of which waited for: 4 -> 4; matrix products, arithmetic and copies ran while one was open for 3% -> 2% of each run, Pallas kernels for 0% -> 43%
where the time goes in v1:
time: 78.4 us; the launch traced here: 77.7 us
  Pallas kernels  46 us (59%)
  starting transfers between devices  15.3 us (20%)
  local copies, waits for them, and re-layouts  7.21 us (9%)
  waiting for transfers between devices  6.01 us (8%)
  other arithmetic  2.48 us (3%)
    pallas_call x2, Pallas kernels, edge_part(): pl.pallas_call(edge_kernel, out_shape=jax.ShapeDtypeStruct((count, width)...  13.1 us
    pallas_call x1, Pallas kernels, own_part(): pl.pallas_call(own_kernel, out_shape=jax.ShapeDtypeStruct((count, columns...  12.7 us
    ppermute x3, starting transfers between devices, per_device(): lax.ppermute(sums, 'sky', [(i, i ^ step) for i in range(strips)])  8.56 us
    unnamed x17, local copies, waits for them, and re-layouts  5.91 us
    ppermute x3, waiting for transfers between devices, per_device(): lax.ppermute(sums, 'sky', [(i, i ^ step) for i in range(strips)])  4.88 us
    pallas_call x1, Pallas kernels, residual_pass(): pl.pallas_call(functools.partial(residual_kernel, visits), out_shape=(jax...  4.56 us
    ppermute x1, starting transfers between devices, per_device(): before = lax.ppermute(last, 'sky', up)  4.42 us
    pallas_call x1, Pallas kernels, final_pass(): pl.pallas_call(functools.partial(final_kernel, visits), out_shape=(jax.Sh...  4 us
  transfers between devices with their start and end apart: 8, of which 4 were waited for; matrix products, arithmetic and copies ran while one was open for 2% of the time, Pallas kernels for 43%

profile of v1, /device:TPU:0, one launch (start us, length us, event | category | flops | bytes accessed | tf_op | source)
XLA Modules:
  0.0 77.7 jit_solution(12839839948415448507)
XLA Ops:
  0.6 1.3 %copy.15.cover_ref = s32[4,1]{1,0:T(4,128)} copy(s32[4,1]{0,1:T(1,128)} %param.11) | data formatting | bytes 32 | tf_op args[2]
  1.9 1.3 %copy.16.var_ref = f32[4,1]{1,0:T(4,128)} copy(f32[4,1]{0,1:T(1,128)} %param.12) | data formatting | bytes 32 | tf_op args[3]
  3.3 0.0 copy-start.4
  3.3 0.0 copy-start.5
  3.3 0.0 copy-start.6
  3.3 3.9 %weights.1 = (f32[128,2048]{1,0:T(8,128)}, f32[128,2048]{1,0:T(8,128)}) custom-call(s32[1]{0:T(128)} %bitcast.side_ref, s32[4,1]{1,0:T(4,128)} %copy.15.cover_ref, f32[4,1]{1,0:T(4,128)} %copy.16.var_ref, s32[128,4096]{1,0:T(8,128)} %bitcast.3, s32[128,4096]{1,0:T(8,128)} %bitcast.4), custom_call_target="tpu_custom_call" | custom-call | tf_op jit(solution)/shard_map/weights/pallas_call | solution.py:92
  7.2 0.5 collective-permute-start.3
  7.7 2.5 %pack.1 = (bf16[40,4096]{1,0:T(8,128)(2,1)}, bf16[40,4096]{1,0:T(8,128)(2,1)}) custom-call(bf16[80,128]{1,0:T(8,128)(2,1)} %constant.8.clone.select_ref, bf16[128,4096]{1,0:T(8,128)(2,1)} %bitcast.5), custom_call_target="tpu_custom_call" | custom-call | tf_op jit(solution)/shard_map/pack/pallas_call | solution.py:59
  10.2 4.4 %collective-permute-start = (bf16[40,4096]{1,0:T(8,128)(2,1)}, bf16[40,4096]{1,0:T(8,128)(2,1)S(1)}, u32[]{:S(2)}, u32[]{:S(2)}) collective-permute-start(bf16[40,4096]{1,0:T(8,128)(2,1)} %get-tuple-element.13), channel_id=1, source_target_pairs={{0,2},{2,4},{4,6},{6,8},{8,10},{10,12},{12,14},{1,3},{3,5},{5,7},{... | collective-permute-start | bytes 983048 | tf_op jit(solution)/shard_map/ppermute | solution.py:432
  14.6 1.3 %collective-permute-start.1 = (bf16[40,4096]{1,0:T(8,128)(2,1)}, bf16[40,4096]{1,0:T(8,128)(2,1)S(1)}, u32[]{:S(2)}, u32[]{:S(2)}) collective-permute-start(bf16[40,4096]{1,0:T(8,128)(2,1)} %get-tuple-element.14), channel_id=1, source_target_pairs={{2,0},{4,2},{6,4},{8,6},{10,8},{12,10},{14,12},{3,1},{5,3},{7,5},{... | collective-permute-start | bytes 983048 | tf_op jit(solution)/shard_map/ppermute | solution.py:433
  15.9 0.0 copy-done.4
  15.9 0.7 copy.14.table_ref
  16.6 0.0 copy-done.5
  16.6 0.6 convert_element_type.6.row_ref
  17.2 0.0 copy-done.6
  17.2 0.6 convert_element_type.7.col_ref
  17.7 3.4 %tables.1 = (bf16[256,1024]{1,0:T(8,128)(2,1)}, bf16[256,1024]{1,0:T(8,128)(2,1)}, f32[640,128]{1,0:T(8,128)}) custom-call(s32[4]{0:T(128)} %index_ref.1, f32[16,8]{1,0:T(8,128)} %copy.14.table_ref, f32[8,21]{1,0:T(8,128)} %convert_element_type.6.row_ref, f32[8,21]{1,0:T(8,128)} %convert_element_type.7.col_ref), custom_call_target="tpu_custom_call" | custom-call | tf_op jit(solution)/shard_map/tables/pallas_call | solution.py:170
  21.1 1.9 %turn.1.row_ref = bf16[256,640]{1,0:T(8,128)(2,1)} custom-call(f32[640,128]{1,0:T(8,128)} %get-tuple-element.16.rim_ref), custom_call_target="tpu_custom_call" | custom-call | tf_op jit(solution)/shard_map/turn/pallas_call | solution.py:181
  23.0 12.7 %own_rows.1.part_ref = f32[128,4096]{1,0:T(8,128)} custom-call(bf16[128,4096]{1,0:T(8,128)(2,1)} %bitcast.6, bf16[256,1024]{1,0:T(8,128)(2,1)} %get-tuple-element.15.column_ref, bf16[256,1024]{1,0:T(8,128)(2,1)} %get-tuple-element.17.row_ref), custom_call_target="tpu_custom_call" | custom-call | tf_op jit(solution)/shard_map/own_rows/pallas_call | solution.py:233
  35.7 0.0 collective-permute-done.up_ref
  35.7 0.0 copy-start.1
  35.7 0.0 collective-permute-done.1.down_ref
  35.7 0.7 copy-done.1
  36.5 0.0 copy-start.2
  36.5 0.7 copy-done.2
  37.2 6.5 %edge_rows.3 = bf16[128,2048]{1,0:T(8,128)(2,1)} custom-call(s32[1]{0:T(128)S(6)} %sub.3.side_ref, bf16[40,4096]{1,0:T(8,128)(2,1)} %copy-done.1, bf16[40,4096]{1,0:T(8,128)(2,1)} %copy-done.2, bf16[256,1024]{1,0:T(8,128)(2,1)} %get-tuple-element.15.column_ref, bf16[256,640]{1,0:T(8,128)(2,1)} %turn.1.row_ref, f32[128,4096]{1,0:T(8,128)} %own_rows.1.part_ref), custom_call_target="tpu_custom_call" | custom-call | tf_op jit(solution)/shard_map/edge_rows/pallas_call | solution.py:279
  43.7 0.2 collective-permute-start.2
  44.0 6.6 %edge_rows.2.refs_0_.own_ref = bf16[128,2048]{1,0:T(8,128)(2,1)} custom-call(s32[1]{0:T(128)} %bitcast.side_ref, bf16[40,4096]{1,0:T(8,128)(2,1)} %copy-done.1, bf16[40,4096]{1,0:T(8,128)(2,1)} %copy-done.2, bf16[256,1024]{1,0:T(8,128)(2,1)} %get-tuple-element.15.column_ref, bf16[256,640]{1,0:T(8,128)(2,1)} %turn.1.row_ref, f32[128,4096]{1,0:T(8,128)} %own_rows.1.part_ref), custom_call_target="tpu_custom_call" | custom-call | tf_op jit(solution)/shard_map/edge_rows/pallas_call | solution.py:279
  50.5 0.0 collective-permute-done.2.refs_1_.other_ref
  50.5 0.0 copy-start
  50.5 0.0 collective-permute-done.3.refs_3_
  50.5 0.0 copy-start.3
  50.6 0.8 copy-done
  51.3 0.4 copy-done.3
  51.7 4.6 %residual.1 = (f32[256,2048]{1,0:T(8,128)}, f32[2,8,128]{2,1,0:T(8,128)}) custom-call(bf16[128,2048]{1,0:T(8,128)(2,1)} %edge_rows.2.refs_0_.own_ref, bf16[128,2048]{1,0:T(8,128)(2,1)} %copy-done, f32[128,2048]{1,0:T(8,128)} %get-tuple-element.18.refs_2_, f32[128,2048]{1,0:T(8,128)} %copy-done.3), custom_call_target="tpu_custom_call" | custom-call | tf_op jit(solution)/shard_map/residual/pallas_call | solution.py:350
  56.3 0.3 collective-permute-start.4
  56.5 1.1 %collective-permute-done.4 = f32[2,8,128]{2,1,0:T(8,128)S(1)} collective-permute-done((f32[2,8,128]{2,1,0:T(8,128)}, f32[2,8,128]{2,1,0:T(8,128)S(1)}, u32[]{:S(2)}, u32[]{:S(2)}) %collective-permute-start.4) | collective-permute-done | bytes 8224 | tf_op jit(solution)/shard_map/ppermute | solution.py:443
  57.6 0.7 maximum_add_fusion
  58.4 2.6 %collective-permute-start.5 = (f32[2,8,128]{2,1,0:T(8,128)S(1)}, f32[2,8,128]{2,1,0:T(8,128)S(1)}, u32[]{:S(2)}, u32[]{:S(2)}) collective-permute-start(f32[2,8,128]{2,1,0:T(8,128)S(1)} %maximum_add_fusion), channel_id=1, source_target_pairs={{0,2},{2,0},{4,6},{6,4},{8,10},{10,8},{12,14},{14,12},{1,3},{3,1},... | collective-permute-start | bytes 24584 | tf_op jit(solution)/shard_map/ppermute | solution.py:447
  60.9 1.6 %collective-permute-done.5 = f32[2,8,128]{2,1,0:T(8,128)S(1)} collective-permute-done((f32[2,8,128]{2,1,0:T(8,128)S(1)}, f32[2,8,128]{2,1,0:T(8,128)S(1)}, u32[]{:S(2)}, u32[]{:S(2)}) %collective-permute-start.5) | collective-permute-done | bytes 8224 | tf_op jit(solution)/shard_map/ppermute | solution.py:447
  62.6 3.0 %collective-permute-start.6 = (f32[2,8,128]{2,1,0:T(8,128)S(1)}, f32[2,8,128]{2,1,0:T(8,128)S(1)}, u32[]{:S(2)}, u32[]{:S(2)}) collective-permute-start(f32[2,8,128]{2,1,0:T(8,128)S(1)} %add.13), channel_id=1, source_target_pairs={{0,4},{2,6},{4,0},{6,2},{8,12},{10,14},{12,8},{14,10},{1,5},{3,7},... | collective-permute-start | bytes 24584 | tf_op jit(solution)/shard_map/ppermute | solution.py:447
  65.5 1.6 %collective-permute-done.6 = f32[2,8,128]{2,1,0:T(8,128)S(1)} collective-permute-done((f32[2,8,128]{2,1,0:T(8,128)S(1)}, f32[2,8,128]{2,1,0:T(8,128)S(1)}, u32[]{:S(2)}, u32[]{:S(2)}) %collective-permute-start.6) | collective-permute-done | bytes 8224 | tf_op jit(solution)/shard_map/ppermute | solution.py:447
  67.2 3.0 %collective-permute-start.7 = (f32[2,8,128]{2,1,0:T(8,128)S(1)}, f32[2,8,128]{2,1,0:T(8,128)S(1)}, u32[]{:S(2)}, u32[]{:S(2)}) collective-permute-start(f32[2,8,128]{2,1,0:T(8,128)S(1)} %add.14), channel_id=1, source_target_pairs={{0,8},{2,10},{4,12},{6,14},{8,0},{10,2},{12,4},{14,6},{1,9},{3,11}... | collective-permute-start | bytes 24584 | tf_op jit(solution)/shard_map/ppermute | solution.py:447
  70.2 1.6 %collective-permute-done.7 = f32[2,8,128]{2,1,0:T(8,128)S(1)} collective-permute-done((f32[2,8,128]{2,1,0:T(8,128)S(1)}, f32[2,8,128]{2,1,0:T(8,128)S(1)}, u32[]{:S(2)}, u32[]{:S(2)}) %collective-permute-start.7) | collective-permute-done | bytes 8224 | tf_op jit(solution)/shard_map/ppermute | solution.py:447
  71.8 0.6 add.15.sums_ref
  72.4 4.0 %final.1 = (f32[32,2048]{1,0:T(8,128)}, f32[8,128]{1,0:T(8,128)}) custom-call(f32[2,8,128]{2,1,0:T(8,128)} %add.15.sums_ref, bf16[128,2048]{1,0:T(8,128)(2,1)} %edge_rows.2.refs_0_.own_ref, bf16[128,2048]{1,0:T(8,128)(2,1)} %copy-done, f32[256,2048]{1,0:T(8,128)} %get-tuple-element.21.factor_ref), custom_call_target="tpu_custom_call" | custom-call | tf_op jit(solution)/shard_map/final/pallas_call | solution.py:401
  76.4 1.3 %slice_reduce_fusion = f32[4]{0:T(128)} fusion(f32[8,128]{1,0:T(8,128)} %get-tuple-element.23), kind=kLoop, calls=%fused_computation.1 | loop fusion | bytes 32 | tf_op jit(solution)/shard_map/slice | solution.py:450
  (3 shorter events, 0.0 us)
Async XLA Ops:
  3.3 12.6 %copy-start.4 = (f32[16,8]{0,1:T(8,128)S(1)}, f32[16,8]{0,1:T(8,128)}, u32[]{:S(2)}) copy-start(f32[16,8]{0,1:T(8,128)} %param.14) | copy-start | bytes 1540
  3.3 13.3 %copy-start.5 = (bf16[8,21]{1,0:T(8,128)(2,1)S(1)}, bf16[8,21]{1,0:T(8,128)(2,1)}, u32[]{:S(2)}) copy-start(bf16[8,21]{1,0:T(8,128)(2,1)} %param.15) | copy-start | bytes 1012
  3.3 13.9 %copy-start.6 = (bf16[8,21]{1,0:T(8,128)(2,1)S(1)}, bf16[8,21]{1,0:T(8,128)(2,1)}, u32[]{:S(2)}) copy-start(bf16[8,21]{1,0:T(8,128)(2,1)} %param.16) | copy-start | bytes 1012
  7.2 43.4 %collective-permute-start.3 = (f32[128,2048]{1,0:T(8,128)}, f32[128,2048]{1,0:T(8,128)S(1)}, u32[]{:S(2)}, u32[]{:S(2)}) collective-permute-start(f32[128,2048]{1,0:T(8,128)} %get-tuple-element.19), channel_id=1, source_target_pairs={{0,1},{1,0},{2,3},{3,2},{4,5},{5,4},{6,7},{7,6},{8,9},{9,8},{10,11... | collective-permute-start | bytes 3145736 | tf_op jit(solution)/shard_map/ppermute | solution.py:435
  10.2 25.6 %collective-permute-start = (bf16[40,4096]{1,0:T(8,128)(2,1)}, bf16[40,4096]{1,0:T(8,128)(2,1)S(1)}, u32[]{:S(2)}, u32[]{:S(2)}) collective-permute-start(bf16[40,4096]{1,0:T(8,128)(2,1)} %get-tuple-element.13), channel_id=1, source_target_pairs={{0,2},{2,4},{4,6},{6,8},{8,10},{10,12},{12,14},{1,3},{3,5},{5,7},{... | collective-permute-start | bytes 983048 | tf_op jit(solution)/shard_map/ppermute | solution.py:432
  14.6 21.1 %collective-permute-start.1 = (bf16[40,4096]{1,0:T(8,128)(2,1)}, bf16[40,4096]{1,0:T(8,128)(2,1)S(1)}, u32[]{:S(2)}, u32[]{:S(2)}) collective-permute-start(bf16[40,4096]{1,0:T(8,128)(2,1)} %get-tuple-element.14), channel_id=1, source_target_pairs={{2,0},{4,2},{6,4},{8,6},{10,8},{12,10},{14,12},{3,1},{5,3},{7,5},{... | collective-permute-start | bytes 983048 | tf_op jit(solution)/shard_map/ppermute | solution.py:433
  35.7 0.7 copy-start.1
  36.5 0.7 copy-start.2
  43.7 6.8 %collective-permute-start.2 = (bf16[128,2048]{1,0:T(8,128)(2,1)}, bf16[128,2048]{1,0:T(8,128)(2,1)S(1)}, u32[]{:S(2)}, u32[]{:S(2)}) collective-permute-start(bf16[128,2048]{1,0:T(8,128)(2,1)} %edge_rows.3), channel_id=1, source_target_pairs={{0,1},{1,0},{2,3},{3,2},{4,5},{5,4},{6,7},{7,6},{8,9},{9,8},{10,11... | collective-permute-start | bytes 1572872 | tf_op jit(solution)/shard_map/ppermute | solution.py:439
  50.5 0.8 %copy-start = (bf16[128,2048]{1,0:T(8,128)(2,1)}, bf16[128,2048]{1,0:T(8,128)(2,1)S(1)}, u32[]{:S(2)}) copy-start(bf16[128,2048]{1,0:T(8,128)(2,1)S(1)} %collective-permute-done.2.refs_1_.other_ref) | copy-start | bytes 1572868
  50.5 1.2 %copy-start.3 = (f32[128,2048]{1,0:T(8,128)}, f32[128,2048]{1,0:T(8,128)S(1)}, u32[]{:S(2)}) copy-start(f32[128,2048]{1,0:T(8,128)S(1)} %collective-permute-done.3.refs_3_) | copy-start | bytes 3145732
  56.3 1.4 %collective-permute-start.4 = (f32[2,8,128]{2,1,0:T(8,128)}, f32[2,8,128]{2,1,0:T(8,128)S(1)}, u32[]{:S(2)}, u32[]{:S(2)}) collective-permute-start(f32[2,8,128]{2,1,0:T(8,128)} %get-tuple-element.20), channel_id=1, source_target_pairs={{0,1},{1,0},{2,3},{3,2},{4,5},{5,4},{6,7},{7,6},{8,9},{9,8},{10,11... | collective-permute-start | bytes 24584 | tf_op jit(solution)/shard_map/ppermute | solution.py:443
  58.4 4.2 %collective-permute-start.5 = (f32[2,8,128]{2,1,0:T(8,128)S(1)}, f32[2,8,128]{2,1,0:T(8,128)S(1)}, u32[]{:S(2)}, u32[]{:S(2)}) collective-permute-start(f32[2,8,128]{2,1,0:T(8,128)S(1)} %maximum_add_fusion), channel_id=1, source_target_pairs={{0,2},{2,0},{4,6},{6,4},{8,10},{10,8},{12,14},{14,12},{1,3},{3,1},... | collective-permute-start | bytes 24584 | tf_op jit(solution)/shard_map/ppermute | solution.py:447
  62.6 4.6 %collective-permute-start.6 = (f32[2,8,128]{2,1,0:T(8,128)S(1)}, f32[2,8,128]{2,1,0:T(8,128)S(1)}, u32[]{:S(2)}, u32[]{:S(2)}) collective-permute-start(f32[2,8,128]{2,1,0:T(8,128)S(1)} %add.13), channel_id=1, source_target_pairs={{0,4},{2,6},{4,0},{6,2},{8,12},{10,14},{12,8},{14,10},{1,5},{3,7},... | collective-permute-start | bytes 24584 | tf_op jit(solution)/shard_map/ppermute | solution.py:447
  67.2 4.7 %collective-permute-start.7 = (f32[2,8,128]{2,1,0:T(8,128)S(1)}, f32[2,8,128]{2,1,0:T(8,128)S(1)}, u32[]{:S(2)}, u32[]{:S(2)}) collective-permute-start(f32[2,8,128]{2,1,0:T(8,128)S(1)} %add.14), channel_id=1, source_target_pairs={{0,8},{2,10},{4,12},{6,14},{8,0},{10,2},{12,4},{14,6},{1,9},{3,11}... | collective-permute-start | bytes 24584 | tf_op jit(solution)/shard_map/ppermute | solution.py:447

commit v2 on v1

v2 whole, which is shorter than its diff:
```python
import functools

import jax
import jax.numpy as jnp
import numpy as np
from jax import lax
from jax.experimental import pallas as pl
from jax.experimental.pallas import tpu as pltpu
from jax.sharding import PartitionSpec as P

PRIOR_WEIGHT = 1.0
CLIP_LEVEL = 9.0
CHI_OFFSET = 0.5
LANES = 128
SHIFT = LANES // 2
F32 = jnp.float32
BF16 = jnp.bfloat16


def whole(space=pltpu.VMEM):
    return pl.BlockSpec(memory_space=space)


def kept(*arrays):
    return [pltpu.with_memory_space_constraint(array, pltpu.VMEM) for array in arrays]


def held(shape, dtype):
    return pltpu.VMEM(shape, dtype)


LIMIT = pltpu.CompilerParams(vmem_limit_bytes=20 * 1024 * 1024)


def lane_index(shape):
    return lax.broadcasted_iota(jnp.int32, shape, len(shape) - 1)


def rotated(groups):
    turned = [pltpu.roll(group, SHIFT, 1) for group in groups]
    low = lane_index(groups[0].shape) < SHIFT
    return [jnp.where(low, turned[g - 1], turned[g]) for g in range(len(groups))]


def pack_kernel(select_ref, x_ref, up_ref, down_ref):
    columns = x_ref.shape[1]
    edge = up_ref.shape[0]
    step = 2 * LANES
    groups = []
    for start in range(0, columns, step):
        rows = jnp.dot(
            select_ref[...], x_ref[:, start : start + step], preferred_element_type=F32
        )
        groups += [rows[:, :LANES], rows[:, LANES:]]
    for g, group in enumerate(rotated(groups)):
        lanes = slice(g * LANES, (g + 1) * LANES)
        up_ref[:, lanes] = group[:edge].astype(BF16)
        down_ref[:, lanes] = group[edge:].astype(BF16)


def pack_rows(warps, half):
    visits, rows, columns = warps.shape
    edge = visits * half
    select = np.zeros((2 * edge, visits * rows), np.float32)
    for v in range(visits):
        for i in range(half):
            select[v * half + i, v * rows + rows - half + i] = 1
            select[edge + v * half + i, v * rows + i] = 1
    shape = held((edge, columns), BF16)
    return pl.pallas_call(
        pack_kernel,
        out_shape=(shape, shape),
        in_specs=[whole(), whole()],
        out_specs=(whole(), whole()),
        compiler_params=LIMIT,
        name="pack",
    )(jnp.asarray(select, BF16), *kept(warps.reshape(visits * rows, columns)))


def weight_kernel(visits, bands, side_ref, cover_ref, var_ref, bits_ref, send_ref, keep_ref):
    rows = bits_ref.shape[0] // visits
    high = rows // bands
    width = bits_ref.shape[1]
    tile = (high, width)
    count = send_ref.shape[1] // width
    step = pl.program_id(0)
    half = lax.div(step, count)
    lanes = pl.ds(pl.multiple_of(lax.rem(step, count) * width, width), width)

    def fill(out_ref):
        for v in range(visits):
            for b in range(bands):
                at = slice(v * rows + b * high, v * rows + (b + 1) * high)
                cover = jnp.full((8, LANES), cover_ref[b, v].astype(F32), F32)
                level = (cover / jnp.full((8, LANES), var_ref[b, v], F32))[:1, :1]
                usable = jnp.bitwise_and(bits_ref[at, :], 7) != 7
                out_ref[at, lanes] = jnp.where(usable, jnp.broadcast_to(level, tile), 0.0)

    pl.when(half == 0)(lambda: fill(send_ref))
    pl.when(half == 1)(lambda: fill(keep_ref))


def pixel_weights(badbits, coverage, variance, side):
    visits, rows, columns = badbits.shape
    bits = badbits.reshape(visits * rows, columns)
    width = columns // 2
    tile = min(512, width)
    count = width // tile
    shape = held((visits * rows, width), F32)

    def block(i, s):
        first = i < count
        return 0, jnp.where(first, (1 - s[0]) * count + i, s[0] * count + i - count)

    return pl.pallas_call(
        functools.partial(weight_kernel, visits, coverage.shape[1]),
        out_shape=(shape, shape),
        grid_spec=pltpu.PrefetchScalarGridSpec(
            num_scalar_prefetch=1,
            grid=(2 * count,),
            in_specs=[
                whole(pltpu.SMEM),
                whole(pltpu.SMEM),
                pl.BlockSpec((visits * rows, tile), block),
            ],
            out_specs=(whole(), whole()),
        ),
        compiler_params=LIMIT,
        name="weights",
    )(side, coverage.T, variance.T, bits)


def split(value):
    high = value.astype(BF16)
    return high, (value - high.astype(F32)).astype(BF16)


def padded_rows(half):
    return -(-2 * half // 8) * 8


def table_kernel(visits, rows, half, index_ref, table_ref, profile_ref, column_out, own_out, edge_out):
    bases = table_ref.shape[0]
    taps = 2 * half + 1
    window = 2 * LANES
    padded = padded_rows(half)

    def spread(line, shift, count):
        line = jnp.broadcast_to(line, (8, LANES))
        block = pltpu.roll(line, 0, 1, stride=1, stride_axis=0)
        blocks = [pltpu.roll(block, (shift + i) % LANES, 1) for i in range(0, count, 8)]
        return jnp.concatenate(blocks, axis=0)

    k = lax.broadcasted_iota(jnp.int32, (window, LANES), 0)
    gap = k - lane_index((window, LANES))
    inside = (gap >= 0) & (gap < LANES)
    for b in range(bases):
        line = profile_ref[bases + b : bases + b + 1, :]
        band = jnp.where(inside, spread(line, SHIFT - half, window), 0.0)
        column_out[:, b * LANES : (b + 1) * LANES] = band.astype(BF16)

    r = lax.broadcasted_iota(jnp.int32, (rows, LANES), 0)
    lane = lane_index((rows, LANES))
    tap = lane_index((1, LANES))

    def assemble(out_ref, high, valid, lines):
        groups = -(-bases * high // LANES)
        for g in range(groups):
            total = jnp.zeros((rows, LANES), F32)
            factors = [jnp.zeros((rows, LANES), F32) for _ in range(visits)]
            for b in range(bases):
                start = b * high - g * LANES
                if start >= LANES or start + high <= 0:
                    continue
                here = lane - start
                mask = (here >= 0) & (here < high)
                total = jnp.where(mask & valid(here), spread(lines(b), b * high, rows), total)
                for v in range(visits):
                    factors[v] = jnp.where(mask, table_ref[b, index_ref[v]], factors[v])
            wide = min(LANES, bases * high - g * LANES)
            lanes = slice(g * LANES, g * LANES + wide)
            for v in range(visits):
                top, low = split(total * factors[v])
                at = 2 * v * rows
                out_ref[at : at + rows, lanes] = top[:, :wide]
                out_ref[at + rows : at + 2 * rows, lanes] = low[:, :wide]

    def profile(b):
        return profile_ref[b : b + 1, :]

    def own_line(b):
        return pltpu.roll(profile(b), LANES - half, 1)

    def own_valid(e):
        return (e - r >= -half) & (e - r <= half)

    def edge_line(b):
        above = jnp.where(tap < half, profile(b), 0.0)
        below = jnp.where((tap > half) & (tap < taps), profile(b), 0.0)
        return above + pltpu.roll(below, LANES - rows, 1)

    def edge_valid(p):
        above = (p < half) & (p >= r)
        below = (p >= half) & (p < 2 * half) & (p - r <= 2 * half - rows)
        return above | below

    assemble(own_out, rows, own_valid, own_line)
    assemble(edge_out, padded, edge_valid, edge_line)


def tables(psf_index, psf_table, row_basis, col_basis, visits, rows):
    bases, taps = row_basis.shape
    half = taps // 2
    profile = jnp.concatenate([row_basis, col_basis[:, ::-1]], axis=0).astype(F32)
    profile = jnp.pad(profile, ((0, 0), (0, LANES - taps)))
    return pl.pallas_call(
        functools.partial(table_kernel, visits, rows, half),
        out_shape=(
            held((2 * LANES, bases * LANES), BF16),
            held((2 * visits * rows, bases * rows), BF16),
            held((2 * visits * rows, bases * padded_rows(half)), BF16),
        ),
        in_specs=[whole(pltpu.SMEM), whole(pltpu.SMEM), whole()],
        out_specs=(whole(),) * 3,
        compiler_params=LIMIT,
        name="tables",
    )(psf_index, psf_table.T, profile)


def convolve(windows, column_ref, row_ref, visits):
    bases = column_ref.shape[1] // LANES
    count = windows[0].shape[0]
    rows = count // visits
    layers = jnp.dot(
        jnp.concatenate(windows, axis=0), column_ref[...], preferred_element_type=F32
    )
    high = row_ref.shape[0] // (2 * visits)
    totals = []
    for v in range(visits):
        sides = []
        for n in range(len(windows)):
            at = n * count + v * rows
            part = [layers[at : at + rows, b * LANES : (b + 1) * LANES] for b in range(bases)]
            sides.append(jnp.concatenate(part, axis=0).astype(BF16))
        total = jnp.dot(
            row_ref[2 * v * high : 2 * (v + 1) * high, :],
            jnp.concatenate(sides, axis=1),
            preferred_element_type=F32,
        )
        totals.append(total[:high] + total[high:])
    return totals


def own_kernel(visits, x_ref, column_ref, row_ref, out_ref, shifted):
    count, columns = x_ref.shape
    rows = count // visits
    groups = columns // LANES
    low = lane_index((count, LANES)) < SHIFT

    def turn(g):
        return pltpu.roll(x_ref[:, g * LANES : (g + 1) * LANES].astype(F32), SHIFT, 1)

    before = jnp.zeros((count, LANES), F32)
    for g in range(groups + 1):
        here = turn(g) if g < groups else jnp.zeros((count, LANES), F32)
        shifted[:, g * LANES : (g + 1) * LANES] = jnp.where(low, before, here).astype(BF16)
        before = here

    def window(n):
        return shifted[:, pl.ds(pl.multiple_of(n * LANES, LANES), 2 * LANES)]

    def body(step, carry):
        at = pl.ds(pl.multiple_of(step * 2 * LANES, 2 * LANES), 2 * LANES)
        windows = [window(2 * step), window(2 * step + 1)]
        for v, total in enumerate(convolve(windows, column_ref, row_ref, visits)):
            out_ref[v * rows : (v + 1) * rows, at] = total
        return carry

    lax.fori_loop(0, columns // (2 * LANES), body, 0)


def own_part(warps, column, own):
    visits, rows, columns = warps.shape
    count = visits * rows
    return pl.pallas_call(
        functools.partial(own_kernel, visits),
        out_shape=held((count, columns), F32),
        in_specs=[whole()] * 3,
        out_specs=whole(),
        scratch_shapes=[pltpu.VMEM((count, columns + LANES), BF16)],
        compiler_params=LIMIT,
        cost_estimate=pl.CostEstimate(flops=10**9, bytes_accessed=10**7, transcendentals=0),
        name="own_rows",
    )(*kept(warps.reshape(count, columns), column, own))


def edge_kernel(visits, side_ref, select_ref, up_ref, down_ref, column_ref, row_ref, part_ref, out_ref, shifted):
    columns = up_ref.shape[1]
    rows = out_ref.shape[0] // visits
    width = out_ref.shape[1]
    groups = columns // LANES
    base = side_ref[0] * (width // LANES)
    count = shifted.shape[0]
    lane = lane_index((count, LANES))
    for g in range(width // LANES + 1):
        at = base + g
        lanes = pl.ds(pl.multiple_of(lax.rem(at, groups) * LANES, LANES), LANES)
        value = jnp.dot(select_ref[0], up_ref[:, lanes], preferred_element_type=F32)
        value += jnp.dot(select_ref[1], down_ref[:, lanes], preferred_element_type=F32)
        if g == 0:
            value = jnp.where(lane >= jnp.where(at == 0, SHIFT, 0), value, 0.0)
        if g == width // LANES:
            value = jnp.where(lane < jnp.where(at == groups, SHIFT, LANES), value, 0.0)
        shifted[:, g * LANES : (g + 1) * LANES] = value.astype(BF16)

    def window(n):
        return shifted[:, pl.ds(pl.multiple_of(n * LANES, LANES), 2 * LANES)]

    def body(step, carry):
        start = pl.multiple_of(step * 2 * LANES, 2 * LANES)
        at = pl.ds(start, 2 * LANES)
        source = pl.ds(pl.multiple_of(side_ref[0] * width + start, 2 * LANES), 2 * LANES)
        windows = [window(2 * step), window(2 * step + 1)]
        for v, total in enumerate(convolve(windows, column_ref, row_ref, visits)):
            lines = slice(v * rows, (v + 1) * rows)
            out_ref[lines, at] = (total + part_ref[lines, source]).astype(BF16)
        return carry

    lax.fori_loop(0, width // (2 * LANES), body, 0)


def edge_part(side, up, down, column, edge, part, visits, half):
    count, columns = part.shape
    width = columns // 2
    padded = padded_rows(half)
    select = np.zeros((2, visits * padded, visits * half), np.float32)
    for v in range(visits):
        for i in range(half):
            select[0, v * padded + i, v * half + i] = 1
            select[1, v * padded + half + i, v * half + i] = 1
    return pl.pallas_call(
        functools.partial(edge_kernel, visits),
        out_shape=held((count, width), BF16),
        in_specs=[whole(pltpu.SMEM)] + [whole()] * 6,
        out_specs=whole(),
        scratch_shapes=[pltpu.VMEM((visits * padded, width + LANES), BF16)],
        compiler_params=LIMIT,
        name="edge_rows",
    )(side, jnp.asarray(select, BF16), *kept(up, down, column, edge, part))


def residual_kernel(visits, *refs):
    value_refs, weight_refs = refs[0:2], refs[2:4]
    factor_ref, sums_ref, chi_ref, count_ref = refs[4:]
    rows = value_refs[0].shape[0] // visits
    width = value_refs[0].shape[1]
    high = min(16, rows)
    chi_ref[...] = jnp.zeros_like(chi_ref)
    count_ref[...] = jnp.zeros_like(count_ref)

    def folded(value):
        total = value[:8]
        for start in range(8, high, 8):
            total = total + value[start : start + 8]
        return total

    members = [(side, v) for side in range(2) for v in range(visits)]

    def body(step, carry):
        lanes = pl.ds(pl.multiple_of(step * LANES, LANES), LANES)
        for row in range(0, rows, high):
            values, weights = [], []
            numer = denom = None
            for side, v in members:
                at = slice(v * rows + row, v * rows + row + high)
                value = value_refs[side][at, lanes].astype(F32)
                weight = weight_refs[side][at, lanes]
                values.append(value)
                weights.append(weight)
                numer = weight * value if numer is None else numer + weight * value
                denom = weight if denom is None else denom + weight
            first = numer / (denom + PRIOR_WEIGHT)
            for m, (side, v) in enumerate(members):
                residual = values[m] - first
                term = weights[m] * (residual * residual)
                at = slice(m * 8, (m + 1) * 8)
                chi_ref[at, :] += folded(term)
                count_ref[at, :] += folded(jnp.where(weights[m] > 0.0, 1.0, 0.0))
                target = slice(m * rows + row, m * rows + row + high)
                factor_ref[target, lanes] = weights[m] / (1.0 + term / CLIP_LEVEL)
        return carry

    lax.fori_loop(0, width // LANES, body, 0)
    for m in range(len(members)):
        at = slice(m * 8, (m + 1) * 8)
        sums_ref[0, m : m + 1, :] = jnp.sum(chi_ref[at, :], axis=0, keepdims=True)
        sums_ref[1, m : m + 1, :] = jnp.sum(count_ref[at, :], axis=0, keepdims=True)


def residual_pass(values, weights, visits):
    count, width = values[0].shape
    members = 2 * visits
    return pl.pallas_call(
        functools.partial(residual_kernel, visits),
        out_shape=(held((2 * count, width), F32), held((2, members, LANES), F32)),
        in_specs=[whole()] * 4,
        out_specs=(whole(), whole()),
        scratch_shapes=[pltpu.VMEM((members * 8, LANES), F32)] * 2,
        compiler_params=LIMIT,
        name="residual",
    )(*kept(*values, *weights))


def final_kernel(visits, sums_ref, own_ref, other_ref, factor_ref, out_ref, chi_ref):
    rows = own_ref.shape[0] // visits
    width = out_ref.shape[1]
    high = min(16, rows)
    start = pl.program_id(0) * width
    chi = jnp.sum(sums_ref[0], axis=1, keepdims=True) / jnp.sum(
        sums_ref[1], axis=1, keepdims=True
    )
    scale = 1.0 / (CHI_OFFSET + chi)

    @pl.when(pl.program_id(0) == 0)
    def _():
        for v in range(visits):
            chi_ref[v] = chi[v, 0]

    scales = [jnp.broadcast_to(scale[m : m + 1], (high, LANES)) for m in range(2 * visits)]
    for lane in range(0, width, LANES):
        lanes = pl.ds(pl.multiple_of(start + lane, LANES), LANES)
        for row in range(0, rows, high):
            numer = denom = None
            for m in range(2 * visits):
                source = own_ref if m < visits else other_ref
                v = m % visits
                value = source[v * rows + row : v * rows + row + high, lanes].astype(F32)
                revised = factor_ref[m * rows + row : m * rows + row + high, lanes] * scales[m]
                numer = revised * value if numer is None else numer + revised * value
                denom = revised if denom is None else denom + revised
            out_ref[row : row + high, lane : lane + LANES] = numer / (denom + PRIOR_WEIGHT)


def final_pass(sums, values, factors, visits):
    count, width = values[0].shape
    rows = count // visits
    tile = min(512, width)
    return pl.pallas_call(
        functools.partial(final_kernel, visits),
        out_shape=(
            jax.ShapeDtypeStruct((rows, width), F32),
            jax.ShapeDtypeStruct((visits,), F32),
        ),
        grid=(width // tile,),
        in_specs=[whole()] * 4,
        out_specs=(pl.BlockSpec((rows, tile), lambda i: (0, i)), whole(pltpu.SMEM)),
        compiler_params=LIMIT,
        name="final",
    )(*kept(sums, *values, factors))


def per_device(warps, badbits, coverage, variance, psf_index, psf_table, row_basis, col_basis):
    visits, rows, _ = warps.shape
    half = row_basis.shape[1] // 2
    strips = lax.axis_size("sky")
    up = [(i, i + 1) for i in range(strips - 1)]
    down = [(j, i) for i, j in up]
    swap = [(0, 1), (1, 0)]
    side = lax.axis_index("visit").astype(jnp.int32).reshape(1)

    last, leading = pack_rows(warps, half)
    before = lax.ppermute(last, "sky", up)
    after = lax.ppermute(leading, "sky", down)
    send_weight, own_weight = pixel_weights(badbits, coverage, variance, side)
    other_weight = lax.ppermute(send_weight, "visit", swap)
    column, own, edge = tables(psf_index, psf_table, row_basis, col_basis, visits, rows)
    part = own_part(warps, column, own)
    send_value = edge_part(
        1 - side, before, after, column, edge, part, visits, half
    )
    other_value = lax.ppermute(send_value, "visit", swap)
    own_value = edge_part(side, before, after, column, edge, part, visits, half)
    values = (own_value, other_value)
    factors, sums = residual_pass(values, (own_weight, other_weight), visits)
    theirs = lax.ppermute(sums, "visit", swap)
    sums = sums + jnp.concatenate([theirs[:, visits:], theirs[:, :visits]], axis=1)
    step = 1
    while step < strips:
        sums = sums + lax.ppermute(sums, "sky", [(i, i ^ step) for i in range(strips)])
        step *= 2
    return final_pass(sums, values, factors, visits)


def solution(mesh):
    placed = (
        P(("tract", "visit"), "sky", None),
        P(("tract", "visit"), "sky", None),
        P(("tract", "visit"), "sky"),
        P(("tract", "visit"), "sky"),
        P(("tract", "visit")),
        P(),
        P(),
        P(),
    )
    return jax.shard_map(
        per_device,
        mesh=mesh,
        in_specs=placed,
        out_specs=(P(("tract", "sky"), "visit"), P(("tract", "visit"))),
        check_vma=False,
    )
```

time: 78.4 us -> 53.8 us (0.69)
  Pallas kernels: 46 us -> 24.5 us
  local copies, waits for them, and re-layouts: 7.21 us -> 3.1 us
  waiting for transfers between devices: 6.01 us -> 9.66 us
  other arithmetic: 2.48 us -> 0.03 us
    pallas_call x6 -> x5, Pallas kernels: 34.7 us -> 19 us  [the longest x1 8.11 us: own_part(): pl.pallas_call(functools.partial(own_kernel, visits), out_shape=held((cou...]
    ppermute x1, waiting for transfers between devices: 0.01 us -> 3.94 us  [per_device(): before = lax.ppermute(last, 'sky', up)]
    unnamed x17 -> x20, local copies, waits for them, and re-layouts: 5.91 us -> 3.01 us
    pallas_call x1, Pallas kernels: 3.38 us -> 1.13 us  [tables(): pl.pallas_call(functools.partial(table_kernel, visits, rows, half), out_s...]
    pallas_call x1, Pallas kernels: 4 us -> 2.02 us  [final_pass(): pl.pallas_call(functools.partial(final_kernel, visits), out_shape=(jax.Sh...]
    pallas_call x1, Pallas kernels: 3.91 us -> 2.33 us  [pixel_weights(): pl.pallas_call(functools.partial(weight_kernel, visits, coverage.shape[1]...]
    slice x1 -> x0, local copies, waits for them, and re-layouts: 1.3 us -> none  [per_device(): return (coadd, chi[:visits, 0])]
    convert_element_type x2 -> x0, other arithmetic: 1.18 us -> none  [the longest x1 0.59 us: tables(): row_basis.astype(F32)]
  transfers between devices with their start and end apart: 8 -> 8, of which waited for: 4 -> 5; matrix products, arithmetic and copies ran while one was open for 2% -> 0% of each run, Pallas kernels for 43% -> 33%
where the time goes in v2:
time: 53.8 us; the launch traced here: 53.6 us
  Pallas kernels  24.5 us (46%)
  starting transfers between devices  15.5 us (29%)
  waiting for transfers between devices  9.66 us (18%)
  local copies, waits for them, and re-layouts  3.1 us (6%)
  between operations  0.79 us (1%)
    ppermute x3, starting transfers between devices, per_device(): lax.ppermute(sums, 'sky', [(i, i ^ step) for i in range(strips)])  8.54 us
    pallas_call x1, Pallas kernels, own_part(): pl.pallas_call(functools.partial(own_kernel, visits), out_shape=held((cou...  8.11 us
    pallas_call x2, Pallas kernels, edge_part(): pl.pallas_call(functools.partial(edge_kernel, visits), out_shape=held((co...  7.86 us
    ppermute x3, waiting for transfers between devices, per_device(): lax.ppermute(sums, 'sky', [(i, i ^ step) for i in range(strips)])  4.89 us
    ppermute x1, starting transfers between devices, per_device(): before = lax.ppermute(last, 'sky', up)  4.57 us
    ppermute x1, waiting for transfers between devices, per_device(): before = lax.ppermute(last, 'sky', up)  3.94 us
    unnamed x20, local copies, waits for them, and re-layouts  3.01 us
    pallas_call x1, Pallas kernels, residual_pass(): pl.pallas_call(functools.partial(residual_kernel, visits), out_shape=(hel...  2.62 us
  transfers between devices with their start and end apart: 8, of which 5 were waited for; matrix products, arithmetic and copies ran while one was open for 0% of the time, Pallas kernels for 33%

profile of v2, /device:TPU:0, one launch (start us, length us, event | category | flops | bytes accessed | tf_op | source)
XLA Modules:
  0.0 53.6 jit_solution(4877407542218696261)
XLA Ops:
  0.6 0.0 copy-start
  0.6 0.0 copy-start.1
  0.7 1.7 %copy-done.1 = s32[4,32,4096]{2,1,0:T(8,128)S(1)} copy-done((s32[4,32,4096]{2,1,0:T(8,128)S(1)}, s32[4,32,4096]{2,1,0:T(8,128)}, u32[]{:S(2)}) %copy-start.1) | copy-done | bytes 2097176
  2.3 0.0 copy-start.5
  2.3 0.7 %copy-done.5 = s32[4,1]{0,1:T(1,128)S(1)} copy-done((s32[4,1]{0,1:T(1,128)S(1)}, s32[4,1]{0,1:T(1,128)}, u32[]{:S(2)}) %copy-start.5) | copy-done | bytes 40
  3.0 0.0 copy-start.6
  3.0 0.7 %copy-done.6 = f32[4,1]{0,1:T(1,128)S(1)} copy-done((f32[4,1]{0,1:T(1,128)S(1)}, f32[4,1]{0,1:T(1,128)}, u32[]{:S(2)}) %copy-start.6) | copy-done | bytes 40
  3.6 0.0 copy-start.3
  3.6 0.0 copy-start.8
  3.6 0.0 copy-start.9
  3.6 0.0 copy-start.4
  3.6 0.0 copy-start.7
  3.7 2.3 %weights.1 = (f32[128,2048]{1,0:T(8,128)}, f32[128,2048]{1,0:T(8,128)S(1)}) custom-call(s32[1]{0:T(128)} %bitcast.side_ref, s32[1,4]{1,0:T(1,128)S(1)} %bitcast.10, f32[1,4]{1,0:T(1,128)S(1)} %bitcast.11, s32[128,4096]{1,0:T(8,128)S(1)} %bitcast.8), custom_call_target="tpu_custom_call" | custom-call | tf_op jit(solution)/shard_map/weights/pallas_call | solution.py:115
  6.0 0.5 collective-permute-start.3
  6.5 0.0 copy-done
  6.5 0.0 copy-done.3
  6.5 0.4 pack.1
  6.9 0.0 copy-start.2
  6.9 4.6 %collective-permute-start = (bf16[40,4096]{1,0:T(8,128)(2,1)S(1)}, bf16[40,4096]{1,0:T(8,128)(2,1)S(1)}, u32[]{:S(2)}, u32[]{:S(2)}) collective-permute-start(bf16[40,4096]{1,0:T(8,128)(2,1)S(1)} %get-tuple-element.11), channel_id=1, source_target_pairs={{0,2},{2,4},{4,6},{6,8},{8,10},{10,12},{12,14},{1,3},{3,5},{5,7},{... | collective-permute-start | bytes 983048 | tf_op jit(solution)/shard_map/ppermute | solution.py:472
  11.5 1.3 %collective-permute-start.1 = (bf16[40,4096]{1,0:T(8,128)(2,1)S(1)}, bf16[40,4096]{1,0:T(8,128)(2,1)S(1)}, u32[]{:S(2)}, u32[]{:S(2)}) collective-permute-start(bf16[40,4096]{1,0:T(8,128)(2,1)S(1)} %get-tuple-element.12), channel_id=1, source_target_pairs={{2,0},{4,2},{6,4},{8,6},{10,8},{12,10},{14,12},{3,1},{5,3},{7,5},{... | collective-permute-start | bytes 983048 | tf_op jit(solution)/shard_map/ppermute | solution.py:473
  12.8 0.0 copy-done.8
  12.8 0.1 rev.3
  12.9 0.0 copy-done.9
  12.9 0.0 copy-done.4
  12.9 0.0 copy-done.7
  12.9 1.1 %tables.1 = (bf16[256,1024]{1,0:T(8,128)(2,1)S(1)}, bf16[256,256]{1,0:T(8,128)(2,1)S(1)}, bf16[256,192]{1,0:T(8,128)(2,1)S(1)}) custom-call(s32[4]{0:T(128)S(1)} %copy-done.7, f32[8,16]{1,0:T(8,128)S(1)} %bitcast.9, f32[16,128]{1,0:T(8,128)S(1)} %fusion.3.profile_ref), custom_call_target="tpu_custom_call" | custom-call | tf_op jit(solution)/shard_map/tables/pallas_call | solution.py:216
  14.0 8.1 %own_rows.1.part_ref = f32[128,4096]{1,0:T(8,128)S(1)} custom-call(bf16[128,4096]{1,0:T(8,128)(2,1)S(1)} %bitcast.7, bf16[256,1024]{1,0:T(8,128)(2,1)S(1)} %get-tuple-element.13.column_ref, bf16[256,256]{1,0:T(8,128)(2,1)S(1)} %get-tuple-element.15.row_ref), custom_call_target="tpu_custom_call" | custom-call | flops 1000000000 | bytes 10000000 | tf_op jit(solution)/shard_map/own_rows/pallas_call | solution.py:285
  22.2 3.9 %collective-permute-done.up_ref = bf16[40,4096]{1,0:T(8,128)(2,1)S(1)} collective-permute-done((bf16[40,4096]{1,0:T(8,128)(2,1)S(1)}, bf16[40,4096]{1,0:T(8,128)(2,1)S(1)}, u32[]{:S(2)}, u32[]{:S(2)}) %collective-permute-start) | collective-permute-done | bytes 327712 | tf_op jit(solution)/shard_map/ppermute | solution.py:472
  26.1 0.0 collective-permute-done.1.down_ref
  26.1 0.0 copy-done.2
  26.1 3.9 %edge_rows.3 = bf16[128,2048]{1,0:T(8,128)(2,1)S(1)} custom-call(s32[1]{0:T(128)S(6)} %sub.3.side_ref, bf16[2,96,40]{2,1,0:T(8,128)(2,1)S(1)} %copy-done.2, bf16[40,4096]{1,0:T(8,128)(2,1)S(1)} %collective-permute-done.up_ref, bf16[40,4096]{1,0:T(8,128)(2,1)S(1)} %collective-permute-done.1.down_ref, bf16[256,1024]{1,0:T(8,128)(2,1)S(1)} %get-tuple-element.13.column_ref, ...), custom_call_target="tpu_custom_call" | custom-call | tf_op jit(solution)/shard_map/edge_rows/pallas_call | solution.py:341
  30.0 0.1 collective-permute-start.2
  30.1 3.9 %edge_rows.2.refs_0_.own_ref = bf16[128,2048]{1,0:T(8,128)(2,1)S(1)} custom-call(s32[1]{0:T(128)} %bitcast.side_ref, bf16[2,96,40]{2,1,0:T(8,128)(2,1)S(1)} %copy-done.2, bf16[40,4096]{1,0:T(8,128)(2,1)S(1)} %collective-permute-done.up_ref, bf16[40,4096]{1,0:T(8,128)(2,1)S(1)} %collective-permute-done.1.down_ref, ...), custom_call_target="tpu_custom_call" | custom-call | tf_op jit(solution)/shard_map/edge_rows/pallas_call | solution.py:341
  34.1 0.0 collective-permute-done.2.refs_1_.other_ref
  34.1 0.0 collective-permute-done.3.refs_3_
  34.1 2.6 %residual.1 = (f32[256,2048]{1,0:T(8,128)S(1)}, f32[2,8,128]{2,1,0:T(8,128)S(1)}) custom-call(bf16[128,2048]{1,0:T(8,128)(2,1)S(1)} %edge_rows.2.refs_0_.own_ref, bf16[128,2048]{1,0:T(8,128)(2,1)S(1)} %collective-permute-done.2.refs_1_.other_ref, f32[128,2048]{1,0:T(8,128)S(1)} %get-tuple-element.16.refs_2_, f32[128,2048]{1,0:T(8,128)} %collective-permute-done.3.refs_3_), custom_call_target="tpu_custom_call" | custom-call | tf_op jit(solution)/shard_map/residual/pallas_call | solution.py:403
  36.7 0.5 %collective-permute-start.4 = (f32[2,8,128]{2,1,0:T(8,128)S(1)}, f32[2,8,128]{2,1,0:T(8,128)S(1)}, u32[]{:S(2)}, u32[]{:S(2)}) collective-permute-start(f32[2,8,128]{2,1,0:T(8,128)S(1)} %get-tuple-element.18), channel_id=1, source_target_pairs={{0,1},{1,0},{2,3},{3,2},{4,5},{5,4},{6,7},{7,6},{8,9},{9,8},{10,11... | collective-permute-start | bytes 24584 | tf_op jit(solution)/shard_map/ppermute | solution.py:485
  37.3 0.8 %collective-permute-done.4 = f32[2,8,128]{2,1,0:T(8,128)S(1)} collective-permute-done((f32[2,8,128]{2,1,0:T(8,128)S(1)}, f32[2,8,128]{2,1,0:T(8,128)S(1)}, u32[]{:S(2)}, u32[]{:S(2)}) %collective-permute-start.4) | collective-permute-done | bytes 8224 | tf_op jit(solution)/shard_map/ppermute | solution.py:485
  38.1 2.5 %collective-permute-start.5 = (f32[2,8,128]{2,1,0:T(8,128)S(1)}, f32[2,8,128]{2,1,0:T(8,128)S(1)}, u32[]{:S(2)}, u32[]{:S(2)}) collective-permute-start(f32[2,8,128]{2,1,0:T(8,128)S(1)} %maximum_add_fusion), channel_id=1, source_target_pairs={{0,2},{2,0},{4,6},{6,4},{8,10},{10,8},{12,14},{14,12},{1,3},{3,1},... | collective-permute-start | bytes 24584 | tf_op jit(solution)/shard_map/ppermute | solution.py:489
  40.6 1.6 %collective-permute-done.5 = f32[2,8,128]{2,1,0:T(8,128)S(1)} collective-permute-done((f32[2,8,128]{2,1,0:T(8,128)S(1)}, f32[2,8,128]{2,1,0:T(8,128)S(1)}, u32[]{:S(2)}, u32[]{:S(2)}) %collective-permute-start.5) | collective-permute-done | bytes 8224 | tf_op jit(solution)/shard_map/ppermute | solution.py:489
  42.3 3.0 %collective-permute-start.6 = (f32[2,8,128]{2,1,0:T(8,128)S(1)}, f32[2,8,128]{2,1,0:T(8,128)S(1)}, u32[]{:S(2)}, u32[]{:S(2)}) collective-permute-start(f32[2,8,128]{2,1,0:T(8,128)S(1)} %add.15), channel_id=1, source_target_pairs={{0,4},{2,6},{4,0},{6,2},{8,12},{10,14},{12,8},{14,10},{1,5},{3,7},... | collective-permute-start | bytes 24584 | tf_op jit(solution)/shard_map/ppermute | solution.py:489
  45.3 1.6 %collective-permute-done.6 = f32[2,8,128]{2,1,0:T(8,128)S(1)} collective-permute-done((f32[2,8,128]{2,1,0:T(8,128)S(1)}, f32[2,8,128]{2,1,0:T(8,128)S(1)}, u32[]{:S(2)}, u32[]{:S(2)}) %collective-permute-start.6) | collective-permute-done | bytes 8224 | tf_op jit(solution)/shard_map/ppermute | solution.py:489
  46.9 3.0 %collective-permute-start.7 = (f32[2,8,128]{2,1,0:T(8,128)S(1)}, f32[2,8,128]{2,1,0:T(8,128)S(1)}, u32[]{:S(2)}, u32[]{:S(2)}) collective-permute-start(f32[2,8,128]{2,1,0:T(8,128)S(1)} %add.16), channel_id=1, source_target_pairs={{0,8},{2,10},{4,12},{6,14},{8,0},{10,2},{12,4},{14,6},{1,9},{3,11}... | collective-permute-start | bytes 24584 | tf_op jit(solution)/shard_map/ppermute | solution.py:489
  49.9 1.6 %collective-permute-done.7 = f32[2,8,128]{2,1,0:T(8,128)S(1)} collective-permute-done((f32[2,8,128]{2,1,0:T(8,128)S(1)}, f32[2,8,128]{2,1,0:T(8,128)S(1)}, u32[]{:S(2)}, u32[]{:S(2)}) %collective-permute-start.7) | collective-permute-done | bytes 8224 | tf_op jit(solution)/shard_map/ppermute | solution.py:489
  51.5 2.0 %final.1 = (f32[32,2048]{1,0:T(8,128)}, f32[4]{0:T(128)}) custom-call(f32[2,8,128]{2,1,0:T(8,128)S(1)} %add.17.sums_ref, bf16[128,2048]{1,0:T(8,128)(2,1)S(1)} %edge_rows.2.refs_0_.own_ref, bf16[128,2048]{1,0:T(8,128)(2,1)S(1)} %collective-permute-done.2.refs_1_.other_ref, f32[256,2048]{1,0:T(8,128)S(1)} %get-tuple-element.19.factor_ref), custom_call_target="tpu_custom_call" | custom-call | tf_op jit(solution)/shard_map/final/pallas_call | solution.py:448
  (6 shorter events, 0.0 us)
Async XLA Ops:
  0.6 5.9 %copy-start = (bf16[4,32,4096]{2,1,0:T(8,128)(2,1)S(1)}, bf16[4,32,4096]{2,1,0:T(8,128)(2,1)}, u32[]{:S(2)}) copy-start(bf16[4,32,4096]{2,1,0:T(8,128)(2,1)} %param.11) | copy-start | bytes 3145732
  0.6 1.7 %copy-start.1 = (s32[4,32,4096]{2,1,0:T(8,128)S(1)}, s32[4,32,4096]{2,1,0:T(8,128)}, u32[]{:S(2)}) copy-start(s32[4,32,4096]{2,1,0:T(8,128)} %param.12) | copy-start | bytes 6291460
  2.3 0.7 %copy-start.5 = (s32[4,1]{0,1:T(1,128)S(1)}, s32[4,1]{0,1:T(1,128)}, u32[]{:S(2)}) copy-start(s32[4,1]{0,1:T(1,128)} %param.13) | copy-start | bytes 52
  3.0 0.7 %copy-start.6 = (f32[4,1]{0,1:T(1,128)S(1)}, f32[4,1]{0,1:T(1,128)}, u32[]{:S(2)}) copy-start(f32[4,1]{0,1:T(1,128)} %param.14) | copy-start | bytes 52
  3.6 2.9 %copy-start.3 = (bf16[80,128]{1,0:T(8,128)(2,1)S(1)}, bf16[80,128]{1,0:T(8,128)(2,1)}, u32[]{:S(2)}) copy-start(bf16[80,128]{1,0:T(8,128)(2,1)} %constant.14.clone.select_ref) | copy-start | bytes 61444
  3.6 9.1 %copy-start.8 = (bf16[8,21]{1,0:T(8,128)(2,1)S(1)}, bf16[8,21]{1,0:T(8,128)(2,1)}, u32[]{:S(2)}) copy-start(bf16[8,21]{1,0:T(8,128)(2,1)} %param.18) | copy-start | bytes 1012
  3.6 9.2 %copy-start.9 = (bf16[8,21]{1,0:T(8,128)(2,1)S(1)}, bf16[8,21]{1,0:T(8,128)(2,1)}, u32[]{:S(2)}) copy-start(bf16[8,21]{1,0:T(8,128)(2,1)} %param.17) | copy-start | bytes 1012
  3.6 9.3 %copy-start.4 = (f32[16,8]{0,1:T(8,128)S(1)}, f32[16,8]{0,1:T(8,128)}, u32[]{:S(2)}) copy-start(f32[16,8]{0,1:T(8,128)} %param.16) | copy-start | bytes 1540
  3.6 9.3 %copy-start.7 = (s32[4]{0:T(128)S(1)}, s32[4]{0:T(128)}, u32[]{:S(2)}) copy-start(s32[4]{0:T(128)} %index_ref.1) | copy-start | bytes 52
  6.0 28.1 %collective-permute-start.3 = (f32[128,2048]{1,0:T(8,128)}, f32[128,2048]{1,0:T(8,128)}, u32[]{:S(2)}, u32[]{:S(2)}) collective-permute-start(f32[128,2048]{1,0:T(8,128)} %get-tuple-element.17), channel_id=1, source_target_pairs={{0,1},{1,0},{2,3},{3,2},{4,5},{5,4},{6,7},{7,6},{8,9},{9,8},{10,11... | collective-permute-start | bytes 3145736 | tf_op jit(solution)/shard_map/ppermute | solution.py:475
  6.9 19.2 %copy-start.2 = (bf16[2,96,40]{2,1,0:T(8,128)(2,1)S(1)}, bf16[2,96,40]{2,1,0:T(8,128)(2,1)}, u32[]{:S(2)}) copy-start(bf16[2,96,40]{2,1,0:T(8,128)(2,1)} %constant.15.clone.select_ref) | copy-start | bytes 46084
  6.9 19.2 %collective-permute-start = (bf16[40,4096]{1,0:T(8,128)(2,1)S(1)}, bf16[40,4096]{1,0:T(8,128)(2,1)S(1)}, u32[]{:S(2)}, u32[]{:S(2)}) collective-permute-start(bf16[40,4096]{1,0:T(8,128)(2,1)S(1)} %get-tuple-element.11), channel_id=1, source_target_pairs={{0,2},{2,4},{4,6},{6,8},{8,10},{10,12},{12,14},{1,3},{3,5},{5,7},{... | collective-permute-start | bytes 983048 | tf_op jit(solution)/shard_map/ppermute | solution.py:472
  11.5 14.6 %collective-permute-start.1 = (bf16[40,4096]{1,0:T(8,128)(2,1)S(1)}, bf16[40,4096]{1,0:T(8,128)(2,1)S(1)}, u32[]{:S(2)}, u32[]{:S(2)}) collective-permute-start(bf16[40,4096]{1,0:T(8,128)(2,1)S(1)} %get-tuple-element.12), channel_id=1, source_target_pairs={{2,0},{4,2},{6,4},{8,6},{10,8},{12,10},{14,12},{3,1},{5,3},{7,5},{... | collective-permute-start | bytes 983048 | tf_op jit(solution)/shard_map/ppermute | solution.py:473
  30.0 4.0 %collective-permute-start.2 = (bf16[128,2048]{1,0:T(8,128)(2,1)S(1)}, bf16[128,2048]{1,0:T(8,128)(2,1)S(1)}, u32[]{:S(2)}, u32[]{:S(2)}) collective-permute-start(bf16[128,2048]{1,0:T(8,128)(2,1)S(1)} %edge_rows.3), channel_id=1, source_target_pairs={{0,1},{1,0},{2,3},{3,2},{4,5},{5,4},{6,7},{7,6},{8,9},{9,8},{10,11... | collective-permute-start | bytes 1572872 | tf_op jit(solution)/shard_map/ppermute | solution.py:481
  36.7 1.4 %collective-permute-start.4 = (f32[2,8,128]{2,1,0:T(8,128)S(1)}, f32[2,8,128]{2,1,0:T(8,128)S(1)}, u32[]{:S(2)}, u32[]{:S(2)}) collective-permute-start(f32[2,8,128]{2,1,0:T(8,128)S(1)} %get-tuple-element.18), channel_id=1, source_target_pairs={{0,1},{1,0},{2,3},{3,2},{4,5},{5,4},{6,7},{7,6},{8,9},{9,8},{10,11... | collective-permute-start | bytes 24584 | tf_op jit(solution)/shard_map/ppermute | solution.py:485
  38.1 4.2 %collective-permute-start.5 = (f32[2,8,128]{2,1,0:T(8,128)S(1)}, f32[2,8,128]{2,1,0:T(8,128)S(1)}, u32[]{:S(2)}, u32[]{:S(2)}) collective-permute-start(f32[2,8,128]{2,1,0:T(8,128)S(1)} %maximum_add_fusion), channel_id=1, source_target_pairs={{0,2},{2,0},{4,6},{6,4},{8,10},{10,8},{12,14},{14,12},{1,3},{3,1},... | collective-permute-start | bytes 24584 | tf_op jit(solution)/shard_map/ppermute | solution.py:489
  42.3 4.6 %collective-permute-start.6 = (f32[2,8,128]{2,1,0:T(8,128)S(1)}, f32[2,8,128]{2,1,0:T(8,128)S(1)}, u32[]{:S(2)}, u32[]{:S(2)}) collective-permute-start(f32[2,8,128]{2,1,0:T(8,128)S(1)} %add.15), channel_id=1, source_target_pairs={{0,4},{2,6},{4,0},{6,2},{8,12},{10,14},{12,8},{14,10},{1,5},{3,7},... | collective-permute-start | bytes 24584 | tf_op jit(solution)/shard_map/ppermute | solution.py:489
  46.9 4.7 %collective-permute-start.7 = (f32[2,8,128]{2,1,0:T(8,128)S(1)}, f32[2,8,128]{2,1,0:T(8,128)S(1)}, u32[]{:S(2)}, u32[]{:S(2)}) collective-permute-start(f32[2,8,128]{2,1,0:T(8,128)S(1)} %add.16), channel_id=1, source_target_pairs={{0,8},{2,10},{4,12},{6,14},{8,0},{10,2},{12,4},{14,6},{1,9},{3,11}... | collective-permute-start | bytes 24584 | tf_op jit(solution)/shard_map/ppermute | solution.py:489

commit v3 on v2

--- a/solution.py
+++ b/solution.py
@@ -25,6 +25,10 @@
     return [pltpu.with_memory_space_constraint(array, pltpu.VMEM) for array in arrays]
 
 
+def away(*arrays):
+    return [pltpu.with_memory_space_constraint(array, pltpu.HBM) for array in arrays]
+
+
 def held(shape, dtype):
     return pltpu.VMEM(shape, dtype)
 
@@ -36,45 +40,63 @@
     return lax.broadcasted_iota(jnp.int32, shape, len(shape) - 1)
 
 
-def rotated(groups):
-    turned = [pltpu.roll(group, SHIFT, 1) for group in groups]
-    low = lane_index(groups[0].shape) < SHIFT
-    return [jnp.where(low, turned[g - 1], turned[g]) for g in range(len(groups))]
-
-
-def pack_kernel(select_ref, x_ref, up_ref, down_ref):
-    columns = x_ref.shape[1]
+def pack_kernel(visits, half, x_ref, up_ref, down_ref, rows_ref, arrived):
+    count, columns = x_ref.shape
+    rows = count // visits
     edge = up_ref.shape[0]
+    chunks = arrived.shape[0]
+    width = columns // chunks
+    copies = []
+    for c in range(chunks):
+        lanes = slice(c * width, (c + 1) * width)
+        copies.append(
+            pltpu.make_async_copy(x_ref.at[:, lanes], rows_ref.at[:, lanes], arrived.at[c])
+        )
+        copies[c].start()
+    target = lax.broadcasted_iota(jnp.int32, (2 * edge, count), 0)
+    source = lane_index((2 * edge, count))
+    within = lax.rem(target, edge)
+    line = lax.div(within, half) * rows + lax.rem(within, half)
+    line = line + jnp.where(target < edge, rows - half, 0)
+    select = jnp.where(source == line, 1.0, 0.0).astype(BF16)
+    low = lane_index((2 * edge, LANES)) < SHIFT
     step = 2 * LANES
-    groups = []
+
+    def put(g, value):
+        lanes = slice(g * LANES, (g + 1) * LANES)
+        up_ref[:, lanes] = value[:edge].astype(BF16)
+        down_ref[:, lanes] = value[edge:].astype(BF16)
+
+    before = opening = None
     for start in range(0, columns, step):
-        rows = jnp.dot(
-            select_ref[...], x_ref[:, start : start + step], preferred_element_type=F32
-        )
-        groups += [rows[:, :LANES], rows[:, LANES:]]
-    for g, group in enumerate(rotated(groups)):
-        lanes = slice(g * LANES, (g + 1) * LANES)
-        up_ref[:, lanes] = group[:edge].astype(BF16)
-        down_ref[:, lanes] = group[edge:].astype(BF16)
+        if start % width == 0:
+            copies[start // width].wait()
+        found = jnp.dot(select, rows_ref[:, start : start + step], preferred_element_type=F32)
+        for part in range(2):
+            here = pltpu.roll(found[:, part * LANES : (part + 1) * LANES], SHIFT, 1)
+            if before is None:
+                opening = here
+            else:
+                put(start // LANES + part, jnp.where(low, before, here))
+            before = here
+    put(0, jnp.where(low, before, opening))
 
 
 def pack_rows(warps, half):
     visits, rows, columns = warps.shape
-    edge = visits * half
-    select = np.zeros((2 * edge, visits * rows), np.float32)
-    for v in range(visits):
-        for i in range(half):
-            select[v * half + i, v * rows + rows - half + i] = 1
-            select[edge + v * half + i, v * rows + i] = 1
-    shape = held((edge, columns), BF16)
-    return pl.pallas_call(
-        pack_kernel,
-        out_shape=(shape, shape),
-        in_specs=[whole(), whole()],
-        out_specs=(whole(), whole()),
+    count = visits * rows
+    shape = held((visits * half, columns), BF16)
+    chunks = max(1, columns // 1024)
+    (image,) = away(warps.reshape(count, columns))
+    return pl.pallas_call(
+        functools.partial(pack_kernel, visits, half),
+        out_shape=(shape, shape, held((count, columns), BF16)),
+        in_specs=[pl.BlockSpec(memory_space=pl.ANY)],
+        out_specs=(whole(),) * 3,
+        scratch_shapes=[pltpu.SemaphoreType.DMA((chunks,))],
         compiler_params=LIMIT,
         name="pack",
-    )(jnp.asarray(select, BF16), *kept(warps.reshape(visits * rows, columns)))
+    )(image)
 
 
 def weight_kernel(visits, bands, side_ref, cover_ref, var_ref, bits_ref, send_ref, keep_ref):
@@ -102,7 +124,7 @@
 
 def pixel_weights(badbits, coverage, variance, side):
     visits, rows, columns = badbits.shape
-    bits = badbits.reshape(visits * rows, columns)
+    (bits,) = away(badbits.reshape(visits * rows, columns))
     width = columns // 2
     tile = min(512, width)
     count = width // tile
@@ -127,7 +149,7 @@
         ),
         compiler_params=LIMIT,
         name="weights",
-    )(side, coverage.T, variance.T, bits)
+    )(side, *away(coverage.T, variance.T), bits)
 
 
 def split(value):
@@ -276,12 +298,11 @@
             out_ref[v * rows : (v + 1) * rows, at] = total
         return carry
 
-    lax.fori_loop(0, columns // (2 * LANES), body, 0)
-
-
-def own_part(warps, column, own):
-    visits, rows, columns = warps.shape
-    count = visits * rows
+    lax.fori_loop(0, columns // (2 * LANES), body, 0, unroll=8)
+
+
+def own_part(image, column, own, visits):
+    count, columns = image.shape
     return pl.pallas_call(
         functools.partial(own_kernel, visits),
         out_shape=held((count, columns), F32),
@@ -291,10 +312,17 @@
         compiler_params=LIMIT,
         cost_estimate=pl.CostEstimate(flops=10**9, bytes_accessed=10**7, transcendentals=0),
         name="own_rows",
-    )(*kept(warps.reshape(count, columns), column, own))
-
-
-def edge_kernel(visits, side_ref, select_ref, up_ref, down_ref, column_ref, row_ref, part_ref, out_ref, shifted):
+    )(*kept(image, column, own))
+
+
+def edge_kernel(visits, side_ref, select_ref, up_ref, down_ref, column_ref, row_ref, part_ref, *refs):
+    if len(refs) > 2:
+        far_ref, out_ref, near_ref, shifted, arrived = refs
+        fetch = pltpu.make_async_copy(far_ref, near_ref, arrived)
+        fetch.start()
+    else:
+        fetch = None
+        out_ref, shifted = refs
     columns = up_ref.shape[1]
     rows = out_ref.shape[0] // visits
     width = out_ref.shape[1]
@@ -326,10 +354,12 @@
             out_ref[lines, at] = (total + part_ref[lines, source]).astype(BF16)
         return carry
 
-    lax.fori_loop(0, width // (2 * LANES), body, 0)
-
-
-def edge_part(side, up, down, column, edge, part, visits, half):
+    lax.fori_loop(0, width // (2 * LANES), body, 0, unroll=8)
+    if fetch is not None:
+        fetch.wait()
+
+
+def edge_part(side, up, down, column, edge, part, visits, half, *far):
     count, columns = part.shape
     width = columns // 2
     padded = padded_rows(half)
@@ -340,13 +370,16 @@
             select[1, v * padded + half + i, v * half + i] = 1
     return pl.pallas_call(
         functools.partial(edge_kernel, visits),
-        out_shape=held((count, width), BF16),
-        in_specs=[whole(pltpu.SMEM)] + [whole()] * 6,
-        out_specs=whole(),
-        scratch_shapes=[pltpu.VMEM((visits * padded, width + LANES), BF16)],
+        out_shape=[held((count, width), BF16)] + [held(a.shape, a.dtype) for a in far],
+        in_specs=[whole(pltpu.SMEM)]
+        + [whole()] * 6
+        + [pl.BlockSpec(memory_space=pl.ANY)] * len(far),
+        out_specs=[whole()] * (1 + len(far)),
+        scratch_shapes=[pltpu.VMEM((visits * padded, width + LANES), BF16)]
+        + [pltpu.SemaphoreType.DMA(())] * len(far),
         compiler_params=LIMIT,
         name="edge_rows",
-    )(side, jnp.asarray(select, BF16), *kept(up, down, column, edge, part))
+    )(side, jnp.asarray(select, BF16), *kept(up, down, column, edge, part), *away(*far))
 
 
 def residual_kernel(visits, *refs):
@@ -390,7 +423,7 @@
                 factor_ref[target, lanes] = weights[m] / (1.0 + term / CLIP_LEVEL)
         return carry
 
-    lax.fori_loop(0, width // LANES, body, 0)
+    lax.fori_loop(0, width // LANES, body, 0, unroll=2)
     for m in range(len(members)):
         at = slice(m * 8, (m + 1) * 8)
         sums_ref[0, m : m + 1, :] = jnp.sum(chi_ref[at, :], axis=0, keepdims=True)
@@ -468,18 +501,20 @@
     swap = [(0, 1), (1, 0)]
     side = lax.axis_index("visit").astype(jnp.int32).reshape(1)
 
-    last, leading = pack_rows(warps, half)
+    last, leading, image = pack_rows(warps, half)
     before = lax.ppermute(last, "sky", up)
     after = lax.ppermute(leading, "sky", down)
     send_weight, own_weight = pixel_weights(badbits, coverage, variance, side)
     other_weight = lax.ppermute(send_weight, "visit", swap)
     column, own, edge = tables(psf_index, psf_table, row_basis, col_basis, visits, rows)
-    part = own_part(warps, column, own)
-    send_value = edge_part(
+    part = own_part(image, column, own, visits)
+    (send_value,) = edge_part(
         1 - side, before, after, column, edge, part, visits, half
     )
     other_value = lax.ppermute(send_value, "visit", swap)
-    own_value = edge_part(side, before, after, column, edge, part, visits, half)
+    own_value, other_weight = edge_part(
+        side, before, after, column, edge, part, visits, half, other_weight
+    )
     values = (own_value, other_value)
     factors, sums = residual_pass(values, (own_weight, other_weight), visits)
     theirs = lax.ppermute(sums, "visit", swap)

time: 53.8 us -> 52.8 us (0.981)
  local copies, waits for them, and re-layouts: 3.1 us -> 0.11 us
  waiting for transfers between devices: 9.66 us -> 11.7 us
    unnamed x20 -> x10, local copies, waits for them, and re-layouts: 3.01 us -> 0.02 us
    pallas_call x1, Pallas kernels: 2.33 us -> 5.22 us  [pixel_weights(): pl.pallas_call(functools.partial(weight_kernel, visits, coverage.shape[1]...]
    ppermute x1, waiting for transfers between devices: 3.94 us -> 5.96 us  [per_device(): before = lax.ppermute(last, 'sky', up)]
    pallas_call x1, Pallas kernels: 8.11 us -> 6.1 us  [own_part(): pl.pallas_call(functools.partial(own_kernel, visits), out_shape=held((cou...]
    pallas_call x1, Pallas kernels: 2.62 us -> 1.27 us  [residual_pass(): pl.pallas_call(functools.partial(residual_kernel, visits), out_shape=(hel...]
  transfers between devices with their start and end apart: 8 -> 8, of which waited for: 5 -> 5; matrix products, arithmetic and copies ran while one was open for 0% -> 0% of each run, Pallas kernels for 33% -> 30%
where the time goes in v3:
time: 52.8 us; the launch traced here: 52.5 us
  Pallas kernels  24.4 us (46%)
  starting transfers between devices  15.5 us (29%)
  waiting for transfers between devices  11.7 us (22%)
  between operations  0.79 us (1%)
    ppermute x3, starting transfers between devices, per_device(): lax.ppermute(sums, 'sky', [(i, i ^ step) for i in range(strips)])  8.53 us
    pallas_call x2, Pallas kernels, edge_part(): pl.pallas_call(functools.partial(edge_kernel, visits), out_shape=[held((c...  6.56 us
    pallas_call x1, Pallas kernels, own_part(): pl.pallas_call(functools.partial(own_kernel, visits), out_shape=held((cou...  6.1 us
    ppermute x1, waiting for transfers between devices, per_device(): before = lax.ppermute(last, 'sky', up)  5.96 us
    pallas_call x1, Pallas kernels, pixel_weights(): pl.pallas_call(functools.partial(weight_kernel, visits, coverage.shape[1]...  5.22 us
    ppermute x3, waiting for transfers between devices, per_device(): lax.ppermute(sums, 'sky', [(i, i ^ step) for i in range(strips)])  4.89 us
    ppermute x1, starting transfers between devices, per_device(): before = lax.ppermute(last, 'sky', up)  4.56 us
    pallas_call x1, Pallas kernels, pack_rows(): pl.pallas_call(functools.partial(pack_kernel, visits, half), out_shape=(s...  2.07 us
  transfers between devices with their start and end apart: 8, of which 5 were waited for; matrix products, arithmetic and copies ran while one was open for 0% of the time, Pallas kernels for 30%

profile of v3, /device:TPU:0, one launch (start us, length us, event | category | flops | bytes accessed | tf_op | source)
XLA Modules:
  0.0 52.5 jit_solution(11830516001273143587)
XLA Ops:
  0.6 0.0 copy-start.3
  0.6 0.0 copy-start.4
  0.7 0.0 copy-start.1
  0.7 0.0 copy-start.2
  0.7 5.2 %weights.1 = (f32[128,2048]{1,0:T(8,128)}, f32[128,2048]{1,0:T(8,128)S(1)}) custom-call(s32[1]{0:T(128)} %bitcast.side_ref, s32[1,4]{1,0:T(1,128)} %bitcast.9, f32[1,4]{1,0:T(1,128)} %bitcast.10, s32[128,4096]{1,0:T(8,128)} %bitcast.7), custom_call_target="tpu_custom_call" | custom-call | tf_op jit(solution)/shard_map/weights/pallas_call | solution.py:137
  5.9 0.5 collective-permute-start.2
  6.4 2.1 %pack.1 = (bf16[40,4096]{1,0:T(8,128)(2,1)S(1)}, bf16[40,4096]{1,0:T(8,128)(2,1)S(1)}, bf16[128,4096]{1,0:T(8,128)(2,1)S(1)}) custom-call(bf16[128,4096]{1,0:T(8,128)(2,1)} %bitcast.8), custom_call_target="tpu_custom_call" | custom-call | tf_op jit(solution)/shard_map/pack/pallas_call | solution.py:91
  8.5 0.0 copy-start
  8.5 4.6 %collective-permute-start = (bf16[40,4096]{1,0:T(8,128)(2,1)S(1)}, bf16[40,4096]{1,0:T(8,128)(2,1)S(1)}, u32[]{:S(2)}, u32[]{:S(2)}) collective-permute-start(bf16[40,4096]{1,0:T(8,128)(2,1)S(1)} %get-tuple-element.14), channel_id=1, source_target_pairs={{0,2},{2,4},{4,6},{6,8},{8,10},{10,12},{12,14},{1,3},{3,5},{5,7},{... | collective-permute-start | bytes 983048 | tf_op jit(solution)/shard_map/ppermute | solution.py:505
  13.0 1.3 %collective-permute-start.1 = (bf16[40,4096]{1,0:T(8,128)(2,1)S(1)}, bf16[40,4096]{1,0:T(8,128)(2,1)S(1)}, u32[]{:S(2)}, u32[]{:S(2)}) collective-permute-start(bf16[40,4096]{1,0:T(8,128)(2,1)S(1)} %get-tuple-element.15), channel_id=1, source_target_pairs={{2,0},{4,2},{6,4},{8,6},{10,8},{12,10},{14,12},{3,1},{5,3},{7,5},{... | collective-permute-start | bytes 983048 | tf_op jit(solution)/shard_map/ppermute | solution.py:506
  14.3 0.0 copy-done.3
  14.4 0.1 rev.3
  14.4 0.0 copy-done.4
  14.4 0.0 copy-done.1
  14.5 0.0 copy-done.2
  14.5 1.1 %tables.1 = (bf16[256,1024]{1,0:T(8,128)(2,1)S(1)}, bf16[256,256]{1,0:T(8,128)(2,1)S(1)}, bf16[256,192]{1,0:T(8,128)(2,1)S(1)}) custom-call(s32[4]{0:T(128)S(1)} %copy-done.2, f32[8,16]{1,0:T(8,128)S(1)} %bitcast.6, f32[16,128]{1,0:T(8,128)S(1)} %fusion.3.profile_ref), custom_call_target="tpu_custom_call" | custom-call | tf_op jit(solution)/shard_map/tables/pallas_call | solution.py:238
  15.6 6.1 %own_rows.1.part_ref = f32[128,4096]{1,0:T(8,128)S(1)} custom-call(bf16[128,4096]{1,0:T(8,128)(2,1)S(1)} %get-tuple-element.18.x_ref, bf16[256,1024]{1,0:T(8,128)(2,1)S(1)} %get-tuple-element.16.column_ref, bf16[256,256]{1,0:T(8,128)(2,1)S(1)} %get-tuple-element.19.row_ref), custom_call_target="tpu_custom_call" | custom-call | flops 1000000000 | bytes 10000000 | tf_op jit(solution)/shard_map/own_rows/pallas_call | solution.py:306
  21.7 6.0 %collective-permute-done.up_ref = bf16[40,4096]{1,0:T(8,128)(2,1)S(1)} collective-permute-done((bf16[40,4096]{1,0:T(8,128)(2,1)S(1)}, bf16[40,4096]{1,0:T(8,128)(2,1)S(1)}, u32[]{:S(2)}, u32[]{:S(2)}) %collective-permute-start) | collective-permute-done | bytes 327712 | tf_op jit(solution)/shard_map/ppermute | solution.py:505
  27.7 0.0 collective-permute-done.1.down_ref
  27.7 0.0 copy-done
  27.7 2.8 %edge_rows.3 = bf16[128,2048]{1,0:T(8,128)(2,1)S(1)} custom-call(s32[1]{0:T(128)S(6)} %sub.3.side_ref, bf16[2,96,40]{2,1,0:T(8,128)(2,1)S(1)} %copy-done, bf16[40,4096]{1,0:T(8,128)(2,1)S(1)} %collective-permute-done.up_ref, bf16[40,4096]{1,0:T(8,128)(2,1)S(1)} %collective-permute-done.1.down_ref, bf16[256,1024]{1,0:T(8,128)(2,1)S(1)} %get-tuple-element.16.column_ref, ...), custom_call_target="tpu_custom_call" | custom-call | tf_op jit(solution)/shard_map/edge_rows/pallas_call | solution.py:371
  30.5 0.1 collective-permute-start.3
  30.6 0.0 collective-permute-done.2.refs_0_
  30.6 3.7 %edge_rows.2 = (bf16[128,2048]{1,0:T(8,128)(2,1)S(1)}, f32[128,2048]{1,0:T(8,128)S(1)}) custom-call(s32[1]{0:T(128)} %bitcast.side_ref, bf16[2,96,40]{2,1,0:T(8,128)(2,1)S(1)} %copy-done, bf16[40,4096]{1,0:T(8,128)(2,1)S(1)} %collective-permute-done.up_ref, bf16[40,4096]{1,0:T(8,128)(2,1)S(1)} %collective-permute-done.1.down_ref, ...), custom_call_target="tpu_custom_call" | custom-call | tf_op jit(solution)/shard_map/edge_rows/pallas_call | solution.py:371
  34.3 0.0 collective-permute-done.3.refs_1_.other_ref
  34.4 1.3 %residual.1 = (f32[256,2048]{1,0:T(8,128)S(1)}, f32[2,8,128]{2,1,0:T(8,128)S(1)}) custom-call(bf16[128,2048]{1,0:T(8,128)(2,1)S(1)} %get-tuple-element.21.refs_0_.own_ref, bf16[128,2048]{1,0:T(8,128)(2,1)S(1)} %collective-permute-done.3.refs_1_.other_ref, f32[128,2048]{1,0:T(8,128)S(1)} %get-tuple-element.22.refs_2_, f32[128,2048]{1,0:T(8,128)S(1)} %get-tuple-element.23.refs_3_), custom_call_target="tpu_custom_call" | custom-call | tf_op jit(solution)/shard_map/residual/pallas_call | solution.py:436
  35.6 0.5 %collective-permute-start.4 = (f32[2,8,128]{2,1,0:T(8,128)S(1)}, f32[2,8,128]{2,1,0:T(8,128)S(1)}, u32[]{:S(2)}, u32[]{:S(2)}) collective-permute-start(f32[2,8,128]{2,1,0:T(8,128)S(1)} %get-tuple-element.24), channel_id=1, source_target_pairs={{0,1},{1,0},{2,3},{3,2},{4,5},{5,4},{6,7},{7,6},{8,9},{9,8},{10,11... | collective-permute-start | bytes 24584 | tf_op jit(solution)/shard_map/ppermute | solution.py:520
  36.2 0.8 %collective-permute-done.4 = f32[2,8,128]{2,1,0:T(8,128)S(1)} collective-permute-done((f32[2,8,128]{2,1,0:T(8,128)S(1)}, f32[2,8,128]{2,1,0:T(8,128)S(1)}, u32[]{:S(2)}, u32[]{:S(2)}) %collective-permute-start.4) | collective-permute-done | bytes 8224 | tf_op jit(solution)/shard_map/ppermute | solution.py:520
  37.0 2.5 %collective-permute-start.5 = (f32[2,8,128]{2,1,0:T(8,128)S(1)}, f32[2,8,128]{2,1,0:T(8,128)S(1)}, u32[]{:S(2)}, u32[]{:S(2)}) collective-permute-start(f32[2,8,128]{2,1,0:T(8,128)S(1)} %maximum_add_fusion), channel_id=1, source_target_pairs={{0,2},{2,0},{4,6},{6,4},{8,10},{10,8},{12,14},{14,12},{1,3},{3,1},... | collective-permute-start | bytes 24584 | tf_op jit(solution)/shard_map/ppermute | solution.py:524
  39.5 1.6 %collective-permute-done.5 = f32[2,8,128]{2,1,0:T(8,128)S(1)} collective-permute-done((f32[2,8,128]{2,1,0:T(8,128)S(1)}, f32[2,8,128]{2,1,0:T(8,128)S(1)}, u32[]{:S(2)}, u32[]{:S(2)}) %collective-permute-start.5) | collective-permute-done | bytes 8224 | tf_op jit(solution)/shard_map/ppermute | solution.py:524
  41.2 3.0 %collective-permute-start.6 = (f32[2,8,128]{2,1,0:T(8,128)S(1)}, f32[2,8,128]{2,1,0:T(8,128)S(1)}, u32[]{:S(2)}, u32[]{:S(2)}) collective-permute-start(f32[2,8,128]{2,1,0:T(8,128)S(1)} %add.15), channel_id=1, source_target_pairs={{0,4},{2,6},{4,0},{6,2},{8,12},{10,14},{12,8},{14,10},{1,5},{3,7},... | collective-permute-start | bytes 24584 | tf_op jit(solution)/shard_map/ppermute | solution.py:524
  44.2 1.6 %collective-permute-done.6 = f32[2,8,128]{2,1,0:T(8,128)S(1)} collective-permute-done((f32[2,8,128]{2,1,0:T(8,128)S(1)}, f32[2,8,128]{2,1,0:T(8,128)S(1)}, u32[]{:S(2)}, u32[]{:S(2)}) %collective-permute-start.6) | collective-permute-done | bytes 8224 | tf_op jit(solution)/shard_map/ppermute | solution.py:524
  45.8 3.0 %collective-permute-start.7 = (f32[2,8,128]{2,1,0:T(8,128)S(1)}, f32[2,8,128]{2,1,0:T(8,128)S(1)}, u32[]{:S(2)}, u32[]{:S(2)}) collective-permute-start(f32[2,8,128]{2,1,0:T(8,128)S(1)} %add.16), channel_id=1, source_target_pairs={{0,8},{2,10},{4,12},{6,14},{8,0},{10,2},{12,4},{14,6},{1,9},{3,11}... | collective-permute-start | bytes 24584 | tf_op jit(solution)/shard_map/ppermute | solution.py:524
  48.8 1.6 %collective-permute-done.7 = f32[2,8,128]{2,1,0:T(8,128)S(1)} collective-permute-done((f32[2,8,128]{2,1,0:T(8,128)S(1)}, f32[2,8,128]{2,1,0:T(8,128)S(1)}, u32[]{:S(2)}, u32[]{:S(2)}) %collective-permute-start.7) | collective-permute-done | bytes 8224 | tf_op jit(solution)/shard_map/ppermute | solution.py:524
  50.4 2.0 %final.1 = (f32[32,2048]{1,0:T(8,128)}, f32[4]{0:T(128)}) custom-call(f32[2,8,128]{2,1,0:T(8,128)S(1)} %add.17.sums_ref, bf16[128,2048]{1,0:T(8,128)(2,1)S(1)} %get-tuple-element.21.refs_0_.own_ref, bf16[128,2048]{1,0:T(8,128)(2,1)S(1)} %collective-permute-done.3.refs_1_.other_ref, f32[256,2048]{1,0:T(8,128)S(1)} %get-tuple-element.25.factor_ref), custom_call_target="tpu_custom_call" | custom-call | tf_op jit(solution)/shard_map/final/pallas_call | solution.py:481
  (6 shorter events, 0.0 us)
Async XLA Ops:
  0.6 13.7 %copy-start.3 = (bf16[8,21]{1,0:T(8,128)(2,1)S(1)}, bf16[8,21]{1,0:T(8,128)(2,1)}, u32[]{:S(2)}) copy-start(bf16[8,21]{1,0:T(8,128)(2,1)} %param.17) | copy-start | bytes 1012
  0.6 13.8 %copy-start.4 = (bf16[8,21]{1,0:T(8,128)(2,1)S(1)}, bf16[8,21]{1,0:T(8,128)(2,1)}, u32[]{:S(2)}) copy-start(bf16[8,21]{1,0:T(8,128)(2,1)} %param.16) | copy-start | bytes 1012
  0.7 13.8 %copy-start.1 = (f32[16,8]{0,1:T(8,128)S(1)}, f32[16,8]{0,1:T(8,128)}, u32[]{:S(2)}) copy-start(f32[16,8]{0,1:T(8,128)} %param.15) | copy-start | bytes 1540
  0.7 13.8 %copy-start.2 = (s32[4]{0:T(128)S(1)}, s32[4]{0:T(128)}, u32[]{:S(2)}) copy-start(s32[4]{0:T(128)} %index_ref.1) | copy-start | bytes 52
  5.9 24.7 %collective-permute-start.2 = (f32[128,2048]{1,0:T(8,128)}, f32[128,2048]{1,0:T(8,128)}, u32[]{:S(2)}, u32[]{:S(2)}) collective-permute-start(f32[128,2048]{1,0:T(8,128)} %get-tuple-element.20), channel_id=1, source_target_pairs={{0,1},{1,0},{2,3},{3,2},{4,5},{5,4},{6,7},{7,6},{8,9},{9,8},{10,11... | collective-permute-start | bytes 3145736 | tf_op jit(solution)/shard_map/ppermute | solution.py:508
  8.5 19.2 %copy-start = (bf16[2,96,40]{2,1,0:T(8,128)(2,1)S(1)}, bf16[2,96,40]{2,1,0:T(8,128)(2,1)}, u32[]{:S(2)}) copy-start(bf16[2,96,40]{2,1,0:T(8,128)(2,1)} %constant.12.clone.select_ref) | copy-start | bytes 46084
  8.5 19.2 %collective-permute-start = (bf16[40,4096]{1,0:T(8,128)(2,1)S(1)}, bf16[40,4096]{1,0:T(8,128)(2,1)S(1)}, u32[]{:S(2)}, u32[]{:S(2)}) collective-permute-start(bf16[40,4096]{1,0:T(8,128)(2,1)S(1)} %get-tuple-element.14), channel_id=1, source_target_pairs={{0,2},{2,4},{4,6},{6,8},{8,10},{10,12},{12,14},{1,3},{3,5},{5,7},{... | collective-permute-start | bytes 983048 | tf_op jit(solution)/shard_map/ppermute | solution.py:505
  13.0 14.6 %collective-permute-start.1 = (bf16[40,4096]{1,0:T(8,128)(2,1)S(1)}, bf16[40,4096]{1,0:T(8,128)(2,1)S(1)}, u32[]{:S(2)}, u32[]{:S(2)}) collective-permute-start(bf16[40,4096]{1,0:T(8,128)(2,1)S(1)} %get-tuple-element.15), channel_id=1, source_target_pairs={{2,0},{4,2},{6,4},{8,6},{10,8},{12,10},{14,12},{3,1},{5,3},{7,5},{... | collective-permute-start | bytes 983048 | tf_op jit(solution)/shard_map/ppermute | solution.py:506
  30.5 3.8 %collective-permute-start.3 = (bf16[128,2048]{1,0:T(8,128)(2,1)S(1)}, bf16[128,2048]{1,0:T(8,128)(2,1)S(1)}, u32[]{:S(2)}, u32[]{:S(2)}) collective-permute-start(bf16[128,2048]{1,0:T(8,128)(2,1)S(1)} %edge_rows.3), channel_id=1, source_target_pairs={{0,1},{1,0},{2,3},{3,2},{4,5},{5,4},{6,7},{7,6},{8,9},{9,8},{10,11... | collective-permute-start | bytes 1572872 | tf_op jit(solution)/shard_map/ppermute | solution.py:514
  35.6 1.4 %collective-permute-start.4 = (f32[2,8,128]{2,1,0:T(8,128)S(1)}, f32[2,8,128]{2,1,0:T(8,128)S(1)}, u32[]{:S(2)}, u32[]{:S(2)}) collective-permute-start(f32[2,8,128]{2,1,0:T(8,128)S(1)} %get-tuple-element.24), channel_id=1, source_target_pairs={{0,1},{1,0},{2,3},{3,2},{4,5},{5,4},{6,7},{7,6},{8,9},{9,8},{10,11... | collective-permute-start | bytes 24584 | tf_op jit(solution)/shard_map/ppermute | solution.py:520
  37.0 4.2 %collective-permute-start.5 = (f32[2,8,128]{2,1,0:T(8,128)S(1)}, f32[2,8,128]{2,1,0:T(8,128)S(1)}, u32[]{:S(2)}, u32[]{:S(2)}) collective-permute-start(f32[2,8,128]{2,1,0:T(8,128)S(1)} %maximum_add_fusion), channel_id=1, source_target_pairs={{0,2},{2,0},{4,6},{6,4},{8,10},{10,8},{12,14},{14,12},{1,3},{3,1},... | collective-permute-start | bytes 24584 | tf_op jit(solution)/shard_map/ppermute | solution.py:524
  41.2 4.6 %collective-permute-start.6 = (f32[2,8,128]{2,1,0:T(8,128)S(1)}, f32[2,8,128]{2,1,0:T(8,128)S(1)}, u32[]{:S(2)}, u32[]{:S(2)}) collective-permute-start(f32[2,8,128]{2,1,0:T(8,128)S(1)} %add.15), channel_id=1, source_target_pairs={{0,4},{2,6},{4,0},{6,2},{8,12},{10,14},{12,8},{14,10},{1,5},{3,7},... | collective-permute-start | bytes 24584 | tf_op jit(solution)/shard_map/ppermute | solution.py:524
  45.8 4.6 %collective-permute-start.7 = (f32[2,8,128]{2,1,0:T(8,128)S(1)}, f32[2,8,128]{2,1,0:T(8,128)S(1)}, u32[]{:S(2)}, u32[]{:S(2)}) collective-permute-start(f32[2,8,128]{2,1,0:T(8,128)S(1)} %add.16), channel_id=1, source_target_pairs={{0,8},{2,10},{4,12},{6,14},{8,0},{10,2},{12,4},{14,6},{1,9},{3,11}... | collective-permute-start | bytes 24584 | tf_op jit(solution)/shard_map/ppermute | solution.py:524

commit v4 on v3

v4 whole, which is shorter than its diff:
```python
import functools

import jax
import jax.numpy as jnp
from jax import lax
from jax.experimental import pallas as pl
from jax.experimental.pallas import tpu as pltpu
from jax.sharding import PartitionSpec as P

PRIOR_WEIGHT = 1.0
CLIP_LEVEL = 9.0
CHI_OFFSET = 0.5
LANES = 128
SHIFT = LANES // 2
F32 = jnp.float32
BF16 = jnp.bfloat16


def whole(space=pltpu.VMEM):
    return pl.BlockSpec(memory_space=space)


def kept(*arrays):
    return [pltpu.with_memory_space_constraint(array, pltpu.VMEM) for array in arrays]


def away(*arrays):
    return [pltpu.with_memory_space_constraint(array, pltpu.HBM) for array in arrays]


def held(shape, dtype):
    return pltpu.VMEM(shape, dtype)


LIMIT = pltpu.CompilerParams(vmem_limit_bytes=20 * 1024 * 1024)


def lane_index(shape):
    return lax.broadcasted_iota(jnp.int32, shape, len(shape) - 1)


def pack_kernel(half, first, skip, x_ref, edge_ref, rows_ref, arrived):
    visits, depth, columns = rows_ref.shape
    chunks = arrived.shape[0]
    width = columns // chunks
    copies = []
    for c in range(chunks):
        lanes = slice(c * width, (c + 1) * width)
        copies.append(
            pltpu.make_async_copy(
                x_ref.at[:, first : first + depth, lanes], rows_ref.at[:, :, lanes], arrived.at[c]
            )
        )
        copies[c].start()
    main = half // 8 * 8
    rest = half - main
    shape = (visits * half, visits * depth)
    target = lax.broadcasted_iota(jnp.int32, shape, 0)
    source_row = lane_index(shape)
    line = jnp.where(
        target < visits * main,
        lax.div(target, max(main, 1)) * depth + lax.rem(target, max(main, 1)),
        lax.div(target - visits * main, max(rest, 1)) * depth
        + main
        + lax.rem(target - visits * main, max(rest, 1)),
    )
    select = jnp.where(source_row == line + skip, 1.0, 0.0).astype(BF16)
    low = lane_index((edge_ref.shape[0], LANES)) < SHIFT
    step = 2 * LANES

    def put(g, value):
        edge_ref[:, g * LANES : (g + 1) * LANES] = value.astype(BF16)

    before = opening = None
    for start in range(0, columns, step):
        if start % width == 0:
            copies[start // width].wait()
        source = rows_ref[:, :, start : start + step].reshape(visits * depth, step)
        found = jnp.dot(select, source, preferred_element_type=F32)
        for part in range(2):
            here = pltpu.roll(found[:, part * LANES : (part + 1) * LANES], SHIFT, 1)
            if before is None:
                opening = here
            else:
                put(start // LANES + part, jnp.where(low, before, here))
            before = here
    put(0, jnp.where(low, before, opening))


def pack_rows(warps, half, upper):
    visits, rows, columns = warps.shape
    depth = rows // 2
    assert depth >= half and rows % 2 == 0
    first = 0 if upper else depth
    skip = 0 if upper else depth - half
    chunks = max(1, columns // 1024)
    return pl.pallas_call(
        functools.partial(pack_kernel, half, first, skip),
        out_shape=(held((visits * half, columns), BF16), held((visits, depth, columns), BF16)),
        in_specs=[pl.BlockSpec(memory_space=pl.ANY)],
        out_specs=(whole(),) * 2,
        scratch_shapes=[pltpu.SemaphoreType.DMA((chunks,))],
        compiler_params=LIMIT,
        name="pack_upper" if upper else "pack_lower",
    )(*away(warps))


def level_rows(visits, bands):
    return -(-3 * visits * bands // 16) * 16


def weight_kernel(visits, bands, side_ref, cover_ref, var_ref, bits_ref, send_ref, keep_ref):
    count = bits_ref.shape[0]
    rows = count // visits
    high = rows // bands
    width = bits_ref.shape[1]
    steps = send_ref.shape[1] // width
    step = pl.program_id(0)
    half = lax.div(step, steps)
    lanes = pl.ds(pl.multiple_of(lax.rem(step, steps) * width, width), width)
    extra = level_rows(visits, bands)

    def fill(out_ref):
        line = lax.broadcasted_iota(jnp.int32, (extra, LANES), 0)
        levels = jnp.zeros((extra, LANES), F32)
        for v in range(visits):
            for b in range(bands):
                at = slice(v * rows + b * high, v * rows + (b + 1) * high)
                covers = jnp.where(cover_ref[b, v] != 0, 7, 0)
                usable = jnp.bitwise_and(bits_ref[at, :], 7) < covers
                out_ref[at, lanes] = jnp.where(usable, 1.0, 0.0).astype(BF16)
                left = 1.0 / jnp.full((8, LANES), var_ref[b, v], F32)
                for k in range(3):
                    part = left.astype(BF16).astype(F32)
                    left = left - part
                    spot = (k * bands + b) * visits + v
                    levels = jnp.where(line == spot, part[:1], levels)
        wide = jnp.concatenate([levels.astype(BF16)] * (width // LANES), axis=1)
        out_ref[count:, lanes] = wide

    pl.when(half == 0)(lambda: fill(send_ref))
    pl.when(half == 1)(lambda: fill(keep_ref))


def pixel_weights(badbits, coverage, variance, side):
    visits, rows, columns = badbits.shape
    bands = coverage.shape[1]
    (bits,) = away(badbits.reshape(visits * rows, columns))
    width = columns // 2
    tile = min(1024, width)
    count = width // tile
    shape = held((visits * rows + level_rows(visits, bands), width), BF16)

    def block(i, s):
        first = i < count
        return 0, jnp.where(first, (1 - s[0]) * count + i, s[0] * count + i - count)

    return pl.pallas_call(
        functools.partial(weight_kernel, visits, bands),
        out_shape=(shape, shape),
        grid_spec=pltpu.PrefetchScalarGridSpec(
            num_scalar_prefetch=1,
            grid=(2 * count,),
            in_specs=[
                whole(pltpu.SMEM),
                whole(pltpu.SMEM),
                pl.BlockSpec((visits * rows, tile), block),
            ],
            out_specs=(whole(), whole()),
        ),
        compiler_params=LIMIT,
        name="weights",
    )(side, *away(coverage.T, variance.T), bits)


def split(value):
    high = value.astype(BF16)
    return high, (value - high.astype(F32)).astype(BF16)


def edge_segments(visits, rows, half):
    main = half // 8 * 8
    rest = half - main
    segments = []
    for v in range(visits):
        here, start = [], 0
        for below in (0, 1):
            here.append((start, start + main, (half + rows if below else 0) - start))
            start += main
        for below in (0, 1):
            first = start + v * rest
            offset = (half + rows if below else 0) + main - first
            here.append((first, first + rest, offset))
            start += visits * rest
        segments.append(here)
    return segments, start


def table_kernel(visits, rows, half, index_ref, table_ref, profile_ref, column_out, own_out, edge_out):
    bases = table_ref.shape[0]
    window = 2 * LANES

    def spread(line, shift, count):
        line = jnp.broadcast_to(line, (8, LANES))
        block = pltpu.roll(line, 0, 1, stride=1, stride_axis=0)
        blocks = [pltpu.roll(block, (shift + i) % LANES, 1) for i in range(0, count, 8)]
        return jnp.concatenate(blocks, axis=0)

    k = lax.broadcasted_iota(jnp.int32, (window, LANES), 0)
    gap = k - lane_index((window, LANES))
    inside = (gap >= 0) & (gap < LANES)
    for b in range(bases):
        line = profile_ref[bases + b : bases + b + 1, :]
        band = jnp.where(inside, spread(line, SHIFT - half, window), 0.0)
        column_out[:, b * LANES : (b + 1) * LANES] = band.astype(BF16)

    lane = lane_index((rows, LANES))

    def assemble(out_ref, high, segments):
        for b in range(bases):
            start = b * high % LANES
            group = b * high // LANES * LANES
            line = profile_ref[b : b + 1, :]
            found = {}
            for v in range(visits):
                total = jnp.zeros((rows, LANES), F32)
                for first, last, offset in segments[v]:
                    if first == last:
                        continue
                    key = (first, last, offset)
                    if key not in found:
                        mask = (lane >= start + first) & (lane < start + last)
                        found[key] = jnp.where(mask, spread(line, start - offset, rows), 0.0)
                    total = total + found[key]
                top, low = split(total * table_ref[b, index_ref[v]])
                at = 2 * v * rows
                lanes = slice(group, group + LANES)
                if start == 0:
                    out_ref[at : at + rows, lanes] = top
                    out_ref[at + rows : at + 2 * rows, lanes] = low
                else:
                    out_ref[at : at + rows, lanes] += top
                    out_ref[at + rows : at + 2 * rows, lanes] += low

    assemble(own_out, rows, [[(0, rows, half)]] * visits)
    segments, high = edge_segments(visits, rows, half)
    assemble(edge_out, high, segments)


def tables(psf_index, psf_table, row_basis, col_basis, visits, rows):
    bases, taps = row_basis.shape
    half = taps // 2
    profile = jnp.concatenate([row_basis, col_basis[:, ::-1]], axis=0).astype(F32)
    profile = jnp.pad(profile, ((0, 0), (0, LANES - taps)))
    return pl.pallas_call(
        functools.partial(table_kernel, visits, rows, half),
        out_shape=(
            held((2 * LANES, bases * LANES), BF16),
            held((2 * visits * rows, bases * rows), BF16),
            held((2 * visits * rows, bases * edge_segments(visits, rows, half)[1]), BF16),
        ),
        in_specs=[whole(pltpu.SMEM), whole(pltpu.SMEM), whole()],
        out_specs=(whole(),) * 3,
        compiler_params=LIMIT,
        name="tables",
    )(psf_index, psf_table.T, profile)


BLOCKS = 4


def convolve(windows, column_ref, row_ref, pieces):
    bases = column_ref.shape[1] // LANES
    count = windows[0].shape[0]
    layers = jnp.dot(
        jnp.concatenate(windows, axis=0), column_ref[...], preferred_element_type=F32
    )
    high = row_ref.shape[0] // (2 * len(pieces))
    for first in range(0, len(windows), 2):
        totals = []
        for v, parts in enumerate(pieces):
            sides = []
            for n in (first, first + 1):
                taken = [
                    layers[n * count + top : n * count + last, b * LANES : (b + 1) * LANES]
                    for b in range(bases)
                    for top, last in parts
                ]
                sides.append(jnp.concatenate(taken, axis=0).astype(BF16))
            total = jnp.dot(
                row_ref[2 * v * high : 2 * (v + 1) * high, :],
                jnp.concatenate(sides, axis=1),
                preferred_element_type=F32,
            )
            totals.append(total[:high] + total[high:])
        yield first, totals


def own_kernel(visits, upper_ref, lower_ref, column_ref, row_ref, out_ref, shifted):
    half_count, columns = upper_ref.shape
    depth = half_count // visits
    rows = 2 * depth
    groups = columns // LANES
    low = lane_index((half_count, LANES)) < SHIFT
    for place, ref in enumerate((upper_ref, lower_ref)):
        lines = slice(place * half_count, (place + 1) * half_count)
        before = jnp.zeros((half_count, LANES), F32)
        for g in range(groups + 1):
            here = jnp.zeros((half_count, LANES), F32)
            if g < groups:
                here = pltpu.roll(ref[:, g * LANES : (g + 1) * LANES].astype(F32), SHIFT, 1)
            value = jnp.where(low, before, here).astype(BF16)
            shifted[lines, g * LANES : (g + 1) * LANES] = value
            before = here
    pieces = [
        [(place * half_count + v * depth, place * half_count + (v + 1) * depth) for place in (0, 1)]
        for v in range(visits)
    ]
    blocks = min(BLOCKS, groups)

    def body(step, carry):
        windows = [
            shifted[:, pl.ds(pl.multiple_of((blocks * step + n) * LANES, LANES), 2 * LANES)]
            for n in range(blocks)
        ]
        for first, totals in convolve(windows, column_ref, row_ref, pieces):
            start = (blocks * step + first) * LANES
            at = pl.ds(pl.multiple_of(start, 2 * LANES), 2 * LANES)
            for v, total in enumerate(totals):
                out_ref[v * rows : (v + 1) * rows, at] = total
        return carry

    lax.fori_loop(0, groups // blocks, body, 0, unroll=4)


def own_part(upper, lower, column, own, visits):
    half_count, columns = upper.shape
    return pl.pallas_call(
        functools.partial(own_kernel, visits),
        out_shape=held((2 * half_count, columns), F32),
        in_specs=[whole()] * 4,
        out_specs=whole(),
        scratch_shapes=[pltpu.VMEM((2 * half_count, columns + LANES), BF16)],
        compiler_params=LIMIT,
        cost_estimate=pl.CostEstimate(flops=10**9, bytes_accessed=10**7, transcendentals=0),
        name="own_rows",
    )(*kept(upper, lower, column, own))


def edge_kernel(visits, half, side_ref, up_ref, down_ref, column_ref, row_ref, part_ref, *refs):
    out_ref, shifted = refs
    edge, columns = up_ref.shape
    rows = out_ref.shape[0] // visits
    width = out_ref.shape[1]
    groups = columns // LANES
    inner = width // LANES
    base = side_ref[0] * inner
    lane = lane_index((2 * edge, LANES))
    for g in range(inner + 1):
        at = base + g
        lanes = pl.ds(pl.multiple_of(lax.rem(at, groups) * LANES, LANES), LANES)
        value = jnp.concatenate(
            [up_ref[:, lanes].astype(F32), down_ref[:, lanes].astype(F32)], axis=0
        )
        if g == 0:
            value = jnp.where(lane >= jnp.where(at == 0, SHIFT, 0), value, 0.0)
        if g == inner:
            value = jnp.where(lane < jnp.where(at == groups, SHIFT, LANES), value, 0.0)
        shifted[:, g * LANES : (g + 1) * LANES] = value.astype(BF16)
    main = half // 8 * 8
    pieces = [
        [(top + v * main, top + (v + 1) * main) for top in (0, edge)]
        + [(top + visits * main, top + edge) for top in (0, edge)]
        for v in range(visits)
    ]
    pieces = [[(top, last) for top, last in parts if last > top] for parts in pieces]
    blocks = min(BLOCKS, inner)

    def body(step, carry):
        windows = [
            shifted[:, pl.ds(pl.multiple_of((blocks * step + n) * LANES, LANES), 2 * LANES)]
            for n in range(blocks)
        ]
        for first, totals in convolve(windows, column_ref, row_ref, pieces):
            start = (blocks * step + first) * LANES
            at = pl.ds(pl.multiple_of(start, 2 * LANES), 2 * LANES)
            source = pl.ds(pl.multiple_of(base * LANES + start, 2 * LANES), 2 * LANES)
            for v, total in enumerate(totals):
                lines = slice(v * rows, (v + 1) * rows)
                out_ref[lines, at] = (total + part_ref[lines, source]).astype(BF16)
        return carry

    lax.fori_loop(0, inner // blocks, body, 0, unroll=4)


def edge_part(side, up, down, column, edge, part, visits, half):
    count, columns = part.shape
    width = columns // 2
    return pl.pallas_call(
        functools.partial(edge_kernel, visits, half),
        out_shape=held((count, width), BF16),
        in_specs=[whole(pltpu.SMEM)] + [whole()] * 5,
        out_specs=whole(),
        scratch_shapes=[pltpu.VMEM((2 * up.shape[0], width + LANES), BF16)],
        compiler_params=LIMIT,
        name="edge_rows",
    )(side, *kept(up, down, column, edge, part))


def residual_kernel(visits, bands, *refs):
    value_refs, weight_refs = refs[0:2], refs[2:4]
    factor_ref, sums_ref, chi_ref, count_ref = refs[4:]
    rows = value_refs[0].shape[0] // visits
    width = value_refs[0].shape[1]
    high = min(16, rows // bands)
    chi_ref[...] = jnp.zeros_like(chi_ref)
    count_ref[...] = jnp.zeros_like(count_ref)

    def folded(value):
        total = value[:8]
        for start in range(8, high, 8):
            total = total + value[start : start + 8]
        return total

    members = [(side, v) for side in range(2) for v in range(visits)]
    count = value_refs[0].shape[0]
    levels = {}
    for side in range(2):
        found = weight_refs[side][count:, :LANES].astype(F32)
        for v in range(visits):
            for b in range(bands):
                spots = [(k * bands + b) * visits + v for k in range(3)]
                parts = [found[spot : spot + 1] for spot in spots]
                level = (parts[0] + parts[1]) + parts[2]
                levels[side, v, b] = jnp.broadcast_to(level, (high, LANES))

    def body(step, carry):
        lanes = pl.ds(pl.multiple_of(step * LANES, LANES), LANES)
        for row in range(0, rows, high):
            band = row // (rows // bands)
            values, weights, flags = [], [], []
            numer = denom = None
            for side, v in members:
                at = slice(v * rows + row, v * rows + row + high)
                value = value_refs[side][at, lanes].astype(F32)
                flag = weight_refs[side][at, lanes].astype(F32)
                weight = flag * levels[side, v, band]
                flags.append(flag)
                values.append(value)
                weights.append(weight)
                numer = weight * value if numer is None else numer + weight * value
                denom = weight if denom is None else denom + weight
            first = numer / (denom + PRIOR_WEIGHT)
            for m, (side, v) in enumerate(members):
                residual = values[m] - first
                term = weights[m] * (residual * residual)
                at = slice(m * 8, (m + 1) * 8)
                chi_ref[at, :] += folded(term)
                count_ref[at, :] += folded(flags[m])
                target = slice(m * rows + row, m * rows + row + high)
                factor_ref[target, lanes] = weights[m] / (1.0 + term / CLIP_LEVEL)
        return carry

    lax.fori_loop(0, width // LANES, body, 0, unroll=2)
    for m in range(len(members)):
        at = slice(m * 8, (m + 1) * 8)
        sums_ref[0, m : m + 1, :] = jnp.sum(chi_ref[at, :], axis=0, keepdims=True)
        sums_ref[1, m : m + 1, :] = jnp.sum(count_ref[at, :], axis=0, keepdims=True)


def residual_pass(values, weights, visits, bands):
    count, width = values[0].shape
    members = 2 * visits
    return pl.pallas_call(
        functools.partial(residual_kernel, visits, bands),
        out_shape=(held((2 * count, width), F32), held((2, members, LANES), F32)),
        in_specs=[whole()] * 4,
        out_specs=(whole(), whole()),
        scratch_shapes=[pltpu.VMEM((members * 8, LANES), F32)] * 2,
        compiler_params=LIMIT,
        name="residual",
    )(*kept(*values, *weights))


def final_kernel(visits, sums_ref, own_ref, other_ref, factor_ref, out_ref, chi_ref, done, sent):
    rows, width = done.shape
    chunks = sent.shape[0]
    high = min(16, rows)
    chi = jnp.sum(sums_ref[0], axis=1, keepdims=True) / jnp.sum(
        sums_ref[1], axis=1, keepdims=True
    )
    scale = 1.0 / (CHI_OFFSET + chi)
    for v in range(visits):
        chi_ref[v] = chi[v, 0]
    scales = [jnp.broadcast_to(scale[m : m + 1], (high, LANES)) for m in range(2 * visits)]
    copies = []
    for c in range(chunks):
        for lane in range(c * width // chunks, (c + 1) * width // chunks, LANES):
            lanes = slice(lane, lane + LANES)
            for row in range(0, rows, high):
                numer = denom = None
                for m in range(2 * visits):
                    source = own_ref if m < visits else other_ref
                    at = (m % visits) * rows + row
                    value = source[at : at + high, lanes].astype(F32)
                    at = m * rows + row
                    revised = factor_ref[at : at + high, lanes] * scales[m]
                    numer = revised * value if numer is None else numer + revised * value
                    denom = revised if denom is None else denom + revised
                done[row : row + high, lanes] = numer / (denom + PRIOR_WEIGHT)
        lanes = slice(c * width // chunks, (c + 1) * width // chunks)
        copies.append(
            pltpu.make_async_copy(done.at[:, lanes], out_ref.at[:, lanes], sent.at[c])
        )
        copies[c].start()
    for copy in copies:
        copy.wait()


def final_pass(sums, values, factors, visits):
    count, width = values[0].shape
    rows = count // visits
    chunks = max(1, width // 512)
    return pl.pallas_call(
        functools.partial(final_kernel, visits),
        out_shape=(
            jax.ShapeDtypeStruct((rows, width), F32),
            jax.ShapeDtypeStruct((visits,), F32),
        ),
        in_specs=[whole()] * 4,
        out_specs=(pl.BlockSpec(memory_space=pl.ANY), whole(pltpu.SMEM)),
        scratch_shapes=[pltpu.VMEM((rows, width), F32), pltpu.SemaphoreType.DMA((chunks,))],
        compiler_params=LIMIT,
        name="final",
    )(*kept(sums, *values, factors))


def per_device(warps, badbits, coverage, variance, psf_index, psf_table, row_basis, col_basis):
    visits, rows, columns = warps.shape
    half = row_basis.shape[1] // 2
    strips = lax.axis_size("sky")
    up = [(i, i + 1) for i in range(strips - 1)]
    down = [(j, i) for i, j in up]
    swap = [(0, 1), (1, 0)]
    side = lax.axis_index("visit").astype(jnp.int32).reshape(1)

    last, lower = pack_rows(warps, half, False)
    before = lax.ppermute(last, "sky", up)
    leading, upper = pack_rows(warps, half, True)
    after = lax.ppermute(leading, "sky", down)
    send_weight, own_weight = pixel_weights(badbits, coverage, variance, side)
    other_weight = lax.ppermute(send_weight, "visit", swap)
    column, own, edge = tables(psf_index, psf_table, row_basis, col_basis, visits, rows)
    part = own_part(upper.reshape(-1, columns), lower.reshape(-1, columns), column, own, visits)
    send_value = edge_part(1 - side, before, after, column, edge, part, visits, half)
    other_value = lax.ppermute(send_value, "visit", swap)
    own_value = edge_part(side, before, after, column, edge, part, visits, half)
    values = (own_value, other_value)
    factors, sums = residual_pass(values, (own_weight, other_weight), visits, coverage.shape[1])
    theirs = lax.ppermute(sums, "visit", swap)
    sums = sums + jnp.concatenate([theirs[:, visits:], theirs[:, :visits]], axis=1)
    step = 1
    while step < strips:
        sums = sums + lax.ppermute(sums, "sky", [(i, i ^ step) for i in range(strips)])
        step *= 2
    return final_pass(sums, values, factors, visits)


def solution(mesh):
    placed = (
        P(("tract", "visit"), "sky", None),
        P(("tract", "visit"), "sky", None),
        P(("tract", "visit"), "sky"),
        P(("tract", "visit"), "sky"),
        P(("tract", "visit")),
        P(),
        P(),
        P(),
    )
    return jax.shard_map(
        per_device,
        mesh=mesh,
        in_specs=placed,
        out_specs=(P(("tract", "sky"), "visit"), P(("tract", "visit"))),
        check_vma=False,
    )
```

time: 52.8 us -> 44.6 us (0.84)
  waiting for transfers between devices: 11.7 us -> 6.42 us
  Pallas kernels: 24.4 us -> 21.7 us
    ppermute x1, waiting for transfers between devices: 5.96 us -> 0.7 us  [per_device(): before = lax.ppermute(last, 'sky', up)]
    pallas_call x6 -> x7, Pallas kernels: 21.2 us -> 17.9 us  [the longest x2 5.19 us: pack_rows(): pl.pallas_call(functools.partial(pack_kernel, half, first, skip), out_sha...]
    pallas_call x1, Pallas kernels: 1.13 us -> 2.13 us  [tables(): pl.pallas_call(functools.partial(table_kernel, visits, rows, half), out_s...]
  transfers between devices with their start and end apart: 8 -> 8, of which waited for: 5 -> 5; matrix products, arithmetic and copies ran while one was open for 0% -> 0% of each run, Pallas kernels for 30% -> 36%
where the time goes in v4:
time: 44.6 us; the launch traced here: 44.3 us
  Pallas kernels  21.7 us (49%)
  starting transfers between devices  15.3 us (34%)
  waiting for transfers between devices  6.42 us (14%)
  between operations  0.78 us (2%)
    ppermute x3, starting transfers between devices, per_device(): lax.ppermute(sums, 'sky', [(i, i ^ step) for i in range(strips)])  8.4 us
    pallas_call x2, Pallas kernels, pack_rows(): pl.pallas_call(functools.partial(pack_kernel, half, first, skip), out_sha...  5.19 us
    ppermute x1, starting transfers between devices, per_device(): before = lax.ppermute(last, 'sky', up)  4.92 us
    ppermute x3, waiting for transfers between devices, per_device(): lax.ppermute(sums, 'sky', [(i, i ^ step) for i in range(strips)])  4.89 us
    pallas_call x1, Pallas kernels, own_part(): pl.pallas_call(functools.partial(own_kernel, visits), out_shape=held((2 *...  4.83 us
    pallas_call x2, Pallas kernels, edge_part(): pl.pallas_call(functools.partial(edge_kernel, visits, half), out_shape=he...  3.97 us
    pallas_call x1, Pallas kernels, pixel_weights(): pl.pallas_call(functools.partial(weight_kernel, visits, bands), out_shape...  2.54 us
    pallas_call x1, Pallas kernels, tables(): pl.pallas_call(functools.partial(table_kernel, visits, rows, half), out_s...  2.13 us
  transfers between devices with their start and end apart: 8, of which 5 were waited for; matrix products, arithmetic and copies ran while one was open for 0% of the time, Pallas kernels for 36%

profile of v4, /device:TPU:0, one launch (start us, length us, event | category | flops | bytes accessed | tf_op | source)
XLA Modules:
  0.0 44.3 jit_solution(11090053316160182279)
XLA Ops:
  0.6 0.0 copy-start.2
  0.6 0.0 copy-start.3
  0.7 0.0 copy-start
  0.7 0.0 copy-start.1
  0.7 2.6 %pack_lower.1 = (bf16[40,4096]{1,0:T(8,128)(2,1)}, bf16[4,16,4096]{2,1,0:T(8,128)(2,1)S(1)}) custom-call(bf16[4,32,4096]{2,1,0:T(8,128)(2,1)} %x_ref.3), custom_call_target="tpu_custom_call" | custom-call | tf_op jit(solution)/shard_map/pack_lower/pallas_call | solution.py:97
  3.3 4.9 %collective-permute-start = (bf16[40,4096]{1,0:T(8,128)(2,1)}, bf16[40,4096]{1,0:T(8,128)(2,1)S(1)}, u32[]{:S(2)}, u32[]{:S(2)}) collective-permute-start(bf16[40,4096]{1,0:T(8,128)(2,1)} %get-tuple-element.13), channel_id=1, source_target_pairs={{0,2},{2,4},{4,6},{6,8},{8,10},{10,12},{12,14},{1,3},{3,5},{5,7},{... | collective-permute-start | bytes 983048 | tf_op jit(solution)/shard_map/ppermute | solution.py:548
  8.2 2.6 %pack_upper.1 = (bf16[40,4096]{1,0:T(8,128)(2,1)}, bf16[4,16,4096]{2,1,0:T(8,128)(2,1)S(1)}) custom-call(bf16[4,32,4096]{2,1,0:T(8,128)(2,1)} %x_ref.3), custom_call_target="tpu_custom_call" | custom-call | tf_op jit(solution)/shard_map/pack_upper/pallas_call | solution.py:97
  10.8 1.3 %collective-permute-start.1 = (bf16[40,4096]{1,0:T(8,128)(2,1)}, bf16[40,4096]{1,0:T(8,128)(2,1)S(1)}, u32[]{:S(2)}, u32[]{:S(2)}) collective-permute-start(bf16[40,4096]{1,0:T(8,128)(2,1)} %get-tuple-element.14), channel_id=1, source_target_pairs={{2,0},{4,2},{6,4},{8,6},{10,8},{12,10},{14,12},{3,1},{5,3},{7,5},{... | collective-permute-start | bytes 983048 | tf_op jit(solution)/shard_map/ppermute | solution.py:550
  12.1 2.5 %weights.1 = (bf16[144,2048]{1,0:T(8,128)(2,1)S(1)}, bf16[144,2048]{1,0:T(8,128)(2,1)S(1)}) custom-call(s32[1]{0:T(128)} %bitcast.side_ref, s32[1,4]{1,0:T(1,128)} %bitcast.11, f32[1,4]{1,0:T(1,128)} %bitcast.12, s32[128,4096]{1,0:T(8,128)} %bitcast.10), custom_call_target="tpu_custom_call" | custom-call | tf_op jit(solution)/shard_map/weights/pallas_call | solution.py:158
  14.6 0.1 collective-permute-start.3
  14.7 0.0 copy-done.2
  14.7 0.1 rev.3
  14.8 0.0 copy-done.3
  14.8 0.0 copy-done
  14.8 0.0 copy-done.1
  14.8 2.1 %tables.1 = (bf16[256,1024]{1,0:T(8,128)(2,1)S(1)}, bf16[256,256]{1,0:T(8,128)(2,1)S(1)}, bf16[256,256]{1,0:T(8,128)(2,1)S(1)}) custom-call(s32[4]{0:T(128)S(1)} %copy-done.1, f32[8,16]{1,0:T(8,128)S(1)} %bitcast.9, f32[16,128]{1,0:T(8,128)S(1)} %fusion.3.profile_ref), custom_call_target="tpu_custom_call" | custom-call | tf_op jit(solution)/shard_map/tables/pallas_call | solution.py:255
  17.0 4.8 %own_rows.1.part_ref = f32[128,4096]{1,0:T(8,128)S(1)} custom-call(bf16[64,4096]{1,0:T(8,128)(2,1)S(1)} %bitcast.8, bf16[64,4096]{1,0:T(8,128)(2,1)S(1)} %bitcast.7, bf16[256,1024]{1,0:T(8,128)(2,1)S(1)} %get-tuple-element.15.column_ref, bf16[256,256]{1,0:T(8,128)(2,1)S(1)} %get-tuple-element.19.row_ref), custom_call_target="tpu_custom_call" | custom-call | flops 1000000000 | bytes 10000000 | tf_op jit(solution)/shard_map/own_rows/pallas_call | solution.py:338
  21.8 0.7 %collective-permute-done.up_ref = bf16[40,4096]{1,0:T(8,128)(2,1)S(1)} collective-permute-done((bf16[40,4096]{1,0:T(8,128)(2,1)}, bf16[40,4096]{1,0:T(8,128)(2,1)S(1)}, u32[]{:S(2)}, u32[]{:S(2)}) %collective-permute-start) | collective-permute-done | bytes 327712 | tf_op jit(solution)/shard_map/ppermute | solution.py:548
  22.5 0.0 collective-permute-done.1.down_ref
  22.5 2.0 %edge_rows.3 = bf16[128,2048]{1,0:T(8,128)(2,1)S(1)} custom-call(s32[1]{0:T(128)S(6)} %sub.3.side_ref, bf16[40,4096]{1,0:T(8,128)(2,1)S(1)} %collective-permute-done.up_ref, bf16[40,4096]{1,0:T(8,128)(2,1)S(1)} %collective-permute-done.1.down_ref, bf16[256,1024]{1,0:T(8,128)(2,1)S(1)} %get-tuple-element.15.column_ref, ...), custom_call_target="tpu_custom_call" | custom-call | tf_op jit(solution)/shard_map/edge_rows/pallas_call | solution.py:399
  24.5 0.0 collective-permute-start.2
  24.6 2.0 %edge_rows.2.refs_0_.own_ref = bf16[128,2048]{1,0:T(8,128)(2,1)S(1)} custom-call(s32[1]{0:T(128)} %bitcast.side_ref, bf16[40,4096]{1,0:T(8,128)(2,1)S(1)} %collective-permute-done.up_ref, bf16[40,4096]{1,0:T(8,128)(2,1)S(1)} %collective-permute-done.1.down_ref, bf16[256,1024]{1,0:T(8,128)(2,1)S(1)} %get-tuple-element.15.column_ref, ...), custom_call_target="tpu_custom_call" | custom-call | tf_op jit(solution)/shard_map/edge_rows/pallas_call | solution.py:399
  26.5 0.0 collective-permute-done.3.refs_3_
  26.5 0.0 collective-permute-done.2.refs_1_.other_ref
  26.6 1.4 %residual.1 = (f32[256,2048]{1,0:T(8,128)S(1)}, f32[2,8,128]{2,1,0:T(8,128)S(1)}) custom-call(bf16[128,2048]{1,0:T(8,128)(2,1)S(1)} %edge_rows.2.refs_0_.own_ref, bf16[128,2048]{1,0:T(8,128)(2,1)S(1)} %collective-permute-done.2.refs_1_.other_ref, bf16[144,2048]{1,0:T(8,128)(2,1)S(1)} %get-tuple-element.20.refs_2_, ...), custom_call_target="tpu_custom_call" | custom-call | tf_op jit(solution)/shard_map/residual/pallas_call | solution.py:474
  28.0 0.6 %collective-permute-start.4 = (f32[2,8,128]{2,1,0:T(8,128)S(1)}, f32[2,8,128]{2,1,0:T(8,128)S(1)}, u32[]{:S(2)}, u32[]{:S(2)}) collective-permute-start(f32[2,8,128]{2,1,0:T(8,128)S(1)} %get-tuple-element.22), channel_id=1, source_target_pairs={{0,1},{1,0},{2,3},{3,2},{4,5},{5,4},{6,7},{7,6},{8,9},{9,8},{10,11... | collective-permute-start | bytes 24584 | tf_op jit(solution)/shard_map/ppermute | solution.py:560
  28.5 0.8 %collective-permute-done.4 = f32[2,8,128]{2,1,0:T(8,128)S(1)} collective-permute-done((f32[2,8,128]{2,1,0:T(8,128)S(1)}, f32[2,8,128]{2,1,0:T(8,128)S(1)}, u32[]{:S(2)}, u32[]{:S(2)}) %collective-permute-start.4) | collective-permute-done | bytes 8224 | tf_op jit(solution)/shard_map/ppermute | solution.py:560
  29.4 2.4 %collective-permute-start.5 = (f32[2,8,128]{2,1,0:T(8,128)S(1)}, f32[2,8,128]{2,1,0:T(8,128)S(1)}, u32[]{:S(2)}, u32[]{:S(2)}) collective-permute-start(f32[2,8,128]{2,1,0:T(8,128)S(1)} %maximum_add_fusion), channel_id=1, source_target_pairs={{0,2},{2,0},{4,6},{6,4},{8,10},{10,8},{12,14},{14,12},{1,3},{3,1},... | collective-permute-start | bytes 24584 | tf_op jit(solution)/shard_map/ppermute | solution.py:564
  31.8 1.6 %collective-permute-done.5 = f32[2,8,128]{2,1,0:T(8,128)S(1)} collective-permute-done((f32[2,8,128]{2,1,0:T(8,128)S(1)}, f32[2,8,128]{2,1,0:T(8,128)S(1)}, u32[]{:S(2)}, u32[]{:S(2)}) %collective-permute-start.5) | collective-permute-done | bytes 8224 | tf_op jit(solution)/shard_map/ppermute | solution.py:564
  33.4 3.0 %collective-permute-start.6 = (f32[2,8,128]{2,1,0:T(8,128)S(1)}, f32[2,8,128]{2,1,0:T(8,128)S(1)}, u32[]{:S(2)}, u32[]{:S(2)}) collective-permute-start(f32[2,8,128]{2,1,0:T(8,128)S(1)} %add.15), channel_id=1, source_target_pairs={{0,4},{2,6},{4,0},{6,2},{8,12},{10,14},{12,8},{14,10},{1,5},{3,7},... | collective-permute-start | bytes 24584 | tf_op jit(solution)/shard_map/ppermute | solution.py:564
  36.4 1.6 %collective-permute-done.6 = f32[2,8,128]{2,1,0:T(8,128)S(1)} collective-permute-done((f32[2,8,128]{2,1,0:T(8,128)S(1)}, f32[2,8,128]{2,1,0:T(8,128)S(1)}, u32[]{:S(2)}, u32[]{:S(2)}) %collective-permute-start.6) | collective-permute-done | bytes 8224 | tf_op jit(solution)/shard_map/ppermute | solution.py:564
  38.0 3.0 %collective-permute-start.7 = (f32[2,8,128]{2,1,0:T(8,128)S(1)}, f32[2,8,128]{2,1,0:T(8,128)S(1)}, u32[]{:S(2)}, u32[]{:S(2)}) collective-permute-start(f32[2,8,128]{2,1,0:T(8,128)S(1)} %add.16), channel_id=1, source_target_pairs={{0,8},{2,10},{4,12},{6,14},{8,0},{10,2},{12,4},{14,6},{1,9},{3,11}... | collective-permute-start | bytes 24584 | tf_op jit(solution)/shard_map/ppermute | solution.py:564
  41.0 1.6 %collective-permute-done.7 = f32[2,8,128]{2,1,0:T(8,128)S(1)} collective-permute-done((f32[2,8,128]{2,1,0:T(8,128)S(1)}, f32[2,8,128]{2,1,0:T(8,128)S(1)}, u32[]{:S(2)}, u32[]{:S(2)}) %collective-permute-start.7) | collective-permute-done | bytes 8224 | tf_op jit(solution)/shard_map/ppermute | solution.py:564
  42.7 1.7 %final.1 = (f32[32,2048]{1,0:T(8,128)}, f32[4]{0:T(128)}) custom-call(f32[2,8,128]{2,1,0:T(8,128)S(1)} %add.17.sums_ref, bf16[128,2048]{1,0:T(8,128)(2,1)S(1)} %edge_rows.2.refs_0_.own_ref, bf16[128,2048]{1,0:T(8,128)(2,1)S(1)} %collective-permute-done.2.refs_1_.other_ref, f32[256,2048]{1,0:T(8,128)S(1)} %get-tuple-element.23.factor_ref), custom_call_target="tpu_custom_call" | custom-call | tf_op jit(solution)/shard_map/final/pallas_call | solution.py:524
  (6 shorter events, 0.0 us)
Async XLA Ops:
  0.6 14.1 %copy-start.2 = (bf16[8,21]{1,0:T(8,128)(2,1)S(1)}, bf16[8,21]{1,0:T(8,128)(2,1)}, u32[]{:S(2)}) copy-start(bf16[8,21]{1,0:T(8,128)(2,1)} %param.15) | copy-start | bytes 1012
  0.6 14.2 %copy-start.3 = (bf16[8,21]{1,0:T(8,128)(2,1)S(1)}, bf16[8,21]{1,0:T(8,128)(2,1)}, u32[]{:S(2)}) copy-start(bf16[8,21]{1,0:T(8,128)(2,1)} %param.14) | copy-start | bytes 1012
  0.7 14.2 %copy-start = (f32[16,8]{0,1:T(8,128)S(1)}, f32[16,8]{0,1:T(8,128)}, u32[]{:S(2)}) copy-start(f32[16,8]{0,1:T(8,128)} %param.13) | copy-start | bytes 1540
  0.7 14.2 %copy-start.1 = (s32[4]{0:T(128)S(1)}, s32[4]{0:T(128)}, u32[]{:S(2)}) copy-start(s32[4]{0:T(128)} %index_ref.1) | copy-start | bytes 52
  3.3 19.2 %collective-permute-start = (bf16[40,4096]{1,0:T(8,128)(2,1)}, bf16[40,4096]{1,0:T(8,128)(2,1)S(1)}, u32[]{:S(2)}, u32[]{:S(2)}) collective-permute-start(bf16[40,4096]{1,0:T(8,128)(2,1)} %get-tuple-element.13), channel_id=1, source_target_pairs={{0,2},{2,4},{4,6},{6,8},{8,10},{10,12},{12,14},{1,3},{3,5},{5,7},{... | collective-permute-start | bytes 983048 | tf_op jit(solution)/shard_map/ppermute | solution.py:548
  10.8 11.7 %collective-permute-start.1 = (bf16[40,4096]{1,0:T(8,128)(2,1)}, bf16[40,4096]{1,0:T(8,128)(2,1)S(1)}, u32[]{:S(2)}, u32[]{:S(2)}) collective-permute-start(bf16[40,4096]{1,0:T(8,128)(2,1)} %get-tuple-element.14), channel_id=1, source_target_pairs={{2,0},{4,2},{6,4},{8,6},{10,8},{12,10},{14,12},{3,1},{5,3},{7,5},{... | collective-permute-start | bytes 983048 | tf_op jit(solution)/shard_map/ppermute | solution.py:550
  14.6 11.9 %collective-permute-start.3 = (bf16[144,2048]{1,0:T(8,128)(2,1)S(1)}, bf16[144,2048]{1,0:T(8,128)(2,1)S(1)}, u32[]{:S(2)}, u32[]{:S(2)}) collective-permute-start(bf16[144,2048]{1,0:T(8,128)(2,1)S(1)} %get-tuple-element.21), channel_id=1, source_target_pairs={{0,1},{1,0},{2,3},{3,2},{4,5},{5,4},{6,7},{7,6},{8,9},{9,8},{10,11... | collective-permute-start | bytes 1769480 | tf_op jit(solution)/shard_map/ppermute | solution.py:552
  24.5 2.0 %collective-permute-start.2 = (bf16[128,2048]{1,0:T(8,128)(2,1)S(1)}, bf16[128,2048]{1,0:T(8,128)(2,1)S(1)}, u32[]{:S(2)}, u32[]{:S(2)}) collective-permute-start(bf16[128,2048]{1,0:T(8,128)(2,1)S(1)} %edge_rows.3), channel_id=1, source_target_pairs={{0,1},{1,0},{2,3},{3,2},{4,5},{5,4},{6,7},{7,6},{8,9},{9,8},{10,11... | collective-permute-start | bytes 1572872 | tf_op jit(solution)/shard_map/ppermute | solution.py:556
  28.0 1.4 %collective-permute-start.4 = (f32[2,8,128]{2,1,0:T(8,128)S(1)}, f32[2,8,128]{2,1,0:T(8,128)S(1)}, u32[]{:S(2)}, u32[]{:S(2)}) collective-permute-start(f32[2,8,128]{2,1,0:T(8,128)S(1)} %get-tuple-element.22), channel_id=1, source_target_pairs={{0,1},{1,0},{2,3},{3,2},{4,5},{5,4},{6,7},{7,6},{8,9},{9,8},{10,11... | collective-permute-start | bytes 24584 | tf_op jit(solution)/shard_map/ppermute | solution.py:560
  29.4 4.0 %collective-permute-start.5 = (f32[2,8,128]{2,1,0:T(8,128)S(1)}, f32[2,8,128]{2,1,0:T(8,128)S(1)}, u32[]{:S(2)}, u32[]{:S(2)}) collective-permute-start(f32[2,8,128]{2,1,0:T(8,128)S(1)} %maximum_add_fusion), channel_id=1, source_target_pairs={{0,2},{2,0},{4,6},{6,4},{8,10},{10,8},{12,14},{14,12},{1,3},{3,1},... | collective-permute-start | bytes 24584 | tf_op jit(solution)/shard_map/ppermute | solution.py:564
  33.4 4.6 %collective-permute-start.6 = (f32[2,8,128]{2,1,0:T(8,128)S(1)}, f32[2,8,128]{2,1,0:T(8,128)S(1)}, u32[]{:S(2)}, u32[]{:S(2)}) collective-permute-start(f32[2,8,128]{2,1,0:T(8,128)S(1)} %add.15), channel_id=1, source_target_pairs={{0,4},{2,6},{4,0},{6,2},{8,12},{10,14},{12,8},{14,10},{1,5},{3,7},... | collective-permute-start | bytes 24584 | tf_op jit(solution)/shard_map/ppermute | solution.py:564
  38.0 4.6 %collective-permute-start.7 = (f32[2,8,128]{2,1,0:T(8,128)S(1)}, f32[2,8,128]{2,1,0:T(8,128)S(1)}, u32[]{:S(2)}, u32[]{:S(2)}) collective-permute-start(f32[2,8,128]{2,1,0:T(8,128)S(1)} %add.16), channel_id=1, source_target_pairs={{0,8},{2,10},{4,12},{6,14},{8,0},{10,2},{12,4},{14,6},{1,9},{3,11}... | collective-permute-start | bytes 24584 | tf_op jit(solution)/shard_map/ppermute | solution.py:564

commit v5 on v4

--- a/solution.py
+++ b/solution.py
@@ -196,8 +196,8 @@
     return segments, start
 
 
-def table_kernel(visits, rows, half, index_ref, table_ref, profile_ref, column_out, own_out, edge_out):
-    bases = table_ref.shape[0]
+def table_kernel(visits, rows, half, index_ref, table_ref, row_ref, col_ref, column_out, own_out, edge_out):
+    bases, taps = row_ref.shape
     window = 2 * LANES
 
     def spread(line, shift, count):
@@ -206,11 +206,17 @@
         blocks = [pltpu.roll(block, (shift + i) % LANES, 1) for i in range(0, count, 8)]
         return jnp.concatenate(blocks, axis=0)
 
+    tap = lax.broadcasted_iota(jnp.int32, (taps, LANES), 0)
+    place = lane_index((taps, LANES))
+    ahead = jnp.where(place == tap, 1.0, 0.0).astype(BF16)
+    back = jnp.where(place == taps - 1 - tap, 1.0, 0.0).astype(BF16)
+    row_lines = jnp.dot(row_ref[...], ahead, preferred_element_type=F32)
+    col_lines = jnp.dot(col_ref[...], back, preferred_element_type=F32)
     k = lax.broadcasted_iota(jnp.int32, (window, LANES), 0)
     gap = k - lane_index((window, LANES))
     inside = (gap >= 0) & (gap < LANES)
     for b in range(bases):
-        line = profile_ref[bases + b : bases + b + 1, :]
+        line = col_lines[b : b + 1, :]
         band = jnp.where(inside, spread(line, SHIFT - half, window), 0.0)
         column_out[:, b * LANES : (b + 1) * LANES] = band.astype(BF16)
 
@@ -220,7 +226,7 @@
         for b in range(bases):
             start = b * high % LANES
             group = b * high // LANES * LANES
-            line = profile_ref[b : b + 1, :]
+            line = row_lines[b : b + 1, :]
             found = {}
             for v in range(visits):
                 total = jnp.zeros((rows, LANES), F32)
@@ -250,8 +256,6 @@
 def tables(psf_index, psf_table, row_basis, col_basis, visits, rows):
     bases, taps = row_basis.shape
     half = taps // 2
-    profile = jnp.concatenate([row_basis, col_basis[:, ::-1]], axis=0).astype(F32)
-    profile = jnp.pad(profile, ((0, 0), (0, LANES - taps)))
     return pl.pallas_call(
         functools.partial(table_kernel, visits, rows, half),
         out_shape=(
@@ -259,11 +263,11 @@
             held((2 * visits * rows, bases * rows), BF16),
             held((2 * visits * rows, bases * edge_segments(visits, rows, half)[1]), BF16),
         ),
-        in_specs=[whole(pltpu.SMEM), whole(pltpu.SMEM), whole()],
+        in_specs=[whole(pltpu.SMEM)] * 2 + [whole()] * 2,
         out_specs=(whole(),) * 3,
         compiler_params=LIMIT,
         name="tables",
-    )(psf_index, psf_table.T, profile)
+    )(psf_index, psf_table.T, row_basis, col_basis)
 
 
 BLOCKS = 4

time: 44.6 us -> 43.6 us (0.978)
  Pallas kernels: 21.7 us -> 19.5 us
  waiting for transfers between devices: 6.42 us -> 7.66 us
    pallas_call x2, Pallas kernels: 5.19 us -> 3.75 us  [pack_rows(): pl.pallas_call(functools.partial(pack_kernel, half, first, skip), out_sha...]
    ppermute x1, waiting for transfers between devices: 0.7 us -> 1.94 us  [per_device(): before = lax.ppermute(last, 'sky', up)]
    pallas_call x1, Pallas kernels: 2.13 us -> 1.34 us  [tables(): pl.pallas_call(functools.partial(table_kernel, visits, rows, half), out_s...]
  transfers between devices with their start and end apart: 8 -> 8, of which waited for: 5 -> 5; matrix products, arithmetic and copies ran while one was open for 0% -> 0% of each run, Pallas kernels for 36% -> 33%
where the time goes in v5:
time: 43.6 us; the launch traced here: 43.4 us
  Pallas kernels  19.5 us (45%)
  starting transfers between devices  15.4 us (35%)
  waiting for transfers between devices  7.66 us (18%)
  between operations  0.79 us (2%)
    ppermute x3, starting transfers between devices, per_device(): lax.ppermute(sums, 'sky', [(i, i ^ step) for i in range(strips)])  8.55 us
    ppermute x1, starting transfers between devices, per_device(): before = lax.ppermute(last, 'sky', up)  4.92 us
    ppermute x3, waiting for transfers between devices, per_device(): lax.ppermute(sums, 'sky', [(i, i ^ step) for i in range(strips)])  4.89 us
    pallas_call x1, Pallas kernels, own_part(): pl.pallas_call(functools.partial(own_kernel, visits), out_shape=held((2 *...  4.83 us
    pallas_call x2, Pallas kernels, edge_part(): pl.pallas_call(functools.partial(edge_kernel, visits, half), out_shape=he...  3.95 us
    pallas_call x2, Pallas kernels, pack_rows(): pl.pallas_call(functools.partial(pack_kernel, half, first, skip), out_sha...  3.75 us
    pallas_call x1, Pallas kernels, pixel_weights(): pl.pallas_call(functools.partial(weight_kernel, visits, bands), out_shape...  2.54 us
    ppermute x1, waiting for transfers between devices, per_device(): before = lax.ppermute(last, 'sky', up)  1.94 us
  transfers between devices with their start and end apart: 8, of which 5 were waited for; matrix products, arithmetic and copies ran while one was open for 0% of the time, Pallas kernels for 33%

profile of v5, /device:TPU:0, one launch (start us, length us, event | category | flops | bytes accessed | tf_op | source)
XLA Modules:
  0.0 43.4 jit_solution(1539024802507787653)
XLA Ops:
  0.6 0.0 copy-start
  0.6 0.0 copy-start.3
  0.7 0.0 copy-start.1
  0.7 0.0 copy-start.2
  0.7 1.9 %pack_lower.1 = (bf16[40,4096]{1,0:T(8,128)(2,1)S(1)}, bf16[4,16,4096]{2,1,0:T(8,128)(2,1)S(1)}) custom-call(bf16[4,32,4096]{2,1,0:T(8,128)(2,1)} %x_ref.3), custom_call_target="tpu_custom_call" | custom-call | tf_op jit(solution)/shard_map/pack_lower/pallas_call | solution.py:97
  2.6 4.9 %collective-permute-start = (bf16[40,4096]{1,0:T(8,128)(2,1)S(1)}, bf16[40,4096]{1,0:T(8,128)(2,1)S(1)}, u32[]{:S(2)}, u32[]{:S(2)}) collective-permute-start(bf16[40,4096]{1,0:T(8,128)(2,1)S(1)} %get-tuple-element.13), channel_id=1, source_target_pairs={{0,2},{2,4},{4,6},{6,8},{8,10},{10,12},{12,14},{1,3},{3,5},{5,7},{... | collective-permute-start | bytes 983048 | tf_op jit(solution)/shard_map/ppermute | solution.py:552
  7.5 1.9 %pack_upper.1 = (bf16[40,4096]{1,0:T(8,128)(2,1)S(1)}, bf16[4,16,4096]{2,1,0:T(8,128)(2,1)S(1)}) custom-call(bf16[4,32,4096]{2,1,0:T(8,128)(2,1)} %x_ref.3), custom_call_target="tpu_custom_call" | custom-call | tf_op jit(solution)/shard_map/pack_upper/pallas_call | solution.py:97
  9.4 1.3 %collective-permute-start.1 = (bf16[40,4096]{1,0:T(8,128)(2,1)S(1)}, bf16[40,4096]{1,0:T(8,128)(2,1)S(1)}, u32[]{:S(2)}, u32[]{:S(2)}) collective-permute-start(bf16[40,4096]{1,0:T(8,128)(2,1)S(1)} %get-tuple-element.14), channel_id=1, source_target_pairs={{2,0},{4,2},{6,4},{8,6},{10,8},{12,10},{14,12},{3,1},{5,3},{7,5},{... | collective-permute-start | bytes 983048 | tf_op jit(solution)/shard_map/ppermute | solution.py:554
  10.7 2.5 %weights.1 = (bf16[144,2048]{1,0:T(8,128)(2,1)S(1)}, bf16[144,2048]{1,0:T(8,128)(2,1)S(1)}) custom-call(s32[1]{0:T(128)} %bitcast.side_ref, s32[1,4]{1,0:T(1,128)} %bitcast.11, f32[1,4]{1,0:T(1,128)} %bitcast.12, s32[128,4096]{1,0:T(8,128)} %bitcast.10), custom_call_target="tpu_custom_call" | custom-call | tf_op jit(solution)/shard_map/weights/pallas_call | solution.py:158
  13.2 0.1 collective-permute-start.3
  13.3 0.0 copy-done
  13.3 0.0 copy-done.3
  13.3 0.0 copy-done.1
  13.3 0.0 copy-done.2
  13.3 1.3 %tables.1 = (bf16[256,1024]{1,0:T(8,128)(2,1)S(1)}, bf16[256,256]{1,0:T(8,128)(2,1)S(1)}, bf16[256,256]{1,0:T(8,128)(2,1)S(1)}) custom-call(s32[4]{0:T(128)S(1)} %copy-done.3, f32[8,16]{1,0:T(8,128)S(1)} %bitcast.9, bf16[8,21]{1,0:T(8,128)(2,1)S(1)} %copy-done.1, bf16[8,21]{1,0:T(8,128)(2,1)S(1)} %copy-done.2), custom_call_target="tpu_custom_call" | custom-call | tf_op jit(solution)/shard_map/tables/pallas_call | solution.py:259
  14.7 4.8 %own_rows.1.part_ref = f32[128,4096]{1,0:T(8,128)S(1)} custom-call(bf16[64,4096]{1,0:T(8,128)(2,1)S(1)} %bitcast.8, bf16[64,4096]{1,0:T(8,128)(2,1)S(1)} %bitcast.7, bf16[256,1024]{1,0:T(8,128)(2,1)S(1)} %get-tuple-element.15.column_ref, bf16[256,256]{1,0:T(8,128)(2,1)S(1)} %get-tuple-element.19.row_ref), custom_call_target="tpu_custom_call" | custom-call | flops 1000000000 | bytes 10000000 | tf_op jit(solution)/shard_map/own_rows/pallas_call | solution.py:342
  19.5 1.9 %collective-permute-done.up_ref = bf16[40,4096]{1,0:T(8,128)(2,1)S(1)} collective-permute-done((bf16[40,4096]{1,0:T(8,128)(2,1)S(1)}, bf16[40,4096]{1,0:T(8,128)(2,1)S(1)}, u32[]{:S(2)}, u32[]{:S(2)}) %collective-permute-start) | collective-permute-done | bytes 327712 | tf_op jit(solution)/shard_map/ppermute | solution.py:552
  21.4 0.0 collective-permute-done.1.down_ref
  21.4 2.0 %edge_rows.3 = bf16[128,2048]{1,0:T(8,128)(2,1)S(1)} custom-call(s32[1]{0:T(128)S(6)} %sub.3.side_ref, bf16[40,4096]{1,0:T(8,128)(2,1)S(1)} %collective-permute-done.up_ref, bf16[40,4096]{1,0:T(8,128)(2,1)S(1)} %collective-permute-done.1.down_ref, bf16[256,1024]{1,0:T(8,128)(2,1)S(1)} %get-tuple-element.15.column_ref, ...), custom_call_target="tpu_custom_call" | custom-call | tf_op jit(solution)/shard_map/edge_rows/pallas_call | solution.py:403
  23.4 0.0 collective-permute-start.2
  23.5 2.0 %edge_rows.2.refs_0_.own_ref = bf16[128,2048]{1,0:T(8,128)(2,1)S(1)} custom-call(s32[1]{0:T(128)} %bitcast.side_ref, bf16[40,4096]{1,0:T(8,128)(2,1)S(1)} %collective-permute-done.up_ref, bf16[40,4096]{1,0:T(8,128)(2,1)S(1)} %collective-permute-done.1.down_ref, bf16[256,1024]{1,0:T(8,128)(2,1)S(1)} %get-tuple-element.15.column_ref, ...), custom_call_target="tpu_custom_call" | custom-call | tf_op jit(solution)/shard_map/edge_rows/pallas_call | solution.py:403
  25.5 0.0 collective-permute-done.3.refs_3_
  25.5 0.0 collective-permute-done.2.refs_1_.other_ref
  25.5 1.4 %residual.1 = (f32[256,2048]{1,0:T(8,128)S(1)}, f32[2,8,128]{2,1,0:T(8,128)S(1)}) custom-call(bf16[128,2048]{1,0:T(8,128)(2,1)S(1)} %edge_rows.2.refs_0_.own_ref, bf16[128,2048]{1,0:T(8,128)(2,1)S(1)} %collective-permute-done.2.refs_1_.other_ref, bf16[144,2048]{1,0:T(8,128)(2,1)S(1)} %get-tuple-element.20.refs_2_, ...), custom_call_target="tpu_custom_call" | custom-call | tf_op jit(solution)/shard_map/residual/pallas_call | solution.py:478
  26.9 0.6 %collective-permute-start.4 = (f32[2,8,128]{2,1,0:T(8,128)S(1)}, f32[2,8,128]{2,1,0:T(8,128)S(1)}, u32[]{:S(2)}, u32[]{:S(2)}) collective-permute-start(f32[2,8,128]{2,1,0:T(8,128)S(1)} %get-tuple-element.22), channel_id=1, source_target_pairs={{0,1},{1,0},{2,3},{3,2},{4,5},{5,4},{6,7},{7,6},{8,9},{9,8},{10,11... | collective-permute-start | bytes 24584 | tf_op jit(solution)/shard_map/ppermute | solution.py:564
  27.4 0.8 %collective-permute-done.4 = f32[2,8,128]{2,1,0:T(8,128)S(1)} collective-permute-done((f32[2,8,128]{2,1,0:T(8,128)S(1)}, f32[2,8,128]{2,1,0:T(8,128)S(1)}, u32[]{:S(2)}, u32[]{:S(2)}) %collective-permute-start.4) | collective-permute-done | bytes 8224 | tf_op jit(solution)/shard_map/ppermute | solution.py:564
  28.3 2.6 %collective-permute-start.5 = (f32[2,8,128]{2,1,0:T(8,128)S(1)}, f32[2,8,128]{2,1,0:T(8,128)S(1)}, u32[]{:S(2)}, u32[]{:S(2)}) collective-permute-start(f32[2,8,128]{2,1,0:T(8,128)S(1)} %maximum_add_fusion), channel_id=1, source_target_pairs={{0,2},{2,0},{4,6},{6,4},{8,10},{10,8},{12,14},{14,12},{1,3},{3,1},... | collective-permute-start | bytes 24584 | tf_op jit(solution)/shard_map/ppermute | solution.py:568
  30.9 1.6 %collective-permute-done.5 = f32[2,8,128]{2,1,0:T(8,128)S(1)} collective-permute-done((f32[2,8,128]{2,1,0:T(8,128)S(1)}, f32[2,8,128]{2,1,0:T(8,128)S(1)}, u32[]{:S(2)}, u32[]{:S(2)}) %collective-permute-start.5) | collective-permute-done | bytes 8224 | tf_op jit(solution)/shard_map/ppermute | solution.py:568
  32.5 3.0 %collective-permute-start.6 = (f32[2,8,128]{2,1,0:T(8,128)S(1)}, f32[2,8,128]{2,1,0:T(8,128)S(1)}, u32[]{:S(2)}, u32[]{:S(2)}) collective-permute-start(f32[2,8,128]{2,1,0:T(8,128)S(1)} %add.13), channel_id=1, source_target_pairs={{0,4},{2,6},{4,0},{6,2},{8,12},{10,14},{12,8},{14,10},{1,5},{3,7},... | collective-permute-start | bytes 24584 | tf_op jit(solution)/shard_map/ppermute | solution.py:568
  35.5 1.6 %collective-permute-done.6 = f32[2,8,128]{2,1,0:T(8,128)S(1)} collective-permute-done((f32[2,8,128]{2,1,0:T(8,128)S(1)}, f32[2,8,128]{2,1,0:T(8,128)S(1)}, u32[]{:S(2)}, u32[]{:S(2)}) %collective-permute-start.6) | collective-permute-done | bytes 8224 | tf_op jit(solution)/shard_map/ppermute | solution.py:568
  37.1 3.0 %collective-permute-start.7 = (f32[2,8,128]{2,1,0:T(8,128)S(1)}, f32[2,8,128]{2,1,0:T(8,128)S(1)}, u32[]{:S(2)}, u32[]{:S(2)}) collective-permute-start(f32[2,8,128]{2,1,0:T(8,128)S(1)} %add.14), channel_id=1, source_target_pairs={{0,8},{2,10},{4,12},{6,14},{8,0},{10,2},{12,4},{14,6},{1,9},{3,11}... | collective-permute-start | bytes 24584 | tf_op jit(solution)/shard_map/ppermute | solution.py:568
  40.1 1.6 %collective-permute-done.7 = f32[2,8,128]{2,1,0:T(8,128)S(1)} collective-permute-done((f32[2,8,128]{2,1,0:T(8,128)S(1)}, f32[2,8,128]{2,1,0:T(8,128)S(1)}, u32[]{:S(2)}, u32[]{:S(2)}) %collective-permute-start.7) | collective-permute-done | bytes 8224 | tf_op jit(solution)/shard_map/ppermute | solution.py:568
  41.7 1.7 %final.1 = (f32[32,2048]{1,0:T(8,128)}, f32[4]{0:T(128)}) custom-call(f32[2,8,128]{2,1,0:T(8,128)S(1)} %add.15.sums_ref, bf16[128,2048]{1,0:T(8,128)(2,1)S(1)} %edge_rows.2.refs_0_.own_ref, bf16[128,2048]{1,0:T(8,128)(2,1)S(1)} %collective-permute-done.2.refs_1_.other_ref, f32[256,2048]{1,0:T(8,128)S(1)} %get-tuple-element.23.factor_ref), custom_call_target="tpu_custom_call" | custom-call | tf_op jit(solution)/shard_map/final/pallas_call | solution.py:528
  (5 shorter events, 0.0 us)
Async XLA Ops:
  0.6 12.7 %copy-start = (f32[16,8]{0,1:T(8,128)S(1)}, f32[16,8]{0,1:T(8,128)}, u32[]{:S(2)}) copy-start(f32[16,8]{0,1:T(8,128)} %param.13) | copy-start | bytes 1540
  0.6 12.7 %copy-start.3 = (s32[4]{0:T(128)S(1)}, s32[4]{0:T(128)}, u32[]{:S(2)}) copy-start(s32[4]{0:T(128)} %index_ref.1) | copy-start | bytes 52
  0.7 12.7 %copy-start.1 = (bf16[8,21]{1,0:T(8,128)(2,1)S(1)}, bf16[8,21]{1,0:T(8,128)(2,1)}, u32[]{:S(2)}) copy-start(bf16[8,21]{1,0:T(8,128)(2,1)} %row_ref.1) | copy-start | bytes 1012
  0.7 12.7 %copy-start.2 = (bf16[8,21]{1,0:T(8,128)(2,1)S(1)}, bf16[8,21]{1,0:T(8,128)(2,1)}, u32[]{:S(2)}) copy-start(bf16[8,21]{1,0:T(8,128)(2,1)} %col_ref.1) | copy-start | bytes 1012
  2.6 18.9 %collective-permute-start = (bf16[40,4096]{1,0:T(8,128)(2,1)S(1)}, bf16[40,4096]{1,0:T(8,128)(2,1)S(1)}, u32[]{:S(2)}, u32[]{:S(2)}) collective-permute-start(bf16[40,4096]{1,0:T(8,128)(2,1)S(1)} %get-tuple-element.13), channel_id=1, source_target_pairs={{0,2},{2,4},{4,6},{6,8},{8,10},{10,12},{12,14},{1,3},{3,5},{5,7},{... | collective-permute-start | bytes 983048 | tf_op jit(solution)/shard_map/ppermute | solution.py:552
  9.4 12.1 %collective-permute-start.1 = (bf16[40,4096]{1,0:T(8,128)(2,1)S(1)}, bf16[40,4096]{1,0:T(8,128)(2,1)S(1)}, u32[]{:S(2)}, u32[]{:S(2)}) collective-permute-start(bf16[40,4096]{1,0:T(8,128)(2,1)S(1)} %get-tuple-element.14), channel_id=1, source_target_pairs={{2,0},{4,2},{6,4},{8,6},{10,8},{12,10},{14,12},{3,1},{5,3},{7,5},{... | collective-permute-start | bytes 983048 | tf_op jit(solution)/shard_map/ppermute | solution.py:554
  13.2 12.2 %collective-permute-start.3 = (bf16[144,2048]{1,0:T(8,128)(2,1)S(1)}, bf16[144,2048]{1,0:T(8,128)(2,1)S(1)}, u32[]{:S(2)}, u32[]{:S(2)}) collective-permute-start(bf16[144,2048]{1,0:T(8,128)(2,1)S(1)} %get-tuple-element.21), channel_id=1, source_target_pairs={{0,1},{1,0},{2,3},{3,2},{4,5},{5,4},{6,7},{7,6},{8,9},{9,8},{10,11... | collective-permute-start | bytes 1769480 | tf_op jit(solution)/shard_map/ppermute | solution.py:556
  23.4 2.0 %collective-permute-start.2 = (bf16[128,2048]{1,0:T(8,128)(2,1)S(1)}, bf16[128,2048]{1,0:T(8,128)(2,1)S(1)}, u32[]{:S(2)}, u32[]{:S(2)}) collective-permute-start(bf16[128,2048]{1,0:T(8,128)(2,1)S(1)} %edge_rows.3), channel_id=1, source_target_pairs={{0,1},{1,0},{2,3},{3,2},{4,5},{5,4},{6,7},{7,6},{8,9},{9,8},{10,11... | collective-permute-start | bytes 1572872 | tf_op jit(solution)/shard_map/ppermute | solution.py:560
  26.9 1.4 %collective-permute-start.4 = (f32[2,8,128]{2,1,0:T(8,128)S(1)}, f32[2,8,128]{2,1,0:T(8,128)S(1)}, u32[]{:S(2)}, u32[]{:S(2)}) collective-permute-start(f32[2,8,128]{2,1,0:T(8,128)S(1)} %get-tuple-element.22), channel_id=1, source_target_pairs={{0,1},{1,0},{2,3},{3,2},{4,5},{5,4},{6,7},{7,6},{8,9},{9,8},{10,11... | collective-permute-start | bytes 24584 | tf_op jit(solution)/shard_map/ppermute | solution.py:564
  28.3 4.2 %collective-permute-start.5 = (f32[2,8,128]{2,1,0:T(8,128)S(1)}, f32[2,8,128]{2,1,0:T(8,128)S(1)}, u32[]{:S(2)}, u32[]{:S(2)}) collective-permute-start(f32[2,8,128]{2,1,0:T(8,128)S(1)} %maximum_add_fusion), channel_id=1, source_target_pairs={{0,2},{2,0},{4,6},{6,4},{8,10},{10,8},{12,14},{14,12},{1,3},{3,1},... | collective-permute-start | bytes 24584 | tf_op jit(solution)/shard_map/ppermute | solution.py:568
  32.5 4.6 %collective-permute-start.6 = (f32[2,8,128]{2,1,0:T(8,128)S(1)}, f32[2,8,128]{2,1,0:T(8,128)S(1)}, u32[]{:S(2)}, u32[]{:S(2)}) collective-permute-start(f32[2,8,128]{2,1,0:T(8,128)S(1)} %add.13), channel_id=1, source_target_pairs={{0,4},{2,6},{4,0},{6,2},{8,12},{10,14},{12,8},{14,10},{1,5},{3,7},... | collective-permute-start | bytes 24584 | tf_op jit(solution)/shard_map/ppermute | solution.py:568
  37.1 4.6 %collective-permute-start.7 = (f32[2,8,128]{2,1,0:T(8,128)S(1)}, f32[2,8,128]{2,1,0:T(8,128)S(1)}, u32[]{:S(2)}, u32[]{:S(2)}) collective-permute-start(f32[2,8,128]{2,1,0:T(8,128)S(1)} %add.14), channel_id=1, source_target_pairs={{0,8},{2,10},{4,12},{6,14},{8,0},{10,2},{12,4},{14,6},{1,9},{3,11}... | collective-permute-start | bytes 24584 | tf_op jit(solution)/shard_map/ppermute | solution.py:568

commit v6 on v5

--- a/solution.py
+++ b/solution.py
@@ -39,7 +39,8 @@
     return lax.broadcasted_iota(jnp.int32, shape, len(shape) - 1)
 
 
-def pack_kernel(half, first, skip, x_ref, edge_ref, rows_ref, arrived):
+def pack_kernel(half, first, skip, x_ref, *refs):
+    edge_ref, rows_ref, arrived = refs[-3:]
     visits, depth, columns = rows_ref.shape
     chunks = arrived.shape[0]
     width = columns // chunks
@@ -87,22 +88,22 @@
     put(0, jnp.where(low, before, opening))
 
 
-def pack_rows(warps, half, upper):
+def pack_rows(warps, half, upper, *after):
     visits, rows, columns = warps.shape
     depth = rows // 2
     assert depth >= half and rows % 2 == 0
     first = 0 if upper else depth
     skip = 0 if upper else depth - half
-    chunks = max(1, columns // 1024)
+    chunks = 1
     return pl.pallas_call(
         functools.partial(pack_kernel, half, first, skip),
         out_shape=(held((visits * half, columns), BF16), held((visits, depth, columns), BF16)),
-        in_specs=[pl.BlockSpec(memory_space=pl.ANY)],
+        in_specs=[pl.BlockSpec(memory_space=pl.ANY)] * (1 + len(after)),
         out_specs=(whole(),) * 2,
         scratch_shapes=[pltpu.SemaphoreType.DMA((chunks,))],
         compiler_params=LIMIT,
         name="pack_upper" if upper else "pack_lower",
-    )(*away(warps))
+    )(*away(warps), *after)
 
 
 def level_rows(visits, bands):
@@ -147,7 +148,7 @@
     bands = coverage.shape[1]
     (bits,) = away(badbits.reshape(visits * rows, columns))
     width = columns // 2
-    tile = min(1024, width)
+    tile = width
     count = width // tile
     shape = held((visits * rows + level_rows(visits, bands), width), BF16)
 
@@ -178,25 +179,18 @@
     return high, (value - high.astype(F32)).astype(BF16)
 
 
-def edge_segments(visits, rows, half):
+def edge_segments(visits, rows, half, below):
     main = half // 8 * 8
     rest = half - main
+    origin = half + rows if below else 0
     segments = []
     for v in range(visits):
-        here, start = [], 0
-        for below in (0, 1):
-            here.append((start, start + main, (half + rows if below else 0) - start))
-            start += main
-        for below in (0, 1):
-            first = start + v * rest
-            offset = (half + rows if below else 0) + main - first
-            here.append((first, first + rest, offset))
-            start += visits * rest
-        segments.append(here)
-    return segments, start
-
-
-def table_kernel(visits, rows, half, index_ref, table_ref, row_ref, col_ref, column_out, own_out, edge_out):
+        first = main + v * rest
+        segments.append([(0, main, origin), (first, first + rest, origin + main - first)])
+    return segments, main + visits * rest
+
+
+def table_kernel(visits, rows, half, index_ref, table_ref, row_ref, col_ref, column_out, own_out, above_out, below_out):
     bases, taps = row_ref.shape
     window = 2 * LANES
 
@@ -249,22 +243,25 @@
                     out_ref[at + rows : at + 2 * rows, lanes] += low
 
     assemble(own_out, rows, [[(0, rows, half)]] * visits)
-    segments, high = edge_segments(visits, rows, half)
-    assemble(edge_out, high, segments)
+    for below, out in enumerate((above_out, below_out)):
+        segments, high = edge_segments(visits, rows, half, below)
+        assemble(out, high, segments)
 
 
 def tables(psf_index, psf_table, row_basis, col_basis, visits, rows):
     bases, taps = row_basis.shape
     half = taps // 2
+    rim = (2 * visits * rows, bases * edge_segments(visits, rows, half, 0)[1])
     return pl.pallas_call(
         functools.partial(table_kernel, visits, rows, half),
         out_shape=(
             held((2 * LANES, bases * LANES), BF16),
             held((2 * visits * rows, bases * rows), BF16),
-            held((2 * visits * rows, bases * edge_segments(visits, rows, half)[1]), BF16),
+            held(rim, BF16),
+            held(rim, BF16),
         ),
         in_specs=[whole(pltpu.SMEM)] * 2 + [whole()] * 2,
-        out_specs=(whole(),) * 3,
+        out_specs=(whole(),) * 4,
         compiler_params=LIMIT,
         name="tables",
     )(psf_index, psf_table.T, row_basis, col_basis)
@@ -273,14 +270,15 @@
 BLOCKS = 4
 
 
-def convolve(windows, column_ref, row_ref, pieces):
-    bases = column_ref.shape[1] // LANES
-    count = windows[0].shape[0]
-    layers = jnp.dot(
+def column_pass(windows, column_ref):
+    return jnp.dot(
         jnp.concatenate(windows, axis=0), column_ref[...], preferred_element_type=F32
     )
+
+
+def row_pass(layers, count, row_ref, pieces, bases):
     high = row_ref.shape[0] // (2 * len(pieces))
-    for first in range(0, len(windows), 2):
+    for first in range(0, layers.shape[0] // count, 2):
         totals = []
         for v, parts in enumerate(pieces):
             sides = []
@@ -289,6 +287,7 @@
                     layers[n * count + top : n * count + last, b * LANES : (b + 1) * LANES]
                     for b in range(bases)
                     for top, last in parts
+                    if last > top
                 ]
                 sides.append(jnp.concatenate(taken, axis=0).astype(BF16))
             total = jnp.dot(
@@ -300,41 +299,59 @@
         yield first, totals
 
 
+def convolve(make_group, shifted, column_ref, row_ref, pieces, put):
+    count = shifted.shape[0]
+    groups = shifted.shape[1] // LANES - 1
+    bases = column_ref.shape[1] // LANES
+    blocks = min(BLOCKS, groups)
+    made = [0]
+
+    def columns_of(step):
+        while made[0] <= blocks * (step + 1):
+            g = made[0]
+            shifted[:, g * LANES : (g + 1) * LANES] = make_group(g)
+            made[0] += 1
+        starts = [(blocks * step + n) * LANES for n in range(blocks)]
+        return column_pass([shifted[:, at : at + 2 * LANES] for at in starts], column_ref)
+
+    ahead = columns_of(0)
+    for step in range(groups // blocks):
+        layers = ahead
+        if step + 1 < groups // blocks:
+            ahead = columns_of(step + 1)
+        for first, totals in row_pass(layers, count, row_ref, pieces, bases):
+            put((blocks * step + first) * LANES, totals)
+
+
 def own_kernel(visits, upper_ref, lower_ref, column_ref, row_ref, out_ref, shifted):
     half_count, columns = upper_ref.shape
     depth = half_count // visits
     rows = 2 * depth
     groups = columns // LANES
-    low = lane_index((half_count, LANES)) < SHIFT
-    for place, ref in enumerate((upper_ref, lower_ref)):
-        lines = slice(place * half_count, (place + 1) * half_count)
-        before = jnp.zeros((half_count, LANES), F32)
-        for g in range(groups + 1):
-            here = jnp.zeros((half_count, LANES), F32)
-            if g < groups:
-                here = pltpu.roll(ref[:, g * LANES : (g + 1) * LANES].astype(F32), SHIFT, 1)
-            value = jnp.where(low, before, here).astype(BF16)
-            shifted[lines, g * LANES : (g + 1) * LANES] = value
-            before = here
+    low = lane_index((2 * half_count, LANES)) < SHIFT
+    nothing = jnp.zeros((2 * half_count, LANES), F32)
+    turned = {-1: nothing, groups: nothing}
+
+    def turn(g):
+        if g not in turned:
+            lanes = slice(g * LANES, (g + 1) * LANES)
+            value = jnp.concatenate([upper_ref[:, lanes], lower_ref[:, lanes]], axis=0)
+            turned[g] = pltpu.roll(value.astype(F32), SHIFT, 1)
+        return turned[g]
+
+    def make_group(g):
+        return jnp.where(low, turn(g - 1), turn(g)).astype(BF16)
+
     pieces = [
         [(place * half_count + v * depth, place * half_count + (v + 1) * depth) for place in (0, 1)]
         for v in range(visits)
     ]
-    blocks = min(BLOCKS, groups)
-
-    def body(step, carry):
-        windows = [
-            shifted[:, pl.ds(pl.multiple_of((blocks * step + n) * LANES, LANES), 2 * LANES)]
-            for n in range(blocks)
-        ]
-        for first, totals in convolve(windows, column_ref, row_ref, pieces):
-            start = (blocks * step + first) * LANES
-            at = pl.ds(pl.multiple_of(start, 2 * LANES), 2 * LANES)
-            for v, total in enumerate(totals):
-                out_ref[v * rows : (v + 1) * rows, at] = total
-        return carry
-
-    lax.fori_loop(0, groups // blocks, body, 0, unroll=4)
+
+    def put(start, totals):
+        for v, total in enumerate(totals):
+            out_ref[v * rows : (v + 1) * rows, start : start + 2 * LANES] = total
+
+    convolve(make_group, shifted, column_ref, row_ref, pieces, put)
 
 
 def own_part(upper, lower, column, own, visits):
@@ -351,64 +368,51 @@
     )(*kept(upper, lower, column, own))
 
 
-def edge_kernel(visits, half, side_ref, up_ref, down_ref, column_ref, row_ref, part_ref, *refs):
-    out_ref, shifted = refs
-    edge, columns = up_ref.shape
+def rim_kernel(visits, half, side_ref, edge_ref, column_ref, row_ref, part_ref, out_ref, shifted):
+    edge, columns = edge_ref.shape
     rows = out_ref.shape[0] // visits
     width = out_ref.shape[1]
     groups = columns // LANES
     inner = width // LANES
-    base = side_ref[0] * inner
-    lane = lane_index((2 * edge, LANES))
-    for g in range(inner + 1):
+    base = side_ref[0] * inner if width < columns else 0
+    lane = lane_index((edge, LANES))
+
+    def make_group(g):
         at = base + g
         lanes = pl.ds(pl.multiple_of(lax.rem(at, groups) * LANES, LANES), LANES)
-        value = jnp.concatenate(
-            [up_ref[:, lanes].astype(F32), down_ref[:, lanes].astype(F32)], axis=0
-        )
+        value = edge_ref[:, lanes]
         if g == 0:
-            value = jnp.where(lane >= jnp.where(at == 0, SHIFT, 0), value, 0.0)
+            value = value.astype(F32)
+            value = jnp.where(lane >= jnp.where(at == 0, SHIFT, 0), value, 0.0).astype(BF16)
         if g == inner:
+            value = value.astype(F32)
             value = jnp.where(lane < jnp.where(at == groups, SHIFT, LANES), value, 0.0)
-        shifted[:, g * LANES : (g + 1) * LANES] = value.astype(BF16)
+            value = value.astype(BF16)
+        return value
+
     main = half // 8 * 8
-    pieces = [
-        [(top + v * main, top + (v + 1) * main) for top in (0, edge)]
-        + [(top + visits * main, top + edge) for top in (0, edge)]
-        for v in range(visits)
-    ]
-    pieces = [[(top, last) for top, last in parts if last > top] for parts in pieces]
-    blocks = min(BLOCKS, inner)
-
-    def body(step, carry):
-        windows = [
-            shifted[:, pl.ds(pl.multiple_of((blocks * step + n) * LANES, LANES), 2 * LANES)]
-            for n in range(blocks)
-        ]
-        for first, totals in convolve(windows, column_ref, row_ref, pieces):
-            start = (blocks * step + first) * LANES
-            at = pl.ds(pl.multiple_of(start, 2 * LANES), 2 * LANES)
-            source = pl.ds(pl.multiple_of(base * LANES + start, 2 * LANES), 2 * LANES)
-            for v, total in enumerate(totals):
-                lines = slice(v * rows, (v + 1) * rows)
-                out_ref[lines, at] = (total + part_ref[lines, source]).astype(BF16)
-        return carry
-
-    lax.fori_loop(0, inner // blocks, body, 0, unroll=4)
-
-
-def edge_part(side, up, down, column, edge, part, visits, half):
-    count, columns = part.shape
-    width = columns // 2
-    return pl.pallas_call(
-        functools.partial(edge_kernel, visits, half),
-        out_shape=held((count, width), BF16),
-        in_specs=[whole(pltpu.SMEM)] + [whole()] * 5,
+    pieces = [[(v * main, (v + 1) * main), (visits * main, edge)] for v in range(visits)]
+
+    def put(start, totals):
+        source = pl.ds(pl.multiple_of(base * LANES + start, 2 * LANES), 2 * LANES)
+        for v, total in enumerate(totals):
+            lines = slice(v * rows, (v + 1) * rows)
+            value = (total + part_ref[lines, source]).astype(out_ref.dtype)
+            out_ref[lines, start : start + 2 * LANES] = value
+
+    convolve(make_group, shifted, column_ref, row_ref, pieces, put)
+
+
+def rim_part(side, edge, column, table, part, visits, half, width, dtype):
+    count = part.shape[0]
+    return pl.pallas_call(
+        functools.partial(rim_kernel, visits, half),
+        out_shape=held((count, width), dtype),
+        in_specs=[whole(pltpu.SMEM)] + [whole()] * 4,
         out_specs=whole(),
-        scratch_shapes=[pltpu.VMEM((2 * up.shape[0], width + LANES), BF16)],
-        compiler_params=LIMIT,
-        name="edge_rows",
-    )(side, *kept(up, down, column, edge, part))
+        scratch_shapes=[pltpu.VMEM((edge.shape[0], width + LANES), BF16)],
+        compiler_params=LIMIT,
+    )(side, *kept(edge, column, table, part))
 
 
 def residual_kernel(visits, bands, *refs):
@@ -465,7 +469,7 @@
                 factor_ref[target, lanes] = weights[m] / (1.0 + term / CLIP_LEVEL)
         return carry
 
-    lax.fori_loop(0, width // LANES, body, 0, unroll=2)
+    lax.fori_loop(0, width // LANES, body, 0, unroll=4)
     for m in range(len(members)):
         at = slice(m * 8, (m + 1) * 8)
         sums_ref[0, m : m + 1, :] = jnp.sum(chi_ref[at, :], axis=0, keepdims=True)
@@ -524,7 +528,7 @@
 def final_pass(sums, values, factors, visits):
     count, width = values[0].shape
     rows = count // visits
-    chunks = max(1, width // 512)
+    chunks = 1
     return pl.pallas_call(
         functools.partial(final_kernel, visits),
         out_shape=(
@@ -550,15 +554,16 @@
 
     last, lower = pack_rows(warps, half, False)
     before = lax.ppermute(last, "sky", up)
-    leading, upper = pack_rows(warps, half, True)
-    after = lax.ppermute(leading, "sky", down)
     send_weight, own_weight = pixel_weights(badbits, coverage, variance, side)
     other_weight = lax.ppermute(send_weight, "visit", swap)
-    column, own, edge = tables(psf_index, psf_table, row_basis, col_basis, visits, rows)
+    column, own, above, below = tables(psf_index, psf_table, row_basis, col_basis, visits, rows)
+    leading, upper = pack_rows(warps, half, True, send_weight)
+    after = lax.ppermute(leading, "sky", down)
     part = own_part(upper.reshape(-1, columns), lower.reshape(-1, columns), column, own, visits)
-    send_value = edge_part(1 - side, before, after, column, edge, part, visits, half)
+    part = rim_part(side, before, column, above, part, visits, half, columns, F32)
+    send_value = rim_part(1 - side, after, column, below, part, visits, half, columns // 2, BF16)
     other_value = lax.ppermute(send_value, "visit", swap)
-    own_value = edge_part(side, before, after, column, edge, part, visits, half)
+    own_value = rim_part(side, after, column, below, part, visits, half, columns // 2, BF16)
     values = (own_value, other_value)
     factors, sums = residual_pass(values, (own_weight, other_weight), visits, coverage.shape[1])
     theirs = lax.ppermute(sums, "visit", swap)

time: 43.6 us -> 42.1 us (0.966)
  Pallas kernels: 19.5 us -> 16.7 us
  waiting for transfers between devices: 7.66 us -> 9.23 us
    ppermute x1, waiting for transfers between devices: 0.01 us -> 2.39 us  [per_device(): after = lax.ppermute(leading, 'sky', down)]
    ppermute x1, waiting for transfers between devices: 1.94 us -> 0.01 us  [per_device(): before = lax.ppermute(last, 'sky', up)]
    pallas_call x2, Pallas kernels: 3.75 us -> 2.75 us  [pack_rows(): pl.pallas_call(functools.partial(pack_kernel, half, first, skip), out_sha...]
    ppermute x1, waiting for transfers between devices: 0.01 us -> 0.92 us  [per_device(): other_value = lax.ppermute(send_value, 'visit', swap)]
    pallas_call x1, Pallas kernels: 4.83 us -> 3.99 us  [own_part(): pl.pallas_call(functools.partial(own_kernel, visits), out_shape=held((2 *...]
    pallas_call x1, Pallas kernels: 2.54 us -> 1.74 us  [pixel_weights(): pl.pallas_call(functools.partial(weight_kernel, visits, bands), out_shape...]
    pallas_call x2 -> x3, Pallas kernels: 3.95 us -> 3.7 us  [rim_part(): pl.pallas_call(functools.partial(rim_kernel, visits, half), out_shape=hel...]
  transfers between devices with their start and end apart: 8 -> 8, of which waited for: 5 -> 6; matrix products, arithmetic and copies ran while one was open for 0% -> 0% of each run, Pallas kernels for 33% -> 29%
where the time goes in v6:
time: 42.1 us; the launch traced here: 41.8 us
  Pallas kernels  16.7 us (40%)
  starting transfers between devices  15 us (36%)
  waiting for transfers between devices  9.23 us (22%)
  between operations  0.79 us (2%)
    ppermute x3, starting transfers between devices, per_device(): lax.ppermute(sums, 'sky', [(i, i ^ step) for i in range(strips)])  8.31 us
    ppermute x1, starting transfers between devices, per_device(): before = lax.ppermute(last, 'sky', up)  5.05 us
    ppermute x3, waiting for transfers between devices, per_device(): lax.ppermute(sums, 'sky', [(i, i ^ step) for i in range(strips)])  4.89 us
    pallas_call x1, Pallas kernels, own_part(): pl.pallas_call(functools.partial(own_kernel, visits), out_shape=held((2 *...  3.99 us
    pallas_call x3, Pallas kernels, rim_part(): pl.pallas_call(functools.partial(rim_kernel, visits, half), out_shape=hel...  3.7 us
    pallas_call x2, Pallas kernels, pack_rows(): pl.pallas_call(functools.partial(pack_kernel, half, first, skip), out_sha...  2.75 us
    ppermute x1, waiting for transfers between devices, per_device(): after = lax.ppermute(leading, 'sky', down)  2.39 us
    pallas_call x1, Pallas kernels, pixel_weights(): pl.pallas_call(functools.partial(weight_kernel, visits, bands), out_shape...  1.74 us
  transfers between devices with their start and end apart: 8, of which 6 were waited for; matrix products, arithmetic and copies ran while one was open for 0% of the time, Pallas kernels for 29%

profile of v6, /device:TPU:0, one launch (start us, length us, event | category | flops | bytes accessed | tf_op | source)
XLA Modules:
  0.0 41.8 jit_solution(11996298271090253316)
XLA Ops:
  0.6 1.4 %pack_lower.1 = (bf16[40,4096]{1,0:T(8,128)(2,1)S(1)}, bf16[4,16,4096]{2,1,0:T(8,128)(2,1)S(1)}) custom-call(bf16[4,32,4096]{2,1,0:T(8,128)(2,1)} %x_ref.3), custom_call_target="tpu_custom_call" | custom-call | tf_op jit(solution)/shard_map/pack_lower/pallas_call | solution.py:98
  2.0 0.0 copy-start
  2.0 0.0 copy-start.1
  2.0 0.0 copy-start.2
  2.0 0.0 copy-start.3
  2.1 5.1 %collective-permute-start.1 = (bf16[40,4096]{1,0:T(8,128)(2,1)S(1)}, bf16[40,4096]{1,0:T(8,128)(2,1)S(1)}, u32[]{:S(2)}, u32[]{:S(2)}) collective-permute-start(bf16[40,4096]{1,0:T(8,128)(2,1)S(1)} %get-tuple-element.18), channel_id=1, source_target_pairs={{0,2},{2,4},{4,6},{6,8},{8,10},{10,12},{12,14},{1,3},{3,5},{5,7},{... | collective-permute-start | bytes 983048 | tf_op jit(solution)/shard_map/ppermute | solution.py:556
  7.1 1.7 %weights.1 = (bf16[144,2048]{1,0:T(8,128)(2,1)S(1)}, bf16[144,2048]{1,0:T(8,128)(2,1)S(1)}) custom-call(s32[1]{0:T(128)} %bitcast.side_ref, s32[1,4]{1,0:T(1,128)} %bitcast.11, f32[1,4]{1,0:T(1,128)} %bitcast.12, s32[128,4096]{1,0:T(8,128)} %bitcast.10), custom_call_target="tpu_custom_call" | custom-call | tf_op jit(solution)/shard_map/weights/pallas_call | solution.py:159
  8.9 1.4 %pack_upper.1 = (bf16[40,4096]{1,0:T(8,128)(2,1)S(1)}, bf16[4,16,4096]{2,1,0:T(8,128)(2,1)S(1)}) custom-call(bf16[4,32,4096]{2,1,0:T(8,128)(2,1)} %x_ref.3, bf16[144,2048]{1,0:T(8,128)(2,1)S(1)} %get-tuple-element.14.refs_0_), custom_call_target="tpu_custom_call" | custom-call | tf_op jit(solution)/shard_map/pack_upper/pallas_call | solution.py:98
  10.3 1.3 %collective-permute-start = (bf16[40,4096]{1,0:T(8,128)(2,1)S(1)}, bf16[40,4096]{1,0:T(8,128)(2,1)S(1)}, u32[]{:S(2)}, u32[]{:S(2)}) collective-permute-start(bf16[40,4096]{1,0:T(8,128)(2,1)S(1)} %get-tuple-element.15), channel_id=1, source_target_pairs={{2,0},{4,2},{6,4},{8,6},{10,8},{12,10},{14,12},{3,1},{5,3},{7,5},{... | collective-permute-start | bytes 983048 | tf_op jit(solution)/shard_map/ppermute | solution.py:561
  11.6 0.1 collective-permute-start.3
  11.6 0.0 copy-done
  11.7 0.0 copy-done.1
  11.7 0.0 copy-done.2
  11.7 0.0 copy-done.3
  11.7 1.5 %tables.1 = (bf16[256,1024]{1,0:T(8,128)(2,1)S(1)}, bf16[256,256]{1,0:T(8,128)(2,1)S(1)}, bf16[256,128]{1,0:T(8,128)(2,1)S(1)}, bf16[256,128]{1,0:T(8,128)(2,1)S(1)}) custom-call(s32[4]{0:T(128)S(1)} %copy-done.3, f32[8,16]{1,0:T(8,128)S(1)} %bitcast.9, bf16[8,21]{1,0:T(8,128)(2,1)S(1)} %copy-done.1, bf16[8,21]{1,0:T(8,128)(2,1)S(1)} %copy-done.2), custom_call_target="tpu_custom_call" | custom-call | tf_op jit(solution)/shard_map/tables/pallas_call | solution.py:255
  13.2 4.0 %own_rows.1.part_ref = f32[128,4096]{1,0:T(8,128)S(1)} custom-call(bf16[64,4096]{1,0:T(8,128)(2,1)S(1)} %bitcast.8, bf16[64,4096]{1,0:T(8,128)(2,1)S(1)} %bitcast.7, bf16[256,1024]{1,0:T(8,128)(2,1)S(1)} %get-tuple-element.16.column_ref, bf16[256,256]{1,0:T(8,128)(2,1)S(1)} %get-tuple-element.22.row_ref), custom_call_target="tpu_custom_call" | custom-call | flops 1000000000 | bytes 10000000 | tf_op jit(solution)/shard_map/own_rows/pallas_call | solution.py:359
  17.2 0.0 collective-permute-done.1.edge_ref
  17.2 1.8 %shard_map.95.part_ref = f32[128,4096]{1,0:T(8,128)S(1)} custom-call(s32[1]{0:T(128)} %bitcast.side_ref, bf16[40,4096]{1,0:T(8,128)(2,1)S(1)} %collective-permute-done.1.edge_ref, bf16[256,1024]{1,0:T(8,128)(2,1)S(1)} %get-tuple-element.16.column_ref, bf16[256,128]{1,0:T(8,128)(2,1)S(1)} %get-tuple-element.19.row_ref, f32[128,4096]{1,0:T(8,128)S(1)} %own_rows.1.part_ref), custom_call_target="tpu_custom_call" | custom-call | tf_op jit(solution)/shard_map/pallas_call | solution.py:408
  18.9 2.4 %collective-permute-done.edge_ref = bf16[40,4096]{1,0:T(8,128)(2,1)S(1)} collective-permute-done((bf16[40,4096]{1,0:T(8,128)(2,1)S(1)}, bf16[40,4096]{1,0:T(8,128)(2,1)S(1)}, u32[]{:S(2)}, u32[]{:S(2)}) %collective-permute-start) | collective-permute-done | bytes 327712 | tf_op jit(solution)/shard_map/ppermute | solution.py:561
  21.3 1.0 %shard_map.97 = bf16[128,2048]{1,0:T(8,128)(2,1)S(1)} custom-call(s32[1]{0:T(128)S(6)} %sub.3.side_ref, bf16[40,4096]{1,0:T(8,128)(2,1)S(1)} %collective-permute-done.edge_ref, bf16[256,1024]{1,0:T(8,128)(2,1)S(1)} %get-tuple-element.16.column_ref, bf16[256,128]{1,0:T(8,128)(2,1)S(1)} %get-tuple-element.17.row_ref, f32[128,4096]{1,0:T(8,128)S(1)} %shard_map.95.part_ref), custom_call_target="tpu_custom_call" | custom-call | tf_op jit(solution)/shard_map/pallas_call | solution.py:408
  22.3 0.1 collective-permute-start.2
  22.4 1.0 %shard_map.96.refs_0_.own_ref = bf16[128,2048]{1,0:T(8,128)(2,1)S(1)} custom-call(s32[1]{0:T(128)} %bitcast.side_ref, bf16[40,4096]{1,0:T(8,128)(2,1)S(1)} %collective-permute-done.edge_ref, bf16[256,1024]{1,0:T(8,128)(2,1)S(1)} %get-tuple-element.16.column_ref, bf16[256,128]{1,0:T(8,128)(2,1)S(1)} %get-tuple-element.17.row_ref, ...), custom_call_target="tpu_custom_call" | custom-call | tf_op jit(solution)/shard_map/pallas_call | solution.py:408
  23.3 0.0 collective-permute-done.3.refs_3_
  23.4 0.9 %collective-permute-done.2.refs_1_.other_ref = bf16[128,2048]{1,0:T(8,128)(2,1)S(1)} collective-permute-done((bf16[128,2048]{1,0:T(8,128)(2,1)S(1)}, bf16[128,2048]{1,0:T(8,128)(2,1)S(1)}, u32[]{:S(2)}, u32[]{:S(2)}) %collective-permute-start.2) | collective-permute-done | bytes 524320 | tf_op jit(solution)/shard_map/ppermute | solution.py:565
  24.3 1.3 %residual.1 = (f32[256,2048]{1,0:T(8,128)S(1)}, f32[2,8,128]{2,1,0:T(8,128)S(1)}) custom-call(bf16[128,2048]{1,0:T(8,128)(2,1)S(1)} %shard_map.96.refs_0_.own_ref, bf16[128,2048]{1,0:T(8,128)(2,1)S(1)} %collective-permute-done.2.refs_1_.other_ref, bf16[144,2048]{1,0:T(8,128)(2,1)S(1)} %get-tuple-element.23.refs_2_, ...), custom_call_target="tpu_custom_call" | custom-call | tf_op jit(solution)/shard_map/residual/pallas_call | solution.py:482
  25.6 0.2 collective-permute-start.4
  25.8 1.0 %collective-permute-done.4 = f32[2,8,128]{2,1,0:T(8,128)S(1)} collective-permute-done((f32[2,8,128]{2,1,0:T(8,128)S(1)}, f32[2,8,128]{2,1,0:T(8,128)S(1)}, u32[]{:S(2)}, u32[]{:S(2)}) %collective-permute-start.4) | collective-permute-done | bytes 8224 | tf_op jit(solution)/shard_map/ppermute | solution.py:569
  26.9 2.5 %collective-permute-start.5 = (f32[2,8,128]{2,1,0:T(8,128)S(1)}, f32[2,8,128]{2,1,0:T(8,128)S(1)}, u32[]{:S(2)}, u32[]{:S(2)}) collective-permute-start(f32[2,8,128]{2,1,0:T(8,128)S(1)} %maximum_add_fusion), channel_id=1, source_target_pairs={{0,2},{2,0},{4,6},{6,4},{8,10},{10,8},{12,14},{14,12},{1,3},{3,1},... | collective-permute-start | bytes 24584 | tf_op jit(solution)/shard_map/ppermute | solution.py:573
  29.3 1.6 %collective-permute-done.5 = f32[2,8,128]{2,1,0:T(8,128)S(1)} collective-permute-done((f32[2,8,128]{2,1,0:T(8,128)S(1)}, f32[2,8,128]{2,1,0:T(8,128)S(1)}, u32[]{:S(2)}, u32[]{:S(2)}) %collective-permute-start.5) | collective-permute-done | bytes 8224 | tf_op jit(solution)/shard_map/ppermute | solution.py:573
  31.0 2.8 %collective-permute-start.6 = (f32[2,8,128]{2,1,0:T(8,128)S(1)}, f32[2,8,128]{2,1,0:T(8,128)S(1)}, u32[]{:S(2)}, u32[]{:S(2)}) collective-permute-start(f32[2,8,128]{2,1,0:T(8,128)S(1)} %add.13), channel_id=1, source_target_pairs={{0,4},{2,6},{4,0},{6,2},{8,12},{10,14},{12,8},{14,10},{1,5},{3,7},... | collective-permute-start | bytes 24584 | tf_op jit(solution)/shard_map/ppermute | solution.py:573
  33.8 1.6 %collective-permute-done.6 = f32[2,8,128]{2,1,0:T(8,128)S(1)} collective-permute-done((f32[2,8,128]{2,1,0:T(8,128)S(1)}, f32[2,8,128]{2,1,0:T(8,128)S(1)}, u32[]{:S(2)}, u32[]{:S(2)}) %collective-permute-start.6) | collective-permute-done | bytes 8224 | tf_op jit(solution)/shard_map/ppermute | solution.py:573
  35.4 3.0 %collective-permute-start.7 = (f32[2,8,128]{2,1,0:T(8,128)S(1)}, f32[2,8,128]{2,1,0:T(8,128)S(1)}, u32[]{:S(2)}, u32[]{:S(2)}) collective-permute-start(f32[2,8,128]{2,1,0:T(8,128)S(1)} %add.14), channel_id=1, source_target_pairs={{0,8},{2,10},{4,12},{6,14},{8,0},{10,2},{12,4},{14,6},{1,9},{3,11}... | collective-permute-start | bytes 24584 | tf_op jit(solution)/shard_map/ppermute | solution.py:573
  38.5 1.6 %collective-permute-done.7 = f32[2,8,128]{2,1,0:T(8,128)S(1)} collective-permute-done((f32[2,8,128]{2,1,0:T(8,128)S(1)}, f32[2,8,128]{2,1,0:T(8,128)S(1)}, u32[]{:S(2)}, u32[]{:S(2)}) %collective-permute-start.7) | collective-permute-done | bytes 8224 | tf_op jit(solution)/shard_map/ppermute | solution.py:573
  40.1 1.7 %final.1 = (f32[32,2048]{1,0:T(8,128)}, f32[4]{0:T(128)}) custom-call(f32[2,8,128]{2,1,0:T(8,128)S(1)} %add.15.sums_ref, bf16[128,2048]{1,0:T(8,128)(2,1)S(1)} %shard_map.96.refs_0_.own_ref, bf16[128,2048]{1,0:T(8,128)(2,1)S(1)} %collective-permute-done.2.refs_1_.other_ref, f32[256,2048]{1,0:T(8,128)S(1)} %get-tuple-element.25.factor_ref), custom_call_target="tpu_custom_call" | custom-call | tf_op jit(solution)/shard_map/final/pallas_call | solution.py:532
  (5 shorter events, 0.0 us)
Async XLA Ops:
  2.0 9.6 %copy-start = (f32[16,8]{0,1:T(8,128)S(1)}, f32[16,8]{0,1:T(8,128)}, u32[]{:S(2)}) copy-start(f32[16,8]{0,1:T(8,128)} %param.13) | copy-start | bytes 1540
  2.0 9.6 %copy-start.1 = (bf16[8,21]{1,0:T(8,128)(2,1)S(1)}, bf16[8,21]{1,0:T(8,128)(2,1)}, u32[]{:S(2)}) copy-start(bf16[8,21]{1,0:T(8,128)(2,1)} %row_ref.1) | copy-start | bytes 1012
  2.0 9.6 %copy-start.2 = (bf16[8,21]{1,0:T(8,128)(2,1)S(1)}, bf16[8,21]{1,0:T(8,128)(2,1)}, u32[]{:S(2)}) copy-start(bf16[8,21]{1,0:T(8,128)(2,1)} %col_ref.1) | copy-start | bytes 1012
  2.0 9.6 %copy-start.3 = (s32[4]{0:T(128)S(1)}, s32[4]{0:T(128)}, u32[]{:S(2)}) copy-start(s32[4]{0:T(128)} %index_ref.1) | copy-start | bytes 52
  2.1 15.1 %collective-permute-start.1 = (bf16[40,4096]{1,0:T(8,128)(2,1)S(1)}, bf16[40,4096]{1,0:T(8,128)(2,1)S(1)}, u32[]{:S(2)}, u32[]{:S(2)}) collective-permute-start(bf16[40,4096]{1,0:T(8,128)(2,1)S(1)} %get-tuple-element.18), channel_id=1, source_target_pairs={{0,2},{2,4},{4,6},{6,8},{8,10},{10,12},{12,14},{1,3},{3,5},{5,7},{... | collective-permute-start | bytes 983048 | tf_op jit(solution)/shard_map/ppermute | solution.py:556
  10.3 11.1 %collective-permute-start = (bf16[40,4096]{1,0:T(8,128)(2,1)S(1)}, bf16[40,4096]{1,0:T(8,128)(2,1)S(1)}, u32[]{:S(2)}, u32[]{:S(2)}) collective-permute-start(bf16[40,4096]{1,0:T(8,128)(2,1)S(1)} %get-tuple-element.15), channel_id=1, source_target_pairs={{2,0},{4,2},{6,4},{8,6},{10,8},{12,10},{14,12},{3,1},{5,3},{7,5},{... | collective-permute-start | bytes 983048 | tf_op jit(solution)/shard_map/ppermute | solution.py:561
  11.6 11.8 %collective-permute-start.3 = (bf16[144,2048]{1,0:T(8,128)(2,1)S(1)}, bf16[144,2048]{1,0:T(8,128)(2,1)S(1)}, u32[]{:S(2)}, u32[]{:S(2)}) collective-permute-start(bf16[144,2048]{1,0:T(8,128)(2,1)S(1)} %get-tuple-element.14.refs_0_), channel_id=1, source_target_pairs={{0,1},{1,0},{2,3},{3,2},{4,5},{5,4},{6,7},{7,6},{8,9},{9,8},{10,11... | collective-permute-start | bytes 1769480 | tf_op jit(solution)/shard_map/ppermute | solution.py:558
  22.3 2.0 %collective-permute-start.2 = (bf16[128,2048]{1,0:T(8,128)(2,1)S(1)}, bf16[128,2048]{1,0:T(8,128)(2,1)S(1)}, u32[]{:S(2)}, u32[]{:S(2)}) collective-permute-start(bf16[128,2048]{1,0:T(8,128)(2,1)S(1)} %shard_map.97), channel_id=1, source_target_pairs={{0,1},{1,0},{2,3},{3,2},{4,5},{5,4},{6,7},{7,6},{8,9},{9,8},{10,11... | collective-permute-start | bytes 1572872 | tf_op jit(solution)/shard_map/ppermute | solution.py:565
  25.6 1.2 %collective-permute-start.4 = (f32[2,8,128]{2,1,0:T(8,128)S(1)}, f32[2,8,128]{2,1,0:T(8,128)S(1)}, u32[]{:S(2)}, u32[]{:S(2)}) collective-permute-start(f32[2,8,128]{2,1,0:T(8,128)S(1)} %get-tuple-element.24), channel_id=1, source_target_pairs={{0,1},{1,0},{2,3},{3,2},{4,5},{5,4},{6,7},{7,6},{8,9},{9,8},{10,11... | collective-permute-start | bytes 24584 | tf_op jit(solution)/shard_map/ppermute | solution.py:569
  26.9 4.1 %collective-permute-start.5 = (f32[2,8,128]{2,1,0:T(8,128)S(1)}, f32[2,8,128]{2,1,0:T(8,128)S(1)}, u32[]{:S(2)}, u32[]{:S(2)}) collective-permute-start(f32[2,8,128]{2,1,0:T(8,128)S(1)} %maximum_add_fusion), channel_id=1, source_target_pairs={{0,2},{2,0},{4,6},{6,4},{8,10},{10,8},{12,14},{14,12},{1,3},{3,1},... | collective-permute-start | bytes 24584 | tf_op jit(solution)/shard_map/ppermute | solution.py:573
  31.0 4.4 %collective-permute-start.6 = (f32[2,8,128]{2,1,0:T(8,128)S(1)}, f32[2,8,128]{2,1,0:T(8,128)S(1)}, u32[]{:S(2)}, u32[]{:S(2)}) collective-permute-start(f32[2,8,128]{2,1,0:T(8,128)S(1)} %add.13), channel_id=1, source_target_pairs={{0,4},{2,6},{4,0},{6,2},{8,12},{10,14},{12,8},{14,10},{1,5},{3,7},... | collective-permute-start | bytes 24584 | tf_op jit(solution)/shard_map/ppermute | solution.py:573
  35.4 4.7 %collective-permute-start.7 = (f32[2,8,128]{2,1,0:T(8,128)S(1)}, f32[2,8,128]{2,1,0:T(8,128)S(1)}, u32[]{:S(2)}, u32[]{:S(2)}) collective-permute-start(f32[2,8,128]{2,1,0:T(8,128)S(1)} %add.14), channel_id=1, source_target_pairs={{0,8},{2,10},{4,12},{6,14},{8,0},{10,2},{12,4},{14,6},{1,9},{3,11}... | collective-permute-start | bytes 24584 | tf_op jit(solution)/shard_map/ppermute | solution.py:573

commit v7 on v6

--- a/solution.py
+++ b/solution.py
@@ -190,7 +190,7 @@
     return segments, main + visits * rest
 
 
-def table_kernel(visits, rows, half, index_ref, table_ref, row_ref, col_ref, column_out, own_out, above_out, below_out):
+def table_kernel(visits, rows, half, index_ref, table_ref, row_ref, col_ref, after_ref, column_out, own_out, above_out, below_out):
     bases, taps = row_ref.shape
     window = 2 * LANES
 
@@ -248,7 +248,7 @@
         assemble(out, high, segments)
 
 
-def tables(psf_index, psf_table, row_basis, col_basis, visits, rows):
+def tables(psf_index, psf_table, row_basis, col_basis, visits, rows, after):
     bases, taps = row_basis.shape
     half = taps // 2
     rim = (2 * visits * rows, bases * edge_segments(visits, rows, half, 0)[1])
@@ -260,11 +260,11 @@
             held(rim, BF16),
             held(rim, BF16),
         ),
-        in_specs=[whole(pltpu.SMEM)] * 2 + [whole()] * 2,
+        in_specs=[whole(pltpu.SMEM)] * 2 + [whole()] * 2 + [pl.BlockSpec(memory_space=pl.ANY)],
         out_specs=(whole(),) * 4,
         compiler_params=LIMIT,
         name="tables",
-    )(psf_index, psf_table.T, row_basis, col_basis)
+    )(psf_index, psf_table.T, row_basis, col_basis, after)
 
 
 BLOCKS = 4
@@ -415,132 +415,162 @@
     )(side, *kept(edge, column, table, part))
 
 
-def residual_kernel(visits, bands, *refs):
-    value_refs, weight_refs = refs[0:2], refs[2:4]
-    factor_ref, sums_ref, chi_ref, count_ref = refs[4:]
-    rows = value_refs[0].shape[0] // visits
-    width = value_refs[0].shape[1]
+def norm_kernel(visits, bands, *refs):
+    flag_refs = refs[:2]
+    weight_ref, inverse_ref, count_ref = refs[2:]
+    rows, width = inverse_ref.shape
+    count = visits * rows
     high = min(16, rows // bands)
-    chi_ref[...] = jnp.zeros_like(chi_ref)
-    count_ref[...] = jnp.zeros_like(count_ref)
-
-    def folded(value):
-        total = value[:8]
-        for start in range(8, high, 8):
-            total = total + value[start : start + 8]
-        return total
-
     members = [(side, v) for side in range(2) for v in range(visits)]
-    count = value_refs[0].shape[0]
     levels = {}
     for side in range(2):
-        found = weight_refs[side][count:, :LANES].astype(F32)
+        found = flag_refs[side][count:, :LANES].astype(F32)
         for v in range(visits):
             for b in range(bands):
                 spots = [(k * bands + b) * visits + v for k in range(3)]
                 parts = [found[spot : spot + 1] for spot in spots]
                 level = (parts[0] + parts[1]) + parts[2]
                 levels[side, v, b] = jnp.broadcast_to(level, (high, LANES))
+    count_ref[...] = jnp.zeros_like(count_ref)
 
     def body(step, carry):
         lanes = pl.ds(pl.multiple_of(step * LANES, LANES), LANES)
         for row in range(0, rows, high):
-            band = row // (rows // bands)
-            values, weights, flags = [], [], []
-            numer = denom = None
-            for side, v in members:
+            denom = PRIOR_WEIGHT
+            for m, (side, v) in enumerate(members):
+                flag = flag_refs[side][v * rows + row : v * rows + row + high, lanes].astype(F32)
+                weight = flag * levels[side, v, row // (rows // bands)]
+                weight_ref[m * rows + row : m * rows + row + high, lanes] = weight
+                count_ref[m * 8 : (m + 1) * 8, :] += folded(flag)
+                denom = denom + weight
+            inverse_ref[row : row + high, lanes] = 1.0 / denom
+        return carry
+
+    lax.fori_loop(0, width // LANES, body, 0, unroll=4)
+
+
+def folded(value):
+    total = value[:8]
+    for start in range(8, value.shape[0], 8):
+        total = total + value[start : start + 8]
+    return total
+
+
+def norms(own_flags, other_flags, visits, bands, rows):
+    width = own_flags.shape[1]
+    members = 2 * visits
+    return pl.pallas_call(
+        functools.partial(norm_kernel, visits, bands),
+        out_shape=(
+            held((members * rows, width), F32),
+            held((rows, width), F32),
+            held((members * 8, LANES), F32),
+        ),
+        in_specs=[whole()] * 2,
+        out_specs=(whole(),) * 3,
+        compiler_params=LIMIT,
+        name="norms",
+    )(*kept(own_flags, other_flags))
+
+
+def residual_kernel(visits, side_ref, *refs):
+    value_refs = refs[:2]
+    weight_ref, inverse_ref, count_ref, factor_ref, sums_ref, chi_ref = refs[2:]
+    rows, width = inverse_ref.shape
+    high = min(16, rows)
+    chi_ref[...] = jnp.zeros_like(chi_ref)
+    members = [(side, v) for side in range(2) for v in range(visits)]
+
+    def body(step, carry):
+        lanes = pl.ds(pl.multiple_of(step * LANES, LANES), LANES)
+        for row in range(0, rows, high):
+            values, weights = [], []
+            numer = None
+            for m, (side, v) in enumerate(members):
                 at = slice(v * rows + row, v * rows + row + high)
                 value = value_refs[side][at, lanes].astype(F32)
-                flag = weight_refs[side][at, lanes].astype(F32)
-                weight = flag * levels[side, v, band]
-                flags.append(flag)
+                weight = weight_ref[m * rows + row : m * rows + row + high, lanes]
                 values.append(value)
                 weights.append(weight)
                 numer = weight * value if numer is None else numer + weight * value
-                denom = weight if denom is None else denom + weight
-            first = numer / (denom + PRIOR_WEIGHT)
-            for m, (side, v) in enumerate(members):
+            first = numer * inverse_ref[row : row + high, lanes]
+            for m in range(len(members)):
                 residual = values[m] - first
                 term = weights[m] * (residual * residual)
-                at = slice(m * 8, (m + 1) * 8)
-                chi_ref[at, :] += folded(term)
-                count_ref[at, :] += folded(flags[m])
+                chi_ref[m * 8 : (m + 1) * 8, :] += folded(term)
                 target = slice(m * rows + row, m * rows + row + high)
-                factor_ref[target, lanes] = weights[m] / (1.0 + term / CLIP_LEVEL)
+                factor_ref[target, lanes] = weights[m] / (CLIP_LEVEL + term)
         return carry
 
     lax.fori_loop(0, width // LANES, body, 0, unroll=4)
-    for m in range(len(members)):
-        at = slice(m * 8, (m + 1) * 8)
-        sums_ref[0, m : m + 1, :] = jnp.sum(chi_ref[at, :], axis=0, keepdims=True)
-        sums_ref[1, m : m + 1, :] = jnp.sum(count_ref[at, :], axis=0, keepdims=True)
-
-
-def residual_pass(values, weights, visits, bands):
-    count, width = values[0].shape
+    for k, ref in enumerate((chi_ref, count_ref)):
+        lines = [
+            jnp.sum(ref[m * 8 : (m + 1) * 8, :], axis=0, keepdims=True)
+            for m in range(len(members))
+        ]
+        total = jnp.concatenate(lines, axis=0)
+        sums_ref[k] = jnp.where(side_ref[0] == 0, total, pltpu.roll(total, visits, 0))
+
+
+def residual_pass(side, values, weights, inverse, counts, visits):
+    rows, width = inverse.shape
     members = 2 * visits
     return pl.pallas_call(
-        functools.partial(residual_kernel, visits, bands),
-        out_shape=(held((2 * count, width), F32), held((2, members, LANES), F32)),
-        in_specs=[whole()] * 4,
+        functools.partial(residual_kernel, visits),
+        out_shape=(held((members * rows, width), F32), held((2, members, LANES), F32)),
+        in_specs=[whole(pltpu.SMEM)] + [whole()] * 5,
         out_specs=(whole(), whole()),
-        scratch_shapes=[pltpu.VMEM((members * 8, LANES), F32)] * 2,
+        scratch_shapes=[pltpu.VMEM((members * 8, LANES), F32)],
         compiler_params=LIMIT,
         name="residual",
-    )(*kept(*values, *weights))
-
-
-def final_kernel(visits, sums_ref, own_ref, other_ref, factor_ref, out_ref, chi_ref, done, sent):
+    )(side, *kept(*values, weights, inverse, counts))
+
+
+def final_kernel(visits, side_ref, sums_ref, own_ref, other_ref, factor_ref, out_ref, chi_ref, done, sent):
     rows, width = done.shape
-    chunks = sent.shape[0]
     high = min(16, rows)
-    chi = jnp.sum(sums_ref[0], axis=1, keepdims=True) / jnp.sum(
-        sums_ref[1], axis=1, keepdims=True
-    )
-    scale = 1.0 / (CHI_OFFSET + chi)
+    sums = [
+        jnp.where(side_ref[0] == 0, sums_ref[k], pltpu.roll(sums_ref[k], visits, 0))
+        for k in range(2)
+    ]
+    chi = jnp.sum(sums[0], axis=1, keepdims=True) / jnp.sum(sums[1], axis=1, keepdims=True)
+    scale = CLIP_LEVEL / (CHI_OFFSET + chi)
     for v in range(visits):
         chi_ref[v] = chi[v, 0]
     scales = [jnp.broadcast_to(scale[m : m + 1], (high, LANES)) for m in range(2 * visits)]
-    copies = []
-    for c in range(chunks):
-        for lane in range(c * width // chunks, (c + 1) * width // chunks, LANES):
-            lanes = slice(lane, lane + LANES)
-            for row in range(0, rows, high):
-                numer = denom = None
-                for m in range(2 * visits):
-                    source = own_ref if m < visits else other_ref
-                    at = (m % visits) * rows + row
-                    value = source[at : at + high, lanes].astype(F32)
-                    at = m * rows + row
-                    revised = factor_ref[at : at + high, lanes] * scales[m]
-                    numer = revised * value if numer is None else numer + revised * value
-                    denom = revised if denom is None else denom + revised
-                done[row : row + high, lanes] = numer / (denom + PRIOR_WEIGHT)
-        lanes = slice(c * width // chunks, (c + 1) * width // chunks)
-        copies.append(
-            pltpu.make_async_copy(done.at[:, lanes], out_ref.at[:, lanes], sent.at[c])
-        )
-        copies[c].start()
-    for copy in copies:
-        copy.wait()
-
-
-def final_pass(sums, values, factors, visits):
+    for lane in range(0, width, LANES):
+        lanes = slice(lane, lane + LANES)
+        for row in range(0, rows, high):
+            numer = denom = None
+            for m in range(2 * visits):
+                source = own_ref if m < visits else other_ref
+                at = (m % visits) * rows + row
+                value = source[at : at + high, lanes].astype(F32)
+                at = m * rows + row
+                revised = factor_ref[at : at + high, lanes] * scales[m]
+                numer = revised * value if numer is None else numer + revised * value
+                denom = revised if denom is None else denom + revised
+            done[row : row + high, lanes] = numer / (denom + PRIOR_WEIGHT)
+    copy = pltpu.make_async_copy(done, out_ref, sent)
+    copy.start()
+    copy.wait()
+
+
+def final_pass(side, sums, values, factors, visits):
     count, width = values[0].shape
     rows = count // visits
-    chunks = 1
     return pl.pallas_call(
         functools.partial(final_kernel, visits),
         out_shape=(
             jax.ShapeDtypeStruct((rows, width), F32),
             jax.ShapeDtypeStruct((visits,), F32),
         ),
-        in_specs=[whole()] * 4,
+        in_specs=[whole(pltpu.SMEM)] + [whole()] * 4,
         out_specs=(pl.BlockSpec(memory_space=pl.ANY), whole(pltpu.SMEM)),
-        scratch_shapes=[pltpu.VMEM((rows, width), F32), pltpu.SemaphoreType.DMA((chunks,))],
+        scratch_shapes=[pltpu.VMEM((rows, width), F32), pltpu.SemaphoreType.DMA(())],
         compiler_params=LIMIT,
         name="final",
-    )(*kept(sums, *values, factors))
+    )(side, *kept(sums, *values, factors))
 
 
 def per_device(warps, badbits, coverage, variance, psf_index, psf_table, row_basis, col_basis):
@@ -556,23 +586,31 @@
     before = lax.ppermute(last, "sky", up)
     send_weight, own_weight = pixel_weights(badbits, coverage, variance, side)
     other_weight = lax.ppermute(send_weight, "visit", swap)
-    column, own, above, below = tables(psf_index, psf_table, row_basis, col_basis, visits, rows)
-    leading, upper = pack_rows(warps, half, True, send_weight)
+    column, own, above, below = tables(
+        psf_index, psf_table, row_basis, col_basis, visits, rows, own_weight
+    )
+    leading, upper = pack_rows(warps, half, True, column)
     after = lax.ppermute(leading, "sky", down)
     part = own_part(upper.reshape(-1, columns), lower.reshape(-1, columns), column, own, visits)
     part = rim_part(side, before, column, above, part, visits, half, columns, F32)
+    weights, inverse, counts = norms(own_weight, other_weight, visits, coverage.shape[1], rows)
     send_value = rim_part(1 - side, after, column, below, part, visits, half, columns // 2, BF16)
     other_value = lax.ppermute(send_value, "visit", swap)
     own_value = rim_part(side, after, column, below, part, visits, half, columns // 2, BF16)
     values = (own_value, other_value)
-    factors, sums = residual_pass(values, (own_weight, other_weight), visits, coverage.shape[1])
-    theirs = lax.ppermute(sums, "visit", swap)
-    sums = sums + jnp.concatenate([theirs[:, visits:], theirs[:, :visits]], axis=1)
+    factors, sums = residual_pass(side, values, weights, inverse, counts, visits)
+    sums = sums + lax.ppermute(sums, "visit", swap)
     step = 1
     while step < strips:
-        sums = sums + lax.ppermute(sums, "sky", [(i, i ^ step) for i in range(strips)])
+        pairs = [(i, i ^ step) for i in range(strips)]
+        if step == 1:
+            pairs = [(2 * i + v, 2 * j + 1 - v) for i, j in pairs for v in (0, 1)]
+            theirs = lax.ppermute(sums, ("sky", "visit"), pairs)
+        else:
+            theirs = lax.ppermute(sums, "sky", pairs)
+        sums = sums + theirs
         step *= 2
-    return final_pass(sums, values, factors, visits)
+    return final_pass(side, sums, values, factors, visits)
 
 
 def solution(mesh):

time: 42.1 us -> 41.6 us (0.988)
  starting transfers between devices: 15 us -> 12.9 us
  waiting for transfers between devices: 9.23 us -> 10.8 us
    ppermute x4, starting transfers between devices: 8.51 us -> 6.56 us  [the longest x2 4.18 us: per_device(): theirs = lax.ppermute(sums, 'sky', pairs)]
    ppermute x1, waiting for transfers between devices: 2.39 us -> 3.85 us  [per_device(): after = lax.ppermute(leading, 'sky', down)]
    ppermute x4, waiting for transfers between devices: 5.92 us -> 6.42 us  [the longest x2 4.02 us: per_device(): theirs = lax.ppermute(sums, 'sky', pairs)]
    pallas_call x1 -> x2, Pallas kernels: 1.35 us -> 1.35 us  [the longest x1 0.98 us: residual_pass(): pl.pallas_call(functools.partial(residual_kernel, visits), out_shape=(hel...]
  transfers between devices with their start and end apart: 8 -> 8, of which waited for: 6 -> 6; matrix products, arithmetic and copies ran while one was open for 0% -> 0% of each run, Pallas kernels for 29% -> 31%
where the time goes in v7:
time: 41.6 us; the launch traced here: 41.4 us
  Pallas kernels  16.8 us (40%)
  starting transfers between devices  12.9 us (31%)
  waiting for transfers between devices  10.8 us (26%)
  between operations  0.8 us (2%)
    ppermute x1, starting transfers between devices, per_device(): before = lax.ppermute(last, 'sky', up)  4.92 us
    ppermute x2, starting transfers between devices, per_device(): theirs = lax.ppermute(sums, 'sky', pairs)  4.18 us
    ppermute x2, waiting for transfers between devices, per_device(): theirs = lax.ppermute(sums, 'sky', pairs)  4.02 us
    pallas_call x1, Pallas kernels, own_part(): pl.pallas_call(functools.partial(own_kernel, visits), out_shape=held((2 *...  4 us
    ppermute x1, waiting for transfers between devices, per_device(): after = lax.ppermute(leading, 'sky', down)  3.85 us
    pallas_call x3, Pallas kernels, rim_part(): pl.pallas_call(functools.partial(rim_kernel, visits, half), out_shape=hel...  3.76 us
    pallas_call x2, Pallas kernels, pack_rows(): pl.pallas_call(functools.partial(pack_kernel, half, first, skip), out_sha...  2.77 us
    ppermute x1, starting transfers between devices, per_device(): theirs = lax.ppermute(sums, ('sky', 'visit'), pairs)  2.18 us
  transfers between devices with their start and end apart: 8, of which 6 were waited for; matrix products, arithmetic and copies ran while one was open for 0% of the time, Pallas kernels for 31%

profile of v7, /device:TPU:0, one launch (start us, length us, event | category | flops | bytes accessed | tf_op | source)
XLA Modules:
  0.0 41.4 jit_solution(5380012121359727976)
XLA Ops:
  0.6 0.0 copy-start.3
  0.6 0.0 copy-start
  0.7 0.0 copy-start.1
  0.7 0.0 copy-start.2
  0.7 1.4 %pack_lower.1 = (bf16[40,4096]{1,0:T(8,128)(2,1)S(1)}, bf16[4,16,4096]{2,1,0:T(8,128)(2,1)S(1)}) custom-call(bf16[4,32,4096]{2,1,0:T(8,128)(2,1)} %x_ref.3), custom_call_target="tpu_custom_call" | custom-call | tf_op jit(solution)/shard_map/pack_lower/pallas_call | solution.py:98
  2.1 4.9 %collective-permute-start.1 = (bf16[40,4096]{1,0:T(8,128)(2,1)S(1)}, bf16[40,4096]{1,0:T(8,128)(2,1)S(1)}, u32[]{:S(2)}, u32[]{:S(2)}) collective-permute-start(bf16[40,4096]{1,0:T(8,128)(2,1)S(1)} %get-tuple-element.21), channel_id=1, source_target_pairs={{0,2},{2,4},{4,6},{6,8},{8,10},{10,12},{12,14},{1,3},{3,5},{5,7},{... | collective-permute-start | bytes 983048 | tf_op jit(solution)/shard_map/ppermute | solution.py:586
  7.0 1.7 %weights.1 = (bf16[144,2048]{1,0:T(8,128)(2,1)S(1)}, bf16[144,2048]{1,0:T(8,128)(2,1)S(1)}) custom-call(s32[1]{0:T(128)} %bitcast.side_ref, s32[1,4]{1,0:T(1,128)} %bitcast.11, f32[1,4]{1,0:T(1,128)} %bitcast.12, s32[128,4096]{1,0:T(8,128)} %bitcast.10), custom_call_target="tpu_custom_call" | custom-call | tf_op jit(solution)/shard_map/weights/pallas_call | solution.py:159
  8.8 0.0 copy-done.3
  8.8 0.0 copy-done
  8.8 0.0 copy-done.1
  8.8 0.0 copy-done.2
  8.8 1.5 %tables.1 = (bf16[256,1024]{1,0:T(8,128)(2,1)S(1)}, bf16[256,256]{1,0:T(8,128)(2,1)S(1)}, bf16[256,128]{1,0:T(8,128)(2,1)S(1)}, bf16[256,128]{1,0:T(8,128)(2,1)S(1)}) custom-call(s32[4]{0:T(128)S(1)} %copy-done.3, f32[8,16]{1,0:T(8,128)S(1)} %bitcast.9, bf16[8,21]{1,0:T(8,128)(2,1)S(1)} %copy-done.1, bf16[8,21]{1,0:T(8,128)(2,1)S(1)} %copy-done.2, ...), custom_call_target="tpu_custom_call" | custom-call | tf_op jit(solution)/shard_map/tables/pallas_call | solution.py:255
  10.3 1.4 %pack_upper.1 = (bf16[40,4096]{1,0:T(8,128)(2,1)S(1)}, bf16[4,16,4096]{2,1,0:T(8,128)(2,1)S(1)}) custom-call(bf16[4,32,4096]{2,1,0:T(8,128)(2,1)} %x_ref.3, bf16[256,1024]{1,0:T(8,128)(2,1)S(1)} %get-tuple-element.18.refs_0_.column_ref), custom_call_target="tpu_custom_call" | custom-call | tf_op jit(solution)/shard_map/pack_upper/pallas_call | solution.py:98
  11.7 1.3 %collective-permute-start = (bf16[40,4096]{1,0:T(8,128)(2,1)S(1)}, bf16[40,4096]{1,0:T(8,128)(2,1)S(1)}, u32[]{:S(2)}, u32[]{:S(2)}) collective-permute-start(bf16[40,4096]{1,0:T(8,128)(2,1)S(1)} %get-tuple-element.19), channel_id=1, source_target_pairs={{2,0},{4,2},{6,4},{8,6},{10,8},{12,10},{14,12},{3,1},{5,3},{7,5},{... | collective-permute-start | bytes 983048 | tf_op jit(solution)/shard_map/ppermute | solution.py:593
  13.0 0.1 collective-permute-start.3
  13.1 4.0 %own_rows.1.part_ref = f32[128,4096]{1,0:T(8,128)S(1)} custom-call(bf16[64,4096]{1,0:T(8,128)(2,1)S(1)} %bitcast.8, bf16[64,4096]{1,0:T(8,128)(2,1)S(1)} %bitcast.7, bf16[256,1024]{1,0:T(8,128)(2,1)S(1)} %get-tuple-element.18.refs_0_.column_ref, bf16[256,256]{1,0:T(8,128)(2,1)S(1)} %get-tuple-element.25.row_ref), custom_call_target="tpu_custom_call" | custom-call | flops 1000000000 | bytes 10000000 | tf_op jit(solution)/shard_map/own_rows/pallas_call | solution.py:359
  17.1 0.0 collective-permute-done.1.edge_ref
  17.1 1.8 %shard_map.95.part_ref = f32[128,4096]{1,0:T(8,128)S(1)} custom-call(s32[1]{0:T(128)} %bitcast.side_ref, bf16[40,4096]{1,0:T(8,128)(2,1)S(1)} %collective-permute-done.1.edge_ref, bf16[256,1024]{1,0:T(8,128)(2,1)S(1)} %get-tuple-element.18.refs_0_.column_ref, bf16[256,128]{1,0:T(8,128)(2,1)S(1)} %get-tuple-element.22.row_ref, f32[128,4096]{1,0:T(8,128)S(1)} %own_rows.1.part_ref), custom_call_target="tpu_custom_call" | custom-call | tf_op jit(solution)/shard_map/pallas_call | solution.py:408
  18.9 3.9 %collective-permute-done.edge_ref = bf16[40,4096]{1,0:T(8,128)(2,1)S(1)} collective-permute-done((bf16[40,4096]{1,0:T(8,128)(2,1)S(1)}, bf16[40,4096]{1,0:T(8,128)(2,1)S(1)}, u32[]{:S(2)}, u32[]{:S(2)}) %collective-permute-start) | collective-permute-done | bytes 327712 | tf_op jit(solution)/shard_map/ppermute | solution.py:593
  22.7 1.0 %shard_map.97 = bf16[128,2048]{1,0:T(8,128)(2,1)S(1)} custom-call(s32[1]{0:T(128)S(6)} %sub.3.side_ref, bf16[40,4096]{1,0:T(8,128)(2,1)S(1)} %collective-permute-done.edge_ref, bf16[256,1024]{1,0:T(8,128)(2,1)S(1)} %get-tuple-element.18.refs_0_.column_ref, bf16[256,128]{1,0:T(8,128)(2,1)S(1)} %get-tuple-element.20.row_ref, f32[128,4096]{1,0:T(8,128)S(1)} %shard_map.95.part_ref), custom_call_target="tpu_custom_call" | custom-call | tf_op jit(solution)/shard_map/pallas_call | solution.py:408
  23.7 0.1 collective-permute-start.2
  23.8 1.0 %shard_map.96.refs_0_.own_ref = bf16[128,2048]{1,0:T(8,128)(2,1)S(1)} custom-call(s32[1]{0:T(128)} %bitcast.side_ref, bf16[40,4096]{1,0:T(8,128)(2,1)S(1)} %collective-permute-done.edge_ref, bf16[256,1024]{1,0:T(8,128)(2,1)S(1)} %get-tuple-element.18.refs_0_.column_ref, bf16[256,128]{1,0:T(8,128)(2,1)S(1)} %get-tuple-element.20.row_ref, ...), custom_call_target="tpu_custom_call" | custom-call | tf_op jit(solution)/shard_map/pallas_call | solution.py:408
  24.8 0.0 collective-permute-done.3.refs_1_
  24.8 0.4 norms.1
  25.1 0.5 %collective-permute-done.2.refs_1_.other_ref = bf16[128,2048]{1,0:T(8,128)(2,1)S(1)} collective-permute-done((bf16[128,2048]{1,0:T(8,128)(2,1)S(1)}, bf16[128,2048]{1,0:T(8,128)(2,1)S(1)}, u32[]{:S(2)}, u32[]{:S(2)}) %collective-permute-start.2) | collective-permute-done | bytes 524320 | tf_op jit(solution)/shard_map/ppermute | solution.py:598
  25.7 1.0 %residual.1 = (f32[256,2048]{1,0:T(8,128)S(1)}, f32[2,8,128]{2,1,0:T(8,128)S(1)}) custom-call(s32[1]{0:T(128)} %bitcast.side_ref, bf16[128,2048]{1,0:T(8,128)(2,1)S(1)} %shard_map.96.refs_0_.own_ref, bf16[128,2048]{1,0:T(8,128)(2,1)S(1)} %collective-permute-done.2.refs_1_.other_ref, f32[256,2048]{1,0:T(8,128)S(1)} %get-tuple-element.27.refs_2_, ...), custom_call_target="tpu_custom_call" | custom-call | tf_op jit(solution)/shard_map/residual/pallas_call | solution.py:518
  26.7 0.2 collective-permute-start.4
  26.9 1.0 %collective-permute-done.4 = f32[2,8,128]{2,1,0:T(8,128)S(1)} collective-permute-done((f32[2,8,128]{2,1,0:T(8,128)S(1)}, f32[2,8,128]{2,1,0:T(8,128)S(1)}, u32[]{:S(2)}, u32[]{:S(2)}) %collective-permute-start.4) | collective-permute-done | bytes 8224 | tf_op jit(solution)/shard_map/ppermute | solution.py:602
  27.9 2.2 %collective-permute-start.5 = (f32[2,8,128]{2,1,0:T(8,128)S(1)}, f32[2,8,128]{2,1,0:T(8,128)S(1)}, u32[]{:S(2)}, u32[]{:S(2)}) collective-permute-start(f32[2,8,128]{2,1,0:T(8,128)S(1)} %add.12), channel_id=1, source_target_pairs={{0,3},{1,2},{2,1},{3,0},{4,7},{5,6},{6,5},{7,4},{8,11},{9,10},{10,... | collective-permute-start | bytes 24584 | tf_op jit(solution)/shard_map/ppermute | solution.py:608
  30.1 1.4 %collective-permute-done.5 = f32[2,8,128]{2,1,0:T(8,128)S(1)} collective-permute-done((f32[2,8,128]{2,1,0:T(8,128)S(1)}, f32[2,8,128]{2,1,0:T(8,128)S(1)}, u32[]{:S(2)}, u32[]{:S(2)}) %collective-permute-start.5) | collective-permute-done | bytes 8224 | tf_op jit(solution)/shard_map/ppermute | solution.py:608
  31.5 1.6 %collective-permute-start.6 = (f32[2,8,128]{2,1,0:T(8,128)S(1)}, f32[2,8,128]{2,1,0:T(8,128)S(1)}, u32[]{:S(2)}, u32[]{:S(2)}) collective-permute-start(f32[2,8,128]{2,1,0:T(8,128)S(1)} %add.13), channel_id=1, source_target_pairs={{0,4},{2,6},{4,0},{6,2},{8,12},{10,14},{12,8},{14,10},{1,5},{3,7},... | collective-permute-start | bytes 24584 | tf_op jit(solution)/shard_map/ppermute | solution.py:610
  33.0 2.1 %collective-permute-done.6 = f32[2,8,128]{2,1,0:T(8,128)S(1)} collective-permute-done((f32[2,8,128]{2,1,0:T(8,128)S(1)}, f32[2,8,128]{2,1,0:T(8,128)S(1)}, u32[]{:S(2)}, u32[]{:S(2)}) %collective-permute-start.6) | collective-permute-done | bytes 8224 | tf_op jit(solution)/shard_map/ppermute | solution.py:610
  35.1 2.6 %collective-permute-start.7 = (f32[2,8,128]{2,1,0:T(8,128)S(1)}, f32[2,8,128]{2,1,0:T(8,128)S(1)}, u32[]{:S(2)}, u32[]{:S(2)}) collective-permute-start(f32[2,8,128]{2,1,0:T(8,128)S(1)} %add.14), channel_id=1, source_target_pairs={{0,8},{2,10},{4,12},{6,14},{8,0},{10,2},{12,4},{14,6},{1,9},{3,11}... | collective-permute-start | bytes 24584 | tf_op jit(solution)/shard_map/ppermute | solution.py:610
  37.7 2.0 %collective-permute-done.7 = f32[2,8,128]{2,1,0:T(8,128)S(1)} collective-permute-done((f32[2,8,128]{2,1,0:T(8,128)S(1)}, f32[2,8,128]{2,1,0:T(8,128)S(1)}, u32[]{:S(2)}, u32[]{:S(2)}) %collective-permute-start.7) | collective-permute-done | bytes 8224 | tf_op jit(solution)/shard_map/ppermute | solution.py:610
  39.7 1.7 %final.1 = (f32[32,2048]{1,0:T(8,128)}, f32[4]{0:T(128)}) custom-call(s32[1]{0:T(128)} %bitcast.side_ref, f32[2,8,128]{2,1,0:T(8,128)S(1)} %add.15.sums_ref, bf16[128,2048]{1,0:T(8,128)(2,1)S(1)} %shard_map.96.refs_0_.own_ref, bf16[128,2048]{1,0:T(8,128)(2,1)S(1)} %collective-permute-done.2.refs_1_.other_ref, f32[256,2048]{1,0:T(8,128)S(1)} %get-tuple-element.31.factor_ref), custom_call_target="tpu_custom_call" | custom-call | tf_op jit(solution)/shard_map/final/pallas_call | solution.py:562
  (4 shorter events, 0.0 us)
Async XLA Ops:
  0.6 8.1 %copy-start.3 = (s32[4]{0:T(128)S(1)}, s32[4]{0:T(128)}, u32[]{:S(2)}) copy-start(s32[4]{0:T(128)} %index_ref.1) | copy-start | bytes 52
  0.6 8.1 %copy-start = (f32[16,8]{0,1:T(8,128)S(1)}, f32[16,8]{0,1:T(8,128)}, u32[]{:S(2)}) copy-start(f32[16,8]{0,1:T(8,128)} %param.13) | copy-start | bytes 1540
  0.7 8.1 %copy-start.1 = (bf16[8,21]{1,0:T(8,128)(2,1)S(1)}, bf16[8,21]{1,0:T(8,128)(2,1)}, u32[]{:S(2)}) copy-start(bf16[8,21]{1,0:T(8,128)(2,1)} %row_ref.1) | copy-start | bytes 1012
  0.7 8.1 %copy-start.2 = (bf16[8,21]{1,0:T(8,128)(2,1)S(1)}, bf16[8,21]{1,0:T(8,128)(2,1)}, u32[]{:S(2)}) copy-start(bf16[8,21]{1,0:T(8,128)(2,1)} %col_ref.1) | copy-start | bytes 1012
  2.1 15.0 %collective-permute-start.1 = (bf16[40,4096]{1,0:T(8,128)(2,1)S(1)}, bf16[40,4096]{1,0:T(8,128)(2,1)S(1)}, u32[]{:S(2)}, u32[]{:S(2)}) collective-permute-start(bf16[40,4096]{1,0:T(8,128)(2,1)S(1)} %get-tuple-element.21), channel_id=1, source_target_pairs={{0,2},{2,4},{4,6},{6,8},{8,10},{10,12},{12,14},{1,3},{3,5},{5,7},{... | collective-permute-start | bytes 983048 | tf_op jit(solution)/shard_map/ppermute | solution.py:586
  11.7 11.0 %collective-permute-start = (bf16[40,4096]{1,0:T(8,128)(2,1)S(1)}, bf16[40,4096]{1,0:T(8,128)(2,1)S(1)}, u32[]{:S(2)}, u32[]{:S(2)}) collective-permute-start(bf16[40,4096]{1,0:T(8,128)(2,1)S(1)} %get-tuple-element.19), channel_id=1, source_target_pairs={{2,0},{4,2},{6,4},{8,6},{10,8},{12,10},{14,12},{3,1},{5,3},{7,5},{... | collective-permute-start | bytes 983048 | tf_op jit(solution)/shard_map/ppermute | solution.py:593
  13.0 11.8 %collective-permute-start.3 = (bf16[144,2048]{1,0:T(8,128)(2,1)S(1)}, bf16[144,2048]{1,0:T(8,128)(2,1)S(1)}, u32[]{:S(2)}, u32[]{:S(2)}) collective-permute-start(bf16[144,2048]{1,0:T(8,128)(2,1)S(1)} %get-tuple-element.26), channel_id=1, source_target_pairs={{0,1},{1,0},{2,3},{3,2},{4,5},{5,4},{6,7},{7,6},{8,9},{9,8},{10,11... | collective-permute-start | bytes 1769480 | tf_op jit(solution)/shard_map/ppermute | solution.py:588
  23.7 2.0 %collective-permute-start.2 = (bf16[128,2048]{1,0:T(8,128)(2,1)S(1)}, bf16[128,2048]{1,0:T(8,128)(2,1)S(1)}, u32[]{:S(2)}, u32[]{:S(2)}) collective-permute-start(bf16[128,2048]{1,0:T(8,128)(2,1)S(1)} %shard_map.97), channel_id=1, source_target_pairs={{0,1},{1,0},{2,3},{3,2},{4,5},{5,4},{6,7},{7,6},{8,9},{9,8},{10,11... | collective-permute-start | bytes 1572872 | tf_op jit(solution)/shard_map/ppermute | solution.py:598
  26.7 1.2 %collective-permute-start.4 = (f32[2,8,128]{2,1,0:T(8,128)S(1)}, f32[2,8,128]{2,1,0:T(8,128)S(1)}, u32[]{:S(2)}, u32[]{:S(2)}) collective-permute-start(f32[2,8,128]{2,1,0:T(8,128)S(1)} %get-tuple-element.30), channel_id=1, source_target_pairs={{0,1},{1,0},{2,3},{3,2},{4,5},{5,4},{6,7},{7,6},{8,9},{9,8},{10,11... | collective-permute-start | bytes 24584 | tf_op jit(solution)/shard_map/ppermute | solution.py:602
  27.9 3.6 %collective-permute-start.5 = (f32[2,8,128]{2,1,0:T(8,128)S(1)}, f32[2,8,128]{2,1,0:T(8,128)S(1)}, u32[]{:S(2)}, u32[]{:S(2)}) collective-permute-start(f32[2,8,128]{2,1,0:T(8,128)S(1)} %add.12), channel_id=1, source_target_pairs={{0,3},{1,2},{2,1},{3,0},{4,7},{5,6},{6,5},{7,4},{8,11},{9,10},{10,... | collective-permute-start | bytes 24584 | tf_op jit(solution)/shard_map/ppermute | solution.py:608
  31.5 3.7 %collective-permute-start.6 = (f32[2,8,128]{2,1,0:T(8,128)S(1)}, f32[2,8,128]{2,1,0:T(8,128)S(1)}, u32[]{:S(2)}, u32[]{:S(2)}) collective-permute-start(f32[2,8,128]{2,1,0:T(8,128)S(1)} %add.13), channel_id=1, source_target_pairs={{0,4},{2,6},{4,0},{6,2},{8,12},{10,14},{12,8},{14,10},{1,5},{3,7},... | collective-permute-start | bytes 24584 | tf_op jit(solution)/shard_map/ppermute | solution.py:610
  35.1 4.5 %collective-permute-start.7 = (f32[2,8,128]{2,1,0:T(8,128)S(1)}, f32[2,8,128]{2,1,0:T(8,128)S(1)}, u32[]{:S(2)}, u32[]{:S(2)}) collective-permute-start(f32[2,8,128]{2,1,0:T(8,128)S(1)} %add.14), channel_id=1, source_target_pairs={{0,8},{2,10},{4,12},{6,14},{8,0},{10,2},{12,4},{14,6},{1,9},{3,11}... | collective-permute-start | bytes 24584 | tf_op jit(solution)/shard_map/ppermute | solution.py:610

commit v8 on v7

--- a/solution.py
+++ b/solution.py
@@ -190,7 +190,7 @@
     return segments, main + visits * rest
 
 
-def table_kernel(visits, rows, half, index_ref, table_ref, row_ref, col_ref, after_ref, column_out, own_out, above_out, below_out):
+def table_kernel(visits, rows, half, index_ref, table_ref, row_ref, col_ref, column_out, own_out, above_out, below_out):
     bases, taps = row_ref.shape
     window = 2 * LANES
 
@@ -248,7 +248,7 @@
         assemble(out, high, segments)
 
 
-def tables(psf_index, psf_table, row_basis, col_basis, visits, rows, after):
+def tables(psf_index, psf_table, row_basis, col_basis, visits, rows):
     bases, taps = row_basis.shape
     half = taps // 2
     rim = (2 * visits * rows, bases * edge_segments(visits, rows, half, 0)[1])
@@ -260,11 +260,11 @@
             held(rim, BF16),
             held(rim, BF16),
         ),
-        in_specs=[whole(pltpu.SMEM)] * 2 + [whole()] * 2 + [pl.BlockSpec(memory_space=pl.ANY)],
+        in_specs=[whole(pltpu.SMEM)] * 2 + [whole()] * 2,
         out_specs=(whole(),) * 4,
         compiler_params=LIMIT,
         name="tables",
-    )(psf_index, psf_table.T, row_basis, col_basis, after)
+    )(psf_index, psf_table.T, row_basis, col_basis)
 
 
 BLOCKS = 4
@@ -526,7 +526,7 @@
     )(side, *kept(*values, weights, inverse, counts))
 
 
-def final_kernel(visits, side_ref, sums_ref, own_ref, other_ref, factor_ref, out_ref, chi_ref, done, sent):
+def final_kernel(visits, side_ref, sums_ref, own_ref, other_ref, factor_ref, out_ref, chi_ref, done, mean, sent):
     rows, width = done.shape
     high = min(16, rows)
     sums = [
@@ -536,7 +536,9 @@
     chi = jnp.sum(sums[0], axis=1, keepdims=True) / jnp.sum(sums[1], axis=1, keepdims=True)
     scale = CLIP_LEVEL / (CHI_OFFSET + chi)
     for v in range(visits):
-        chi_ref[v] = chi[v, 0]
+        mean[v] = chi[v, 0]
+    chi_copy = pltpu.make_async_copy(mean, chi_ref, sent.at[1])
+    chi_copy.start()
     scales = [jnp.broadcast_to(scale[m : m + 1], (high, LANES)) for m in range(2 * visits)]
     for lane in range(0, width, LANES):
         lanes = slice(lane, lane + LANES)
@@ -551,8 +553,9 @@
                 numer = revised * value if numer is None else numer + revised * value
                 denom = revised if denom is None else denom + revised
             done[row : row + high, lanes] = numer / (denom + PRIOR_WEIGHT)
-    copy = pltpu.make_async_copy(done, out_ref, sent)
+    copy = pltpu.make_async_copy(done, out_ref, sent.at[0])
     copy.start()
+    chi_copy.wait()
     copy.wait()
 
 
@@ -566,8 +569,12 @@
             jax.ShapeDtypeStruct((visits,), F32),
         ),
         in_specs=[whole(pltpu.SMEM)] + [whole()] * 4,
-        out_specs=(pl.BlockSpec(memory_space=pl.ANY), whole(pltpu.SMEM)),
-        scratch_shapes=[pltpu.VMEM((rows, width), F32), pltpu.SemaphoreType.DMA(())],
+        out_specs=(pl.BlockSpec(memory_space=pl.ANY),) * 2,
+        scratch_shapes=[
+            pltpu.VMEM((rows, width), F32),
+            pltpu.SMEM((visits,), F32),
+            pltpu.SemaphoreType.DMA((2,)),
+        ],
         compiler_params=LIMIT,
         name="final",
     )(side, *kept(sums, *values, factors))
@@ -586,10 +593,8 @@
     before = lax.ppermute(last, "sky", up)
     send_weight, own_weight = pixel_weights(badbits, coverage, variance, side)
     other_weight = lax.ppermute(send_weight, "visit", swap)
-    column, own, above, below = tables(
-        psf_index, psf_table, row_basis, col_basis, visits, rows, own_weight
-    )
-    leading, upper = pack_rows(warps, half, True, column)
+    column, own, above, below = tables(psf_index, psf_table, row_basis, col_basis, visits, rows)
+    leading, upper = pack_rows(warps, half, True, send_weight)
     after = lax.ppermute(leading, "sky", down)
     part = own_part(upper.reshape(-1, columns), lower.reshape(-1, columns), column, own, visits)
     part = rim_part(side, before, column, above, part, visits, half, columns, F32)
@@ -602,13 +607,8 @@
     sums = sums + lax.ppermute(sums, "visit", swap)
     step = 1
     while step < strips:
-        pairs = [(i, i ^ step) for i in range(strips)]
-        if step == 1:
-            pairs = [(2 * i + v, 2 * j + 1 - v) for i, j in pairs for v in (0, 1)]
-            theirs = lax.ppermute(sums, ("sky", "visit"), pairs)
-        else:
-            theirs = lax.ppermute(sums, "sky", pairs)
-        sums = sums + theirs
+        pairs = [(2 * i + v, 2 * (i ^ step) + 1 - v) for i in range(strips) for v in (0, 1)]
+        sums = sums + lax.ppermute(sums, ("sky", "visit"), pairs)
         step *= 2
     return final_pass(side, sums, values, factors, visits)
 

time: 41.6 us -> 39.5 us (0.950)
  waiting for transfers between devices: 10.8 us -> 8.05 us
  starting transfers between devices: 12.9 us -> 14.1 us
  Pallas kernels: 16.8 us -> 16.2 us
    ppermute x1, waiting for transfers between devices: 3.85 us -> 2.39 us  [per_device(): after = lax.ppermute(leading, 'sky', down)]
    ppermute x3, waiting for transfers between devices: 5.39 us -> 4.1 us  [per_device(): sums = sums + lax.ppermute(sums, ('sky', 'visit'), pairs)]
    ppermute x3, starting transfers between devices: 6.36 us -> 7.4 us  [per_device(): sums = sums + lax.ppermute(sums, ('sky', 'visit'), pairs)]
    pallas_call x1, Pallas kernels: 1.69 us -> 1.2 us  [final_pass(): pl.pallas_call(functools.partial(final_kernel, visits), out_shape=(jax.Sh...]
  transfers between devices with their start and end apart: 8 -> 8, of which waited for: 6 -> 6; matrix products, arithmetic and copies ran while one was open for 0% -> 0% of each run, Pallas kernels for 31% -> 32%
where the time goes in v8:
time: 39.5 us; the launch traced here: 39.2 us
  Pallas kernels  16.2 us (41%)
  starting transfers between devices  14.1 us (36%)
  waiting for transfers between devices  8.05 us (20%)
  between operations  0.8 us (2%)
    ppermute x3, starting transfers between devices, per_device(): sums = sums + lax.ppermute(sums, ('sky', 'visit'), pairs)  7.4 us
    ppermute x1, starting transfers between devices, per_device(): before = lax.ppermute(last, 'sky', up)  5.05 us
    ppermute x3, waiting for transfers between devices, per_device(): sums = sums + lax.ppermute(sums, ('sky', 'visit'), pairs)  4.1 us
    pallas_call x1, Pallas kernels, own_part(): pl.pallas_call(functools.partial(own_kernel, visits), out_shape=held((2 *...  3.99 us
    pallas_call x3, Pallas kernels, rim_part(): pl.pallas_call(functools.partial(rim_kernel, visits, half), out_shape=hel...  3.7 us
    pallas_call x2, Pallas kernels, pack_rows(): pl.pallas_call(functools.partial(pack_kernel, half, first, skip), out_sha...  2.75 us
    ppermute x1, waiting for transfers between devices, per_device(): after = lax.ppermute(leading, 'sky', down)  2.39 us
    pallas_call x1, Pallas kernels, pixel_weights(): pl.pallas_call(functools.partial(weight_kernel, visits, bands), out_shape...  1.74 us
  transfers between devices with their start and end apart: 8, of which 6 were waited for; matrix products, arithmetic and copies ran while one was open for 0% of the time, Pallas kernels for 32%

profile of v8, /device:TPU:0, one launch (start us, length us, event | category | flops | bytes accessed | tf_op | source)
XLA Modules:
  0.0 39.2 jit_solution(13924513420788005820)
XLA Ops:
  0.6 1.4 %pack_lower.1 = (bf16[40,4096]{1,0:T(8,128)(2,1)S(1)}, bf16[4,16,4096]{2,1,0:T(8,128)(2,1)S(1)}) custom-call(bf16[4,32,4096]{2,1,0:T(8,128)(2,1)} %x_ref.3), custom_call_target="tpu_custom_call" | custom-call | tf_op jit(solution)/shard_map/pack_lower/pallas_call | solution.py:98
  2.0 0.0 copy-start
  2.0 0.0 copy-start.1
  2.0 0.0 copy-start.2
  2.0 0.0 copy-start.3
  2.1 5.1 %collective-permute-start.1 = (bf16[40,4096]{1,0:T(8,128)(2,1)S(1)}, bf16[40,4096]{1,0:T(8,128)(2,1)S(1)}, u32[]{:S(2)}, u32[]{:S(2)}) collective-permute-start(bf16[40,4096]{1,0:T(8,128)(2,1)S(1)} %get-tuple-element.21), channel_id=1, source_target_pairs={{0,2},{2,4},{4,6},{6,8},{8,10},{10,12},{12,14},{1,3},{3,5},{5,7},{... | collective-permute-start | bytes 983048 | tf_op jit(solution)/shard_map/ppermute | solution.py:593
  7.1 1.7 %weights.1 = (bf16[144,2048]{1,0:T(8,128)(2,1)S(1)}, bf16[144,2048]{1,0:T(8,128)(2,1)S(1)}) custom-call(s32[1]{0:T(128)} %bitcast.side_ref, s32[1,4]{1,0:T(1,128)} %bitcast.11, f32[1,4]{1,0:T(1,128)} %bitcast.12, s32[128,4096]{1,0:T(8,128)} %bitcast.10), custom_call_target="tpu_custom_call" | custom-call | tf_op jit(solution)/shard_map/weights/pallas_call | solution.py:159
  8.9 1.4 %pack_upper.1 = (bf16[40,4096]{1,0:T(8,128)(2,1)S(1)}, bf16[4,16,4096]{2,1,0:T(8,128)(2,1)S(1)}) custom-call(bf16[4,32,4096]{2,1,0:T(8,128)(2,1)} %x_ref.3, bf16[144,2048]{1,0:T(8,128)(2,1)S(1)} %get-tuple-element.17.refs_0_), custom_call_target="tpu_custom_call" | custom-call | tf_op jit(solution)/shard_map/pack_upper/pallas_call | solution.py:98
  10.3 1.3 %collective-permute-start = (bf16[40,4096]{1,0:T(8,128)(2,1)S(1)}, bf16[40,4096]{1,0:T(8,128)(2,1)S(1)}, u32[]{:S(2)}, u32[]{:S(2)}) collective-permute-start(bf16[40,4096]{1,0:T(8,128)(2,1)S(1)} %get-tuple-element.18), channel_id=1, source_target_pairs={{2,0},{4,2},{6,4},{8,6},{10,8},{12,10},{14,12},{3,1},{5,3},{7,5},{... | collective-permute-start | bytes 983048 | tf_op jit(solution)/shard_map/ppermute | solution.py:598
  11.6 0.1 collective-permute-start.3
  11.6 0.0 copy-done
  11.7 0.0 copy-done.1
  11.7 0.0 copy-done.2
  11.7 0.0 copy-done.3
  11.7 1.5 %tables.1 = (bf16[256,1024]{1,0:T(8,128)(2,1)S(1)}, bf16[256,256]{1,0:T(8,128)(2,1)S(1)}, bf16[256,128]{1,0:T(8,128)(2,1)S(1)}, bf16[256,128]{1,0:T(8,128)(2,1)S(1)}) custom-call(s32[4]{0:T(128)S(1)} %copy-done.3, f32[8,16]{1,0:T(8,128)S(1)} %bitcast.9, bf16[8,21]{1,0:T(8,128)(2,1)S(1)} %copy-done.1, bf16[8,21]{1,0:T(8,128)(2,1)S(1)} %copy-done.2), custom_call_target="tpu_custom_call" | custom-call | tf_op jit(solution)/shard_map/tables/pallas_call | solution.py:255
  13.2 4.0 %own_rows.1.part_ref = f32[128,4096]{1,0:T(8,128)S(1)} custom-call(bf16[64,4096]{1,0:T(8,128)(2,1)S(1)} %bitcast.8, bf16[64,4096]{1,0:T(8,128)(2,1)S(1)} %bitcast.7, bf16[256,1024]{1,0:T(8,128)(2,1)S(1)} %get-tuple-element.19.column_ref, bf16[256,256]{1,0:T(8,128)(2,1)S(1)} %get-tuple-element.25.row_ref), custom_call_target="tpu_custom_call" | custom-call | flops 1000000000 | bytes 10000000 | tf_op jit(solution)/shard_map/own_rows/pallas_call | solution.py:359
  17.2 0.0 collective-permute-done.1.edge_ref
  17.2 1.8 %shard_map.95.part_ref = f32[128,4096]{1,0:T(8,128)S(1)} custom-call(s32[1]{0:T(128)} %bitcast.side_ref, bf16[40,4096]{1,0:T(8,128)(2,1)S(1)} %collective-permute-done.1.edge_ref, bf16[256,1024]{1,0:T(8,128)(2,1)S(1)} %get-tuple-element.19.column_ref, bf16[256,128]{1,0:T(8,128)(2,1)S(1)} %get-tuple-element.22.row_ref, f32[128,4096]{1,0:T(8,128)S(1)} %own_rows.1.part_ref), custom_call_target="tpu_custom_call" | custom-call | tf_op jit(solution)/shard_map/pallas_call | solution.py:408
  18.9 2.4 %collective-permute-done.edge_ref = bf16[40,4096]{1,0:T(8,128)(2,1)S(1)} collective-permute-done((bf16[40,4096]{1,0:T(8,128)(2,1)S(1)}, bf16[40,4096]{1,0:T(8,128)(2,1)S(1)}, u32[]{:S(2)}, u32[]{:S(2)}) %collective-permute-start) | collective-permute-done | bytes 327712 | tf_op jit(solution)/shard_map/ppermute | solution.py:598
  21.3 1.0 %shard_map.97 = bf16[128,2048]{1,0:T(8,128)(2,1)S(1)} custom-call(s32[1]{0:T(128)S(6)} %sub.3.side_ref, bf16[40,4096]{1,0:T(8,128)(2,1)S(1)} %collective-permute-done.edge_ref, bf16[256,1024]{1,0:T(8,128)(2,1)S(1)} %get-tuple-element.19.column_ref, bf16[256,128]{1,0:T(8,128)(2,1)S(1)} %get-tuple-element.20.row_ref, f32[128,4096]{1,0:T(8,128)S(1)} %shard_map.95.part_ref), custom_call_target="tpu_custom_call" | custom-call | tf_op jit(solution)/shard_map/pallas_call | solution.py:408
  22.3 0.1 collective-permute-start.2
  22.4 1.0 %shard_map.96.refs_0_.own_ref = bf16[128,2048]{1,0:T(8,128)(2,1)S(1)} custom-call(s32[1]{0:T(128)} %bitcast.side_ref, bf16[40,4096]{1,0:T(8,128)(2,1)S(1)} %collective-permute-done.edge_ref, bf16[256,1024]{1,0:T(8,128)(2,1)S(1)} %get-tuple-element.19.column_ref, bf16[256,128]{1,0:T(8,128)(2,1)S(1)} %get-tuple-element.20.row_ref, ...), custom_call_target="tpu_custom_call" | custom-call | tf_op jit(solution)/shard_map/pallas_call | solution.py:408
  23.3 0.0 collective-permute-done.3.refs_1_
  23.4 0.4 norms.1
  23.7 0.5 %collective-permute-done.2.refs_1_.other_ref = bf16[128,2048]{1,0:T(8,128)(2,1)S(1)} collective-permute-done((bf16[128,2048]{1,0:T(8,128)(2,1)S(1)}, bf16[128,2048]{1,0:T(8,128)(2,1)S(1)}, u32[]{:S(2)}, u32[]{:S(2)}) %collective-permute-start.2) | collective-permute-done | bytes 524320 | tf_op jit(solution)/shard_map/ppermute | solution.py:603
  24.3 1.0 %residual.1 = (f32[256,2048]{1,0:T(8,128)S(1)}, f32[2,8,128]{2,1,0:T(8,128)S(1)}) custom-call(s32[1]{0:T(128)} %bitcast.side_ref, bf16[128,2048]{1,0:T(8,128)(2,1)S(1)} %shard_map.96.refs_0_.own_ref, bf16[128,2048]{1,0:T(8,128)(2,1)S(1)} %collective-permute-done.2.refs_1_.other_ref, f32[256,2048]{1,0:T(8,128)S(1)} %get-tuple-element.27.refs_2_, ...), custom_call_target="tpu_custom_call" | custom-call | tf_op jit(solution)/shard_map/residual/pallas_call | solution.py:518
  25.3 0.2 collective-permute-start.4
  25.5 1.0 %collective-permute-done.4 = f32[2,8,128]{2,1,0:T(8,128)S(1)} collective-permute-done((f32[2,8,128]{2,1,0:T(8,128)S(1)}, f32[2,8,128]{2,1,0:T(8,128)S(1)}, u32[]{:S(2)}, u32[]{:S(2)}) %collective-permute-start.4) | collective-permute-done | bytes 8224 | tf_op jit(solution)/shard_map/ppermute | solution.py:607
  26.5 2.2 %collective-permute-start.5 = (f32[2,8,128]{2,1,0:T(8,128)S(1)}, f32[2,8,128]{2,1,0:T(8,128)S(1)}, u32[]{:S(2)}, u32[]{:S(2)}) collective-permute-start(f32[2,8,128]{2,1,0:T(8,128)S(1)} %add.12), channel_id=1, source_target_pairs={{0,3},{1,2},{2,1},{3,0},{4,7},{5,6},{6,5},{7,4},{8,11},{9,10},{10,... | collective-permute-start | bytes 24584 | tf_op jit(solution)/shard_map/ppermute | solution.py:611
  28.7 1.4 %collective-permute-done.5 = f32[2,8,128]{2,1,0:T(8,128)S(1)} collective-permute-done((f32[2,8,128]{2,1,0:T(8,128)S(1)}, f32[2,8,128]{2,1,0:T(8,128)S(1)}, u32[]{:S(2)}, u32[]{:S(2)}) %collective-permute-start.5) | collective-permute-done | bytes 8224 | tf_op jit(solution)/shard_map/ppermute | solution.py:611
  30.0 2.5 %collective-permute-start.6 = (f32[2,8,128]{2,1,0:T(8,128)S(1)}, f32[2,8,128]{2,1,0:T(8,128)S(1)}, u32[]{:S(2)}, u32[]{:S(2)}) collective-permute-start(f32[2,8,128]{2,1,0:T(8,128)S(1)} %add.13), channel_id=1, source_target_pairs={{0,5},{1,4},{2,7},{3,6},{4,1},{5,0},{6,3},{7,2},{8,13},{9,12},{10,... | collective-permute-start | bytes 24584 | tf_op jit(solution)/shard_map/ppermute | solution.py:611
  32.5 1.4 %collective-permute-done.6 = f32[2,8,128]{2,1,0:T(8,128)S(1)} collective-permute-done((f32[2,8,128]{2,1,0:T(8,128)S(1)}, f32[2,8,128]{2,1,0:T(8,128)S(1)}, u32[]{:S(2)}, u32[]{:S(2)}) %collective-permute-start.6) | collective-permute-done | bytes 8224 | tf_op jit(solution)/shard_map/ppermute | solution.py:611
  33.9 2.7 %collective-permute-start.7 = (f32[2,8,128]{2,1,0:T(8,128)S(1)}, f32[2,8,128]{2,1,0:T(8,128)S(1)}, u32[]{:S(2)}, u32[]{:S(2)}) collective-permute-start(f32[2,8,128]{2,1,0:T(8,128)S(1)} %add.14), channel_id=1, source_target_pairs={{0,9},{1,8},{2,11},{3,10},{4,13},{5,12},{6,15},{7,14},{8,1},{9,0},... | collective-permute-start | bytes 24584 | tf_op jit(solution)/shard_map/ppermute | solution.py:611
  36.6 1.4 %collective-permute-done.7 = f32[2,8,128]{2,1,0:T(8,128)S(1)} collective-permute-done((f32[2,8,128]{2,1,0:T(8,128)S(1)}, f32[2,8,128]{2,1,0:T(8,128)S(1)}, u32[]{:S(2)}, u32[]{:S(2)}) %collective-permute-start.7) | collective-permute-done | bytes 8224 | tf_op jit(solution)/shard_map/ppermute | solution.py:611
  38.0 1.2 %final.1 = (f32[32,2048]{1,0:T(8,128)}, f32[4]{0:T(128)}) custom-call(s32[1]{0:T(128)} %bitcast.side_ref, f32[2,8,128]{2,1,0:T(8,128)S(1)} %add.15.sums_ref, bf16[128,2048]{1,0:T(8,128)(2,1)S(1)} %shard_map.96.refs_0_.own_ref, bf16[128,2048]{1,0:T(8,128)(2,1)S(1)} %collective-permute-done.2.refs_1_.other_ref, f32[256,2048]{1,0:T(8,128)S(1)} %get-tuple-element.31.factor_ref), custom_call_target="tpu_custom_call" | custom-call | tf_op jit(solution)/shard_map/final/pallas_call | solution.py:565
  (4 shorter events, 0.0 us)
Async XLA Ops:
  2.0 9.6 %copy-start = (f32[16,8]{0,1:T(8,128)S(1)}, f32[16,8]{0,1:T(8,128)}, u32[]{:S(2)}) copy-start(f32[16,8]{0,1:T(8,128)} %param.13) | copy-start | bytes 1540
  2.0 9.6 %copy-start.1 = (bf16[8,21]{1,0:T(8,128)(2,1)S(1)}, bf16[8,21]{1,0:T(8,128)(2,1)}, u32[]{:S(2)}) copy-start(bf16[8,21]{1,0:T(8,128)(2,1)} %row_ref.1) | copy-start | bytes 1012
  2.0 9.6 %copy-start.2 = (bf16[8,21]{1,0:T(8,128)(2,1)S(1)}, bf16[8,21]{1,0:T(8,128)(2,1)}, u32[]{:S(2)}) copy-start(bf16[8,21]{1,0:T(8,128)(2,1)} %col_ref.1) | copy-start | bytes 1012
  2.0 9.6 %copy-start.3 = (s32[4]{0:T(128)S(1)}, s32[4]{0:T(128)}, u32[]{:S(2)}) copy-start(s32[4]{0:T(128)} %index_ref.1) | copy-start | bytes 52
  2.1 15.1 %collective-permute-start.1 = (bf16[40,4096]{1,0:T(8,128)(2,1)S(1)}, bf16[40,4096]{1,0:T(8,128)(2,1)S(1)}, u32[]{:S(2)}, u32[]{:S(2)}) collective-permute-start(bf16[40,4096]{1,0:T(8,128)(2,1)S(1)} %get-tuple-element.21), channel_id=1, source_target_pairs={{0,2},{2,4},{4,6},{6,8},{8,10},{10,12},{12,14},{1,3},{3,5},{5,7},{... | collective-permute-start | bytes 983048 | tf_op jit(solution)/shard_map/ppermute | solution.py:593
  10.3 11.1 %collective-permute-start = (bf16[40,4096]{1,0:T(8,128)(2,1)S(1)}, bf16[40,4096]{1,0:T(8,128)(2,1)S(1)}, u32[]{:S(2)}, u32[]{:S(2)}) collective-permute-start(bf16[40,4096]{1,0:T(8,128)(2,1)S(1)} %get-tuple-element.18), channel_id=1, source_target_pairs={{2,0},{4,2},{6,4},{8,6},{10,8},{12,10},{14,12},{3,1},{5,3},{7,5},{... | collective-permute-start | bytes 983048 | tf_op jit(solution)/shard_map/ppermute | solution.py:598
  11.6 11.8 %collective-permute-start.3 = (bf16[144,2048]{1,0:T(8,128)(2,1)S(1)}, bf16[144,2048]{1,0:T(8,128)(2,1)S(1)}, u32[]{:S(2)}, u32[]{:S(2)}) collective-permute-start(bf16[144,2048]{1,0:T(8,128)(2,1)S(1)} %get-tuple-element.17.refs_0_), channel_id=1, source_target_pairs={{0,1},{1,0},{2,3},{3,2},{4,5},{5,4},{6,7},{7,6},{8,9},{9,8},{10,11... | collective-permute-start | bytes 1769480 | tf_op jit(solution)/shard_map/ppermute | solution.py:595
  22.3 2.0 %collective-permute-start.2 = (bf16[128,2048]{1,0:T(8,128)(2,1)S(1)}, bf16[128,2048]{1,0:T(8,128)(2,1)S(1)}, u32[]{:S(2)}, u32[]{:S(2)}) collective-permute-start(bf16[128,2048]{1,0:T(8,128)(2,1)S(1)} %shard_map.97), channel_id=1, source_target_pairs={{0,1},{1,0},{2,3},{3,2},{4,5},{5,4},{6,7},{7,6},{8,9},{9,8},{10,11... | collective-permute-start | bytes 1572872 | tf_op jit(solution)/shard_map/ppermute | solution.py:603
  25.3 1.2 %collective-permute-start.4 = (f32[2,8,128]{2,1,0:T(8,128)S(1)}, f32[2,8,128]{2,1,0:T(8,128)S(1)}, u32[]{:S(2)}, u32[]{:S(2)}) collective-permute-start(f32[2,8,128]{2,1,0:T(8,128)S(1)} %get-tuple-element.30), channel_id=1, source_target_pairs={{0,1},{1,0},{2,3},{3,2},{4,5},{5,4},{6,7},{7,6},{8,9},{9,8},{10,11... | collective-permute-start | bytes 24584 | tf_op jit(solution)/shard_map/ppermute | solution.py:607
  26.5 3.5 %collective-permute-start.5 = (f32[2,8,128]{2,1,0:T(8,128)S(1)}, f32[2,8,128]{2,1,0:T(8,128)S(1)}, u32[]{:S(2)}, u32[]{:S(2)}) collective-permute-start(f32[2,8,128]{2,1,0:T(8,128)S(1)} %add.12), channel_id=1, source_target_pairs={{0,3},{1,2},{2,1},{3,0},{4,7},{5,6},{6,5},{7,4},{8,11},{9,10},{10,... | collective-permute-start | bytes 24584 | tf_op jit(solution)/shard_map/ppermute | solution.py:611
  30.0 3.9 %collective-permute-start.6 = (f32[2,8,128]{2,1,0:T(8,128)S(1)}, f32[2,8,128]{2,1,0:T(8,128)S(1)}, u32[]{:S(2)}, u32[]{:S(2)}) collective-permute-start(f32[2,8,128]{2,1,0:T(8,128)S(1)} %add.13), channel_id=1, source_target_pairs={{0,5},{1,4},{2,7},{3,6},{4,1},{5,0},{6,3},{7,2},{8,13},{9,12},{10,... | collective-permute-start | bytes 24584 | tf_op jit(solution)/shard_map/ppermute | solution.py:611
  33.9 4.1 %collective-permute-start.7 = (f32[2,8,128]{2,1,0:T(8,128)S(1)}, f32[2,8,128]{2,1,0:T(8,128)S(1)}, u32[]{:S(2)}, u32[]{:S(2)}) collective-permute-start(f32[2,8,128]{2,1,0:T(8,128)S(1)} %add.14), channel_id=1, source_target_pairs={{0,9},{1,8},{2,11},{3,10},{4,13},{5,12},{6,15},{7,14},{8,1},{9,0},... | collective-permute-start | bytes 24584 | tf_op jit(solution)/shard_map/ppermute | solution.py:611

commit v9 on v8

--- a/solution.py
+++ b/solution.py
@@ -214,44 +214,46 @@
         band = jnp.where(inside, spread(line, SHIFT - half, window), 0.0)
         column_out[:, b * LANES : (b + 1) * LANES] = band.astype(BF16)
 
-    lane = lane_index((rows, LANES))
-
-    def assemble(out_ref, high, segments):
+    depth = rows // 2
+
+    def assemble(out_ref, high, segments, top, lines):
+        lane = lane_index((lines, LANES))
         for b in range(bases):
             start = b * high % LANES
             group = b * high // LANES * LANES
             line = row_lines[b : b + 1, :]
             found = {}
             for v in range(visits):
-                total = jnp.zeros((rows, LANES), F32)
+                total = jnp.zeros((lines, LANES), F32)
                 for first, last, offset in segments[v]:
                     if first == last:
                         continue
                     key = (first, last, offset)
                     if key not in found:
                         mask = (lane >= start + first) & (lane < start + last)
-                        found[key] = jnp.where(mask, spread(line, start - offset, rows), 0.0)
+                        turned = spread(line, start - offset + top, lines)
+                        found[key] = jnp.where(mask, turned, 0.0)
                     total = total + found[key]
-                top, low = split(total * table_ref[b, index_ref[v]])
-                at = 2 * v * rows
+                high_part, low_part = split(total * table_ref[b, index_ref[v]])
+                at = 2 * v * lines
                 lanes = slice(group, group + LANES)
                 if start == 0:
-                    out_ref[at : at + rows, lanes] = top
-                    out_ref[at + rows : at + 2 * rows, lanes] = low
+                    out_ref[at : at + lines, lanes] = high_part
+                    out_ref[at + lines : at + 2 * lines, lanes] = low_part
                 else:
-                    out_ref[at : at + rows, lanes] += top
-                    out_ref[at + rows : at + 2 * rows, lanes] += low
-
-    assemble(own_out, rows, [[(0, rows, half)]] * visits)
+                    out_ref[at : at + lines, lanes] += high_part
+                    out_ref[at + lines : at + 2 * lines, lanes] += low_part
+
+    assemble(own_out, rows, [[(0, rows, half)]] * visits, 0, rows)
     for below, out in enumerate((above_out, below_out)):
         segments, high = edge_segments(visits, rows, half, below)
-        assemble(out, high, segments)
+        assemble(out, high, segments, below * depth, depth)
 
 
 def tables(psf_index, psf_table, row_basis, col_basis, visits, rows):
     bases, taps = row_basis.shape
     half = taps // 2
-    rim = (2 * visits * rows, bases * edge_segments(visits, rows, half, 0)[1])
+    rim = (visits * rows, bases * edge_segments(visits, rows, half, 0)[1])
     return pl.pallas_call(
         functools.partial(table_kernel, visits, rows, half),
         out_shape=(
@@ -323,10 +325,9 @@
             put((blocks * step + first) * LANES, totals)
 
 
-def own_kernel(visits, upper_ref, lower_ref, column_ref, row_ref, out_ref, shifted):
+def own_kernel(visits, upper_ref, lower_ref, column_ref, row_ref, top_ref, bottom_ref, shifted):
     half_count, columns = upper_ref.shape
     depth = half_count // visits
-    rows = 2 * depth
     groups = columns // LANES
     low = lane_index((2 * half_count, LANES)) < SHIFT
     nothing = jnp.zeros((2 * half_count, LANES), F32)
@@ -349,7 +350,9 @@
 
     def put(start, totals):
         for v, total in enumerate(totals):
-            out_ref[v * rows : (v + 1) * rows, start : start + 2 * LANES] = total
+            lines = slice(v * depth, (v + 1) * depth)
+            top_ref[lines, start : start + 2 * LANES] = total[:depth]
+            bottom_ref[lines, start : start + 2 * LANES] = total[depth:]
 
     convolve(make_group, shifted, column_ref, row_ref, pieces, put)
 
@@ -358,9 +361,9 @@
     half_count, columns = upper.shape
     return pl.pallas_call(
         functools.partial(own_kernel, visits),
-        out_shape=held((2 * half_count, columns), F32),
+        out_shape=(held((half_count, columns), F32),) * 2,
         in_specs=[whole()] * 4,
-        out_specs=whole(),
+        out_specs=(whole(),) * 2,
         scratch_shapes=[pltpu.VMEM((2 * half_count, columns + LANES), BF16)],
         compiler_params=LIMIT,
         cost_estimate=pl.CostEstimate(flops=10**9, bytes_accessed=10**7, transcendentals=0),
@@ -374,7 +377,7 @@
     width = out_ref.shape[1]
     groups = columns // LANES
     inner = width // LANES
-    base = side_ref[0] * inner if width < columns else 0
+    base = side_ref[0] * inner
     lane = lane_index((edge, LANES))
 
     def make_group(g):
@@ -403,11 +406,12 @@
     convolve(make_group, shifted, column_ref, row_ref, pieces, put)
 
 
-def rim_part(side, edge, column, table, part, visits, half, width, dtype):
-    count = part.shape[0]
+def rim_part(side, edge, column, table, part, visits, half):
+    count, columns = part.shape
+    width = columns // 2
     return pl.pallas_call(
         functools.partial(rim_kernel, visits, half),
-        out_shape=held((count, width), dtype),
+        out_shape=held((count, width), BF16),
         in_specs=[whole(pltpu.SMEM)] + [whole()] * 4,
         out_specs=whole(),
         scratch_shapes=[pltpu.VMEM((edge.shape[0], width + LANES), BF16)],
@@ -473,36 +477,45 @@
     )(*kept(own_flags, other_flags))
 
 
-def residual_kernel(visits, side_ref, *refs):
+def residual_kernel(visits, first, last, side_ref, *refs):
     value_refs = refs[:2]
-    weight_ref, inverse_ref, count_ref, factor_ref, sums_ref, chi_ref = refs[2:]
+    weight_ref, inverse_ref = refs[2:4]
+    if last:
+        so_far_ref, count_ref, factor_ref, sums_ref, chi_ref = refs[4:]
+        chi_ref[...] = so_far_ref[...]
+    else:
+        factor_ref, chi_ref = refs[4:]
+        chi_ref[...] = jnp.zeros_like(chi_ref)
+    depth = value_refs[0].shape[0] // visits
     rows, width = inverse_ref.shape
-    high = min(16, rows)
-    chi_ref[...] = jnp.zeros_like(chi_ref)
+    high = min(16, depth)
     members = [(side, v) for side in range(2) for v in range(visits)]
 
     def body(step, carry):
         lanes = pl.ds(pl.multiple_of(step * LANES, LANES), LANES)
-        for row in range(0, rows, high):
+        for row in range(0, depth, high):
             values, weights = [], []
             numer = None
             for m, (side, v) in enumerate(members):
-                at = slice(v * rows + row, v * rows + row + high)
+                at = slice(v * depth + row, v * depth + row + high)
                 value = value_refs[side][at, lanes].astype(F32)
-                weight = weight_ref[m * rows + row : m * rows + row + high, lanes]
+                at = m * rows + first + row
+                weight = weight_ref[at : at + high, lanes]
                 values.append(value)
                 weights.append(weight)
                 numer = weight * value if numer is None else numer + weight * value
-            first = numer * inverse_ref[row : row + high, lanes]
+            mean = numer * inverse_ref[first + row : first + row + high, lanes]
             for m in range(len(members)):
-                residual = values[m] - first
+                residual = values[m] - mean
                 term = weights[m] * (residual * residual)
                 chi_ref[m * 8 : (m + 1) * 8, :] += folded(term)
-                target = slice(m * rows + row, m * rows + row + high)
+                target = slice(m * depth + row, m * depth + row + high)
                 factor_ref[target, lanes] = weights[m] / (CLIP_LEVEL + term)
         return carry
 
     lax.fori_loop(0, width // LANES, body, 0, unroll=4)
+    if not last:
+        return
     for k, ref in enumerate((chi_ref, count_ref)):
         lines = [
             jnp.sum(ref[m * 8 : (m + 1) * 8, :], axis=0, keepdims=True)
@@ -512,23 +525,30 @@
         sums_ref[k] = jnp.where(side_ref[0] == 0, total, pltpu.roll(total, visits, 0))
 
 
-def residual_pass(side, values, weights, inverse, counts, visits):
-    rows, width = inverse.shape
+def residual_pass(side, values, weights, inverse, visits, first, *ending):
+    count, width = values[0].shape
     members = 2 * visits
-    return pl.pallas_call(
-        functools.partial(residual_kernel, visits),
-        out_shape=(held((members * rows, width), F32), held((2, members, LANES), F32)),
-        in_specs=[whole(pltpu.SMEM)] + [whole()] * 5,
+    last = len(ending) > 0
+    chi = (members * 8, LANES)
+    return pl.pallas_call(
+        functools.partial(residual_kernel, visits, first, last),
+        out_shape=(
+            held((2 * count, width), F32),
+            held((2, members, LANES) if last else chi, F32),
+        ),
+        in_specs=[whole(pltpu.SMEM)] + [whole()] * (4 + len(ending)),
         out_specs=(whole(), whole()),
-        scratch_shapes=[pltpu.VMEM((members * 8, LANES), F32)],
-        compiler_params=LIMIT,
-        name="residual",
-    )(side, *kept(*values, weights, inverse, counts))
-
-
-def final_kernel(visits, side_ref, sums_ref, own_ref, other_ref, factor_ref, out_ref, chi_ref, done, mean, sent):
+        scratch_shapes=[pltpu.VMEM(chi, F32)] * last,
+        compiler_params=LIMIT,
+        name="residual_last" if last else "residual",
+    )(side, *kept(*values, weights, inverse, *ending))
+
+
+def final_kernel(visits, side_ref, sums_ref, *refs):
+    parts = [refs[:3], refs[3:6]]
+    out_ref, chi_ref, done, mean, sent = refs[6:]
     rows, width = done.shape
-    high = min(16, rows)
+    high = min(16, rows // 2)
     sums = [
         jnp.where(side_ref[0] == 0, sums_ref[k], pltpu.roll(sums_ref[k], visits, 0))
         for k in range(2)
@@ -540,35 +560,36 @@
     chi_copy = pltpu.make_async_copy(mean, chi_ref, sent.at[1])
     chi_copy.start()
     scales = [jnp.broadcast_to(scale[m : m + 1], (high, LANES)) for m in range(2 * visits)]
+    depth = rows // 2
     for lane in range(0, width, LANES):
         lanes = slice(lane, lane + LANES)
-        for row in range(0, rows, high):
-            numer = denom = None
-            for m in range(2 * visits):
-                source = own_ref if m < visits else other_ref
-                at = (m % visits) * rows + row
-                value = source[at : at + high, lanes].astype(F32)
-                at = m * rows + row
-                revised = factor_ref[at : at + high, lanes] * scales[m]
-                numer = revised * value if numer is None else numer + revised * value
-                denom = revised if denom is None else denom + revised
-            done[row : row + high, lanes] = numer / (denom + PRIOR_WEIGHT)
+        for top, part in zip((0, depth), parts):
+            for row in range(0, depth, high):
+                numer = denom = None
+                for m in range(2 * visits):
+                    at = (m % visits) * depth + row
+                    value = part[m // visits][at : at + high, lanes].astype(F32)
+                    at = m * depth + row
+                    revised = part[2][at : at + high, lanes] * scales[m]
+                    numer = revised * value if numer is None else numer + revised * value
+                    denom = revised if denom is None else denom + revised
+                done[top + row : top + row + high, lanes] = numer / (denom + PRIOR_WEIGHT)
     copy = pltpu.make_async_copy(done, out_ref, sent.at[0])
     copy.start()
     chi_copy.wait()
     copy.wait()
 
 
-def final_pass(side, sums, values, factors, visits):
-    count, width = values[0].shape
-    rows = count // visits
+def final_pass(side, sums, upper, lower, visits):
+    count, width = upper[0].shape
+    rows = 2 * count // visits
     return pl.pallas_call(
         functools.partial(final_kernel, visits),
         out_shape=(
             jax.ShapeDtypeStruct((rows, width), F32),
             jax.ShapeDtypeStruct((visits,), F32),
         ),
-        in_specs=[whole(pltpu.SMEM)] + [whole()] * 4,
+        in_specs=[whole(pltpu.SMEM)] + [whole()] * 7,
         out_specs=(pl.BlockSpec(memory_space=pl.ANY),) * 2,
         scratch_shapes=[
             pltpu.VMEM((rows, width), F32),
@@ -577,7 +598,7 @@
         ],
         compiler_params=LIMIT,
         name="final",
-    )(side, *kept(sums, *values, factors))
+    )(side, *kept(sums, *upper, *lower))
 
 
 def per_device(warps, badbits, coverage, variance, psf_index, psf_table, row_basis, col_basis):
@@ -596,21 +617,28 @@
     column, own, above, below = tables(psf_index, psf_table, row_basis, col_basis, visits, rows)
     leading, upper = pack_rows(warps, half, True, send_weight)
     after = lax.ppermute(leading, "sky", down)
-    part = own_part(upper.reshape(-1, columns), lower.reshape(-1, columns), column, own, visits)
-    part = rim_part(side, before, column, above, part, visits, half, columns, F32)
+    top, bottom = own_part(
+        upper.reshape(-1, columns), lower.reshape(-1, columns), column, own, visits
+    )
+    send_top = rim_part(1 - side, before, column, above, top, visits, half)
+    other_top = lax.ppermute(send_top, "visit", swap)
+    own_top = rim_part(side, before, column, above, top, visits, half)
     weights, inverse, counts = norms(own_weight, other_weight, visits, coverage.shape[1], rows)
-    send_value = rim_part(1 - side, after, column, below, part, visits, half, columns // 2, BF16)
+    top_factors, chi = residual_pass(side, (own_top, other_top), weights, inverse, visits, 0)
+    send_value = rim_part(1 - side, after, column, below, bottom, visits, half)
     other_value = lax.ppermute(send_value, "visit", swap)
-    own_value = rim_part(side, after, column, below, part, visits, half, columns // 2, BF16)
-    values = (own_value, other_value)
-    factors, sums = residual_pass(side, values, weights, inverse, counts, visits)
+    own_value = rim_part(side, after, column, below, bottom, visits, half)
+    factors, sums = residual_pass(
+        side, (own_value, other_value), weights, inverse, visits, rows // 2, chi, counts
+    )
     sums = sums + lax.ppermute(sums, "visit", swap)
     step = 1
     while step < strips:
         pairs = [(2 * i + v, 2 * (i ^ step) + 1 - v) for i in range(strips) for v in (0, 1)]
         sums = sums + lax.ppermute(sums, ("sky", "visit"), pairs)
         step *= 2
-    return final_pass(side, sums, values, factors, visits)
+    upper = (own_top, other_top, top_factors)
+    return final_pass(side, sums, upper, (own_value, other_value, factors), visits)
 
 
 def solution(mesh):

time: 39.5 us -> 40.4 us (1.023)
  waiting for transfers between devices: 8.05 us -> 9.12 us
    ppermute x1, waiting for transfers between devices: 2.39 us -> 3.85 us  [per_device(): after = lax.ppermute(leading, 'sky', down)]
    ppermute x3, starting transfers between devices: 7.4 us -> 6.33 us  [per_device(): sums = sums + lax.ppermute(sums, ('sky', 'visit'), pairs)]
    ppermute x0 -> x1, starting transfers between devices: none -> 0.55 us  [per_device(): other_top = lax.ppermute(send_top, 'visit', swap)]
    ppermute x1, waiting for transfers between devices: 0.53 us -> 0.01 us  [per_device(): other_value = lax.ppermute(send_value, 'visit', swap)]
    pallas_call x2 -> x3, Pallas kernels: 4.97 us -> 5.05 us  [the longest x1 3.99 us: own_part(): pl.pallas_call(functools.partial(own_kernel, visits), out_shape=(held((ha...]
    pallas_call x3 -> x4, Pallas kernels: 3.7 us -> 3.78 us  [rim_part(): pl.pallas_call(functools.partial(rim_kernel, visits, half), out_shape=hel...]
  transfers between devices with their start and end apart: 8 -> 9, of which waited for: 6 -> 5; matrix products, arithmetic and copies ran while one was open for 0% -> 0% of each run, Pallas kernels for 32% -> 33%
where the time goes in v9:
time: 40.4 us; the launch traced here: 40.1 us
  Pallas kernels  16.2 us (40%)
  starting transfers between devices  13.9 us (34%)
  waiting for transfers between devices  9.12 us (23%)
  between operations  0.81 us (2%)
    ppermute x3, starting transfers between devices, per_device(): sums = sums + lax.ppermute(sums, ('sky', 'visit'), pairs)  6.33 us
    ppermute x1, starting transfers between devices, per_device(): before = lax.ppermute(last, 'sky', up)  5.05 us
    ppermute x3, waiting for transfers between devices, per_device(): sums = sums + lax.ppermute(sums, ('sky', 'visit'), pairs)  4.43 us
    pallas_call x1, Pallas kernels, own_part(): pl.pallas_call(functools.partial(own_kernel, visits), out_shape=(held((ha...  3.99 us
    ppermute x1, waiting for transfers between devices, per_device(): after = lax.ppermute(leading, 'sky', down)  3.85 us
    pallas_call x4, Pallas kernels, rim_part(): pl.pallas_call(functools.partial(rim_kernel, visits, half), out_shape=hel...  3.78 us
    pallas_call x2, Pallas kernels, pack_rows(): pl.pallas_call(functools.partial(pack_kernel, half, first, skip), out_sha...  2.75 us
    pallas_call x1, Pallas kernels, pixel_weights(): pl.pallas_call(functools.partial(weight_kernel, visits, bands), out_shape...  1.74 us
  transfers between devices with their start and end apart: 9, of which 5 were waited for; matrix products, arithmetic and copies ran while one was open for 0% of the time, Pallas kernels for 33%

profile of v9, /device:TPU:0, one launch (start us, length us, event | category | flops | bytes accessed | tf_op | source)
XLA Modules:
  0.0 40.1 jit_solution(17088706601307255040)
XLA Ops:
  0.6 1.4 %pack_lower.1 = (bf16[40,4096]{1,0:T(8,128)(2,1)S(1)}, bf16[4,16,4096]{2,1,0:T(8,128)(2,1)S(1)}) custom-call(bf16[4,32,4096]{2,1,0:T(8,128)(2,1)} %x_ref.3), custom_call_target="tpu_custom_call" | custom-call | tf_op jit(solution)/shard_map/pack_lower/pallas_call | solution.py:98
  2.0 0.0 copy-start
  2.0 0.0 copy-start.1
  2.0 0.0 copy-start.2
  2.0 0.0 copy-start.3
  2.1 5.1 %collective-permute-start.3 = (bf16[40,4096]{1,0:T(8,128)(2,1)S(1)}, bf16[40,4096]{1,0:T(8,128)(2,1)S(1)}, u32[]{:S(2)}, u32[]{:S(2)}) collective-permute-start(bf16[40,4096]{1,0:T(8,128)(2,1)S(1)} %get-tuple-element.32), channel_id=1, source_target_pairs={{0,2},{2,4},{4,6},{6,8},{8,10},{10,12},{12,14},{1,3},{3,5},{5,7},{... | collective-permute-start | bytes 983048 | tf_op jit(solution)/shard_map/ppermute | solution.py:614
  7.1 1.7 %weights.1 = (bf16[144,2048]{1,0:T(8,128)(2,1)S(1)}, bf16[144,2048]{1,0:T(8,128)(2,1)S(1)}) custom-call(s32[1]{0:T(128)} %bitcast.side_ref, s32[1,4]{1,0:T(1,128)} %bitcast.11, f32[1,4]{1,0:T(1,128)} %bitcast.12, s32[128,4096]{1,0:T(8,128)} %bitcast.10), custom_call_target="tpu_custom_call" | custom-call | tf_op jit(solution)/shard_map/weights/pallas_call | solution.py:159
  8.9 0.1 collective-permute-start.2
  9.0 1.4 %pack_upper.1 = (bf16[40,4096]{1,0:T(8,128)(2,1)S(1)}, bf16[4,16,4096]{2,1,0:T(8,128)(2,1)S(1)}) custom-call(bf16[4,32,4096]{2,1,0:T(8,128)(2,1)} %x_ref.3, bf16[144,2048]{1,0:T(8,128)(2,1)S(1)} %get-tuple-element.21.refs_0_), custom_call_target="tpu_custom_call" | custom-call | tf_op jit(solution)/shard_map/pack_upper/pallas_call | solution.py:98
  10.3 1.3 %collective-permute-start = (bf16[40,4096]{1,0:T(8,128)(2,1)S(1)}, bf16[40,4096]{1,0:T(8,128)(2,1)S(1)}, u32[]{:S(2)}, u32[]{:S(2)}) collective-permute-start(bf16[40,4096]{1,0:T(8,128)(2,1)S(1)} %get-tuple-element.22), channel_id=1, source_target_pairs={{2,0},{4,2},{6,4},{8,6},{10,8},{12,10},{14,12},{3,1},{5,3},{7,5},{... | collective-permute-start | bytes 983048 | tf_op jit(solution)/shard_map/ppermute | solution.py:619
  11.6 0.0 copy-done
  11.7 0.0 copy-done.1
  11.7 0.0 copy-done.2
  11.7 0.0 copy-done.3
  11.7 1.3 %tables.1 = (bf16[256,1024]{1,0:T(8,128)(2,1)S(1)}, bf16[256,256]{1,0:T(8,128)(2,1)S(1)}, bf16[128,128]{1,0:T(8,128)(2,1)S(1)}, bf16[128,128]{1,0:T(8,128)(2,1)S(1)}) custom-call(s32[4]{0:T(128)S(1)} %copy-done.3, f32[8,16]{1,0:T(8,128)S(1)} %bitcast.7, bf16[8,21]{1,0:T(8,128)(2,1)S(1)} %copy-done.1, bf16[8,21]{1,0:T(8,128)(2,1)S(1)} %copy-done.2), custom_call_target="tpu_custom_call" | custom-call | tf_op jit(solution)/shard_map/tables/pallas_call | solution.py:257
  13.0 4.0 %own_rows.1 = (f32[64,4096]{1,0:T(8,128)S(1)}, f32[64,4096]{1,0:T(8,128)S(1)}) custom-call(bf16[64,4096]{1,0:T(8,128)(2,1)S(1)} %bitcast.9, bf16[64,4096]{1,0:T(8,128)(2,1)S(1)} %bitcast.8, bf16[256,1024]{1,0:T(8,128)(2,1)S(1)} %get-tuple-element.23.column_ref, bf16[256,256]{1,0:T(8,128)(2,1)S(1)} %get-tuple-element.27.row_ref), custom_call_target="tpu_custom_call" | custom-call | flops 1000000000 | bytes 10000000 | tf_op jit(solution)/shard_map/own_rows/pallas_call | solution.py:362
  17.0 0.0 collective-permute-done.3.edge_ref
  17.0 0.9 %shard_map.98 = bf16[64,2048]{1,0:T(8,128)(2,1)S(1)} custom-call(s32[1]{0:T(128)S(6)} %sub.4.side_ref, bf16[40,4096]{1,0:T(8,128)(2,1)S(1)} %collective-permute-done.3.edge_ref, bf16[256,1024]{1,0:T(8,128)(2,1)S(1)} %get-tuple-element.23.column_ref, bf16[128,128]{1,0:T(8,128)(2,1)S(1)} %get-tuple-element.33.row_ref, f32[64,4096]{1,0:T(8,128)S(1)} %get-tuple-element.34.part_ref), custom_call_target="tpu_custom_call" | custom-call | tf_op jit(solution)/shard_map/pallas_call | solution.py:412
  18.0 0.6 %collective-permute-start.4 = (bf16[64,2048]{1,0:T(8,128)(2,1)S(1)}, bf16[64,2048]{1,0:T(8,128)(2,1)S(1)}, u32[]{:S(2)}, u32[]{:S(2)}) collective-permute-start(bf16[64,2048]{1,0:T(8,128)(2,1)S(1)} %shard_map.98), channel_id=1, source_target_pairs={{0,1},{1,0},{2,3},{3,2},{4,5},{5,4},{6,7},{7,6},{8,9},{9,8},{10,11... | collective-permute-start | bytes 786440 | tf_op jit(solution)/shard_map/ppermute | solution.py:624
  18.5 3.8 %collective-permute-done.edge_ref = bf16[40,4096]{1,0:T(8,128)(2,1)S(1)} collective-permute-done((bf16[40,4096]{1,0:T(8,128)(2,1)S(1)}, bf16[40,4096]{1,0:T(8,128)(2,1)S(1)}, u32[]{:S(2)}, u32[]{:S(2)}) %collective-permute-start) | collective-permute-done | bytes 327712 | tf_op jit(solution)/shard_map/ppermute | solution.py:619
  22.4 0.9 %shard_map.96 = bf16[64,2048]{1,0:T(8,128)(2,1)S(1)} custom-call(s32[1]{0:T(128)S(6)} %sub.4.side_ref, bf16[40,4096]{1,0:T(8,128)(2,1)S(1)} %collective-permute-done.edge_ref, bf16[256,1024]{1,0:T(8,128)(2,1)S(1)} %get-tuple-element.23.column_ref, bf16[128,128]{1,0:T(8,128)(2,1)S(1)} %get-tuple-element.24.row_ref, f32[64,4096]{1,0:T(8,128)S(1)} %get-tuple-element.28.part_ref), custom_call_target="tpu_custom_call" | custom-call | tf_op jit(solution)/shard_map/pallas_call | solution.py:412
  23.3 0.1 collective-permute-start.1
  23.4 0.9 %shard_map.95.refs_0_.refs_3_ = bf16[64,2048]{1,0:T(8,128)(2,1)S(1)} custom-call(s32[1]{0:T(128)} %bitcast.side_ref, bf16[40,4096]{1,0:T(8,128)(2,1)S(1)} %collective-permute-done.edge_ref, bf16[256,1024]{1,0:T(8,128)(2,1)S(1)} %get-tuple-element.23.column_ref, bf16[128,128]{1,0:T(8,128)(2,1)S(1)} %get-tuple-element.24.row_ref, ...), custom_call_target="tpu_custom_call" | custom-call | tf_op jit(solution)/shard_map/pallas_call | solution.py:412
  24.3 0.9 %shard_map.97.refs_0_ = bf16[64,2048]{1,0:T(8,128)(2,1)S(1)} custom-call(s32[1]{0:T(128)} %bitcast.side_ref, bf16[40,4096]{1,0:T(8,128)(2,1)S(1)} %collective-permute-done.3.edge_ref, bf16[256,1024]{1,0:T(8,128)(2,1)S(1)} %get-tuple-element.23.column_ref, bf16[128,128]{1,0:T(8,128)(2,1)S(1)} %get-tuple-element.33.row_ref, ...), custom_call_target="tpu_custom_call" | custom-call | tf_op jit(solution)/shard_map/pallas_call | solution.py:412
  25.3 0.0 collective-permute-done.2.refs_1_
  25.3 0.4 norms.1
  25.7 0.0 collective-permute-done.4.refs_1_
  25.7 0.5 %residual.1 = (f32[128,2048]{1,0:T(8,128)S(1)}, f32[64,128]{1,0:T(8,128)S(1)}) custom-call(s32[1]{0:T(128)} %bitcast.side_ref, bf16[64,2048]{1,0:T(8,128)(2,1)S(1)} %shard_map.97.refs_0_, bf16[64,2048]{1,0:T(8,128)(2,1)S(1)} %collective-permute-done.4.refs_1_, f32[256,2048]{1,0:T(8,128)S(1)} %get-tuple-element.30.refs_2_, ...), custom_call_target="tpu_custom_call" | custom-call | tf_op jit(solution)/shard_map/residual/pallas_call | solution.py:533
  26.2 0.0 collective-permute-done.1.refs_1_.refs_4_
  26.2 0.5 %residual_last.1 = (f32[128,2048]{1,0:T(8,128)S(1)}, f32[2,8,128]{2,1,0:T(8,128)S(1)}) custom-call(s32[1]{0:T(128)} %bitcast.side_ref, bf16[64,2048]{1,0:T(8,128)(2,1)S(1)} %shard_map.95.refs_0_.refs_3_, bf16[64,2048]{1,0:T(8,128)(2,1)S(1)} %collective-permute-done.1.refs_1_.refs_4_, f32[256,2048]{1,0:T(8,128)S(1)} %get-tuple-element.30.refs_2_, ...), custom_call_target="tpu_custom_call" | custom-call | tf_op jit(solution)/shard_map/residual_last/pallas_call | solution.py:533
  26.7 0.6 %collective-permute-start.5 = (f32[2,8,128]{2,1,0:T(8,128)S(1)}, f32[2,8,128]{2,1,0:T(8,128)S(1)}, u32[]{:S(2)}, u32[]{:S(2)}) collective-permute-start(f32[2,8,128]{2,1,0:T(8,128)S(1)} %get-tuple-element.37), channel_id=1, source_target_pairs={{0,1},{1,0},{2,3},{3,2},{4,5},{5,4},{6,7},{7,6},{8,9},{9,8},{10,11... | collective-permute-start | bytes 24584 | tf_op jit(solution)/shard_map/ppermute | solution.py:634
  27.3 0.8 %collective-permute-done.5 = f32[2,8,128]{2,1,0:T(8,128)S(1)} collective-permute-done((f32[2,8,128]{2,1,0:T(8,128)S(1)}, f32[2,8,128]{2,1,0:T(8,128)S(1)}, u32[]{:S(2)}, u32[]{:S(2)}) %collective-permute-start.5) | collective-permute-done | bytes 8224 | tf_op jit(solution)/shard_map/ppermute | solution.py:634
  28.1 2.3 %collective-permute-start.6 = (f32[2,8,128]{2,1,0:T(8,128)S(1)}, f32[2,8,128]{2,1,0:T(8,128)S(1)}, u32[]{:S(2)}, u32[]{:S(2)}) collective-permute-start(f32[2,8,128]{2,1,0:T(8,128)S(1)} %add.12), channel_id=1, source_target_pairs={{0,3},{1,2},{2,1},{3,0},{4,7},{5,6},{6,5},{7,4},{8,11},{9,10},{10,... | collective-permute-start | bytes 24584 | tf_op jit(solution)/shard_map/ppermute | solution.py:638
  30.5 1.4 %collective-permute-done.6 = f32[2,8,128]{2,1,0:T(8,128)S(1)} collective-permute-done((f32[2,8,128]{2,1,0:T(8,128)S(1)}, f32[2,8,128]{2,1,0:T(8,128)S(1)}, u32[]{:S(2)}, u32[]{:S(2)}) %collective-permute-start.6) | collective-permute-done | bytes 8224 | tf_op jit(solution)/shard_map/ppermute | solution.py:638
  31.9 1.5 %collective-permute-start.7 = (f32[2,8,128]{2,1,0:T(8,128)S(1)}, f32[2,8,128]{2,1,0:T(8,128)S(1)}, u32[]{:S(2)}, u32[]{:S(2)}) collective-permute-start(f32[2,8,128]{2,1,0:T(8,128)S(1)} %add.13), channel_id=1, source_target_pairs={{0,5},{1,4},{2,7},{3,6},{4,1},{5,0},{6,3},{7,2},{8,13},{9,12},{10,... | collective-permute-start | bytes 24584 | tf_op jit(solution)/shard_map/ppermute | solution.py:638
  33.3 1.6 %collective-permute-done.7 = f32[2,8,128]{2,1,0:T(8,128)S(1)} collective-permute-done((f32[2,8,128]{2,1,0:T(8,128)S(1)}, f32[2,8,128]{2,1,0:T(8,128)S(1)}, u32[]{:S(2)}, u32[]{:S(2)}) %collective-permute-start.7) | collective-permute-done | bytes 8224 | tf_op jit(solution)/shard_map/ppermute | solution.py:638
  34.9 2.5 %collective-permute-start.8 = (f32[2,8,128]{2,1,0:T(8,128)S(1)}, f32[2,8,128]{2,1,0:T(8,128)S(1)}, u32[]{:S(2)}, u32[]{:S(2)}) collective-permute-start(f32[2,8,128]{2,1,0:T(8,128)S(1)} %add.14), channel_id=1, source_target_pairs={{0,9},{1,8},{2,11},{3,10},{4,13},{5,12},{6,15},{7,14},{8,1},{9,0},... | collective-permute-start | bytes 24584 | tf_op jit(solution)/shard_map/ppermute | solution.py:638
  37.4 1.5 %collective-permute-done.8 = f32[2,8,128]{2,1,0:T(8,128)S(1)} collective-permute-done((f32[2,8,128]{2,1,0:T(8,128)S(1)}, f32[2,8,128]{2,1,0:T(8,128)S(1)}, u32[]{:S(2)}, u32[]{:S(2)}) %collective-permute-start.8) | collective-permute-done | bytes 8224 | tf_op jit(solution)/shard_map/ppermute | solution.py:638
  38.9 1.2 %final.1 = (f32[32,2048]{1,0:T(8,128)}, f32[4]{0:T(128)}) custom-call(s32[1]{0:T(128)} %bitcast.side_ref, f32[2,8,128]{2,1,0:T(8,128)S(1)} %add.15.sums_ref, bf16[64,2048]{1,0:T(8,128)(2,1)S(1)} %shard_map.97.refs_0_, bf16[64,2048]{1,0:T(8,128)(2,1)S(1)} %collective-permute-done.4.refs_1_, f32[128,2048]{1,0:T(8,128)S(1)} %get-tuple-element.38.refs_2_, ...), custom_call_target="tpu_custom_call" | custom-call | tf_op jit(solution)/shard_map/final/pallas_call | solution.py:586
  (4 shorter events, 0.0 us)
Async XLA Ops:
  2.0 9.6 %copy-start = (f32[16,8]{0,1:T(8,128)S(1)}, f32[16,8]{0,1:T(8,128)}, u32[]{:S(2)}) copy-start(f32[16,8]{0,1:T(8,128)} %param.13) | copy-start | bytes 1540
  2.0 9.6 %copy-start.1 = (bf16[8,21]{1,0:T(8,128)(2,1)S(1)}, bf16[8,21]{1,0:T(8,128)(2,1)}, u32[]{:S(2)}) copy-start(bf16[8,21]{1,0:T(8,128)(2,1)} %row_ref.1) | copy-start | bytes 1012
  2.0 9.6 %copy-start.2 = (bf16[8,21]{1,0:T(8,128)(2,1)S(1)}, bf16[8,21]{1,0:T(8,128)(2,1)}, u32[]{:S(2)}) copy-start(bf16[8,21]{1,0:T(8,128)(2,1)} %col_ref.1) | copy-start | bytes 1012
  2.0 9.6 %copy-start.3 = (s32[4]{0:T(128)S(1)}, s32[4]{0:T(128)}, u32[]{:S(2)}) copy-start(s32[4]{0:T(128)} %index_ref.1) | copy-start | bytes 52
  2.1 14.9 %collective-permute-start.3 = (bf16[40,4096]{1,0:T(8,128)(2,1)S(1)}, bf16[40,4096]{1,0:T(8,128)(2,1)S(1)}, u32[]{:S(2)}, u32[]{:S(2)}) collective-permute-start(bf16[40,4096]{1,0:T(8,128)(2,1)S(1)} %get-tuple-element.32), channel_id=1, source_target_pairs={{0,2},{2,4},{4,6},{6,8},{8,10},{10,12},{12,14},{1,3},{3,5},{5,7},{... | collective-permute-start | bytes 983048 | tf_op jit(solution)/shard_map/ppermute | solution.py:614
  8.9 16.4 %collective-permute-start.2 = (bf16[144,2048]{1,0:T(8,128)(2,1)S(1)}, bf16[144,2048]{1,0:T(8,128)(2,1)S(1)}, u32[]{:S(2)}, u32[]{:S(2)}) collective-permute-start(bf16[144,2048]{1,0:T(8,128)(2,1)S(1)} %get-tuple-element.21.refs_0_), channel_id=1, source_target_pairs={{0,1},{1,0},{2,3},{3,2},{4,5},{5,4},{6,7},{7,6},{8,9},{9,8},{10,11... | collective-permute-start | bytes 1769480 | tf_op jit(solution)/shard_map/ppermute | solution.py:616
  10.3 12.0 %collective-permute-start = (bf16[40,4096]{1,0:T(8,128)(2,1)S(1)}, bf16[40,4096]{1,0:T(8,128)(2,1)S(1)}, u32[]{:S(2)}, u32[]{:S(2)}) collective-permute-start(bf16[40,4096]{1,0:T(8,128)(2,1)S(1)} %get-tuple-element.22), channel_id=1, source_target_pairs={{2,0},{4,2},{6,4},{8,6},{10,8},{12,10},{14,12},{3,1},{5,3},{7,5},{... | collective-permute-start | bytes 983048 | tf_op jit(solution)/shard_map/ppermute | solution.py:619
  18.0 7.7 %collective-permute-start.4 = (bf16[64,2048]{1,0:T(8,128)(2,1)S(1)}, bf16[64,2048]{1,0:T(8,128)(2,1)S(1)}, u32[]{:S(2)}, u32[]{:S(2)}) collective-permute-start(bf16[64,2048]{1,0:T(8,128)(2,1)S(1)} %shard_map.98), channel_id=1, source_target_pairs={{0,1},{1,0},{2,3},{3,2},{4,5},{5,4},{6,7},{7,6},{8,9},{9,8},{10,11... | collective-permute-start | bytes 786440 | tf_op jit(solution)/shard_map/ppermute | solution.py:624
  23.3 2.9 %collective-permute-start.1 = (bf16[64,2048]{1,0:T(8,128)(2,1)S(1)}, bf16[64,2048]{1,0:T(8,128)(2,1)S(1)}, u32[]{:S(2)}, u32[]{:S(2)}) collective-permute-start(bf16[64,2048]{1,0:T(8,128)(2,1)S(1)} %shard_map.96), channel_id=1, source_target_pairs={{0,1},{1,0},{2,3},{3,2},{4,5},{5,4},{6,7},{7,6},{8,9},{9,8},{10,11... | collective-permute-start | bytes 786440 | tf_op jit(solution)/shard_map/ppermute | solution.py:629
  26.7 1.4 %collective-permute-start.5 = (f32[2,8,128]{2,1,0:T(8,128)S(1)}, f32[2,8,128]{2,1,0:T(8,128)S(1)}, u32[]{:S(2)}, u32[]{:S(2)}) collective-permute-start(f32[2,8,128]{2,1,0:T(8,128)S(1)} %get-tuple-element.37), channel_id=1, source_target_pairs={{0,1},{1,0},{2,3},{3,2},{4,5},{5,4},{6,7},{7,6},{8,9},{9,8},{10,11... | collective-permute-start | bytes 24584 | tf_op jit(solution)/shard_map/ppermute | solution.py:634
  28.1 3.7 %collective-permute-start.6 = (f32[2,8,128]{2,1,0:T(8,128)S(1)}, f32[2,8,128]{2,1,0:T(8,128)S(1)}, u32[]{:S(2)}, u32[]{:S(2)}) collective-permute-start(f32[2,8,128]{2,1,0:T(8,128)S(1)} %add.12), channel_id=1, source_target_pairs={{0,3},{1,2},{2,1},{3,0},{4,7},{5,6},{6,5},{7,4},{8,11},{9,10},{10,... | collective-permute-start | bytes 24584 | tf_op jit(solution)/shard_map/ppermute | solution.py:638
  31.9 3.1 %collective-permute-start.7 = (f32[2,8,128]{2,1,0:T(8,128)S(1)}, f32[2,8,128]{2,1,0:T(8,128)S(1)}, u32[]{:S(2)}, u32[]{:S(2)}) collective-permute-start(f32[2,8,128]{2,1,0:T(8,128)S(1)} %add.13), channel_id=1, source_target_pairs={{0,5},{1,4},{2,7},{3,6},{4,1},{5,0},{6,3},{7,2},{8,13},{9,12},{10,... | collective-permute-start | bytes 24584 | tf_op jit(solution)/shard_map/ppermute | solution.py:638
  34.9 4.0 %collective-permute-start.8 = (f32[2,8,128]{2,1,0:T(8,128)S(1)}, f32[2,8,128]{2,1,0:T(8,128)S(1)}, u32[]{:S(2)}, u32[]{:S(2)}) collective-permute-start(f32[2,8,128]{2,1,0:T(8,128)S(1)} %add.14), channel_id=1, source_target_pairs={{0,9},{1,8},{2,11},{3,10},{4,13},{5,12},{6,15},{7,14},{8,1},{9,0},... | collective-permute-start | bytes 24584 | tf_op jit(solution)/shard_map/ppermute | solution.py:638

commit v10 on v9

--- a/solution.py
+++ b/solution.py
@@ -269,9 +269,6 @@
     )(psf_index, psf_table.T, row_basis, col_basis)
 
 
-BLOCKS = 4
-
-
 def column_pass(windows, column_ref):
     return jnp.dot(
         jnp.concatenate(windows, axis=0), column_ref[...], preferred_element_type=F32
@@ -301,11 +298,11 @@
         yield first, totals
 
 
-def convolve(make_group, shifted, column_ref, row_ref, pieces, put):
+def convolve(make_group, shifted, column_ref, row_ref, pieces, put, blocks):
     count = shifted.shape[0]
     groups = shifted.shape[1] // LANES - 1
     bases = column_ref.shape[1] // LANES
-    blocks = min(BLOCKS, groups)
+    blocks = min(blocks, groups)
     made = [0]
 
     def columns_of(step):
@@ -354,7 +351,7 @@
             top_ref[lines, start : start + 2 * LANES] = total[:depth]
             bottom_ref[lines, start : start + 2 * LANES] = total[depth:]
 
-    convolve(make_group, shifted, column_ref, row_ref, pieces, put)
+    convolve(make_group, shifted, column_ref, row_ref, pieces, put, 4)
 
 
 def own_part(upper, lower, column, own, visits):
@@ -403,7 +400,7 @@
             value = (total + part_ref[lines, source]).astype(out_ref.dtype)
             out_ref[lines, start : start + 2 * LANES] = value
 
-    convolve(make_group, shifted, column_ref, row_ref, pieces, put)
+    convolve(make_group, shifted, column_ref, row_ref, pieces, put, 8)
 
 
 def rim_part(side, edge, column, table, part, visits, half):

time: 40.4 us -> 40 us (0.990)
  Pallas kernels: 16.2 us -> 15.7 us
    pallas_call x4, Pallas kernels: 3.78 us -> 3.21 us  [rim_part(): pl.pallas_call(functools.partial(rim_kernel, visits, half), out_shape=hel...]
  transfers between devices with their start and end apart: 9 -> 9, of which waited for: 5 -> 5; matrix products, arithmetic and copies ran while one was open for 0% -> 0% of each run, Pallas kernels for 33% -> 32%
where the time goes in v10:
time: 40 us; the launch traced here: 39.7 us
  Pallas kernels  15.7 us (39%)
  starting transfers between devices  13.9 us (35%)
  waiting for transfers between devices  9.26 us (23%)
  between operations  0.81 us (2%)
    ppermute x3, starting transfers between devices, per_device(): sums = sums + lax.ppermute(sums, ('sky', 'visit'), pairs)  6.32 us
    ppermute x1, starting transfers between devices, per_device(): before = lax.ppermute(last, 'sky', up)  5.05 us
    ppermute x3, waiting for transfers between devices, per_device(): sums = sums + lax.ppermute(sums, ('sky', 'visit'), pairs)  4.44 us
    pallas_call x1, Pallas kernels, own_part(): pl.pallas_call(functools.partial(own_kernel, visits), out_shape=(held((ha...  3.99 us
    ppermute x1, waiting for transfers between devices, per_device(): after = lax.ppermute(leading, 'sky', down)  3.98 us
    pallas_call x4, Pallas kernels, rim_part(): pl.pallas_call(functools.partial(rim_kernel, visits, half), out_shape=hel...  3.21 us
    pallas_call x2, Pallas kernels, pack_rows(): pl.pallas_call(functools.partial(pack_kernel, half, first, skip), out_sha...  2.75 us
    pallas_call x1, Pallas kernels, pixel_weights(): pl.pallas_call(functools.partial(weight_kernel, visits, bands), out_shape...  1.74 us
  transfers between devices with their start and end apart: 9, of which 5 were waited for; matrix products, arithmetic and copies ran while one was open for 0% of the time, Pallas kernels for 32%

profile of v10, /device:TPU:0, one launch (start us, length us, event | category | flops | bytes accessed | tf_op | source)
XLA Modules:
  0.0 39.7 jit_solution(12121935804274311473)
XLA Ops:
  0.6 1.4 %pack_lower.1 = (bf16[40,4096]{1,0:T(8,128)(2,1)S(1)}, bf16[4,16,4096]{2,1,0:T(8,128)(2,1)S(1)}) custom-call(bf16[4,32,4096]{2,1,0:T(8,128)(2,1)} %x_ref.3), custom_call_target="tpu_custom_call" | custom-call | tf_op jit(solution)/shard_map/pack_lower/pallas_call | solution.py:98
  2.0 0.0 copy-start
  2.0 0.0 copy-start.1
  2.0 0.0 copy-start.2
  2.0 0.0 copy-start.3
  2.1 5.1 %collective-permute-start.3 = (bf16[40,4096]{1,0:T(8,128)(2,1)S(1)}, bf16[40,4096]{1,0:T(8,128)(2,1)S(1)}, u32[]{:S(2)}, u32[]{:S(2)}) collective-permute-start(bf16[40,4096]{1,0:T(8,128)(2,1)S(1)} %get-tuple-element.32), channel_id=1, source_target_pairs={{0,2},{2,4},{4,6},{6,8},{8,10},{10,12},{12,14},{1,3},{3,5},{5,7},{... | collective-permute-start | bytes 983048 | tf_op jit(solution)/shard_map/ppermute | solution.py:611
  7.1 1.7 %weights.1 = (bf16[144,2048]{1,0:T(8,128)(2,1)S(1)}, bf16[144,2048]{1,0:T(8,128)(2,1)S(1)}) custom-call(s32[1]{0:T(128)} %bitcast.side_ref, s32[1,4]{1,0:T(1,128)} %bitcast.11, f32[1,4]{1,0:T(1,128)} %bitcast.12, s32[128,4096]{1,0:T(8,128)} %bitcast.10), custom_call_target="tpu_custom_call" | custom-call | tf_op jit(solution)/shard_map/weights/pallas_call | solution.py:159
  8.9 0.1 collective-permute-start.2
  9.0 1.4 %pack_upper.1 = (bf16[40,4096]{1,0:T(8,128)(2,1)S(1)}, bf16[4,16,4096]{2,1,0:T(8,128)(2,1)S(1)}) custom-call(bf16[4,32,4096]{2,1,0:T(8,128)(2,1)} %x_ref.3, bf16[144,2048]{1,0:T(8,128)(2,1)S(1)} %get-tuple-element.21.refs_0_), custom_call_target="tpu_custom_call" | custom-call | tf_op jit(solution)/shard_map/pack_upper/pallas_call | solution.py:98
  10.3 1.3 %collective-permute-start = (bf16[40,4096]{1,0:T(8,128)(2,1)S(1)}, bf16[40,4096]{1,0:T(8,128)(2,1)S(1)}, u32[]{:S(2)}, u32[]{:S(2)}) collective-permute-start(bf16[40,4096]{1,0:T(8,128)(2,1)S(1)} %get-tuple-element.22), channel_id=1, source_target_pairs={{2,0},{4,2},{6,4},{8,6},{10,8},{12,10},{14,12},{3,1},{5,3},{7,5},{... | collective-permute-start | bytes 983048 | tf_op jit(solution)/shard_map/ppermute | solution.py:616
  11.6 0.0 copy-done
  11.7 0.0 copy-done.1
  11.7 0.0 copy-done.2
  11.7 0.0 copy-done.3
  11.7 1.3 %tables.1 = (bf16[256,1024]{1,0:T(8,128)(2,1)S(1)}, bf16[256,256]{1,0:T(8,128)(2,1)S(1)}, bf16[128,128]{1,0:T(8,128)(2,1)S(1)}, bf16[128,128]{1,0:T(8,128)(2,1)S(1)}) custom-call(s32[4]{0:T(128)S(1)} %copy-done.3, f32[8,16]{1,0:T(8,128)S(1)} %bitcast.7, bf16[8,21]{1,0:T(8,128)(2,1)S(1)} %copy-done.1, bf16[8,21]{1,0:T(8,128)(2,1)S(1)} %copy-done.2), custom_call_target="tpu_custom_call" | custom-call | tf_op jit(solution)/shard_map/tables/pallas_call | solution.py:257
  13.0 4.0 %own_rows.1 = (f32[64,4096]{1,0:T(8,128)S(1)}, f32[64,4096]{1,0:T(8,128)S(1)}) custom-call(bf16[64,4096]{1,0:T(8,128)(2,1)S(1)} %bitcast.9, bf16[64,4096]{1,0:T(8,128)(2,1)S(1)} %bitcast.8, bf16[256,1024]{1,0:T(8,128)(2,1)S(1)} %get-tuple-element.23.column_ref, bf16[256,256]{1,0:T(8,128)(2,1)S(1)} %get-tuple-element.27.row_ref), custom_call_target="tpu_custom_call" | custom-call | flops 1000000000 | bytes 10000000 | tf_op jit(solution)/shard_map/own_rows/pallas_call | solution.py:359
  17.0 0.0 collective-permute-done.3.edge_ref
  17.0 0.8 %shard_map.98 = bf16[64,2048]{1,0:T(8,128)(2,1)S(1)} custom-call(s32[1]{0:T(128)S(6)} %sub.4.side_ref, bf16[40,4096]{1,0:T(8,128)(2,1)S(1)} %collective-permute-done.3.edge_ref, bf16[256,1024]{1,0:T(8,128)(2,1)S(1)} %get-tuple-element.23.column_ref, bf16[128,128]{1,0:T(8,128)(2,1)S(1)} %get-tuple-element.33.row_ref, f32[64,4096]{1,0:T(8,128)S(1)} %get-tuple-element.34.part_ref), custom_call_target="tpu_custom_call" | custom-call | tf_op jit(solution)/shard_map/pallas_call | solution.py:409
  17.8 0.6 %collective-permute-start.4 = (bf16[64,2048]{1,0:T(8,128)(2,1)S(1)}, bf16[64,2048]{1,0:T(8,128)(2,1)S(1)}, u32[]{:S(2)}, u32[]{:S(2)}) collective-permute-start(bf16[64,2048]{1,0:T(8,128)(2,1)S(1)} %shard_map.98), channel_id=1, source_target_pairs={{0,1},{1,0},{2,3},{3,2},{4,5},{5,4},{6,7},{7,6},{8,9},{9,8},{10,11... | collective-permute-start | bytes 786440 | tf_op jit(solution)/shard_map/ppermute | solution.py:621
  18.4 4.0 %collective-permute-done.edge_ref = bf16[40,4096]{1,0:T(8,128)(2,1)S(1)} collective-permute-done((bf16[40,4096]{1,0:T(8,128)(2,1)S(1)}, bf16[40,4096]{1,0:T(8,128)(2,1)S(1)}, u32[]{:S(2)}, u32[]{:S(2)}) %collective-permute-start) | collective-permute-done | bytes 327712 | tf_op jit(solution)/shard_map/ppermute | solution.py:616
  22.4 0.8 %shard_map.96 = bf16[64,2048]{1,0:T(8,128)(2,1)S(1)} custom-call(s32[1]{0:T(128)S(6)} %sub.4.side_ref, bf16[40,4096]{1,0:T(8,128)(2,1)S(1)} %collective-permute-done.edge_ref, bf16[256,1024]{1,0:T(8,128)(2,1)S(1)} %get-tuple-element.23.column_ref, bf16[128,128]{1,0:T(8,128)(2,1)S(1)} %get-tuple-element.24.row_ref, f32[64,4096]{1,0:T(8,128)S(1)} %get-tuple-element.28.part_ref), custom_call_target="tpu_custom_call" | custom-call | tf_op jit(solution)/shard_map/pallas_call | solution.py:409
  23.2 0.1 collective-permute-start.1
  23.2 0.8 %shard_map.95.refs_0_.refs_3_ = bf16[64,2048]{1,0:T(8,128)(2,1)S(1)} custom-call(s32[1]{0:T(128)} %bitcast.side_ref, bf16[40,4096]{1,0:T(8,128)(2,1)S(1)} %collective-permute-done.edge_ref, bf16[256,1024]{1,0:T(8,128)(2,1)S(1)} %get-tuple-element.23.column_ref, bf16[128,128]{1,0:T(8,128)(2,1)S(1)} %get-tuple-element.24.row_ref, ...), custom_call_target="tpu_custom_call" | custom-call | tf_op jit(solution)/shard_map/pallas_call | solution.py:409
  24.0 0.8 %shard_map.97.refs_0_ = bf16[64,2048]{1,0:T(8,128)(2,1)S(1)} custom-call(s32[1]{0:T(128)} %bitcast.side_ref, bf16[40,4096]{1,0:T(8,128)(2,1)S(1)} %collective-permute-done.3.edge_ref, bf16[256,1024]{1,0:T(8,128)(2,1)S(1)} %get-tuple-element.23.column_ref, bf16[128,128]{1,0:T(8,128)(2,1)S(1)} %get-tuple-element.33.row_ref, ...), custom_call_target="tpu_custom_call" | custom-call | tf_op jit(solution)/shard_map/pallas_call | solution.py:409
  24.8 0.0 collective-permute-done.2.refs_1_
  24.8 0.4 norms.1
  25.2 0.0 collective-permute-done.4.refs_1_
  25.3 0.5 %residual.1 = (f32[128,2048]{1,0:T(8,128)S(1)}, f32[64,128]{1,0:T(8,128)S(1)}) custom-call(s32[1]{0:T(128)} %bitcast.side_ref, bf16[64,2048]{1,0:T(8,128)(2,1)S(1)} %shard_map.97.refs_0_, bf16[64,2048]{1,0:T(8,128)(2,1)S(1)} %collective-permute-done.4.refs_1_, f32[256,2048]{1,0:T(8,128)S(1)} %get-tuple-element.30.refs_2_, ...), custom_call_target="tpu_custom_call" | custom-call | tf_op jit(solution)/shard_map/residual/pallas_call | solution.py:530
  25.8 0.0 collective-permute-done.1.refs_1_.refs_4_
  25.8 0.5 %residual_last.1 = (f32[128,2048]{1,0:T(8,128)S(1)}, f32[2,8,128]{2,1,0:T(8,128)S(1)}) custom-call(s32[1]{0:T(128)} %bitcast.side_ref, bf16[64,2048]{1,0:T(8,128)(2,1)S(1)} %shard_map.95.refs_0_.refs_3_, bf16[64,2048]{1,0:T(8,128)(2,1)S(1)} %collective-permute-done.1.refs_1_.refs_4_, f32[256,2048]{1,0:T(8,128)S(1)} %get-tuple-element.30.refs_2_, ...), custom_call_target="tpu_custom_call" | custom-call | tf_op jit(solution)/shard_map/residual_last/pallas_call | solution.py:530
  26.3 0.6 %collective-permute-start.5 = (f32[2,8,128]{2,1,0:T(8,128)S(1)}, f32[2,8,128]{2,1,0:T(8,128)S(1)}, u32[]{:S(2)}, u32[]{:S(2)}) collective-permute-start(f32[2,8,128]{2,1,0:T(8,128)S(1)} %get-tuple-element.37), channel_id=1, source_target_pairs={{0,1},{1,0},{2,3},{3,2},{4,5},{5,4},{6,7},{7,6},{8,9},{9,8},{10,11... | collective-permute-start | bytes 24584 | tf_op jit(solution)/shard_map/ppermute | solution.py:631
  26.9 0.8 %collective-permute-done.5 = f32[2,8,128]{2,1,0:T(8,128)S(1)} collective-permute-done((f32[2,8,128]{2,1,0:T(8,128)S(1)}, f32[2,8,128]{2,1,0:T(8,128)S(1)}, u32[]{:S(2)}, u32[]{:S(2)}) %collective-permute-start.5) | collective-permute-done | bytes 8224 | tf_op jit(solution)/shard_map/ppermute | solution.py:631
  27.7 2.3 %collective-permute-start.6 = (f32[2,8,128]{2,1,0:T(8,128)S(1)}, f32[2,8,128]{2,1,0:T(8,128)S(1)}, u32[]{:S(2)}, u32[]{:S(2)}) collective-permute-start(f32[2,8,128]{2,1,0:T(8,128)S(1)} %add.12), channel_id=1, source_target_pairs={{0,3},{1,2},{2,1},{3,0},{4,7},{5,6},{6,5},{7,4},{8,11},{9,10},{10,... | collective-permute-start | bytes 24584 | tf_op jit(solution)/shard_map/ppermute | solution.py:635
  30.1 1.4 %collective-permute-done.6 = f32[2,8,128]{2,1,0:T(8,128)S(1)} collective-permute-done((f32[2,8,128]{2,1,0:T(8,128)S(1)}, f32[2,8,128]{2,1,0:T(8,128)S(1)}, u32[]{:S(2)}, u32[]{:S(2)}) %collective-permute-start.6) | collective-permute-done | bytes 8224 | tf_op jit(solution)/shard_map/ppermute | solution.py:635
  31.4 1.5 %collective-permute-start.7 = (f32[2,8,128]{2,1,0:T(8,128)S(1)}, f32[2,8,128]{2,1,0:T(8,128)S(1)}, u32[]{:S(2)}, u32[]{:S(2)}) collective-permute-start(f32[2,8,128]{2,1,0:T(8,128)S(1)} %add.13), channel_id=1, source_target_pairs={{0,5},{1,4},{2,7},{3,6},{4,1},{5,0},{6,3},{7,2},{8,13},{9,12},{10,... | collective-permute-start | bytes 24584 | tf_op jit(solution)/shard_map/ppermute | solution.py:635
  32.9 1.6 %collective-permute-done.7 = f32[2,8,128]{2,1,0:T(8,128)S(1)} collective-permute-done((f32[2,8,128]{2,1,0:T(8,128)S(1)}, f32[2,8,128]{2,1,0:T(8,128)S(1)}, u32[]{:S(2)}, u32[]{:S(2)}) %collective-permute-start.7) | collective-permute-done | bytes 8224 | tf_op jit(solution)/shard_map/ppermute | solution.py:635
  34.5 2.5 %collective-permute-start.8 = (f32[2,8,128]{2,1,0:T(8,128)S(1)}, f32[2,8,128]{2,1,0:T(8,128)S(1)}, u32[]{:S(2)}, u32[]{:S(2)}) collective-permute-start(f32[2,8,128]{2,1,0:T(8,128)S(1)} %add.14), channel_id=1, source_target_pairs={{0,9},{1,8},{2,11},{3,10},{4,13},{5,12},{6,15},{7,14},{8,1},{9,0},... | collective-permute-start | bytes 24584 | tf_op jit(solution)/shard_map/ppermute | solution.py:635
  37.0 1.5 %collective-permute-done.8 = f32[2,8,128]{2,1,0:T(8,128)S(1)} collective-permute-done((f32[2,8,128]{2,1,0:T(8,128)S(1)}, f32[2,8,128]{2,1,0:T(8,128)S(1)}, u32[]{:S(2)}, u32[]{:S(2)}) %collective-permute-start.8) | collective-permute-done | bytes 8224 | tf_op jit(solution)/shard_map/ppermute | solution.py:635
  38.5 1.2 %final.1 = (f32[32,2048]{1,0:T(8,128)}, f32[4]{0:T(128)}) custom-call(s32[1]{0:T(128)} %bitcast.side_ref, f32[2,8,128]{2,1,0:T(8,128)S(1)} %add.15.sums_ref, bf16[64,2048]{1,0:T(8,128)(2,1)S(1)} %shard_map.97.refs_0_, bf16[64,2048]{1,0:T(8,128)(2,1)S(1)} %collective-permute-done.4.refs_1_, f32[128,2048]{1,0:T(8,128)S(1)} %get-tuple-element.38.refs_2_, ...), custom_call_target="tpu_custom_call" | custom-call | tf_op jit(solution)/shard_map/final/pallas_call | solution.py:583
  (4 shorter events, 0.0 us)
Async XLA Ops:
  2.0 9.6 %copy-start = (f32[16,8]{0,1:T(8,128)S(1)}, f32[16,8]{0,1:T(8,128)}, u32[]{:S(2)}) copy-start(f32[16,8]{0,1:T(8,128)} %param.13) | copy-start | bytes 1540
  2.0 9.6 %copy-start.1 = (bf16[8,21]{1,0:T(8,128)(2,1)S(1)}, bf16[8,21]{1,0:T(8,128)(2,1)}, u32[]{:S(2)}) copy-start(bf16[8,21]{1,0:T(8,128)(2,1)} %row_ref.1) | copy-start | bytes 1012
  2.0 9.6 %copy-start.2 = (bf16[8,21]{1,0:T(8,128)(2,1)S(1)}, bf16[8,21]{1,0:T(8,128)(2,1)}, u32[]{:S(2)}) copy-start(bf16[8,21]{1,0:T(8,128)(2,1)} %col_ref.1) | copy-start | bytes 1012
  2.0 9.6 %copy-start.3 = (s32[4]{0:T(128)S(1)}, s32[4]{0:T(128)}, u32[]{:S(2)}) copy-start(s32[4]{0:T(128)} %index_ref.1) | copy-start | bytes 52
  2.1 14.9 %collective-permute-start.3 = (bf16[40,4096]{1,0:T(8,128)(2,1)S(1)}, bf16[40,4096]{1,0:T(8,128)(2,1)S(1)}, u32[]{:S(2)}, u32[]{:S(2)}) collective-permute-start(bf16[40,4096]{1,0:T(8,128)(2,1)S(1)} %get-tuple-element.32), channel_id=1, source_target_pairs={{0,2},{2,4},{4,6},{6,8},{8,10},{10,12},{12,14},{1,3},{3,5},{5,7},{... | collective-permute-start | bytes 983048 | tf_op jit(solution)/shard_map/ppermute | solution.py:611
  8.9 16.0 %collective-permute-start.2 = (bf16[144,2048]{1,0:T(8,128)(2,1)S(1)}, bf16[144,2048]{1,0:T(8,128)(2,1)S(1)}, u32[]{:S(2)}, u32[]{:S(2)}) collective-permute-start(bf16[144,2048]{1,0:T(8,128)(2,1)S(1)} %get-tuple-element.21.refs_0_), channel_id=1, source_target_pairs={{0,1},{1,0},{2,3},{3,2},{4,5},{5,4},{6,7},{7,6},{8,9},{9,8},{10,11... | collective-permute-start | bytes 1769480 | tf_op jit(solution)/shard_map/ppermute | solution.py:613
  10.3 12.0 %collective-permute-start = (bf16[40,4096]{1,0:T(8,128)(2,1)S(1)}, bf16[40,4096]{1,0:T(8,128)(2,1)S(1)}, u32[]{:S(2)}, u32[]{:S(2)}) collective-permute-start(bf16[40,4096]{1,0:T(8,128)(2,1)S(1)} %get-tuple-element.22), channel_id=1, source_target_pairs={{2,0},{4,2},{6,4},{8,6},{10,8},{12,10},{14,12},{3,1},{5,3},{7,5},{... | collective-permute-start | bytes 983048 | tf_op jit(solution)/shard_map/ppermute | solution.py:616
  17.8 7.4 %collective-permute-start.4 = (bf16[64,2048]{1,0:T(8,128)(2,1)S(1)}, bf16[64,2048]{1,0:T(8,128)(2,1)S(1)}, u32[]{:S(2)}, u32[]{:S(2)}) collective-permute-start(bf16[64,2048]{1,0:T(8,128)(2,1)S(1)} %shard_map.98), channel_id=1, source_target_pairs={{0,1},{1,0},{2,3},{3,2},{4,5},{5,4},{6,7},{7,6},{8,9},{9,8},{10,11... | collective-permute-start | bytes 786440 | tf_op jit(solution)/shard_map/ppermute | solution.py:621
  23.2 2.6 %collective-permute-start.1 = (bf16[64,2048]{1,0:T(8,128)(2,1)S(1)}, bf16[64,2048]{1,0:T(8,128)(2,1)S(1)}, u32[]{:S(2)}, u32[]{:S(2)}) collective-permute-start(bf16[64,2048]{1,0:T(8,128)(2,1)S(1)} %shard_map.96), channel_id=1, source_target_pairs={{0,1},{1,0},{2,3},{3,2},{4,5},{5,4},{6,7},{7,6},{8,9},{9,8},{10,11... | collective-permute-start | bytes 786440 | tf_op jit(solution)/shard_map/ppermute | solution.py:626
  26.3 1.4 %collective-permute-start.5 = (f32[2,8,128]{2,1,0:T(8,128)S(1)}, f32[2,8,128]{2,1,0:T(8,128)S(1)}, u32[]{:S(2)}, u32[]{:S(2)}) collective-permute-start(f32[2,8,128]{2,1,0:T(8,128)S(1)} %get-tuple-element.37), channel_id=1, source_target_pairs={{0,1},{1,0},{2,3},{3,2},{4,5},{5,4},{6,7},{7,6},{8,9},{9,8},{10,11... | collective-permute-start | bytes 24584 | tf_op jit(solution)/shard_map/ppermute | solution.py:631
  27.7 3.7 %collective-permute-start.6 = (f32[2,8,128]{2,1,0:T(8,128)S(1)}, f32[2,8,128]{2,1,0:T(8,128)S(1)}, u32[]{:S(2)}, u32[]{:S(2)}) collective-permute-start(f32[2,8,128]{2,1,0:T(8,128)S(1)} %add.12), channel_id=1, source_target_pairs={{0,3},{1,2},{2,1},{3,0},{4,7},{5,6},{6,5},{7,4},{8,11},{9,10},{10,... | collective-permute-start | bytes 24584 | tf_op jit(solution)/shard_map/ppermute | solution.py:635
  31.4 3.1 %collective-permute-start.7 = (f32[2,8,128]{2,1,0:T(8,128)S(1)}, f32[2,8,128]{2,1,0:T(8,128)S(1)}, u32[]{:S(2)}, u32[]{:S(2)}) collective-permute-start(f32[2,8,128]{2,1,0:T(8,128)S(1)} %add.13), channel_id=1, source_target_pairs={{0,5},{1,4},{2,7},{3,6},{4,1},{5,0},{6,3},{7,2},{8,13},{9,12},{10,... | collective-permute-start | bytes 24584 | tf_op jit(solution)/shard_map/ppermute | solution.py:635
  34.5 4.0 %collective-permute-start.8 = (f32[2,8,128]{2,1,0:T(8,128)S(1)}, f32[2,8,128]{2,1,0:T(8,128)S(1)}, u32[]{:S(2)}, u32[]{:S(2)}) collective-permute-start(f32[2,8,128]{2,1,0:T(8,128)S(1)} %add.14), channel_id=1, source_target_pairs={{0,9},{1,8},{2,11},{3,10},{4,13},{5,12},{6,15},{7,14},{8,1},{9,0},... | collective-permute-start | bytes 24584 | tf_op jit(solution)/shard_map/ppermute | solution.py:635

commit v11 on v10

--- a/solution.py
+++ b/solution.py
@@ -598,6 +598,11 @@
     )(side, *kept(sums, *upper, *lower))
 
 
+def partners(strips, step, crossing):
+    turn = 1 if crossing else 0
+    return [(2 * i + v, 2 * (i ^ step) + (v ^ turn)) for i in range(strips) for v in (0, 1)]
+
+
 def per_device(warps, badbits, coverage, variance, psf_index, psf_table, row_basis, col_basis):
     visits, rows, columns = warps.shape
     half = row_basis.shape[1] // 2
@@ -628,12 +633,18 @@
     factors, sums = residual_pass(
         side, (own_value, other_value), weights, inverse, visits, rows // 2, chi, counts
     )
-    sums = sums + lax.ppermute(sums, "visit", swap)
     step = 1
     while step < strips:
-        pairs = [(2 * i + v, 2 * (i ^ step) + 1 - v) for i in range(strips) for v in (0, 1)]
-        sums = sums + lax.ppermute(sums, ("sky", "visit"), pairs)
-        step *= 2
+        crossing = lax.ppermute(sums, ("sky", "visit"), partners(strips, step, True))
+        if 4 * step <= strips:
+            second = lax.ppermute(sums, ("sky", "visit"), partners(strips, 2 * step, True))
+            third = lax.ppermute(sums, ("sky", "visit"), partners(strips, 3 * step, False))
+            sums = (sums + crossing) + (second + third)
+            step *= 4
+        else:
+            sums = sums + crossing
+            step *= 2
+    sums = sums + lax.ppermute(sums, "visit", swap)
     upper = (own_top, other_top, top_factors)
     return final_pass(side, sums, upper, (own_value, other_value, factors), visits)
 

time: 40 us -> 39.8 us (level)
    ppermute x3 -> x4, waiting for transfers between devices: 4.44 us -> 4.46 us  [the longest x2 1.75 us: per_device(): lax.ppermute(sums, ('sky', 'visit'), partners(strips, step, True))]
    ppermute x3 -> x4, starting transfers between devices: 6.32 us -> 6.33 us  [the longest x1 3.47 us: per_device(): lax.ppermute(sums, ('sky', 'visit'), partners(strips, 3 * step, False))]
  transfers between devices with their start and end apart: 9 -> 10, of which waited for: 5 -> 6; matrix products, arithmetic and copies ran while one was open for 0% -> 0% of each run, Pallas kernels for 32% -> 32%
where the time goes in v11:
time: 39.8 us; the launch traced here: 39.5 us
  Pallas kernels  15.7 us (39%)
  starting transfers between devices  13.7 us (34%)
  waiting for transfers between devices  9.32 us (23%)
  between operations  0.81 us (2%)
    ppermute x1, starting transfers between devices, per_device(): before = lax.ppermute(last, 'sky', up)  5.05 us
    pallas_call x1, Pallas kernels, own_part(): pl.pallas_call(functools.partial(own_kernel, visits), out_shape=(held((ha...  3.99 us
    ppermute x1, waiting for transfers between devices, per_device(): after = lax.ppermute(leading, 'sky', down)  3.98 us
    ppermute x1, starting transfers between devices, per_device(): lax.ppermute(sums, ('sky', 'visit'), partners(strips, 3 * step, False))  3.47 us
    pallas_call x4, Pallas kernels, rim_part(): pl.pallas_call(functools.partial(rim_kernel, visits, half), out_shape=hel...  3.21 us
    pallas_call x2, Pallas kernels, pack_rows(): pl.pallas_call(functools.partial(pack_kernel, half, first, skip), out_sha...  2.75 us
    ppermute x2, starting transfers between devices, per_device(): lax.ppermute(sums, ('sky', 'visit'), partners(strips, step, True))  2.59 us
    ppermute x2, waiting for transfers between devices, per_device(): lax.ppermute(sums, ('sky', 'visit'), partners(strips, step, True))  1.75 us
  transfers between devices with their start and end apart: 10, of which 6 were waited for; matrix products, arithmetic and copies ran while one was open for 0% of the time, Pallas kernels for 32%

profile of v11, /device:TPU:0, one launch (start us, length us, event | category | flops | bytes accessed | tf_op | source)
XLA Modules:
  0.0 39.5 jit_solution(12231890234803244608)
XLA Ops:
  0.6 1.4 %pack_lower.1 = (bf16[40,4096]{1,0:T(8,128)(2,1)S(1)}, bf16[4,16,4096]{2,1,0:T(8,128)(2,1)S(1)}) custom-call(bf16[4,32,4096]{2,1,0:T(8,128)(2,1)} %x_ref.3), custom_call_target="tpu_custom_call" | custom-call | tf_op jit(solution)/shard_map/pack_lower/pallas_call | solution.py:98
  2.0 0.0 copy-start
  2.0 0.0 copy-start.1
  2.0 0.0 copy-start.2
  2.0 0.0 copy-start.3
  2.1 5.1 %collective-permute-start.3 = (bf16[40,4096]{1,0:T(8,128)(2,1)S(1)}, bf16[40,4096]{1,0:T(8,128)(2,1)S(1)}, u32[]{:S(2)}, u32[]{:S(2)}) collective-permute-start(bf16[40,4096]{1,0:T(8,128)(2,1)S(1)} %get-tuple-element.32), channel_id=1, source_target_pairs={{0,2},{2,4},{4,6},{6,8},{8,10},{10,12},{12,14},{1,3},{3,5},{5,7},{... | collective-permute-start | bytes 983048 | tf_op jit(solution)/shard_map/ppermute | solution.py:616
  7.1 1.7 %weights.1 = (bf16[144,2048]{1,0:T(8,128)(2,1)S(1)}, bf16[144,2048]{1,0:T(8,128)(2,1)S(1)}) custom-call(s32[1]{0:T(128)} %bitcast.side_ref, s32[1,4]{1,0:T(1,128)} %bitcast.11, f32[1,4]{1,0:T(1,128)} %bitcast.12, s32[128,4096]{1,0:T(8,128)} %bitcast.10), custom_call_target="tpu_custom_call" | custom-call | tf_op jit(solution)/shard_map/weights/pallas_call | solution.py:159
  8.9 0.1 collective-permute-start.2
  9.0 1.4 %pack_upper.1 = (bf16[40,4096]{1,0:T(8,128)(2,1)S(1)}, bf16[4,16,4096]{2,1,0:T(8,128)(2,1)S(1)}) custom-call(bf16[4,32,4096]{2,1,0:T(8,128)(2,1)} %x_ref.3, bf16[144,2048]{1,0:T(8,128)(2,1)S(1)} %get-tuple-element.21.refs_0_), custom_call_target="tpu_custom_call" | custom-call | tf_op jit(solution)/shard_map/pack_upper/pallas_call | solution.py:98
  10.3 1.3 %collective-permute-start = (bf16[40,4096]{1,0:T(8,128)(2,1)S(1)}, bf16[40,4096]{1,0:T(8,128)(2,1)S(1)}, u32[]{:S(2)}, u32[]{:S(2)}) collective-permute-start(bf16[40,4096]{1,0:T(8,128)(2,1)S(1)} %get-tuple-element.22), channel_id=1, source_target_pairs={{2,0},{4,2},{6,4},{8,6},{10,8},{12,10},{14,12},{3,1},{5,3},{7,5},{... | collective-permute-start | bytes 983048 | tf_op jit(solution)/shard_map/ppermute | solution.py:621
  11.6 0.0 copy-done
  11.7 0.0 copy-done.1
  11.7 0.0 copy-done.2
  11.7 0.0 copy-done.3
  11.7 1.3 %tables.1 = (bf16[256,1024]{1,0:T(8,128)(2,1)S(1)}, bf16[256,256]{1,0:T(8,128)(2,1)S(1)}, bf16[128,128]{1,0:T(8,128)(2,1)S(1)}, bf16[128,128]{1,0:T(8,128)(2,1)S(1)}) custom-call(s32[4]{0:T(128)S(1)} %copy-done.3, f32[8,16]{1,0:T(8,128)S(1)} %bitcast.7, bf16[8,21]{1,0:T(8,128)(2,1)S(1)} %copy-done.1, bf16[8,21]{1,0:T(8,128)(2,1)S(1)} %copy-done.2), custom_call_target="tpu_custom_call" | custom-call | tf_op jit(solution)/shard_map/tables/pallas_call | solution.py:257
  13.0 4.0 %own_rows.1 = (f32[64,4096]{1,0:T(8,128)S(1)}, f32[64,4096]{1,0:T(8,128)S(1)}) custom-call(bf16[64,4096]{1,0:T(8,128)(2,1)S(1)} %bitcast.9, bf16[64,4096]{1,0:T(8,128)(2,1)S(1)} %bitcast.8, bf16[256,1024]{1,0:T(8,128)(2,1)S(1)} %get-tuple-element.23.column_ref, bf16[256,256]{1,0:T(8,128)(2,1)S(1)} %get-tuple-element.27.row_ref), custom_call_target="tpu_custom_call" | custom-call | flops 1000000000 | bytes 10000000 | tf_op jit(solution)/shard_map/own_rows/pallas_call | solution.py:359
  17.0 0.0 collective-permute-done.3.edge_ref
  17.0 0.8 %shard_map.98 = bf16[64,2048]{1,0:T(8,128)(2,1)S(1)} custom-call(s32[1]{0:T(128)S(6)} %sub.4.side_ref, bf16[40,4096]{1,0:T(8,128)(2,1)S(1)} %collective-permute-done.3.edge_ref, bf16[256,1024]{1,0:T(8,128)(2,1)S(1)} %get-tuple-element.23.column_ref, bf16[128,128]{1,0:T(8,128)(2,1)S(1)} %get-tuple-element.33.row_ref, f32[64,4096]{1,0:T(8,128)S(1)} %get-tuple-element.34.part_ref), custom_call_target="tpu_custom_call" | custom-call | tf_op jit(solution)/shard_map/pallas_call | solution.py:409
  17.8 0.6 %collective-permute-start.4 = (bf16[64,2048]{1,0:T(8,128)(2,1)S(1)}, bf16[64,2048]{1,0:T(8,128)(2,1)S(1)}, u32[]{:S(2)}, u32[]{:S(2)}) collective-permute-start(bf16[64,2048]{1,0:T(8,128)(2,1)S(1)} %shard_map.98), channel_id=1, source_target_pairs={{0,1},{1,0},{2,3},{3,2},{4,5},{5,4},{6,7},{7,6},{8,9},{9,8},{10,11... | collective-permute-start | bytes 786440 | tf_op jit(solution)/shard_map/ppermute | solution.py:626
  18.4 4.0 %collective-permute-done.edge_ref = bf16[40,4096]{1,0:T(8,128)(2,1)S(1)} collective-permute-done((bf16[40,4096]{1,0:T(8,128)(2,1)S(1)}, bf16[40,4096]{1,0:T(8,128)(2,1)S(1)}, u32[]{:S(2)}, u32[]{:S(2)}) %collective-permute-start) | collective-permute-done | bytes 327712 | tf_op jit(solution)/shard_map/ppermute | solution.py:621
  22.4 0.8 %shard_map.96 = bf16[64,2048]{1,0:T(8,128)(2,1)S(1)} custom-call(s32[1]{0:T(128)S(6)} %sub.4.side_ref, bf16[40,4096]{1,0:T(8,128)(2,1)S(1)} %collective-permute-done.edge_ref, bf16[256,1024]{1,0:T(8,128)(2,1)S(1)} %get-tuple-element.23.column_ref, bf16[128,128]{1,0:T(8,128)(2,1)S(1)} %get-tuple-element.24.row_ref, f32[64,4096]{1,0:T(8,128)S(1)} %get-tuple-element.28.part_ref), custom_call_target="tpu_custom_call" | custom-call | tf_op jit(solution)/shard_map/pallas_call | solution.py:409
  23.2 0.1 collective-permute-start.1
  23.2 0.8 %shard_map.95.refs_0_.refs_3_ = bf16[64,2048]{1,0:T(8,128)(2,1)S(1)} custom-call(s32[1]{0:T(128)} %bitcast.side_ref, bf16[40,4096]{1,0:T(8,128)(2,1)S(1)} %collective-permute-done.edge_ref, bf16[256,1024]{1,0:T(8,128)(2,1)S(1)} %get-tuple-element.23.column_ref, bf16[128,128]{1,0:T(8,128)(2,1)S(1)} %get-tuple-element.24.row_ref, ...), custom_call_target="tpu_custom_call" | custom-call | tf_op jit(solution)/shard_map/pallas_call | solution.py:409
  24.0 0.8 %shard_map.97.refs_0_ = bf16[64,2048]{1,0:T(8,128)(2,1)S(1)} custom-call(s32[1]{0:T(128)} %bitcast.side_ref, bf16[40,4096]{1,0:T(8,128)(2,1)S(1)} %collective-permute-done.3.edge_ref, bf16[256,1024]{1,0:T(8,128)(2,1)S(1)} %get-tuple-element.23.column_ref, bf16[128,128]{1,0:T(8,128)(2,1)S(1)} %get-tuple-element.33.row_ref, ...), custom_call_target="tpu_custom_call" | custom-call | tf_op jit(solution)/shard_map/pallas_call | solution.py:409
  24.8 0.0 collective-permute-done.2.refs_1_
  24.8 0.4 norms.1
  25.2 0.0 collective-permute-done.4.refs_1_
  25.3 0.5 %residual.1 = (f32[128,2048]{1,0:T(8,128)S(1)}, f32[64,128]{1,0:T(8,128)S(1)}) custom-call(s32[1]{0:T(128)} %bitcast.side_ref, bf16[64,2048]{1,0:T(8,128)(2,1)S(1)} %shard_map.97.refs_0_, bf16[64,2048]{1,0:T(8,128)(2,1)S(1)} %collective-permute-done.4.refs_1_, f32[256,2048]{1,0:T(8,128)S(1)} %get-tuple-element.30.refs_2_, ...), custom_call_target="tpu_custom_call" | custom-call | tf_op jit(solution)/shard_map/residual/pallas_call | solution.py:530
  25.8 0.0 collective-permute-done.1.refs_1_.refs_4_
  25.8 0.5 %residual_last.1 = (f32[128,2048]{1,0:T(8,128)S(1)}, f32[2,8,128]{2,1,0:T(8,128)S(1)}) custom-call(s32[1]{0:T(128)} %bitcast.side_ref, bf16[64,2048]{1,0:T(8,128)(2,1)S(1)} %shard_map.95.refs_0_.refs_3_, bf16[64,2048]{1,0:T(8,128)(2,1)S(1)} %collective-permute-done.1.refs_1_.refs_4_, f32[256,2048]{1,0:T(8,128)S(1)} %get-tuple-element.30.refs_2_, ...), custom_call_target="tpu_custom_call" | custom-call | tf_op jit(solution)/shard_map/residual_last/pallas_call | solution.py:530
  26.3 3.5 %collective-permute-start.7 = (f32[2,8,128]{2,1,0:T(8,128)S(1)}, f32[2,8,128]{2,1,0:T(8,128)S(1)}, u32[]{:S(2)}, u32[]{:S(2)}) collective-permute-start(f32[2,8,128]{2,1,0:T(8,128)S(1)} %get-tuple-element.37), channel_id=1, source_target_pairs={{0,6},{1,7},{2,4},{3,5},{4,2},{5,3},{6,0},{7,1},{8,14},{9,15},{10,... | collective-permute-start | bytes 24584 | tf_op jit(solution)/shard_map/ppermute | solution.py:641
  29.8 0.3 collective-permute-start.6
  30.1 0.1 collective-permute-start.5
  30.2 1.3 %collective-permute-done.7 = f32[2,8,128]{2,1,0:T(8,128)S(1)} collective-permute-done((f32[2,8,128]{2,1,0:T(8,128)S(1)}, f32[2,8,128]{2,1,0:T(8,128)S(1)}, u32[]{:S(2)}, u32[]{:S(2)}) %collective-permute-start.7) | collective-permute-done | bytes 8224 | tf_op jit(solution)/shard_map/ppermute | solution.py:641
  31.4 1.4 %collective-permute-done.6 = f32[2,8,128]{2,1,0:T(8,128)S(1)} collective-permute-done((f32[2,8,128]{2,1,0:T(8,128)S(1)}, f32[2,8,128]{2,1,0:T(8,128)S(1)}, u32[]{:S(2)}, u32[]{:S(2)}) %collective-permute-start.6) | collective-permute-done | bytes 8224 | tf_op jit(solution)/shard_map/ppermute | solution.py:640
  32.9 0.3 collective-permute-done.5
  33.1 2.5 %collective-permute-start.8 = (f32[2,8,128]{2,1,0:T(8,128)S(1)}, f32[2,8,128]{2,1,0:T(8,128)S(1)}, u32[]{:S(2)}, u32[]{:S(2)}) collective-permute-start(f32[2,8,128]{2,1,0:T(8,128)S(1)} %add_add_fusion), channel_id=1, source_target_pairs={{0,9},{1,8},{2,11},{3,10},{4,13},{5,12},{6,15},{7,14},{8,1},{9,0},... | collective-permute-start | bytes 24584 | tf_op jit(solution)/shard_map/ppermute | solution.py:638
  35.6 1.5 %collective-permute-done.8 = f32[2,8,128]{2,1,0:T(8,128)S(1)} collective-permute-done((f32[2,8,128]{2,1,0:T(8,128)S(1)}, f32[2,8,128]{2,1,0:T(8,128)S(1)}, u32[]{:S(2)}, u32[]{:S(2)}) %collective-permute-start.8) | collective-permute-done | bytes 8224 | tf_op jit(solution)/shard_map/ppermute | solution.py:638
  37.1 0.3 collective-permute-start.9
  37.4 0.9 %collective-permute-done.9 = f32[2,8,128]{2,1,0:T(8,128)S(1)} collective-permute-done((f32[2,8,128]{2,1,0:T(8,128)S(1)}, f32[2,8,128]{2,1,0:T(8,128)S(1)}, u32[]{:S(2)}, u32[]{:S(2)}) %collective-permute-start.9) | collective-permute-done | bytes 8224 | tf_op jit(solution)/shard_map/ppermute | solution.py:647
  38.3 1.2 %final.1 = (f32[32,2048]{1,0:T(8,128)}, f32[4]{0:T(128)}) custom-call(s32[1]{0:T(128)} %bitcast.side_ref, f32[2,8,128]{2,1,0:T(8,128)S(1)} %add.19.sums_ref, bf16[64,2048]{1,0:T(8,128)(2,1)S(1)} %shard_map.97.refs_0_, bf16[64,2048]{1,0:T(8,128)(2,1)S(1)} %collective-permute-done.4.refs_1_, f32[128,2048]{1,0:T(8,128)S(1)} %get-tuple-element.38.refs_2_, ...), custom_call_target="tpu_custom_call" | custom-call | tf_op jit(solution)/shard_map/final/pallas_call | solution.py:583
  (3 shorter events, 0.0 us)
Async XLA Ops:
  2.0 9.6 %copy-start = (f32[16,8]{0,1:T(8,128)S(1)}, f32[16,8]{0,1:T(8,128)}, u32[]{:S(2)}) copy-start(f32[16,8]{0,1:T(8,128)} %param.13) | copy-start | bytes 1540
  2.0 9.6 %copy-start.1 = (bf16[8,21]{1,0:T(8,128)(2,1)S(1)}, bf16[8,21]{1,0:T(8,128)(2,1)}, u32[]{:S(2)}) copy-start(bf16[8,21]{1,0:T(8,128)(2,1)} %row_ref.1) | copy-start | bytes 1012
  2.0 9.6 %copy-start.2 = (bf16[8,21]{1,0:T(8,128)(2,1)S(1)}, bf16[8,21]{1,0:T(8,128)(2,1)}, u32[]{:S(2)}) copy-start(bf16[8,21]{1,0:T(8,128)(2,1)} %col_ref.1) | copy-start | bytes 1012
  2.0 9.6 %copy-start.3 = (s32[4]{0:T(128)S(1)}, s32[4]{0:T(128)}, u32[]{:S(2)}) copy-start(s32[4]{0:T(128)} %index_ref.1) | copy-start | bytes 52
  2.1 14.9 %collective-permute-start.3 = (bf16[40,4096]{1,0:T(8,128)(2,1)S(1)}, bf16[40,4096]{1,0:T(8,128)(2,1)S(1)}, u32[]{:S(2)}, u32[]{:S(2)}) collective-permute-start(bf16[40,4096]{1,0:T(8,128)(2,1)S(1)} %get-tuple-element.32), channel_id=1, source_target_pairs={{0,2},{2,4},{4,6},{6,8},{8,10},{10,12},{12,14},{1,3},{3,5},{5,7},{... | collective-permute-start | bytes 983048 | tf_op jit(solution)/shard_map/ppermute | solution.py:616
  8.9 16.0 %collective-permute-start.2 = (bf16[144,2048]{1,0:T(8,128)(2,1)S(1)}, bf16[144,2048]{1,0:T(8,128)(2,1)S(1)}, u32[]{:S(2)}, u32[]{:S(2)}) collective-permute-start(bf16[144,2048]{1,0:T(8,128)(2,1)S(1)} %get-tuple-element.21.refs_0_), channel_id=1, source_target_pairs={{0,1},{1,0},{2,3},{3,2},{4,5},{5,4},{6,7},{7,6},{8,9},{9,8},{10,11... | collective-permute-start | bytes 1769480 | tf_op jit(solution)/shard_map/ppermute | solution.py:618
  10.3 12.0 %collective-permute-start = (bf16[40,4096]{1,0:T(8,128)(2,1)S(1)}, bf16[40,4096]{1,0:T(8,128)(2,1)S(1)}, u32[]{:S(2)}, u32[]{:S(2)}) collective-permute-start(bf16[40,4096]{1,0:T(8,128)(2,1)S(1)} %get-tuple-element.22), channel_id=1, source_target_pairs={{2,0},{4,2},{6,4},{8,6},{10,8},{12,10},{14,12},{3,1},{5,3},{7,5},{... | collective-permute-start | bytes 983048 | tf_op jit(solution)/shard_map/ppermute | solution.py:621
  17.8 7.4 %collective-permute-start.4 = (bf16[64,2048]{1,0:T(8,128)(2,1)S(1)}, bf16[64,2048]{1,0:T(8,128)(2,1)S(1)}, u32[]{:S(2)}, u32[]{:S(2)}) collective-permute-start(bf16[64,2048]{1,0:T(8,128)(2,1)S(1)} %shard_map.98), channel_id=1, source_target_pairs={{0,1},{1,0},{2,3},{3,2},{4,5},{5,4},{6,7},{7,6},{8,9},{9,8},{10,11... | collective-permute-start | bytes 786440 | tf_op jit(solution)/shard_map/ppermute | solution.py:626
  23.2 2.6 %collective-permute-start.1 = (bf16[64,2048]{1,0:T(8,128)(2,1)S(1)}, bf16[64,2048]{1,0:T(8,128)(2,1)S(1)}, u32[]{:S(2)}, u32[]{:S(2)}) collective-permute-start(bf16[64,2048]{1,0:T(8,128)(2,1)S(1)} %shard_map.96), channel_id=1, source_target_pairs={{0,1},{1,0},{2,3},{3,2},{4,5},{5,4},{6,7},{7,6},{8,9},{9,8},{10,11... | collective-permute-start | bytes 786440 | tf_op jit(solution)/shard_map/ppermute | solution.py:631
  26.3 5.1 %collective-permute-start.7 = (f32[2,8,128]{2,1,0:T(8,128)S(1)}, f32[2,8,128]{2,1,0:T(8,128)S(1)}, u32[]{:S(2)}, u32[]{:S(2)}) collective-permute-start(f32[2,8,128]{2,1,0:T(8,128)S(1)} %get-tuple-element.37), channel_id=1, source_target_pairs={{0,6},{1,7},{2,4},{3,5},{4,2},{5,3},{6,0},{7,1},{8,14},{9,15},{10,... | collective-permute-start | bytes 24584 | tf_op jit(solution)/shard_map/ppermute | solution.py:641
  29.8 3.1 %collective-permute-start.6 = (f32[2,8,128]{2,1,0:T(8,128)S(1)}, f32[2,8,128]{2,1,0:T(8,128)S(1)}, u32[]{:S(2)}, u32[]{:S(2)}) collective-permute-start(f32[2,8,128]{2,1,0:T(8,128)S(1)} %get-tuple-element.37), channel_id=1, source_target_pairs={{0,5},{1,4},{2,7},{3,6},{4,1},{5,0},{6,3},{7,2},{8,13},{9,12},{10,... | collective-permute-start | bytes 24584 | tf_op jit(solution)/shard_map/ppermute | solution.py:640
  30.1 3.1 %collective-permute-start.5 = (f32[2,8,128]{2,1,0:T(8,128)S(1)}, f32[2,8,128]{2,1,0:T(8,128)S(1)}, u32[]{:S(2)}, u32[]{:S(2)}) collective-permute-start(f32[2,8,128]{2,1,0:T(8,128)S(1)} %get-tuple-element.37), channel_id=1, source_target_pairs={{0,3},{1,2},{2,1},{3,0},{4,7},{5,6},{6,5},{7,4},{8,11},{9,10},{10,... | collective-permute-start | bytes 24584 | tf_op jit(solution)/shard_map/ppermute | solution.py:638
  33.1 4.0 %collective-permute-start.8 = (f32[2,8,128]{2,1,0:T(8,128)S(1)}, f32[2,8,128]{2,1,0:T(8,128)S(1)}, u32[]{:S(2)}, u32[]{:S(2)}) collective-permute-start(f32[2,8,128]{2,1,0:T(8,128)S(1)} %add_add_fusion), channel_id=1, source_target_pairs={{0,9},{1,8},{2,11},{3,10},{4,13},{5,12},{6,15},{7,14},{8,1},{9,0},... | collective-permute-start | bytes 24584 | tf_op jit(solution)/shard_map/ppermute | solution.py:638
  37.1 1.2 %collective-permute-start.9 = (f32[2,8,128]{2,1,0:T(8,128)S(1)}, f32[2,8,128]{2,1,0:T(8,128)S(1)}, u32[]{:S(2)}, u32[]{:S(2)}) collective-permute-start(f32[2,8,128]{2,1,0:T(8,128)S(1)} %add.18), channel_id=1, source_target_pairs={{0,1},{1,0},{2,3},{3,2},{4,5},{5,4},{6,7},{7,6},{8,9},{9,8},{10,11... | collective-permute-start | bytes 24584 | tf_op jit(solution)/shard_map/ppermute | solution.py:647

commit v12 on v11

--- a/solution.py
+++ b/solution.py
@@ -558,9 +558,10 @@
     chi_copy.start()
     scales = [jnp.broadcast_to(scale[m : m + 1], (high, LANES)) for m in range(2 * visits)]
     depth = rows // 2
-    for lane in range(0, width, LANES):
-        lanes = slice(lane, lane + LANES)
-        for top, part in zip((0, depth), parts):
+    copies = []
+    for k, part in enumerate(parts):
+        for lane in range(0, width, LANES):
+            lanes = slice(lane, lane + LANES)
             for row in range(0, depth, high):
                 numer = denom = None
                 for m in range(2 * visits):
@@ -570,11 +571,16 @@
                     revised = part[2][at : at + high, lanes] * scales[m]
                     numer = revised * value if numer is None else numer + revised * value
                     denom = revised if denom is None else denom + revised
-                done[top + row : top + row + high, lanes] = numer / (denom + PRIOR_WEIGHT)
-    copy = pltpu.make_async_copy(done, out_ref, sent.at[0])
-    copy.start()
+                at = k * depth + row
+                done[at : at + high, lanes] = numer / (denom + PRIOR_WEIGHT)
+        lines = slice(k * depth, (k + 1) * depth)
+        copies.append(
+            pltpu.make_async_copy(done.at[lines], out_ref.at[lines], sent.at[2 * k])
+        )
+        copies[k].start()
     chi_copy.wait()
-    copy.wait()
+    for copy in copies:
+        copy.wait()
 
 
 def final_pass(side, sums, upper, lower, visits):
@@ -591,7 +597,7 @@
         scratch_shapes=[
             pltpu.VMEM((rows, width), F32),
             pltpu.SMEM((visits,), F32),
-            pltpu.SemaphoreType.DMA((2,)),
+            pltpu.SemaphoreType.DMA((3,)),
         ],
         compiler_params=LIMIT,
         name="final",

time: 39.8 us -> 39.8 us (level)
  no operation moved by 1% of the time
where the time goes in v12:
time: 39.8 us; the launch traced here: 39.5 us
  Pallas kernels  15.6 us (39%)
  starting transfers between devices  13.7 us (34%)
  waiting for transfers between devices  9.32 us (23%)
  between operations  0.81 us (2%)
    ppermute x1, starting transfers between devices, per_device(): before = lax.ppermute(last, 'sky', up)  5.05 us
    pallas_call x1, Pallas kernels, own_part(): pl.pallas_call(functools.partial(own_kernel, visits), out_shape=(held((ha...  3.99 us
    ppermute x1, waiting for transfers between devices, per_device(): after = lax.ppermute(leading, 'sky', down)  3.98 us
    ppermute x1, starting transfers between devices, per_device(): lax.ppermute(sums, ('sky', 'visit'), partners(strips, 3 * step, False))  3.47 us
    pallas_call x4, Pallas kernels, rim_part(): pl.pallas_call(functools.partial(rim_kernel, visits, half), out_shape=hel...  3.21 us
    pallas_call x2, Pallas kernels, pack_rows(): pl.pallas_call(functools.partial(pack_kernel, half, first, skip), out_sha...  2.75 us
    ppermute x2, starting transfers between devices, per_device(): lax.ppermute(sums, ('sky', 'visit'), partners(strips, step, True))  2.59 us
    ppermute x2, waiting for transfers between devices, per_device(): lax.ppermute(sums, ('sky', 'visit'), partners(strips, step, True))  1.75 us
  transfers between devices with their start and end apart: 10, of which 6 were waited for; matrix products, arithmetic and copies ran while one was open for 0% of the time, Pallas kernels for 32%

profile of v12, /device:TPU:0, one launch (start us, length us, event | category | flops | bytes accessed | tf_op | source)
XLA Modules:
  0.0 39.5 jit_solution(17429675506309505441)
XLA Ops:
  0.6 1.4 %pack_lower.1 = (bf16[40,4096]{1,0:T(8,128)(2,1)S(1)}, bf16[4,16,4096]{2,1,0:T(8,128)(2,1)S(1)}) custom-call(bf16[4,32,4096]{2,1,0:T(8,128)(2,1)} %x_ref.3), custom_call_target="tpu_custom_call" | custom-call | tf_op jit(solution)/shard_map/pack_lower/pallas_call | solution.py:98
  2.0 0.0 copy-start
  2.0 0.0 copy-start.1
  2.0 0.0 copy-start.2
  2.0 0.0 copy-start.3
  2.1 5.1 %collective-permute-start.3 = (bf16[40,4096]{1,0:T(8,128)(2,1)S(1)}, bf16[40,4096]{1,0:T(8,128)(2,1)S(1)}, u32[]{:S(2)}, u32[]{:S(2)}) collective-permute-start(bf16[40,4096]{1,0:T(8,128)(2,1)S(1)} %get-tuple-element.32), channel_id=1, source_target_pairs={{0,2},{2,4},{4,6},{6,8},{8,10},{10,12},{12,14},{1,3},{3,5},{5,7},{... | collective-permute-start | bytes 983048 | tf_op jit(solution)/shard_map/ppermute | solution.py:622
  7.1 1.7 %weights.1 = (bf16[144,2048]{1,0:T(8,128)(2,1)S(1)}, bf16[144,2048]{1,0:T(8,128)(2,1)S(1)}) custom-call(s32[1]{0:T(128)} %bitcast.side_ref, s32[1,4]{1,0:T(1,128)} %bitcast.11, f32[1,4]{1,0:T(1,128)} %bitcast.12, s32[128,4096]{1,0:T(8,128)} %bitcast.10), custom_call_target="tpu_custom_call" | custom-call | tf_op jit(solution)/shard_map/weights/pallas_call | solution.py:159
  8.9 0.1 collective-permute-start.2
  9.0 1.4 %pack_upper.1 = (bf16[40,4096]{1,0:T(8,128)(2,1)S(1)}, bf16[4,16,4096]{2,1,0:T(8,128)(2,1)S(1)}) custom-call(bf16[4,32,4096]{2,1,0:T(8,128)(2,1)} %x_ref.3, bf16[144,2048]{1,0:T(8,128)(2,1)S(1)} %get-tuple-element.21.refs_0_), custom_call_target="tpu_custom_call" | custom-call | tf_op jit(solution)/shard_map/pack_upper/pallas_call | solution.py:98
  10.3 1.3 %collective-permute-start = (bf16[40,4096]{1,0:T(8,128)(2,1)S(1)}, bf16[40,4096]{1,0:T(8,128)(2,1)S(1)}, u32[]{:S(2)}, u32[]{:S(2)}) collective-permute-start(bf16[40,4096]{1,0:T(8,128)(2,1)S(1)} %get-tuple-element.22), channel_id=1, source_target_pairs={{2,0},{4,2},{6,4},{8,6},{10,8},{12,10},{14,12},{3,1},{5,3},{7,5},{... | collective-permute-start | bytes 983048 | tf_op jit(solution)/shard_map/ppermute | solution.py:627
  11.6 0.0 copy-done
  11.7 0.0 copy-done.1
  11.7 0.0 copy-done.2
  11.7 0.0 copy-done.3
  11.7 1.3 %tables.1 = (bf16[256,1024]{1,0:T(8,128)(2,1)S(1)}, bf16[256,256]{1,0:T(8,128)(2,1)S(1)}, bf16[128,128]{1,0:T(8,128)(2,1)S(1)}, bf16[128,128]{1,0:T(8,128)(2,1)S(1)}) custom-call(s32[4]{0:T(128)S(1)} %copy-done.3, f32[8,16]{1,0:T(8,128)S(1)} %bitcast.7, bf16[8,21]{1,0:T(8,128)(2,1)S(1)} %copy-done.1, bf16[8,21]{1,0:T(8,128)(2,1)S(1)} %copy-done.2), custom_call_target="tpu_custom_call" | custom-call | tf_op jit(solution)/shard_map/tables/pallas_call | solution.py:257
  13.0 4.0 %own_rows.1 = (f32[64,4096]{1,0:T(8,128)S(1)}, f32[64,4096]{1,0:T(8,128)S(1)}) custom-call(bf16[64,4096]{1,0:T(8,128)(2,1)S(1)} %bitcast.9, bf16[64,4096]{1,0:T(8,128)(2,1)S(1)} %bitcast.8, bf16[256,1024]{1,0:T(8,128)(2,1)S(1)} %get-tuple-element.23.column_ref, bf16[256,256]{1,0:T(8,128)(2,1)S(1)} %get-tuple-element.27.row_ref), custom_call_target="tpu_custom_call" | custom-call | flops 1000000000 | bytes 10000000 | tf_op jit(solution)/shard_map/own_rows/pallas_call | solution.py:359
  17.0 0.0 collective-permute-done.3.edge_ref
  17.0 0.8 %shard_map.98 = bf16[64,2048]{1,0:T(8,128)(2,1)S(1)} custom-call(s32[1]{0:T(128)S(6)} %sub.4.side_ref, bf16[40,4096]{1,0:T(8,128)(2,1)S(1)} %collective-permute-done.3.edge_ref, bf16[256,1024]{1,0:T(8,128)(2,1)S(1)} %get-tuple-element.23.column_ref, bf16[128,128]{1,0:T(8,128)(2,1)S(1)} %get-tuple-element.33.row_ref, f32[64,4096]{1,0:T(8,128)S(1)} %get-tuple-element.34.part_ref), custom_call_target="tpu_custom_call" | custom-call | tf_op jit(solution)/shard_map/pallas_call | solution.py:409
  17.8 0.6 %collective-permute-start.4 = (bf16[64,2048]{1,0:T(8,128)(2,1)S(1)}, bf16[64,2048]{1,0:T(8,128)(2,1)S(1)}, u32[]{:S(2)}, u32[]{:S(2)}) collective-permute-start(bf16[64,2048]{1,0:T(8,128)(2,1)S(1)} %shard_map.98), channel_id=1, source_target_pairs={{0,1},{1,0},{2,3},{3,2},{4,5},{5,4},{6,7},{7,6},{8,9},{9,8},{10,11... | collective-permute-start | bytes 786440 | tf_op jit(solution)/shard_map/ppermute | solution.py:632
  18.4 4.0 %collective-permute-done.edge_ref = bf16[40,4096]{1,0:T(8,128)(2,1)S(1)} collective-permute-done((bf16[40,4096]{1,0:T(8,128)(2,1)S(1)}, bf16[40,4096]{1,0:T(8,128)(2,1)S(1)}, u32[]{:S(2)}, u32[]{:S(2)}) %collective-permute-start) | collective-permute-done | bytes 327712 | tf_op jit(solution)/shard_map/ppermute | solution.py:627
  22.4 0.8 %shard_map.96 = bf16[64,2048]{1,0:T(8,128)(2,1)S(1)} custom-call(s32[1]{0:T(128)S(6)} %sub.4.side_ref, bf16[40,4096]{1,0:T(8,128)(2,1)S(1)} %collective-permute-done.edge_ref, bf16[256,1024]{1,0:T(8,128)(2,1)S(1)} %get-tuple-element.23.column_ref, bf16[128,128]{1,0:T(8,128)(2,1)S(1)} %get-tuple-element.24.row_ref, f32[64,4096]{1,0:T(8,128)S(1)} %get-tuple-element.28.part_ref), custom_call_target="tpu_custom_call" | custom-call | tf_op jit(solution)/shard_map/pallas_call | solution.py:409
  23.2 0.1 collective-permute-start.1
  23.2 0.8 %shard_map.95.refs_0_.refs_3_ = bf16[64,2048]{1,0:T(8,128)(2,1)S(1)} custom-call(s32[1]{0:T(128)} %bitcast.side_ref, bf16[40,4096]{1,0:T(8,128)(2,1)S(1)} %collective-permute-done.edge_ref, bf16[256,1024]{1,0:T(8,128)(2,1)S(1)} %get-tuple-element.23.column_ref, bf16[128,128]{1,0:T(8,128)(2,1)S(1)} %get-tuple-element.24.row_ref, ...), custom_call_target="tpu_custom_call" | custom-call | tf_op jit(solution)/shard_map/pallas_call | solution.py:409
  24.0 0.8 %shard_map.97.refs_0_ = bf16[64,2048]{1,0:T(8,128)(2,1)S(1)} custom-call(s32[1]{0:T(128)} %bitcast.side_ref, bf16[40,4096]{1,0:T(8,128)(2,1)S(1)} %collective-permute-done.3.edge_ref, bf16[256,1024]{1,0:T(8,128)(2,1)S(1)} %get-tuple-element.23.column_ref, bf16[128,128]{1,0:T(8,128)(2,1)S(1)} %get-tuple-element.33.row_ref, ...), custom_call_target="tpu_custom_call" | custom-call | tf_op jit(solution)/shard_map/pallas_call | solution.py:409
  24.8 0.0 collective-permute-done.2.refs_1_
  24.8 0.4 norms.1
  25.2 0.0 collective-permute-done.4.refs_1_
  25.3 0.5 %residual.1 = (f32[128,2048]{1,0:T(8,128)S(1)}, f32[64,128]{1,0:T(8,128)S(1)}) custom-call(s32[1]{0:T(128)} %bitcast.side_ref, bf16[64,2048]{1,0:T(8,128)(2,1)S(1)} %shard_map.97.refs_0_, bf16[64,2048]{1,0:T(8,128)(2,1)S(1)} %collective-permute-done.4.refs_1_, f32[256,2048]{1,0:T(8,128)S(1)} %get-tuple-element.30.refs_2_, ...), custom_call_target="tpu_custom_call" | custom-call | tf_op jit(solution)/shard_map/residual/pallas_call | solution.py:530
  25.8 0.0 collective-permute-done.1.refs_1_.refs_4_
  25.8 0.5 %residual_last.1 = (f32[128,2048]{1,0:T(8,128)S(1)}, f32[2,8,128]{2,1,0:T(8,128)S(1)}) custom-call(s32[1]{0:T(128)} %bitcast.side_ref, bf16[64,2048]{1,0:T(8,128)(2,1)S(1)} %shard_map.95.refs_0_.refs_3_, bf16[64,2048]{1,0:T(8,128)(2,1)S(1)} %collective-permute-done.1.refs_1_.refs_4_, f32[256,2048]{1,0:T(8,128)S(1)} %get-tuple-element.30.refs_2_, ...), custom_call_target="tpu_custom_call" | custom-call | tf_op jit(solution)/shard_map/residual_last/pallas_call | solution.py:530
  26.3 3.5 %collective-permute-start.7 = (f32[2,8,128]{2,1,0:T(8,128)S(1)}, f32[2,8,128]{2,1,0:T(8,128)S(1)}, u32[]{:S(2)}, u32[]{:S(2)}) collective-permute-start(f32[2,8,128]{2,1,0:T(8,128)S(1)} %get-tuple-element.37), channel_id=1, source_target_pairs={{0,6},{1,7},{2,4},{3,5},{4,2},{5,3},{6,0},{7,1},{8,14},{9,15},{10,... | collective-permute-start | bytes 24584 | tf_op jit(solution)/shard_map/ppermute | solution.py:647
  29.8 0.3 collective-permute-start.6
  30.1 0.1 collective-permute-start.5
  30.2 1.3 %collective-permute-done.7 = f32[2,8,128]{2,1,0:T(8,128)S(1)} collective-permute-done((f32[2,8,128]{2,1,0:T(8,128)S(1)}, f32[2,8,128]{2,1,0:T(8,128)S(1)}, u32[]{:S(2)}, u32[]{:S(2)}) %collective-permute-start.7) | collective-permute-done | bytes 8224 | tf_op jit(solution)/shard_map/ppermute | solution.py:647
  31.4 1.4 %collective-permute-done.6 = f32[2,8,128]{2,1,0:T(8,128)S(1)} collective-permute-done((f32[2,8,128]{2,1,0:T(8,128)S(1)}, f32[2,8,128]{2,1,0:T(8,128)S(1)}, u32[]{:S(2)}, u32[]{:S(2)}) %collective-permute-start.6) | collective-permute-done | bytes 8224 | tf_op jit(solution)/shard_map/ppermute | solution.py:646
  32.9 0.3 collective-permute-done.5
  33.1 2.5 %collective-permute-start.8 = (f32[2,8,128]{2,1,0:T(8,128)S(1)}, f32[2,8,128]{2,1,0:T(8,128)S(1)}, u32[]{:S(2)}, u32[]{:S(2)}) collective-permute-start(f32[2,8,128]{2,1,0:T(8,128)S(1)} %add_add_fusion), channel_id=1, source_target_pairs={{0,9},{1,8},{2,11},{3,10},{4,13},{5,12},{6,15},{7,14},{8,1},{9,0},... | collective-permute-start | bytes 24584 | tf_op jit(solution)/shard_map/ppermute | solution.py:644
  35.6 1.5 %collective-permute-done.8 = f32[2,8,128]{2,1,0:T(8,128)S(1)} collective-permute-done((f32[2,8,128]{2,1,0:T(8,128)S(1)}, f32[2,8,128]{2,1,0:T(8,128)S(1)}, u32[]{:S(2)}, u32[]{:S(2)}) %collective-permute-start.8) | collective-permute-done | bytes 8224 | tf_op jit(solution)/shard_map/ppermute | solution.py:644
  37.1 0.3 collective-permute-start.9
  37.4 0.9 %collective-permute-done.9 = f32[2,8,128]{2,1,0:T(8,128)S(1)} collective-permute-done((f32[2,8,128]{2,1,0:T(8,128)S(1)}, f32[2,8,128]{2,1,0:T(8,128)S(1)}, u32[]{:S(2)}, u32[]{:S(2)}) %collective-permute-start.9) | collective-permute-done | bytes 8224 | tf_op jit(solution)/shard_map/ppermute | solution.py:653
  38.3 1.1 %final.1 = (f32[32,2048]{1,0:T(8,128)}, f32[4]{0:T(128)}) custom-call(s32[1]{0:T(128)} %bitcast.side_ref, f32[2,8,128]{2,1,0:T(8,128)S(1)} %add.19.sums_ref, bf16[64,2048]{1,0:T(8,128)(2,1)S(1)} %shard_map.97.refs_0_, bf16[64,2048]{1,0:T(8,128)(2,1)S(1)} %collective-permute-done.4.refs_1_, f32[128,2048]{1,0:T(8,128)S(1)} %get-tuple-element.38.refs_2_, ...), custom_call_target="tpu_custom_call" | custom-call | tf_op jit(solution)/shard_map/final/pallas_call | solution.py:589
  (3 shorter events, 0.0 us)
Async XLA Ops:
  2.0 9.6 %copy-start = (f32[16,8]{0,1:T(8,128)S(1)}, f32[16,8]{0,1:T(8,128)}, u32[]{:S(2)}) copy-start(f32[16,8]{0,1:T(8,128)} %param.13) | copy-start | bytes 1540
  2.0 9.6 %copy-start.1 = (bf16[8,21]{1,0:T(8,128)(2,1)S(1)}, bf16[8,21]{1,0:T(8,128)(2,1)}, u32[]{:S(2)}) copy-start(bf16[8,21]{1,0:T(8,128)(2,1)} %row_ref.1) | copy-start | bytes 1012
  2.0 9.6 %copy-start.2 = (bf16[8,21]{1,0:T(8,128)(2,1)S(1)}, bf16[8,21]{1,0:T(8,128)(2,1)}, u32[]{:S(2)}) copy-start(bf16[8,21]{1,0:T(8,128)(2,1)} %col_ref.1) | copy-start | bytes 1012
  2.0 9.6 %copy-start.3 = (s32[4]{0:T(128)S(1)}, s32[4]{0:T(128)}, u32[]{:S(2)}) copy-start(s32[4]{0:T(128)} %index_ref.1) | copy-start | bytes 52
  2.1 14.9 %collective-permute-start.3 = (bf16[40,4096]{1,0:T(8,128)(2,1)S(1)}, bf16[40,4096]{1,0:T(8,128)(2,1)S(1)}, u32[]{:S(2)}, u32[]{:S(2)}) collective-permute-start(bf16[40,4096]{1,0:T(8,128)(2,1)S(1)} %get-tuple-element.32), channel_id=1, source_target_pairs={{0,2},{2,4},{4,6},{6,8},{8,10},{10,12},{12,14},{1,3},{3,5},{5,7},{... | collective-permute-start | bytes 983048 | tf_op jit(solution)/shard_map/ppermute | solution.py:622
  8.9 16.0 %collective-permute-start.2 = (bf16[144,2048]{1,0:T(8,128)(2,1)S(1)}, bf16[144,2048]{1,0:T(8,128)(2,1)S(1)}, u32[]{:S(2)}, u32[]{:S(2)}) collective-permute-start(bf16[144,2048]{1,0:T(8,128)(2,1)S(1)} %get-tuple-element.21.refs_0_), channel_id=1, source_target_pairs={{0,1},{1,0},{2,3},{3,2},{4,5},{5,4},{6,7},{7,6},{8,9},{9,8},{10,11... | collective-permute-start | bytes 1769480 | tf_op jit(solution)/shard_map/ppermute | solution.py:624
  10.3 12.0 %collective-permute-start = (bf16[40,4096]{1,0:T(8,128)(2,1)S(1)}, bf16[40,4096]{1,0:T(8,128)(2,1)S(1)}, u32[]{:S(2)}, u32[]{:S(2)}) collective-permute-start(bf16[40,4096]{1,0:T(8,128)(2,1)S(1)} %get-tuple-element.22), channel_id=1, source_target_pairs={{2,0},{4,2},{6,4},{8,6},{10,8},{12,10},{14,12},{3,1},{5,3},{7,5},{... | collective-permute-start | bytes 983048 | tf_op jit(solution)/shard_map/ppermute | solution.py:627
  17.8 7.4 %collective-permute-start.4 = (bf16[64,2048]{1,0:T(8,128)(2,1)S(1)}, bf16[64,2048]{1,0:T(8,128)(2,1)S(1)}, u32[]{:S(2)}, u32[]{:S(2)}) collective-permute-start(bf16[64,2048]{1,0:T(8,128)(2,1)S(1)} %shard_map.98), channel_id=1, source_target_pairs={{0,1},{1,0},{2,3},{3,2},{4,5},{5,4},{6,7},{7,6},{8,9},{9,8},{10,11... | collective-permute-start | bytes 786440 | tf_op jit(solution)/shard_map/ppermute | solution.py:632
  23.2 2.6 %collective-permute-start.1 = (bf16[64,2048]{1,0:T(8,128)(2,1)S(1)}, bf16[64,2048]{1,0:T(8,128)(2,1)S(1)}, u32[]{:S(2)}, u32[]{:S(2)}) collective-permute-start(bf16[64,2048]{1,0:T(8,128)(2,1)S(1)} %shard_map.96), channel_id=1, source_target_pairs={{0,1},{1,0},{2,3},{3,2},{4,5},{5,4},{6,7},{7,6},{8,9},{9,8},{10,11... | collective-permute-start | bytes 786440 | tf_op jit(solution)/shard_map/ppermute | solution.py:637
  26.3 5.1 %collective-permute-start.7 = (f32[2,8,128]{2,1,0:T(8,128)S(1)}, f32[2,8,128]{2,1,0:T(8,128)S(1)}, u32[]{:S(2)}, u32[]{:S(2)}) collective-permute-start(f32[2,8,128]{2,1,0:T(8,128)S(1)} %get-tuple-element.37), channel_id=1, source_target_pairs={{0,6},{1,7},{2,4},{3,5},{4,2},{5,3},{6,0},{7,1},{8,14},{9,15},{10,... | collective-permute-start | bytes 24584 | tf_op jit(solution)/shard_map/ppermute | solution.py:647
  29.8 3.1 %collective-permute-start.6 = (f32[2,8,128]{2,1,0:T(8,128)S(1)}, f32[2,8,128]{2,1,0:T(8,128)S(1)}, u32[]{:S(2)}, u32[]{:S(2)}) collective-permute-start(f32[2,8,128]{2,1,0:T(8,128)S(1)} %get-tuple-element.37), channel_id=1, source_target_pairs={{0,5},{1,4},{2,7},{3,6},{4,1},{5,0},{6,3},{7,2},{8,13},{9,12},{10,... | collective-permute-start | bytes 24584 | tf_op jit(solution)/shard_map/ppermute | solution.py:646
  30.1 3.1 %collective-permute-start.5 = (f32[2,8,128]{2,1,0:T(8,128)S(1)}, f32[2,8,128]{2,1,0:T(8,128)S(1)}, u32[]{:S(2)}, u32[]{:S(2)}) collective-permute-start(f32[2,8,128]{2,1,0:T(8,128)S(1)} %get-tuple-element.37), channel_id=1, source_target_pairs={{0,3},{1,2},{2,1},{3,0},{4,7},{5,6},{6,5},{7,4},{8,11},{9,10},{10,... | collective-permute-start | bytes 24584 | tf_op jit(solution)/shard_map/ppermute | solution.py:644
  33.1 4.0 %collective-permute-start.8 = (f32[2,8,128]{2,1,0:T(8,128)S(1)}, f32[2,8,128]{2,1,0:T(8,128)S(1)}, u32[]{:S(2)}, u32[]{:S(2)}) collective-permute-start(f32[2,8,128]{2,1,0:T(8,128)S(1)} %add_add_fusion), channel_id=1, source_target_pairs={{0,9},{1,8},{2,11},{3,10},{4,13},{5,12},{6,15},{7,14},{8,1},{9,0},... | collective-permute-start | bytes 24584 | tf_op jit(solution)/shard_map/ppermute | solution.py:644
  37.1 1.2 %collective-permute-start.9 = (f32[2,8,128]{2,1,0:T(8,128)S(1)}, f32[2,8,128]{2,1,0:T(8,128)S(1)}, u32[]{:S(2)}, u32[]{:S(2)}) collective-permute-start(f32[2,8,128]{2,1,0:T(8,128)S(1)} %add.18), channel_id=1, source_target_pairs={{0,1},{1,0},{2,3},{3,2},{4,5},{5,4},{6,7},{7,6},{8,9},{9,8},{10,11... | collective-permute-start | bytes 24584 | tf_op jit(solution)/shard_map/ppermute | solution.py:653
